TPU v7x, 256 devices: a whole 4x4x8 slice. The times are simulated.
256 devices in a mesh: dp: 32 (over y, z_hi, core), seq: 8 (over x, z_lo).
Axes of the slice: x: 4, y: 4, z: 8 (z_hi: 4, z_lo: 2; z = z_hi * 2 + z_lo), core: 2. Of those that a mesh axis runs over, the one named last changes fastest.
Arguments:
- qkv_input: bfloat16 [32768, 3, 3072], P(('dp', 'seq')), may hold values from -40 to 40
- latents: bfloat16 [32768, 3072], P(('dp', 'seq')), may hold values from -0.29882812 to 0.29882812
- cotangent: bfloat16 [32768, 3072], P(('dp', 'seq')), may hold values from -6 to 6
- out_weight: bfloat16 [3072, 3072], P('seq', 'dp'), may hold values from -0.109375 to 0.109375
- gate_table: float32 [64, 3072], replicated, may hold values from -8 to 8
- timesteps: int32 [32, 3], P('dp'), may hold values from 0 to 63
- frames: int32 [32, 3], P('dp'), may hold values from 1 to 10, 16 in all within a row
Outputs:
- output: bfloat16 [32768, 3072], P(('dp', 'seq'))
- grad_qkv: bfloat16 [32768, 3, 3072], P(('dp', 'seq'))
- grad_weight: float32 [3072, 3072], P('seq', 'dp')
Inputs may be any that keep to these rules, and one draw needn't show every extreme that they name: Each pack's 3 clips cover its 16 frames exactly; in every pack the longest clip has 10 frames.
All inputs are finite; a program needn't handle non-finite values.
Results may differ from a plain program's by a relative error of at most 0.019.
Values may be sent and summed in bfloat16 or wider, within the bound.
No kernel may reach another device: no remote copies, remote signals or barrier semaphores. Data moves between devices by JAX's collectives and lax.ppermute only.
A program may use at most 192 MiB of HBM per device.

v0:
```python
import jax
import jax.numpy as jnp
from jax import lax
from jax.sharding import PartitionSpec as P

HD = 128
FRAME_TOK = 64


def clip_index(frame_row, start, count):
    ends = jnp.cumsum(frame_row) * FRAME_TOK
    places = start + jnp.arange(count, dtype=jnp.int32)
    return jnp.sum((places[:, None] >= ends[None, :]).astype(jnp.int32), axis=1)


def token_gate(frame_row, step_row, table, start, count):
    bins = jnp.arange(table.shape[0], dtype=jnp.int32)
    pick = (step_row[:, None] == bins[None, :]).astype(jnp.float32)
    clip_rows = jnp.dot(pick, table, precision=lax.Precision.HIGHEST)
    which = clip_index(frame_row, start, count)
    member = (which[:, None] == jnp.arange(frame_row.shape[0], dtype=jnp.int32)[None, :]).astype(
        jnp.float32
    )
    return jnp.dot(member, clip_rows, precision=lax.Precision.HIGHEST)


def attend(query, keys, values, which):
    rows = query.shape[0]
    count = query.shape[1] // HD
    qf = query.reshape(rows, count, HD).astype(jnp.float32)
    kf = keys.reshape(rows, count, HD).astype(jnp.float32)
    vf = values.reshape(rows, count, HD).astype(jnp.float32)
    scores = jnp.einsum("qhd,khd->hqk", qf, kf) / jnp.sqrt(jnp.float32(HD))
    same = which[:, None] == which[None, :]
    scores = jnp.where(same[None], scores, jnp.float32(-1e30))
    top = jnp.max(scores, axis=-1, keepdims=True)
    expo = jnp.exp(scores - top)
    probs = expo / jnp.sum(expo, axis=-1, keepdims=True)
    probs_b = probs.astype(jnp.bfloat16)
    mixed = jnp.einsum("hqk,khd->qhd", probs_b.astype(jnp.float32), vf)
    return mixed.reshape(rows, count * HD)


def body(qkv_input, latents, cotangent, out_weight, gate_table, timesteps, frames):
    tok_rows = latents.shape[0]
    seq_count = lax.axis_size("seq")
    pack_rows = tok_rows * seq_count
    frame_row = frames[0]
    step_row = timesteps[0]
    heads = lax.all_to_all(qkv_input, "seq", split_axis=2, concat_axis=0, tiled=True)
    which = clip_index(frame_row, 0, pack_rows)
    attn_f, back = jax.vjp(
        lambda a, b, c: attend(a, b, c, which), heads[:, 0], heads[:, 1], heads[:, 2]
    )
    attn = attn_f.astype(jnp.bfloat16)
    w_rows = lax.all_gather(out_weight, "dp", axis=1, tiled=True)
    my_start = lax.axis_index("seq") * tok_rows
    gate_mine = token_gate(frame_row, step_row, gate_table, my_start, tok_rows)
    part = jnp.dot(attn, w_rows, preferred_element_type=jnp.float32).astype(jnp.bfloat16)
    part = lax.optimization_barrier(part)
    proj = lax.psum_scatter(
        part.astype(jnp.float32).astype(jnp.bfloat16), "seq", scatter_dimension=0, tiled=True
    ).astype(jnp.float32)
    output = (latents.astype(jnp.float32) + gate_mine * proj).astype(jnp.bfloat16)
    dproj = (gate_mine * cotangent.astype(jnp.float32)).astype(jnp.bfloat16)
    piece = lax.all_gather(dproj, "seq", axis=0, tiled=True)
    d_weight = jnp.einsum("th,td->hd", attn, piece, preferred_element_type=jnp.float32)
    update = jnp.einsum("td,hd->th", piece, w_rows, preferred_element_type=jnp.float32)
    d_attn = update
    d_attn, d_weight = (d_attn, d_weight)
    grad_weight = lax.psum_scatter(
        d_weight.astype(jnp.bfloat16), "dp", scatter_dimension=1, tiled=True
    ).astype(jnp.float32)
    rounded = lax.optimization_barrier(d_attn.astype(jnp.bfloat16))
    grad_q, grad_k, grad_v = back(rounded.astype(jnp.float32))
    grads = jnp.stack([grad_q, grad_k, grad_v], axis=1)
    grad_qkv = lax.all_to_all(grads, "seq", split_axis=0, concat_axis=2, tiled=True)
    return (output, grad_qkv, grad_weight)


def solution(mesh):
    placed = (
        P(("dp", "seq"), None, None),
        P(("dp", "seq"), None),
        P(("dp", "seq"), None),
        P("seq", "dp"),
        P(),
        P("dp", None),
        P("dp", None),
    )
    return jax.shard_map(
        body,
        mesh=mesh,
        in_specs=placed,
        out_specs=(P(("dp", "seq"), None), P(("dp", "seq"), None, None), P("seq", "dp")),
        check_vma=False,
    )
```

profile of v0, /device:TPU:32, one launch (start us, length us, event | category | flops | bytes accessed | tf_op | source)
XLA Modules:
  0.0 484.9 jit_solution(12294228111605507791)
XLA Ops:
  10.1 3.4 multiply_convert_fusion
  13.5 3.6 copy.44
  17.1 6.2 %all-to-all-start = ((bf16[128,3,3072]{0,1,2:T(4,128)(2,1)}), bf16[128,3,3072]{0,1,2:T(4,128)(2,1)}, u32[]{:S(2)}, u32[]{:S(2)}) async-start(bf16[128,3,3072]{0,1,2:T(4,128)(2,1)} %copy.44), calls=%async_computation | async-start | bytes 6291456 | tf_op jit(solution)/shard_map/all_to_all | solution.py:50
  23.4 1.6 broadcast_compare_fusion
  25.0 44.3 %all-to-all-done = bf16[128,3,3072]{0,1,2:T(4,128)(2,1)} async-done(((bf16[128,3,3072]{0,1,2:T(4,128)(2,1)}), bf16[128,3,3072]{0,1,2:T(4,128)(2,1)}, u32[]{:S(2)}, u32[]{:S(2)}) %all-to-all-start) | async-done | bytes 2359328 | tf_op jit(solution)/shard_map/all_to_all | solution.py:50
  69.4 5.2 %copy.66 = bf16[128,3,8,384]{0,2,3,1:T(8,128)(2,1)} copy(bf16[128,3,8,384]{0,1,3,2:T(4,128)(2,1)} %bitcast.3) | data formatting | bytes 4718592 | tf_op jit(solution)/shard_map/all_to_all | solution.py:50
  74.6 3.6 all_to_all.29
  78.5 7.7 %fusion.5 = (f32[3,1024]{1,0:T(4,128)S(1)}, f32[3,1024,1024]{1,2,0:T(8,128)}) fusion(pred[1024,1024]{0,1:T(8,128)(4,1)} %broadcast_compare_fusion, bf16[1024,3,128]{0,2,1:T(8,128)(2,1)S(1)} %bitcast.65, bf16[1024,3,128]{0,2,1:T(8,128)(2,1)S(1)} %bitcast.63), kind=kOutput, calls=%fused_computation.12 | convolution fusion | flops 814740480 | bytes 15216640 | tf_op jit(solution)/shard_map/jvp(qhd,khd->hqk)/dot_general | solution.py:33
  86.2 7.4 %fusion.16 = f32[3,1024]{1,0:T(4,128)S(1)} fusion(f32[3,1024]{1,0:T(4,128)S(1)} %get-tuple-element.12, f32[3,1024,1024]{1,2,0:T(8,128)} %get-tuple-element.13, pred[1024,1024]{0,1:T(8,128)(4,1)S(1)} %copy-done.3), kind=kLoop, calls=%fused_computation.29 | loop fusion | flops 12579840 | bytes 13656064 | tf_op jit(solution)/shard_map/jvp()/reduce_sum | solution.py:38
  93.6 109.5 %all-gather.5.cloned.1.call-done = bf16[1024,3072]{1,0:T(8,128)(2,1)} async-done(((bf16[128,3072]{1,0:T(8,128)(2,1)}), bf16[1024,3072]{1,0:T(8,128)(2,1)}) %all-gather.5.cloned.1.call-update) | async-done | bytes 6291472 | tf_op jit(solution)/shard_map/all_gather | solution.py:66
  203.1 7.0 %convolution_convert_fusion.5 = bf16[1024,384]{1,0:T(8,128)(2,1)S(1)} fusion(bf16[1024,3072]{1,0:T(8,128)(2,1)} %all-gather.5.cloned.1.call-done, bf16[384,3072]{0,1:T(8,128)(2,1)} %all-gather.3.cloned.1.call-done), kind=kOutput, calls=%fused_computation.36 | convolution fusion | flops 2416312320 | bytes 9437184 | tf_op jit(solution)/shard_map/td,hd->th/dot_general | solution.py:68
  210.4 14.7 %convert_reduce_fusion = (f32[3,1024]{1,0:T(4,128)S(1)}, pred[3,1024,1024]{1,2,0:T(32,128)(4,1)}, f32[3,1024]{1,0:T(4,128)S(1)}, bf16[3,1024,1024]{1,2,0:T(8,128)(2,1)}) fusion(f32[3,1024]{1,0:T(4,128)S(1)} %get-tuple-element.12, f32[3,1024,1024]{1,2,0:T(8,128)} %get-tuple-element.13, pred[1024,1024]{0,1:T(8,128)(4,1)S(1)} %copy-done.3, ...), kind=kOutput, calls=%fused_computation.7 | convolution fusion | flops 839903232 | bytes 24690688 | tf_op jit(solution)/shard_map/transpose(jvp(hqk,khd->qhd))/dot_general | solution.py:40
  225.2 10.3 %fusion.27 = (f32[3,1024]{1,0:T(4,128)S(1)}, f32[3,1024,1024]{1,2,0:T(8,128)}, bf16[3,1024,1024]{1,2,0:T(8,128)(2,1)S(1)}) fusion(f32[3,1024]{1,0:T(4,128)S(1)} %get-tuple-element.12, f32[3,1024,1024]{1,2,0:T(8,128)S(1)} %bitcast.56, pred[1024,1024]{0,1:T(8,128)(4,1)S(1)} %copy-done.3, f32[3,1024]{1,0:T(4,128)S(1)} %neg.9, f32[3,1024]{1,0:T(4,128)S(1)} %fusion.16, ...), kind=kLoop, calls=%fused_computation.54 | loop fusion | flops 31454208 | bytes 38846464 | tf_op jit(solution)/shard_map/transpose(jvp())/reduce_sum | solution.py:37
  235.5 2.6 copy-done.2
  238.1 1.0 convolution_convert_fusion.3
  239.1 7.7 %convolution_convert_fusion.1 = bf16[384,3072]{0,1:T(8,128)(2,1)} fusion(bf16[1024,384]{0,1:T(8,128)(2,1)S(1)} %bitcast.69, bf16[1024,3072]{1,0:T(8,128)(2,1)} %all-gather.5.cloned.1.call-done), kind=kOutput, calls=%fused_computation.24 | convolution fusion | flops 2417098752 | bytes 9437184 | tf_op jit(solution)/shard_map/th,td->hd/dot_general | solution.py:67
  246.9 7.1 %convolution_convert_fusion = bf16[1024,3072]{1,0:T(8,128)(2,1)} fusion(bf16[1024,384]{0,1:T(8,128)(2,1)S(1)} %bitcast.70, bf16[384,3072]{0,1:T(8,128)(2,1)} %all-gather.3.cloned.1.call-done), kind=kOutput, calls=%fused_computation.23 | convolution fusion | flops 2419064832 | bytes 9437184 | tf_op jit(solution)/shard_map/dot_general | solution.py:59
  254.0 5.0 %convolution_convert_fusion.4 = bf16[3,128,1024]{2,1,0:T(8,128)(2,1)S(1)} fusion(bf16[3,128,1024]{2,1,0:T(8,128)(2,1)S(1)} %bitcast.61, bf16[3,1024,1024]{1,2,0:T(8,128)(2,1)} %copy-done.2), kind=kOutput, calls=%fused_computation.35 | convolution fusion | flops 805699584 | bytes 7864320 | tf_op jit(solution)/shard_map/transpose(jvp(hqk,khd->qhd))/dot_general | solution.py:40
  259.0 2.2 copy.56
  261.2 10.8 %fusion.18 = bf16[3,1024,128]{1,2,0:T(8,128)(2,1)} fusion(bf16[1024,3,128]{0,2,1:T(8,128)(2,1)} %bitcast.66, f32[3,1024,1024]{1,2,0:T(8,128)} %get-tuple-element.4, pred[3,1024,1024]{1,2,0:T(32,128)(4,1)} %get-tuple-element.6, f32[3,1024]{1,0:T(4,128)S(1)} %negate_divide_fusion, pred[1024,1024]{0,1:T(8,128)(4,1)S(1)} %copy-done.3), kind=kOutput, calls=%fused_computation.33 | convolution fusion | flops 818282496 | bytes 18362368 | tf_op jit(solution)/shard_map/transpose(jvp(qhd,khd->hqk))/dot_general | solution.py:33
  272.0 4.8 copy.55
  276.8 8.7 %fusion.17 = bf16[3,1024,128]{1,2,0:T(8,128)(2,1)} fusion(bf16[1024,3,128]{0,2,1:T(8,128)(2,1)S(1)} %bitcast.64, f32[3,1024,1024]{1,2,0:T(8,128)} %get-tuple-element.4, pred[3,1024,1024]{1,2,0:T(32,128)(4,1)} %get-tuple-element.6, f32[3,1024]{1,0:T(4,128)S(1)} %negate_divide_fusion, pred[1024,1024]{0,1:T(8,128)(4,1)S(1)} %copy-done.3), kind=kOutput, calls=%fused_computation.32 | convolution fusion | flops 818282496 | bytes 18362368 | tf_op jit(solution)/shard_map/transpose(jvp(qhd,khd->hqk))/dot_general | solution.py:33
  285.5 4.8 copy.54
  290.3 7.7 %pad_maximum_fusion = bf16[1024,3,384]{2,1,0:T(4,128)(2,1)} fusion(bf16[1024,1,384]{2,1,0:T(2,128)(2,1)S(1)} %copy.56, bf16[1024,1,384]{2,1,0:T(2,128)(2,1)} %copy.55, bf16[1024,1,384]{2,1,0:T(2,128)(2,1)} %copy.54), kind=kLoop, calls=%fused_computation.26 | loop fusion | flops 7077888 | bytes 4718592 | tf_op jit(solution)/shard_map/stack | solution.py:76
  298.0 5.4 %all-to-all-start.1 = ((bf16[1024,3,384]{2,1,0:T(4,128)(2,1)}), bf16[1024,3,384]{2,1,0:T(4,128)(2,1)}, u32[]{:S(2)}, u32[]{:S(2)}) async-start(bf16[1024,3,384]{2,1,0:T(4,128)(2,1)} %pad_maximum_fusion), calls=%async_computation.2 | async-start | bytes 6291456 | tf_op jit(solution)/shard_map/all_to_all | solution.py:77
  303.4 39.0 %reduce-scatter.5.cloned.1.call-done = bf16[384,96]{0,1:T(8,128)(2,1)} async-done(((bf16[384,3072]{0,1:T(8,128)(2,1)}), bf16[384,96]{0,1:T(8,128)(2,1)}) %reduce-scatter.5.cloned.1.call-update) | async-done | bytes 73744 | tf_op jit(solution)/shard_map/reduce_scatter | solution.py:71
  342.4 1.6 convert_element_type.104
  343.9 3.6 all-to-all-done.1
  347.6 3.8 copy.57
  351.3 2.5 all_to_all.33
  353.8 121.5 %reduce-scatter.3.cloned.1.call-done = bf16[128,3072]{1,0:T(8,128)(2,1)} async-done(((bf16[1024,3072]{1,0:T(8,128)(2,1)}), bf16[128,3072]{1,0:T(8,128)(2,1)}) %reduce-scatter.3.cloned.1.call-update) | async-done | bytes 786448 | tf_op jit(solution)/shard_map/reduce_scatter | solution.py:61
  475.3 3.0 add_convert_fusion
  (42 shorter events, 3.6 us)
Async XLA Ops:
  7.2 1.9 copy-start
  7.2 6.3 %copy-start.4 = (bf16[128,3,3072]{2,0,1:T(8,128)(2,1)S(1)}, bf16[128,3,3072]{2,0,1:T(8,128)(2,1)}, u32[]{:S(2)}) copy-start(bf16[128,3,3072]{2,0,1:T(8,128)(2,1)} %param.7) | copy-start | bytes 7077892
  7.2 86.4 %all-gather.3.cloned.1.call-start = ((), (), s32[]{:S(2)}) async-start(), calls=%async_computation.4 | async-start | bytes 2433024 | tf_op jit(solution)/shard_map/all_gather | solution.py:56
  7.9 195.2 %all-gather.5.cloned.1.call-start = ((), (), s32[]{:S(2)}) async-start(), calls=%async_computation.6 | async-start | bytes 7077888 | tf_op jit(solution)/shard_map/all_gather | solution.py:66
  17.1 52.2 %all-to-all-start = ((bf16[128,3,3072]{0,1,2:T(4,128)(2,1)}), bf16[128,3,3072]{0,1,2:T(4,128)(2,1)}, u32[]{:S(2)}, u32[]{:S(2)}) async-start(bf16[128,3,3072]{0,1,2:T(4,128)(2,1)} %copy.44), calls=%async_computation | async-start | bytes 6291456 | tf_op jit(solution)/shard_map/all_to_all | solution.py:50
  23.3 319.1 %reduce-scatter.5.cloned.1.call-start = ((), (), s32[]{:S(2)}) async-start(), calls=%async_computation.7 | async-start | bytes 2433024 | tf_op jit(solution)/shard_map/reduce_scatter | solution.py:71
  78.5 7.7 %copy-start.5 = (bf16[1024,1,384]{0,2,1:T(8,128)(2,1)}, bf16[1024,1,384]{0,2,1:T(8,128)(2,1)S(1)}, u32[]{:S(2)}) copy-start(bf16[1024,1,384]{0,2,1:T(8,128)(2,1)S(1)} %get-tuple-element.9) | copy-start | bytes 2359300
  78.5 7.7 %copy-start.7 = (bf16[1024,1,384]{0,2,1:T(8,128)(2,1)}, bf16[1024,1,384]{0,2,1:T(8,128)(2,1)S(1)}, u32[]{:S(2)}) copy-start(bf16[1024,1,384]{0,2,1:T(8,128)(2,1)S(1)} %get-tuple-element.11) | copy-start | bytes 2359300
  78.5 7.7 %copy-start.3 = (pred[1024,1024]{0,1:T(8,128)(4,1)S(1)}, pred[1024,1024]{0,1:T(8,128)(4,1)}, u32[]{:S(2)}) copy-start(pred[1024,1024]{0,1:T(8,128)(4,1)} %broadcast_compare_fusion) | copy-start | bytes 3145732
  210.4 14.7 %slice-start = ((s8[12582912]{0:T(1024)(128)(4,1)}), s8[4194304]{0:T(1024)(128)(4,1)S(1)}, s32[]{:S(2)}) async-start(s8[12582912]{0:T(1024)(128)(4,1)} %bitcast.55), calls=%async_computation.8 | async-start | bytes 8388608
  210.4 14.7 %slice-start.1 = ((s8[12582912]{0:T(1024)(128)(4,1)}), s8[4194304]{0:T(1024)(128)(4,1)S(1)}, s32[]{:S(2)}) async-start(s8[12582912]{0:T(1024)(128)(4,1)} %bitcast.55), calls=%async_computation.9 | async-start | bytes 8388608
  210.4 14.7 %slice-start.2 = ((s8[12582912]{0:T(1024)(128)(4,1)}), s8[4194304]{0:T(1024)(128)(4,1)S(1)}, s32[]{:S(2)}) async-start(s8[12582912]{0:T(1024)(128)(4,1)} %bitcast.55), calls=%async_computation.10 | async-start | bytes 8388608
  235.5 2.6 copy-start.2
  246.8 228.5 %reduce-scatter.3.cloned.1.call-start = ((), (), s32[]{:S(2)}) async-start(), calls=%async_computation.5 | async-start | bytes 7077888 | tf_op jit(solution)/shard_map/reduce_scatter | solution.py:61
  261.2 15.6 %copy-start.6 = (bf16[1024,1,384]{0,2,1:T(8,128)(2,1)S(1)}, bf16[1024,1,384]{0,2,1:T(8,128)(2,1)}, u32[]{:S(2)}) copy-start(bf16[1024,1,384]{0,2,1:T(8,128)(2,1)} %copy-done.5) | copy-start | bytes 2359300
  298.0 49.6 %all-to-all-start.1 = ((bf16[1024,3,384]{2,1,0:T(4,128)(2,1)}), bf16[1024,3,384]{2,1,0:T(4,128)(2,1)}, u32[]{:S(2)}, u32[]{:S(2)}) async-start(bf16[1024,3,384]{2,1,0:T(4,128)(2,1)} %pad_maximum_fusion), calls=%async_computation.2 | async-start | bytes 6291456 | tf_op jit(solution)/shard_map/all_to_all | solution.py:77
  347.6 130.8 %copy-start.1 = (f32[64,3072]{1,0:T(8,128)S(1)}, f32[64,3072]{1,0:T(8,128)}, u32[]{:S(2)}) copy-start(f32[64,3072]{1,0:T(8,128)} %param.11) | copy-start | bytes 2359300
Sparse Core Ops, SparseCore 0:
  10.6 59.6 all-gather.2
  72.6 130.4 all-gather.4
  246.9 95.3 reduce-scatter.4
  345.0 130.3 reduce-scatter.2
where the time goes:
time: 487 us; the launch traced here: 485 us
  waiting for transfers between devices  319 us (66%)
  matrix products  74 us (15%)
  local copies, waits for them, and re-layouts  33.6 us (7%)
  other arithmetic  32.8 us (7%)
  between operations  14 us (3%)
  starting transfers between devices  11.7 us (2%)
    reduce_scatter x1, waiting for transfers between devices, body(): lax.psum_scatter(part.astype(jnp.float32).astype(jnp.bfloat16), 'seq', sc...  122 us
    all_gather x1, waiting for transfers between devices, body(): piece = lax.all_gather(dproj, 'seq', axis=0, tiled=True)  110 us
    all_to_all x1, waiting for transfers between devices, body(): lax.all_to_all(qkv_input, 'seq', split_axis=2, concat_axis=0, tiled=True)  44.3 us
    reduce_scatter x1, waiting for transfers between devices, body(): lax.psum_scatter(d_weight.astype(jnp.bfloat16), 'dp', scatter_dimension=1...  39 us
    dot_general x3, matrix products, attend(): scores = jnp.einsum('qhd,khd->hqk', qf, kf) / jnp.sqrt(jnp.float32(HD))  27.2 us
    dot_general x3, matrix products, attend(): mixed = jnp.einsum('hqk,khd->qhd', probs_b.astype(jnp.float32), vf)  20.7 us
    reshape x3, local copies, waits for them, and re-layouts, body(): grads = jnp.stack([grad_q, grad_k, grad_v], axis=1)  11.8 us
    reduce_sum x1, other arithmetic, attend(): expo = jnp.exp(scores - top)  10.3 us
  transfers between devices with their start and end apart: 6, of which 5 were waited for; matrix products, arithmetic and copies ran while one was open for 18% of the time, Pallas kernels for 0%

commit v1 on v0

v1 whole, which is shorter than its diff:
```python
import jax
import jax.numpy as jnp
from jax import lax
from jax.experimental import pallas as pl
from jax.experimental.pallas import tpu as pltpu
from jax.sharding import PartitionSpec as P

HD = 128
FRAME = 64
LONG = 640
REST = 384
LOG2E = 1.4426950408889634
VMEM_LIMIT = 56 * 1024 * 1024

BF = jnp.bfloat16
F32 = jnp.float32


def dot_nt(a, b):
    return lax.dot_general(a, b, (((1,), (1,)), ((), ())), preferred_element_type=F32)


def dot_nn(a, b):
    return lax.dot_general(a, b, (((1,), (0,)), ((), ())), preferred_element_type=F32)


def dot_tn(a, b):
    return lax.dot_general(a, b, (((0,), (0,)), ((), ())), preferred_element_type=F32)


def clip_places(frames_ref):
    f0, f1, f2 = frames_ref[0, 0], frames_ref[0, 1], frames_ref[0, 2]
    first = jnp.logical_and(f0 > f1, f0 > f2)
    second = f1 > f2
    start = jnp.where(first, 0, jnp.where(second, f0, f0 + f1)) * FRAME
    lead = jnp.where(first, f1, f0)
    return start, lead


def gate_bins(frames_ref, steps_ref, seq_ref):
    f0, f1 = frames_ref[0, 0], frames_ref[0, 1]
    bins = []
    for k in range(2):
        frame = seq_ref[0] * 2 + k
        clip = jnp.where(frame >= f0, 1, 0) + jnp.where(frame >= f0 + f1, 1, 0)
        bins.append(steps_ref[0, clip])
    return bins


def spans(total):
    out, at = [], 0
    while at < total:
        size = min(256, total - at)
        out.append((at, size))
        at += size
    return out


def rest_places(start):
    return [
        pl.multiple_of(jnp.where(t * FRAME >= start, t * FRAME + LONG, t * FRAME), FRAME)
        for t in range(REST // FRAME)
    ]


def load_split(src, start):
    main = src[pl.ds(start, LONG), :]
    rest = jnp.concatenate([src[pl.ds(p, FRAME), :] for p in rest_places(start)], axis=0)
    return main, rest


def rest_mask(lead, at, size):
    rows = lax.broadcasted_iota(jnp.int32, (REST, size), 0)
    cols = lax.broadcasted_iota(jnp.int32, (REST, size), 1) + at
    edge = lead * FRAME
    return (rows < edge) == (cols < edge)


def fwd_kernel(frames_ref, qkv_ref, attn_ref, p1_ref, p2_ref, q_s, k_s, v_s):
    start, lead = clip_places(frames_ref)
    start = pl.multiple_of(start, FRAME)
    q_s[...] = qkv_ref[:, 0].reshape(1024, HD)
    k_s[...] = qkv_ref[:, 1].reshape(1024, HD)
    v_s[...] = qkv_ref[:, 2].reshape(1024, HD)
    factor = LOG2E / (HD**0.5)
    q1, q2 = load_split(q_s, start)
    k1, k2 = load_split(k_s, start)
    v1, v2 = load_split(v_s, start)
    places = rest_places(start)
    for long, (q, k, v, p_ref) in ((True, (q1, k1, v1, p1_ref)), (False, (q2, k2, v2, p2_ref))):
        vt = v.astype(F32).T.astype(BF)
        for at, size in spans(LONG if long else REST):
            s = dot_nt(k, q[at : at + size])
            if not long:
                s = jnp.where(rest_mask(lead, at, size), s, F32(-1e30))
            top = jnp.max(s, axis=0, keepdims=True)
            e = jnp.exp2((s - top) * F32(factor))
            total = jnp.sum(e, axis=0, keepdims=True)
            p = (e * (1.0 / total)).astype(BF)
            p_ref[0, :, at : at + size] = p
            o = dot_nn(vt, p).T.astype(BF)
            if long:
                attn_ref[pl.ds(start + at, size), :] = o
            else:
                for t in range(size // FRAME):
                    attn_ref[pl.ds(places[at // FRAME + t], FRAME), :] = o[
                        t * FRAME : (t + 1) * FRAME
                    ]


def attention_forward(frames, heads):
    return pl.pallas_call(
        fwd_kernel,
        out_shape=(
            jax.ShapeDtypeStruct((1024, 3 * HD), BF),
            jax.ShapeDtypeStruct((3, LONG, LONG), BF),
            jax.ShapeDtypeStruct((3, REST, REST), BF),
        ),
        grid_spec=pltpu.PrefetchScalarGridSpec(
            num_scalar_prefetch=1,
            grid=(3,),
            in_specs=[pl.BlockSpec((8, 3, 128, HD), lambda h, f: (0, 0, 0, h))],
            out_specs=(
                pl.BlockSpec((1024, HD), lambda h, f: (0, h)),
                pl.BlockSpec((1, LONG, LONG), lambda h, f: (h, 0, 0)),
                pl.BlockSpec((1, REST, REST), lambda h, f: (h, 0, 0)),
            ),
            scratch_shapes=[pltpu.VMEM((1024, HD), BF)] * 3,
        ),
        compiler_params=pltpu.CompilerParams(vmem_limit_bytes=VMEM_LIMIT),
        name="attention_forward",
    )(frames, heads)


def bwd_kernel(
    frames_ref, qkv_ref, own_ref, other_ref, p1_ref, p2_ref, out_ref, q_s, k_s, v_s, d_s, ds1, ds2, g_s
):
    start, lead = clip_places(frames_ref)
    start = pl.multiple_of(start, FRAME)
    q_s[...] = qkv_ref[:, 0].reshape(1024, HD)
    k_s[...] = qkv_ref[:, 1].reshape(1024, HD)
    v_s[...] = qkv_ref[:, 2].reshape(1024, HD)
    d_s[...] = (own_ref[...] + other_ref[...].astype(F32)).astype(BF)
    scale = 1.0 / (HD**0.5)
    q1, q2 = load_split(q_s, start)
    k1, k2 = load_split(k_s, start)
    v1, v2 = load_split(v_s, start)
    d1, d2 = load_split(d_s, start)
    places = rest_places(start)

    def put(which, long, value):
        if long:
            g_s[which, pl.ds(start, LONG), :] = value
        else:
            for t in range(REST // FRAME):
                g_s[which, pl.ds(places[t], FRAME), :] = value[t * FRAME : (t + 1) * FRAME]

    for long, (q, k, v, d, p_ref, ds_ref) in (
        (True, (q1, k1, v1, d1, p1_ref, ds1)),
        (False, (q2, k2, v2, d2, p2_ref, ds2)),
    ):
        kt = k.astype(F32).T.astype(BF)
        parts = []
        for at, size in spans(LONG if long else REST):
            dp = dot_nt(v, d[at : at + size]).astype(BF).astype(F32)
            p = p_ref[0, :, at : at + size].astype(F32)
            pd = p * dp
            delta = jnp.sum(pd, axis=0, keepdims=True)
            ds = ((pd - p * delta) * F32(scale)).astype(BF)
            ds_ref[:, at : at + size] = ds
            parts.append(dot_nn(kt, ds).T.astype(BF))
        put(0, long, jnp.concatenate(parts, axis=0))
        put(1, long, dot_nn(ds_ref[...], q).astype(BF))
        put(2, long, dot_nn(p_ref[0], d).astype(BF))
    for which in range(3):
        out_ref[:, which] = g_s[which].reshape(8, 128, HD)


def attention_backward(frames, heads, own, other, p1, p2):
    return pl.pallas_call(
        bwd_kernel,
        out_shape=jax.ShapeDtypeStruct((8, 3, 128, 3 * HD), BF),
        grid_spec=pltpu.PrefetchScalarGridSpec(
            num_scalar_prefetch=1,
            grid=(3,),
            in_specs=[
                pl.BlockSpec((8, 3, 128, HD), lambda h, f: (0, 0, 0, h)),
                pl.BlockSpec((1024, HD), lambda h, f: (0, h)),
                pl.BlockSpec((1024, HD), lambda h, f: (0, h)),
                pl.BlockSpec((1, LONG, LONG), lambda h, f: (h, 0, 0)),
                pl.BlockSpec((1, REST, REST), lambda h, f: (h, 0, 0)),
            ],
            out_specs=pl.BlockSpec((8, 3, 128, HD), lambda h, f: (0, 0, 0, h)),
            scratch_shapes=[pltpu.VMEM((1024, HD), BF)] * 4
            + [
                pltpu.VMEM((LONG, LONG), BF),
                pltpu.VMEM((REST, REST), BF),
                pltpu.VMEM((3, 1024, HD), BF),
            ],
        ),
        compiler_params=pltpu.CompilerParams(vmem_limit_bytes=VMEM_LIMIT),
        name="attention_backward",
    )(frames, heads, own, other, p1, p2)


def pack_kernel(in_ref, out_ref):
    out_ref[0] = in_ref[...]


def pack_heads(qkv):
    return pl.pallas_call(
        pack_kernel,
        out_shape=jax.ShapeDtypeStruct((8, 3, 128, 384), BF),
        grid=(8,),
        in_specs=[pl.BlockSpec((3, 128, 384), lambda j: (0, 0, j))],
        out_specs=pl.BlockSpec((1, 3, 128, 384), lambda j: (j, 0, 0, 0)),
        name="pack_heads",
    )(qkv)


def unpack_kernel(in_ref, out_ref):
    out_ref[...] = in_ref[0]


def unpack_heads(grads):
    return pl.pallas_call(
        unpack_kernel,
        out_shape=jax.ShapeDtypeStruct((3, 128, 3072), BF),
        grid=(8,),
        in_specs=[pl.BlockSpec((1, 3, 128, 384), lambda j: (j, 0, 0, 0))],
        out_specs=pl.BlockSpec((3, 128, 384), lambda j: (0, 0, j)),
        name="unpack_heads",
    )(grads)


def gated_kernel(frames_ref, steps_ref, seq_ref, table_ref, cot_ref, out_ref):
    b0, b1 = gate_bins(frames_ref, steps_ref, seq_ref)
    for k, b in enumerate((b0, b1)):
        rows = slice(k * FRAME, (k + 1) * FRAME)
        out_ref[0, rows, :] = (table_ref[pl.ds(b, 1), :] * cot_ref[rows, :].astype(F32)).astype(BF)


def gated_cotangent(frames, steps, seq, table, cotangent):
    return pl.pallas_call(
        gated_kernel,
        out_shape=jax.ShapeDtypeStruct((8, 128, 1536), BF),
        grid_spec=pltpu.PrefetchScalarGridSpec(
            num_scalar_prefetch=3,
            grid=(2, 4),
            in_specs=[
                pl.BlockSpec((64, 1536), lambda z, x, *_: (0, z)),
                pl.BlockSpec((128, 1536), lambda z, x, *_: (0, z)),
            ],
            out_specs=pl.BlockSpec((1, 128, 1536), lambda z, x, *_: (2 * x + z, 0, 0)),
        ),
        name="gated_cotangent",
    )(frames, steps, seq, table, cotangent)


def output_kernel(frames_ref, steps_ref, seq_ref, table_ref, lat_ref, part_ref, out_ref):
    b0, b1 = gate_bins(frames_ref, steps_ref, seq_ref)
    for k, b in enumerate((b0, b1)):
        rows = slice(k * FRAME, (k + 1) * FRAME)
        proj = part_ref[0, 0, rows, :].astype(F32)
        for x in range(1, 4):
            proj = proj + part_ref[x, 0, rows, :].astype(F32)
        out = lat_ref[rows, :].astype(F32) + table_ref[pl.ds(b, 1), :] * proj
        out_ref[rows, :] = out.astype(BF)


def gated_output(frames, steps, seq, table, latents, parts):
    return pl.pallas_call(
        output_kernel,
        out_shape=jax.ShapeDtypeStruct((128, 3072), BF),
        grid_spec=pltpu.PrefetchScalarGridSpec(
            num_scalar_prefetch=3,
            grid=(2, 2),
            in_specs=[
                pl.BlockSpec((64, 768), lambda z, n, *_: (0, 2 * z + n)),
                pl.BlockSpec((128, 768), lambda z, n, *_: (0, 2 * z + n)),
                pl.BlockSpec((4, 1, 128, 768), lambda z, n, *_: (0, z, 0, n)),
            ],
            out_specs=pl.BlockSpec((128, 768), lambda z, n, *_: (0, 2 * z + n)),
        ),
        name="gated_output",
    )(frames, steps, seq, table, latents, parts.reshape(4, 2, 128, 1536))


def dattn_kernel(d_ref, w_ref, out_ref):
    out_ref[...] = dot_nn(d_ref[...], w_ref[0]).astype(out_ref.dtype)


def dattn_part(dproj, weights, which, dtype):
    return pl.pallas_call(
        dattn_kernel,
        out_shape=jax.ShapeDtypeStruct((1024, 384), dtype),
        grid=(4,),
        in_specs=[
            pl.BlockSpec((256, 1536), lambda m: (m, 0)),
            pl.BlockSpec((1, 1536, 384), lambda m: (which, 0, 0)),
        ],
        out_specs=pl.BlockSpec((256, 384), lambda m: (m, 0)),
        name="dattn_part",
    )(dproj, weights)


def weave_kernel(core_ref, mine_ref, theirs_ref, out_ref):
    even = core_ref[0] == 0
    mine, theirs = mine_ref[...], theirs_ref[...]
    out_ref[:, 0] = jnp.where(even, mine, theirs)
    out_ref[:, 1] = jnp.where(even, theirs, mine)


def weave(core, mine, theirs):
    return pl.pallas_call(
        weave_kernel,
        out_shape=jax.ShapeDtypeStruct((16, 2, 96, 384), BF),
        grid_spec=pltpu.PrefetchScalarGridSpec(
            num_scalar_prefetch=1,
            grid=(4,),
            in_specs=[pl.BlockSpec((4, 96, 384), lambda n, c: (n, 0, 0))] * 2,
            out_specs=pl.BlockSpec((4, 2, 96, 384), lambda n, c: (n, 0, 0, 0)),
        ),
        name="weave",
    )(core, mine, theirs)


def proj_kernel(a0_ref, a1_ref, w_ref, out_ref):
    out_ref[...] = (dot_nt(a0_ref[...], w_ref[0]) + dot_nt(a1_ref[...], w_ref[1])).astype(BF)


def proj_part(own, other, weights):
    return pl.pallas_call(
        proj_kernel,
        out_shape=jax.ShapeDtypeStruct((1024, 1536), BF),
        grid=(4,),
        in_specs=[
            pl.BlockSpec((256, 384), lambda m: (m, 0)),
            pl.BlockSpec((256, 384), lambda m: (m, 0)),
            pl.BlockSpec((2, 1536, 384), lambda m: (0, 0, 0)),
        ],
        out_specs=pl.BlockSpec((256, 1536), lambda m: (m, 0)),
        compiler_params=pltpu.CompilerParams(vmem_limit_bytes=VMEM_LIMIT),
        name="proj_part",
    )(own, other, weights)


def dweight_kernel(core_ref, d_ref, a0_ref, a1_ref, keep_ref, send_ref):
    d = d_ref[...]
    even = core_ref[0] == 0
    for z, a_ref in enumerate((a0_ref, a1_ref)):
        g = dot_tn(d, a_ref[...]).astype(BF)
        for i in range(2):
            p0, p1 = g[i * 192 : i * 192 + 96], g[i * 192 + 96 : i * 192 + 192]
            keep_ref[z, i] = jnp.where(even, p0, p1)
            send_ref[z, i] = jnp.where(even, p1, p0)


def dweight_part(core, dproj, own, other):
    pieces = jax.ShapeDtypeStruct((2, 8, 96, 384), BF)
    return pl.pallas_call(
        dweight_kernel,
        out_shape=(pieces, pieces),
        grid_spec=pltpu.PrefetchScalarGridSpec(
            num_scalar_prefetch=1,
            grid=(4,),
            in_specs=[
                pl.BlockSpec((1024, 384), lambda n, c: (0, n)),
                pl.BlockSpec((1024, 384), lambda n, c: (0, 0)),
                pl.BlockSpec((1024, 384), lambda n, c: (0, 0)),
            ],
            out_specs=(
                pl.BlockSpec((2, 2, 96, 384), lambda n, c: (0, n, 0, 0)),
                pl.BlockSpec((2, 2, 96, 384), lambda n, c: (0, n, 0, 0)),
            ),
        ),
        compiler_params=pltpu.CompilerParams(vmem_limit_bytes=VMEM_LIMIT),
        name="dweight_part",
    )(core, dproj, own, other)


def piece_moves(dp_count, seq_count):
    half = dp_count // 2
    moves = []
    for dp in range(dp_count):
        for seq in range(seq_count):
            top, z = dp // half, seq % 2
            to_dp = (dp % half) + half * (z ^ top)
            to_seq = seq - z + top
            moves.append((dp * seq_count + seq, to_dp * seq_count + to_seq))
    return moves


def body(qkv_input, latents, cotangent, out_weight, gate_table, timesteps, frames):
    dp_count, seq_count = lax.axis_size("dp"), lax.axis_size("seq")
    seq = lax.axis_index("seq").astype(jnp.int32).reshape(1)
    both = ("dp", "seq")
    moves = piece_moves(dp_count, seq_count)
    swap = [(i, i ^ 1) for i in range(seq_count)]

    core = (lax.axis_index("dp") % 2).astype(jnp.int32).reshape(1)
    cores = [(i, i ^ 1) for i in range(dp_count)]
    same_core = [list(range(c, dp_count, 2)) for c in range(2)]

    piece = lax.ppermute(out_weight.T, both, moves)
    packed = pack_heads(qkv_input.transpose(1, 0, 2))
    packed, piece = lax.optimization_barrier((packed, piece))
    mine = lax.all_gather(piece, "dp", axis=0, axis_index_groups=same_core, tiled=False)
    heads = lax.all_to_all(packed, "seq", split_axis=0, concat_axis=0, tiled=True)

    gated = gated_cotangent(frames, timesteps, seq, gate_table, cotangent)
    gated, heads, mine = lax.optimization_barrier((gated, heads, mine))
    theirs = lax.ppermute(mine, "dp", cores)
    dproj = lax.all_to_all(gated, "seq", split_axis=0, concat_axis=0, tiled=True)
    dproj = dproj.reshape(1024, 1536)

    attn, p1, p2 = attention_forward(frames, heads)
    attn_other = lax.ppermute(attn, "seq", swap)
    weights = weave(core, mine, theirs).reshape(2, 1536, 384)

    part = proj_part(attn, attn_other, weights)
    parts = lax.all_to_all(
        part.reshape(8, 128, 1536), "seq", split_axis=0, concat_axis=0, tiled=True
    )
    dproj, part = lax.optimization_barrier((dproj, part))

    d_send = dattn_part(dproj, weights, 1, BF)
    d_recv = lax.ppermute(d_send, "seq", swap)
    d_own = dattn_part(dproj, weights, 0, F32)

    keep, send = dweight_part(core, dproj, attn, attn_other)
    got = lax.ppermute(send, "dp", cores)
    pair = (keep.astype(F32) + got.astype(F32)).astype(BF).reshape(16 * 96, 384)
    total = lax.psum_scatter(
        pair, "dp", scatter_dimension=0, axis_index_groups=same_core, tiled=True
    )

    grads = attention_backward(frames, heads, d_own, d_recv, p1, p2)
    grads = lax.all_to_all(grads, "seq", split_axis=0, concat_axis=0, tiled=True)

    output = gated_output(frames, timesteps, seq, gate_table, latents, parts)
    total = lax.ppermute(total, both, [(b, a) for a, b in moves])
    grad_weight = total.astype(F32).T
    grad_qkv = unpack_heads(grads).transpose(1, 0, 2)
    return (output, grad_qkv, grad_weight)


def solution(mesh):
    placed = (
        P(("dp", "seq"), None, None),
        P(("dp", "seq"), None),
        P(("dp", "seq"), None),
        P("seq", "dp"),
        P(),
        P("dp", None),
        P("dp", None),
    )
    return jax.shard_map(
        body,
        mesh=mesh,
        in_specs=placed,
        out_specs=(P(("dp", "seq"), None), P(("dp", "seq"), None, None), P("seq", "dp")),
        check_vma=False,
    )
```

time: 487 us -> 339 us (0.70)
  waiting for transfers between devices: 319 us -> 208 us
  matrix products: 74 us -> 0 us
  Pallas kernels: 0 us -> 72 us
  other arithmetic: 32.8 us -> 3.25 us
  local copies, waits for them, and re-layouts: 33.6 us -> 6.09 us
  starting transfers between devices: 11.7 us -> 34.3 us
    dot_general x11 -> x0, matrix products: 74 us -> none  [the longest x3 27.2 us: attend(): scores = jnp.einsum('qhd,khd->hqk', qf, kf) / jnp.sqrt(jnp.float32(HD))]
    reduce_scatter x2 -> x1, waiting for transfers between devices: 160 us -> 87.3 us  [body(): lax.psum_scatter(pair, 'dp', scatter_dimension=0, axis_index_groups=same_...]
    pallas_call x0 -> x11, Pallas kernels: none -> 72 us  [the longest x1 11.1 us: attention_backward(): pl.pallas_call(bwd_kernel, out_shape=jax.ShapeDtypeStruct((8, 3, 128, 3 *...]
    ppermute x0 -> x6, waiting for transfers between devices: none -> 69.3 us  [the longest x1 37.1 us: body(): attn_other = lax.ppermute(attn, 'seq', swap)]
    all_gather x2 -> x1, waiting for transfers between devices: 110 us -> 50.6 us  [body(): lax.all_gather(piece, 'dp', axis=0, axis_index_groups=same_core, tiled=Fa...]
    all_to_all x2 -> x4, waiting for transfers between devices: 48 us -> 0.01 us  [the longest x1 0.01 us: body(): lax.all_to_all(packed, 'seq', split_axis=0, concat_axis=0, tiled=True)]
    reduce_sum x4 -> x0, other arithmetic: 17.8 us -> none  [the longest x1 10.3 us: attend(): expo = jnp.exp(scores - top)]
    all_to_all x4 -> x0, local copies, waits for them, and re-layouts: 15.1 us -> none  [the longest x2 8.86 us: body(): lax.all_to_all(qkv_input, 'seq', split_axis=2, concat_axis=0, tiled=True)]
  transfers between devices with their start and end apart: 6 -> 12, of which waited for: 5 -> 4; matrix products, arithmetic and copies ran while one was open for 18% -> 1% of each run, Pallas kernels for 0% -> 20%
where the time goes in v1:
time: 339 us; the launch traced here: 338 us
  waiting for transfers between devices  208 us (61%)
  Pallas kernels  72 us (21%)
  starting transfers between devices  34.3 us (10%)
  between operations  14.1 us (4%)
  local copies, waits for them, and re-layouts  6.09 us (2%)
    reduce_scatter x1, waiting for transfers between devices, body(): lax.psum_scatter(pair, 'dp', scatter_dimension=0, axis_index_groups=same_...  87.3 us
    all_gather x1, waiting for transfers between devices, body(): lax.all_gather(piece, 'dp', axis=0, axis_index_groups=same_core, tiled=Fa...  50.6 us
    ppermute x1, waiting for transfers between devices, body(): attn_other = lax.ppermute(attn, 'seq', swap)  37.1 us
    ppermute x1, waiting for transfers between devices, body(): d_recv = lax.ppermute(d_send, 'seq', swap)  32.2 us
    pallas_call x1, Pallas kernels, attention_backward(): pl.pallas_call(bwd_kernel, out_shape=jax.ShapeDtypeStruct((8, 3, 128, 3 *...  11.1 us
    pallas_call x2, Pallas kernels, dattn_part(): pl.pallas_call(dattn_kernel, out_shape=jax.ShapeDtypeStruct((1024, 384),...  10.6 us
    pallas_call x1, Pallas kernels, attention_forward(): pl.pallas_call(fwd_kernel, out_shape=(jax.ShapeDtypeStruct((1024, 3 * HD)...  9.81 us
    pallas_call x1, Pallas kernels, proj_part(): pl.pallas_call(proj_kernel, out_shape=jax.ShapeDtypeStruct((1024, 1536),...  7.2 us
  transfers between devices with their start and end apart: 12, of which 4 were waited for; matrix products, arithmetic and copies ran while one was open for 1% of the time, Pallas kernels for 20%

profile of v1, /device:TPU:32, one launch (start us, length us, event | category | flops | bytes accessed | tf_op | source)
XLA Modules:
  0.0 337.6 jit_solution(17856702627967153389)
XLA Ops:
  7.2 4.6 %collective-permute-start = (bf16[96,384]{1,0:T(8,128)(2,1)}, bf16[96,384]{1,0:T(8,128)(2,1)S(1)}, u32[]{:S(2)}, u32[]{:S(2)}) collective-permute-start(bf16[96,384]{1,0:T(8,128)(2,1)} %bitcast.25), channel_id=1, source_target_pairs={{0,0},{1,128},{2,2},{3,130},{4,4},{5,132},{6,6},{7,134},{8,8},{9,1... | collective-permute-start | bytes 221192 | tf_op jit(solution)/shard_map/ppermute | solution.py:405
  11.8 5.8 %pack_heads.1 = bf16[8,3,128,384]{3,2,1,0:T(8,128)(2,1)} custom-call(bf16[3,128,3072]{2,1,0:T(8,128)(2,1)} %bitcast.21), custom_call_target="tpu_custom_call" | custom-call | tf_op jit(solution)/shard_map/pack_heads/pallas_call | solution.py:211
  17.6 0.6 copy-done.5
  18.2 5.8 %all-to-all-start = ((bf16[8,3,128,384]{3,2,1,0:T(8,128)(2,1)}), bf16[8,3,128,384]{3,2,1,0:T(8,128)(2,1)S(1)}, u32[]{:S(2)}, u32[]{:S(2)}) async-start(bf16[8,3,128,384]{3,2,1,0:T(8,128)(2,1)} %pack_heads.1), calls=%async_computation | async-start | bytes 4718592 | tf_op jit(solution)/shard_map/all_to_all | solution.py:409
  24.0 0.7 all-gather.3.cloned.1.call-update
  24.7 5.9 %gated_cotangent.1 = bf16[8,128,1536]{2,1,0:T(8,128)(2,1)} custom-call(s32[1,3]{1,0:T(1,128)} %frames_ref.7, s32[1,3]{1,0:T(1,128)} %steps_ref.3, s32[1]{0:T(128)} %bitcast.seq_ref, f32[64,3072]{1,0:T(8,128)} %table_ref.3, bf16[128,3072]{1,0:T(8,128)(2,1)} %cot_ref.1), custom_call_target="tpu_custom_call" | custom-call | tf_op jit(solution)/shard_map/gated_cotangent/pallas_call | solution.py:244
  30.6 50.6 %all-gather.3.cloned.1.call-done = bf16[1536,384]{1,0:T(8,128)(2,1)} async-done(((bf16[96,384]{1,0:T(8,128)(2,1)}), bf16[1536,384]{1,0:T(8,128)(2,1)}) %all-gather.3.cloned.1.call-update) | async-done | bytes 1179664 | tf_op jit(solution)/shard_map/all_gather | solution.py:408
  81.2 1.4 copy-done.1
  82.6 6.4 %all-to-all-start.2 = ((bf16[8,128,1536]{2,1,0:T(8,128)(2,1)}), bf16[8,128,1536]{2,1,0:T(8,128)(2,1)S(1)}, u32[]{:S(2)}, u32[]{:S(2)}) async-start(bf16[8,128,1536]{2,1,0:T(8,128)(2,1)} %gated_cotangent.1), calls=%async_computation.2 | async-start | bytes 6291456 | tf_op jit(solution)/shard_map/all_to_all | solution.py:414
  89.0 9.8 %attention_forward.1 = (bf16[1024,384]{1,0:T(8,128)(2,1)}, bf16[3,640,640]{2,1,0:T(8,128)(2,1)}, bf16[3,384,384]{2,1,0:T(8,128)(2,1)}) custom-call(s32[1,3]{1,0:T(1,128)} %frames_ref.7, bf16[8,3,128,384]{3,2,1,0:T(8,128)(2,1)} %copy-done.1), custom_call_target="tpu_custom_call" | custom-call | tf_op jit(solution)/shard_map/attention_forward/pallas_call | solution.py:112
  98.9 0.0 collective-permute-start.1
  98.9 3.9 %weave.1 = bf16[16,2,96,384]{3,2,1,0:T(8,128)(2,1)} custom-call(s32[1]{0:T(128)} %bitcast.4.core_ref, bf16[16,96,384]{2,1,0:T(8,128)(2,1)} %bitcast.24, bf16[16,96,384]{2,1,0:T(8,128)(2,1)} %collective-permute-done.2.theirs_ref), custom_call_target="tpu_custom_call" | custom-call | tf_op jit(solution)/shard_map/weave/pallas_call | solution.py:315
  102.8 37.1 %collective-permute-done.1.a1_ref = bf16[1024,384]{1,0:T(8,128)(2,1)} collective-permute-done((bf16[1024,384]{1,0:T(8,128)(2,1)}, bf16[1024,384]{1,0:T(8,128)(2,1)}, u32[]{:S(2)}, u32[]{:S(2)}) %collective-permute-start.1) | collective-permute-done | bytes 786464 | tf_op jit(solution)/shard_map/ppermute | solution.py:418
  139.9 7.2 %proj_part.1 = bf16[1024,1536]{1,0:T(8,128)(2,1)} custom-call(bf16[1024,384]{1,0:T(8,128)(2,1)} %get-tuple-element.17.a0_ref, bf16[1024,384]{1,0:T(8,128)(2,1)} %collective-permute-done.1.a1_ref, bf16[2,1536,384]{2,1,0:T(8,128)(2,1)} %bitcast.16), custom_call_target="tpu_custom_call" | custom-call | tf_op jit(solution)/shard_map/proj_part/pallas_call | solution.py:333
  147.1 1.7 copy-done
  148.8 6.7 %all-to-all-start.1 = ((bf16[8,128,1536]{2,1,0:T(8,128)(2,1)}), bf16[8,128,1536]{2,1,0:T(8,128)(2,1)}, u32[]{:S(2)}, u32[]{:S(2)}) async-start(bf16[8,128,1536]{2,1,0:T(8,128)(2,1)} %bitcast.19), calls=%async_computation.1 | async-start | bytes 6291456 | tf_op jit(solution)/shard_map/all_to_all | solution.py:422
  155.5 5.2 %dattn_part.3 = bf16[1024,384]{1,0:T(8,128)(2,1)} custom-call(bf16[1024,1536]{1,0:T(8,128)(2,1)} %bitcast.13, bf16[2,1536,384]{2,1,0:T(8,128)(2,1)} %bitcast.17), custom_call_target="tpu_custom_call" | custom-call | tf_op jit(solution)/shard_map/dattn_part/pallas_call | solution.py:294
  160.7 0.1 collective-permute-start.3
  160.9 6.9 %dweight_part.1 = (bf16[2,8,96,384]{3,2,1,0:T(8,128)(2,1)}, bf16[2,8,96,384]{3,2,1,0:T(8,128)(2,1)}) custom-call(s32[1]{0:T(128)} %bitcast.4.core_ref, bf16[1024,1536]{1,0:T(8,128)(2,1)} %bitcast.14, bf16[1024,384]{1,0:T(8,128)(2,1)} %get-tuple-element.17.a0_ref, bf16[1024,384]{1,0:T(8,128)(2,1)} %collective-permute-done.1.a1_ref), custom_call_target="tpu_custom_call" | custom-call | tf_op jit(solution)/shard_map/dweight_part/pallas_call | solution.py:361
  167.8 5.4 %dattn_part.2.own_ref = f32[1024,384]{1,0:T(8,128)} custom-call(bf16[1024,1536]{1,0:T(8,128)(2,1)} %bitcast.15, bf16[2,1536,384]{2,1,0:T(8,128)(2,1)} %bitcast.18), custom_call_target="tpu_custom_call" | custom-call | tf_op jit(solution)/shard_map/dattn_part/pallas_call | solution.py:294
  173.2 32.2 %collective-permute-done.3.other_ref = bf16[1024,384]{1,0:T(8,128)(2,1)S(1)} collective-permute-done((bf16[1024,384]{1,0:T(8,128)(2,1)}, bf16[1024,384]{1,0:T(8,128)(2,1)S(1)}, u32[]{:S(2)}, u32[]{:S(2)}) %collective-permute-start.3) | collective-permute-done | bytes 786464 | tf_op jit(solution)/shard_map/ppermute | solution.py:428
  205.4 0.9 copy-done.4
  206.2 11.1 %attention_backward.1 = bf16[8,3,128,384]{3,2,1,0:T(8,128)(2,1)} custom-call(s32[1,3]{1,0:T(1,128)} %frames_ref.7, bf16[8,3,128,384]{3,2,1,0:T(8,128)(2,1)} %copy-done.1, f32[1024,384]{1,0:T(8,128)} %dattn_part.2.own_ref, bf16[1024,384]{1,0:T(8,128)(2,1)} %copy-done.4, bf16[3,640,640]{2,1,0:T(8,128)(2,1)} %get-tuple-element.21.p1_ref, ...), custom_call_target="tpu_custom_call" | custom-call | tf_op jit(solution)/shard_map/attention_backward/pallas_call | solution.py:180
  217.4 6.5 %all-to-all-start.3 = ((bf16[8,3,128,384]{3,2,1,0:T(8,128)(2,1)}), bf16[8,3,128,384]{3,2,1,0:T(8,128)(2,1)S(1)}, u32[]{:S(2)}, u32[]{:S(2)}) async-start(bf16[8,3,128,384]{3,2,1,0:T(8,128)(2,1)} %attention_backward.1), calls=%async_computation.3 | async-start | bytes 4718592 | tf_op jit(solution)/shard_map/all_to_all | solution.py:439
  223.9 2.6 add_convert_fusion
  226.5 0.0 reduce-scatter.2.cloned.1.call-update
  226.5 87.3 %reduce-scatter.2.cloned.1.call-done = bf16[96,384]{1,0:T(8,128)(2,1)} async-done(((bf16[1536,384]{1,0:T(8,128)(2,1)}), bf16[96,384]{1,0:T(8,128)(2,1)}) %reduce-scatter.2.cloned.1.call-update) | async-done | bytes 73744 | tf_op jit(solution)/shard_map/reduce_scatter | solution.py:434
  313.8 4.1 %collective-permute-start.5 = (bf16[96,384]{1,0:T(8,128)(2,1)}, bf16[96,384]{1,0:T(8,128)(2,1)S(1)}, u32[]{:S(2)}, u32[]{:S(2)}) collective-permute-start(bf16[96,384]{1,0:T(8,128)(2,1)} %reduce-scatter.2.cloned.1.call-done), channel_id=1, source_target_pairs={{0,0},{128,1},{2,2},{130,3},{4,4},{132,5},{6,6},{134,7},{8,8},{136... | collective-permute-start | bytes 221192 | tf_op jit(solution)/shard_map/ppermute | solution.py:442
  317.9 5.0 %gated_output.1 = bf16[128,3072]{1,0:T(8,128)(2,1)} custom-call(s32[1,3]{1,0:T(1,128)} %frames_ref.7, s32[1,3]{1,0:T(1,128)} %steps_ref.3, s32[1]{0:T(128)} %bitcast.seq_ref, f32[64,3072]{1,0:T(8,128)} %table_ref.3, bf16[128,3072]{1,0:T(8,128)(2,1)} %lat_ref.1, bf16[4,2,128,1536]{3,2,1,0:T(8,128)(2,1)} %bitcast.7.part_ref), custom_call_target="tpu_custom_call" | custom-call | tf_op jit(solution)/shard_map/gated_output/pallas_call | solution.py:272
  322.9 0.7 convert_bitcast_fusion
  323.6 1.4 copy-done.2
  325.0 5.8 %unpack_heads.1 = bf16[3,128,3072]{2,1,0:T(8,128)(2,1)} custom-call(bf16[8,3,128,384]{3,2,1,0:T(8,128)(2,1)} %copy-done.2), custom_call_target="tpu_custom_call" | custom-call | tf_op jit(solution)/shard_map/unpack_heads/pallas_call | solution.py:226
  (19 shorter events, 0.0 us)
Async XLA Ops:
  7.2 10.4 %collective-permute-start = (bf16[96,384]{1,0:T(8,128)(2,1)}, bf16[96,384]{1,0:T(8,128)(2,1)S(1)}, u32[]{:S(2)}, u32[]{:S(2)}) collective-permute-start(bf16[96,384]{1,0:T(8,128)(2,1)} %bitcast.25), channel_id=1, source_target_pairs={{0,0},{1,128},{2,2},{3,130},{4,4},{5,132},{6,6},{7,134},{8,8},{9,1... | collective-permute-start | bytes 221192 | tf_op jit(solution)/shard_map/ppermute | solution.py:405
  17.6 0.6 copy-start.5
  18.2 63.0 %all-to-all-start = ((bf16[8,3,128,384]{3,2,1,0:T(8,128)(2,1)}), bf16[8,3,128,384]{3,2,1,0:T(8,128)(2,1)S(1)}, u32[]{:S(2)}, u32[]{:S(2)}) async-start(bf16[8,3,128,384]{3,2,1,0:T(8,128)(2,1)} %pack_heads.1), calls=%async_computation | async-start | bytes 4718592 | tf_op jit(solution)/shard_map/all_to_all | solution.py:409
  24.0 57.2 %all-gather.3.cloned.1.call-start = ((), (), s32[]{:S(2)}) async-start(), calls=%async_computation.6 | async-start | bytes 1253376 | tf_op jit(solution)/shard_map/all_gather | solution.py:408
  81.2 1.4 copy-start.1
  82.6 64.5 %all-to-all-start.2 = ((bf16[8,128,1536]{2,1,0:T(8,128)(2,1)}), bf16[8,128,1536]{2,1,0:T(8,128)(2,1)S(1)}, u32[]{:S(2)}, u32[]{:S(2)}) async-start(bf16[8,128,1536]{2,1,0:T(8,128)(2,1)} %gated_cotangent.1), calls=%async_computation.2 | async-start | bytes 6291456 | tf_op jit(solution)/shard_map/all_to_all | solution.py:414
  89.0 9.8 %collective-permute-start.2 = (bf16[16,96,384]{2,1,0:T(8,128)(2,1)}, bf16[16,96,384]{2,1,0:T(8,128)(2,1)}, u32[]{:S(2)}, u32[]{:S(2)}) collective-permute-start(bf16[16,96,384]{2,1,0:T(8,128)(2,1)} %bitcast.23), channel_id=1, source_target_pairs={{0,8},{8,0},{16,24},{24,16},{32,40},{40,32},{48,56},{56,48},{64,72... | collective-permute-start | bytes 3538952 | tf_op jit(solution)/shard_map/ppermute | solution.py:413
  98.9 41.0 %collective-permute-start.1 = (bf16[1024,384]{1,0:T(8,128)(2,1)}, bf16[1024,384]{1,0:T(8,128)(2,1)}, u32[]{:S(2)}, u32[]{:S(2)}) collective-permute-start(bf16[1024,384]{1,0:T(8,128)(2,1)} %get-tuple-element.17.a0_ref), channel_id=1, source_target_pairs={{0,1},{1,0},{2,3},{3,2},{4,5},{5,4},{6,7},{7,6},{8,9},{9,8},{10,11... | collective-permute-start | bytes 2359304 | tf_op jit(solution)/shard_map/ppermute | solution.py:418
  147.1 1.7 copy-start
  148.8 68.6 %all-to-all-start.1 = ((bf16[8,128,1536]{2,1,0:T(8,128)(2,1)}), bf16[8,128,1536]{2,1,0:T(8,128)(2,1)}, u32[]{:S(2)}, u32[]{:S(2)}) async-start(bf16[8,128,1536]{2,1,0:T(8,128)(2,1)} %bitcast.19), calls=%async_computation.1 | async-start | bytes 6291456 | tf_op jit(solution)/shard_map/all_to_all | solution.py:422
  160.7 44.7 %collective-permute-start.3 = (bf16[1024,384]{1,0:T(8,128)(2,1)}, bf16[1024,384]{1,0:T(8,128)(2,1)S(1)}, u32[]{:S(2)}, u32[]{:S(2)}) collective-permute-start(bf16[1024,384]{1,0:T(8,128)(2,1)} %dattn_part.3), channel_id=1, source_target_pairs={{0,1},{1,0},{2,3},{3,2},{4,5},{5,4},{6,7},{7,6},{8,9},{9,8},{10,11... | collective-permute-start | bytes 2359304 | tf_op jit(solution)/shard_map/ppermute | solution.py:428
  167.8 56.1 %collective-permute-start.4 = (bf16[2,8,96,384]{3,2,1,0:T(8,128)(2,1)}, bf16[2,8,96,384]{3,2,1,0:T(8,128)(2,1)}, u32[]{:S(2)}, u32[]{:S(2)}) collective-permute-start(bf16[2,8,96,384]{3,2,1,0:T(8,128)(2,1)} %get-tuple-element.24), channel_id=1, source_target_pairs={{0,8},{8,0},{16,24},{24,16},{32,40},{40,32},{48,56},{56,48},{64,72... | collective-permute-start | bytes 3538952 | tf_op jit(solution)/shard_map/ppermute | solution.py:432
  205.4 0.9 copy-start.4
  217.4 6.5 %copy-start.3 = (bf16[2,8,96,384]{3,2,1,0:T(8,128)(2,1)S(1)}, bf16[2,8,96,384]{3,2,1,0:T(8,128)(2,1)}, u32[]{:S(2)}) copy-start(bf16[2,8,96,384]{3,2,1,0:T(8,128)(2,1)} %get-tuple-element.23) | copy-start | bytes 3538948
  217.4 106.2 %all-to-all-start.3 = ((bf16[8,3,128,384]{3,2,1,0:T(8,128)(2,1)}), bf16[8,3,128,384]{3,2,1,0:T(8,128)(2,1)S(1)}, u32[]{:S(2)}, u32[]{:S(2)}) async-start(bf16[8,3,128,384]{3,2,1,0:T(8,128)(2,1)} %attention_backward.1), calls=%async_computation.3 | async-start | bytes 4718592 | tf_op jit(solution)/shard_map/all_to_all | solution.py:439
  223.9 89.9 %reduce-scatter.2.cloned.1.call-start = ((), (), s32[]{:S(2)}) async-start(), calls=%async_computation.5 | async-start | bytes 1253376 | tf_op jit(solution)/shard_map/reduce_scatter | solution.py:434
  313.8 9.1 %collective-permute-start.5 = (bf16[96,384]{1,0:T(8,128)(2,1)}, bf16[96,384]{1,0:T(8,128)(2,1)S(1)}, u32[]{:S(2)}, u32[]{:S(2)}) collective-permute-start(bf16[96,384]{1,0:T(8,128)(2,1)} %reduce-scatter.2.cloned.1.call-done), channel_id=1, source_target_pairs={{0,0},{128,1},{2,2},{130,3},{4,4},{132,5},{6,6},{134,7},{8,8},{136... | collective-permute-start | bytes 221192 | tf_op jit(solution)/shard_map/ppermute | solution.py:442
  323.6 1.4 copy-start.2
Sparse Core Ops, SparseCore 0:
  27.9 53.2 all-gather.2
  228.8 84.9 reduce-scatter.1

commit v2 on v1

--- a/solution.py
+++ b/solution.py
@@ -233,57 +233,86 @@
     )(grads)
 
 
-def gated_kernel(frames_ref, steps_ref, seq_ref, table_ref, cot_ref, out_ref):
-    b0, b1 = gate_bins(frames_ref, steps_ref, seq_ref)
-    for k, b in enumerate((b0, b1)):
-        rows = slice(k * FRAME, (k + 1) * FRAME)
-        out_ref[0, rows, :] = (table_ref[pl.ds(b, 1), :] * cot_ref[rows, :].astype(F32)).astype(BF)
+def gated_kernel(frames_ref, steps_ref, seq_ref, t0_ref, t1_ref, c0_ref, c1_ref, keep_ref, send_ref):
+    bins = gate_bins(frames_ref, steps_ref, seq_ref)
+    for table_ref, cot_ref, out_ref in ((t0_ref, c0_ref, keep_ref), (t1_ref, c1_ref, send_ref)):
+        for k, b in enumerate(bins):
+            rows = slice(k * FRAME, (k + 1) * FRAME)
+            out_ref[rows, :] = (table_ref[pl.ds(b, 1), :] * cot_ref[rows, :].astype(F32)).astype(BF)
 
 
 def gated_cotangent(frames, steps, seq, table, cotangent):
+    def half(rows, flip):
+        return pl.BlockSpec((rows, 768), lambda n, f, t, s: (0, 2 * (s[0] % 2 ^ flip) + n))
+
+    out = pl.BlockSpec((128, 768), lambda n, *_: (0, n))
     return pl.pallas_call(
         gated_kernel,
-        out_shape=jax.ShapeDtypeStruct((8, 128, 1536), BF),
+        out_shape=(jax.ShapeDtypeStruct((128, 1536), BF),) * 2,
         grid_spec=pltpu.PrefetchScalarGridSpec(
             num_scalar_prefetch=3,
-            grid=(2, 4),
-            in_specs=[
-                pl.BlockSpec((64, 1536), lambda z, x, *_: (0, z)),
-                pl.BlockSpec((128, 1536), lambda z, x, *_: (0, z)),
-            ],
-            out_specs=pl.BlockSpec((1, 128, 1536), lambda z, x, *_: (2 * x + z, 0, 0)),
+            grid=(2,),
+            in_specs=[half(64, 0), half(64, 1), half(128, 0), half(128, 1)],
+            out_specs=(out, out),
         ),
         name="gated_cotangent",
-    )(frames, steps, seq, table, cotangent)
-
-
-def output_kernel(frames_ref, steps_ref, seq_ref, table_ref, lat_ref, part_ref, out_ref):
-    b0, b1 = gate_bins(frames_ref, steps_ref, seq_ref)
-    for k, b in enumerate((b0, b1)):
-        rows = slice(k * FRAME, (k + 1) * FRAME)
-        proj = part_ref[0, 0, rows, :].astype(F32)
-        for x in range(1, 4):
-            proj = proj + part_ref[x, 0, rows, :].astype(F32)
-        out = lat_ref[rows, :].astype(F32) + table_ref[pl.ds(b, 1), :] * proj
-        out_ref[rows, :] = out.astype(BF)
-
-
-def gated_output(frames, steps, seq, table, latents, parts):
+    )(frames, steps, seq, table, table, cotangent, cotangent)
+
+
+def assemble_kernel(seq_ref, *refs):
+    blocks, out_ref, sems = refs[:8], refs[8], refs[9]
+    x, z = seq_ref[0] // 2, seq_ref[0] % 2
+    copies = []
+    for i, block in enumerate(blocks):
+        place = 2 * ((x + i // 2) % 4) + (z ^ (i % 2))
+        copies.append(pltpu.make_async_copy(block, out_ref.at[place], sems.at[i]))
+        copies[-1].start()
+    for copy in copies:
+        copy.wait()
+
+
+def assemble(seq, blocks):
+    return pl.pallas_call(
+        assemble_kernel,
+        out_shape=jax.ShapeDtypeStruct((8, 128, 1536), BF),
+        in_specs=[pl.BlockSpec(memory_space=pltpu.SMEM)] + [pl.BlockSpec(memory_space=pl.ANY)] * 8,
+        out_specs=pl.BlockSpec(memory_space=pl.ANY),
+        scratch_shapes=[pltpu.SemaphoreType.DMA((8,))],
+        name="assemble",
+    )(seq, *blocks)
+
+
+def output_kernel(
+    frames_ref, steps_ref, seq_ref, t0_ref, t1_ref, l0_ref, l1_ref, own_ref, other_ref, out_ref
+):
+    bins = gate_bins(frames_ref, steps_ref, seq_ref)
+    z = seq_ref[0] % 2
+    halves = ((z, t0_ref, l0_ref, own_ref), (1 - z, t1_ref, l1_ref, other_ref))
+    for place, table_ref, lat_ref, proj_ref in halves:
+        at = pl.multiple_of(place * 1536, 1536)
+        for k, b in enumerate(bins):
+            rows = slice(k * FRAME, (k + 1) * FRAME)
+            proj = proj_ref[rows, :].astype(F32)
+            out = lat_ref[rows, :].astype(F32) + table_ref[pl.ds(b, 1), :] * proj
+            out_ref[rows, pl.ds(at, 1536)] = out.astype(BF)
+
+
+def gated_output(frames, steps, seq, table, latents, own, other):
+    def half(rows, flip):
+        return pl.BlockSpec((rows, 1536), lambda n, f, t, s: (0, s[0] % 2 ^ flip))
+
+    whole = pl.BlockSpec((128, 1536), lambda n, *_: (0, 0))
     return pl.pallas_call(
         output_kernel,
         out_shape=jax.ShapeDtypeStruct((128, 3072), BF),
         grid_spec=pltpu.PrefetchScalarGridSpec(
             num_scalar_prefetch=3,
-            grid=(2, 2),
-            in_specs=[
-                pl.BlockSpec((64, 768), lambda z, n, *_: (0, 2 * z + n)),
-                pl.BlockSpec((128, 768), lambda z, n, *_: (0, 2 * z + n)),
-                pl.BlockSpec((4, 1, 128, 768), lambda z, n, *_: (0, z, 0, n)),
-            ],
-            out_specs=pl.BlockSpec((128, 768), lambda z, n, *_: (0, 2 * z + n)),
+            grid=(1,),
+            in_specs=[half(64, 0), half(64, 1), half(128, 0), half(128, 1), whole, whole],
+            out_specs=pl.BlockSpec((128, 3072), lambda n, *_: (0, 0)),
         ),
         name="gated_output",
-    )(frames, steps, seq, table, latents, parts.reshape(4, 2, 128, 1536))
+    )(frames, steps, seq, table, table, latents, latents, own, other)
 
 
 def dattn_kernel(d_ref, w_ref, out_ref):
@@ -294,60 +323,132 @@
     return pl.pallas_call(
         dattn_kernel,
         out_shape=jax.ShapeDtypeStruct((1024, 384), dtype),
-        grid=(4,),
+        grid=(2,),
         in_specs=[
-            pl.BlockSpec((256, 1536), lambda m: (m, 0)),
+            pl.BlockSpec((512, 1536), lambda m: (m, 0)),
             pl.BlockSpec((1, 1536, 384), lambda m: (which, 0, 0)),
         ],
-        out_specs=pl.BlockSpec((256, 384), lambda m: (m, 0)),
+        out_specs=pl.BlockSpec((512, 384), lambda m: (m, 0)),
+        compiler_params=pltpu.CompilerParams(vmem_limit_bytes=VMEM_LIMIT),
         name="dattn_part",
     )(dproj, weights)
 
 
-def weave_kernel(core_ref, mine_ref, theirs_ref, out_ref):
-    even = core_ref[0] == 0
-    mine, theirs = mine_ref[...], theirs_ref[...]
-    out_ref[:, 0] = jnp.where(even, mine, theirs)
-    out_ref[:, 1] = jnp.where(even, theirs, mine)
-
-
-def weave(core, mine, theirs):
+def weave_kernel(dp_ref, *refs):
+    out_ref = refs[8]
+    y, zh, core = dp_ref[0] // 8, dp_ref[0] // 2 % 4, dp_ref[0] % 2
+    for flip in range(2):
+        for k in range(4):
+            for m in range(4):
+                place = 4 * ((y + k) % 4) + (zh + m) % 4
+                out_ref[place, core ^ flip] = refs[4 * flip + k][m]
+
+
+def weave(dp, mine, theirs):
     return pl.pallas_call(
         weave_kernel,
         out_shape=jax.ShapeDtypeStruct((16, 2, 96, 384), BF),
+        in_specs=[pl.BlockSpec(memory_space=pltpu.SMEM)]
+        + [pl.BlockSpec((4, 96, 384), lambda: (0, 0, 0))] * 8,
+        out_specs=pl.BlockSpec((16, 2, 96, 384), lambda: (0, 0, 0, 0)),
+        name="weave",
+    )(dp, *mine, *theirs)
+
+
+def stack_kernel(*refs):
+    for i, ref in enumerate(refs[:-1]):
+        refs[-1][i] = ref[...]
+
+
+def stack_pieces(pieces):
+    return pl.pallas_call(
+        stack_kernel, out_shape=jax.ShapeDtypeStruct((4, 96, 384), BF), name="stack_pieces"
+    )(*pieces)
+
+
+def rows_spec(k):
+    return pl.BlockSpec((256, 384), lambda n, s: ((s[0] // 2 + k) % 4, 0))
+
+
+W_SPEC = pl.BlockSpec((2, 512, 384), lambda n, s: (0, n, 0))
+TWO_SPEC = pl.BlockSpec((256, 512), lambda n, s: (0, n))
+ONE_SPEC = pl.BlockSpec((128, 512), lambda n, s: (0, n))
+ONE_BF = jax.ShapeDtypeStruct((128, 1536), BF)
+TWO_BF = jax.ShapeDtypeStruct((256, 1536), BF)
+
+
+def project(own_ref, other_ref, w_ref):
+    return dot_nt(own_ref[...], w_ref[0]) + dot_nt(other_ref[...], w_ref[1])
+
+
+def far_kernel(seq_ref, a_ref, b_ref, w_ref, up_ref, down_ref):
+    part = project(a_ref, b_ref, w_ref).astype(BF)
+    up_ref[...] = part[:128]
+    down_ref[...] = part[128:]
+
+
+def near_kernel(seq_ref, a1_ref, b1_ref, a3_ref, b3_ref, w_ref, up_ref, down_ref, t1_ref, t3_ref):
+    p1 = project(a1_ref, b1_ref, w_ref)
+    t1_ref[:128] = (p1[:128] + up_ref[...].astype(F32)).astype(BF)
+    t1_ref[128:] = p1[128:].astype(BF)
+    p3 = project(a3_ref, b3_ref, w_ref)
+    t3_ref[:128] = p3[:128].astype(BF)
+    t3_ref[128:] = (p3[128:] + down_ref[...].astype(F32)).astype(BF)
+
+
+def home_kernel(seq_ref, a_ref, b_ref, w_ref, c1_ref, c3_ref, keep_ref, send_ref):
+    part = project(a_ref, b_ref, w_ref)
+    part = part + c1_ref[...].astype(F32) + c3_ref[...].astype(F32)
+    first = seq_ref[0] % 2 == 0
+    keep_ref[...] = jnp.where(first, part[:128], part[128:])
+    send_ref[...] = jnp.where(first, part[128:], part[:128]).astype(BF)
+
+
+def project_call(kernel, name, in_specs, out_shape, out_specs):
+    return pl.pallas_call(
+        kernel,
+        out_shape=out_shape,
         grid_spec=pltpu.PrefetchScalarGridSpec(
-            num_scalar_prefetch=1,
-            grid=(4,),
-            in_specs=[pl.BlockSpec((4, 96, 384), lambda n, c: (n, 0, 0))] * 2,
-            out_specs=pl.BlockSpec((4, 2, 96, 384), lambda n, c: (n, 0, 0, 0)),
+            num_scalar_prefetch=1, grid=(3,), in_specs=in_specs, out_specs=out_specs
         ),
-        name="weave",
-    )(core, mine, theirs)
-
-
-def proj_kernel(a0_ref, a1_ref, w_ref, out_ref):
-    out_ref[...] = (dot_nt(a0_ref[...], w_ref[0]) + dot_nt(a1_ref[...], w_ref[1])).astype(BF)
-
-
-def proj_part(own, other, weights):
-    return pl.pallas_call(
-        proj_kernel,
-        out_shape=jax.ShapeDtypeStruct((1024, 1536), BF),
-        grid=(4,),
-        in_specs=[
-            pl.BlockSpec((256, 384), lambda m: (m, 0)),
-            pl.BlockSpec((256, 384), lambda m: (m, 0)),
-            pl.BlockSpec((2, 1536, 384), lambda m: (0, 0, 0)),
-        ],
-        out_specs=pl.BlockSpec((256, 1536), lambda m: (m, 0)),
         compiler_params=pltpu.CompilerParams(vmem_limit_bytes=VMEM_LIMIT),
-        name="proj_part",
-    )(own, other, weights)
+        name=name,
+    )
+
+
+def project_far(seq, own, other, weights):
+    return project_call(
+        far_kernel,
+        "project_far",
+        [rows_spec(2), rows_spec(2), W_SPEC],
+        (ONE_BF, ONE_BF),
+        (ONE_SPEC, ONE_SPEC),
+    )(seq, own, other, weights)
+
+
+def project_near(seq, own, other, weights, up, down):
+    return project_call(
+        near_kernel,
+        "project_near",
+        [rows_spec(1), rows_spec(1), rows_spec(3), rows_spec(3), W_SPEC, ONE_SPEC, ONE_SPEC],
+        (TWO_BF, TWO_BF),
+        (TWO_SPEC, TWO_SPEC),
+    )(seq, own, other, own, other, weights, up, down)
+
+
+def project_home(seq, own, other, weights, c1, c3):
+    return project_call(
+        home_kernel,
+        "project_home",
+        [rows_spec(0), rows_spec(0), W_SPEC, TWO_SPEC, TWO_SPEC],
+        (jax.ShapeDtypeStruct((128, 1536), F32), ONE_BF),
+        (ONE_SPEC, ONE_SPEC),
+    )(seq, own, other, weights, c1, c3)
 
 
 def dweight_kernel(core_ref, d_ref, a0_ref, a1_ref, keep_ref, send_ref):
     d = d_ref[...]
-    even = core_ref[0] == 0
+    even = core_ref[0] % 2 == 0
     for z, a_ref in enumerate((a0_ref, a1_ref)):
         g = dot_tn(d, a_ref[...]).astype(BF)
         for i in range(2):
@@ -379,6 +480,43 @@
     )(core, dproj, own, other)
 
 
+def pair_kernel(dp_ref, keep_ref, got_ref, *out_refs):
+    y = dp_ref[0] // 8
+    for k, out_ref in enumerate(out_refs):
+        at = (y + k) % 4
+        out_ref[...] = (keep_ref[at].astype(F32) + got_ref[at].astype(F32)).astype(BF)
+
+
+def pair_sum(dp, keep, got):
+    return pl.pallas_call(
+        pair_kernel,
+        out_shape=(jax.ShapeDtypeStruct((4, 96, 384), BF),) * 4,
+        in_specs=[pl.BlockSpec(memory_space=pltpu.SMEM)]
+        + [pl.BlockSpec((4, 4, 96, 384), lambda: (0, 0, 0, 0))] * 2,
+        out_specs=(pl.BlockSpec((4, 96, 384), lambda: (0, 0, 0)),) * 4,
+        name="pair_sum",
+    )(dp, keep.reshape(4, 4, 96, 384), got.reshape(4, 4, 96, 384))
+
+
+def ring_kernel(dp_ref, a_ref, b_ref, c_ref, d_ref, *out_refs):
+    zh = dp_ref[0] // 2 % 4
+    for k, out_ref in enumerate(out_refs):
+        at = (zh + k) % 4
+        total = a_ref[at].astype(F32) + b_ref[at].astype(F32)
+        out_ref[...] = (total + c_ref[at].astype(F32) + d_ref[at].astype(F32)).astype(BF)
+
+
+def ring_sum(dp, parts):
+    return pl.pallas_call(
+        ring_kernel,
+        out_shape=(jax.ShapeDtypeStruct((96, 384), BF),) * 4,
+        in_specs=[pl.BlockSpec(memory_space=pltpu.SMEM)]
+        + [pl.BlockSpec((4, 96, 384), lambda: (0, 0, 0))] * 4,
+        out_specs=(pl.BlockSpec((96, 384), lambda: (0, 0)),) * 4,
+        name="ring_sum",
+    )(dp, *parts)
+
+
 def piece_moves(dp_count, seq_count):
     half = dp_count // 2
     moves = []
@@ -391,56 +529,86 @@
     return moves
 
 
+def along(x, axis, stride, places):
+    size = lax.axis_size(axis)
+    moves = []
+    for i in range(size):
+        at = i // stride % 4
+        moves.append((i, i + ((at + places) % 4 - at) * stride))
+    return lax.ppermute(x, axis, moves)
+
+
+def along_x(x, places):
+    return along(x, "seq", 2, places)
+
+
+def along_y(x, places):
+    return along(x, "dp", 8, places)
+
+
+def along_z(x, places):
+    return along(x, "dp", 2, places)
+
+
+def swap_z(x):
+    return lax.ppermute(x, "seq", [(i, i ^ 1) for i in range(lax.axis_size("seq"))])
+
+
+def swap_core(x):
+    return lax.ppermute(x, "dp", [(i, i ^ 1) for i in range(lax.axis_size("dp"))])
+
+
 def body(qkv_input, latents, cotangent, out_weight, gate_table, timesteps, frames):
-    dp_count, seq_count = lax.axis_size("dp"), lax.axis_size("seq")
     seq = lax.axis_index("seq").astype(jnp.int32).reshape(1)
+    dp = lax.axis_index("dp").astype(jnp.int32).reshape(1)
     both = ("dp", "seq")
-    moves = piece_moves(dp_count, seq_count)
-    swap = [(i, i ^ 1) for i in range(seq_count)]
-
-    core = (lax.axis_index("dp") % 2).astype(jnp.int32).reshape(1)
-    cores = [(i, i ^ 1) for i in range(dp_count)]
-    same_core = [list(range(c, dp_count, 2)) for c in range(2)]
+    moves = piece_moves(lax.axis_size("dp"), lax.axis_size("seq"))
 
     piece = lax.ppermute(out_weight.T, both, moves)
+    keep, send = gated_cotangent(frames, timesteps, seq, gate_table, cotangent)
     packed = pack_heads(qkv_input.transpose(1, 0, 2))
-    packed, piece = lax.optimization_barrier((packed, piece))
-    mine = lax.all_gather(piece, "dp", axis=0, axis_index_groups=same_core, tiled=False)
+    packed, piece, keep, send = lax.optimization_barrier((packed, piece, keep, send))
     heads = lax.all_to_all(packed, "seq", split_axis=0, concat_axis=0, tiled=True)
-
-    gated = gated_cotangent(frames, timesteps, seq, gate_table, cotangent)
-    gated, heads, mine = lax.optimization_barrier((gated, heads, mine))
-    theirs = lax.ppermute(mine, "dp", cores)
-    dproj = lax.all_to_all(gated, "seq", split_axis=0, concat_axis=0, tiled=True)
-    dproj = dproj.reshape(1024, 1536)
-
+    got = swap_z(send)
+
+    pieces = stack_pieces([piece] + [along_z(piece, -k) for k in range(1, 4)])
+    mine = [pieces] + [along_y(pieces, -k) for k in range(1, 4)]
+    heads, keep, got, mine = lax.optimization_barrier((heads, keep, got, mine))
+
+    b1 = [along_x(keep, -1), along_x(got, -1)]
+    b3 = [along_x(keep, 1), along_x(got, 1)]
+    b2 = [along_x(b3[0], 1), along_x(b1[1], -1)]
+    theirs = [swap_core(p) for p in mine]
     attn, p1, p2 = attention_forward(frames, heads)
-    attn_other = lax.ppermute(attn, "seq", swap)
-    weights = weave(core, mine, theirs).reshape(2, 1536, 384)
-
-    part = proj_part(attn, attn_other, weights)
-    parts = lax.all_to_all(
-        part.reshape(8, 128, 1536), "seq", split_axis=0, concat_axis=0, tiled=True
-    )
-    dproj, part = lax.optimization_barrier((dproj, part))
-
-    d_send = dattn_part(dproj, weights, 1, BF)
-    d_recv = lax.ppermute(d_send, "seq", swap)
+    attn_other = swap_z(attn)
+    weights = weave(dp, mine, theirs).reshape(2, 1536, 384)
+    dproj = assemble(seq, [keep, got, *b1, *b2, *b3]).reshape(1024, 1536)
+
+    d_recv = swap_z(dattn_part(dproj, weights, 1, BF))
+    up, down = project_far(seq, attn, attn_other, weights)
+    up, down = along_x(up, 1), along_x(down, -1)
     d_own = dattn_part(dproj, weights, 0, F32)
-
-    keep, send = dweight_part(core, dproj, attn, attn_other)
-    got = lax.ppermute(send, "dp", cores)
-    pair = (keep.astype(F32) + got.astype(F32)).astype(BF).reshape(16 * 96, 384)
-    total = lax.psum_scatter(
-        pair, "dp", scatter_dimension=0, axis_index_groups=same_core, tiled=True
-    )
+    w_keep, w_send = dweight_part(dp, dproj, attn, attn_other)
+    w_got = swap_core(w_send)
+    t1, t3 = project_near(seq, attn, attn_other, weights, up, down)
+    d_own, d_recv, t1, t3, w_got = lax.optimization_barrier((d_own, d_recv, t1, t3, w_got))
+    c1, c3 = along_x(t1, 1), along_x(t3, -1)
+    terms = pair_sum(dp, w_keep, w_got)
+    terms = [terms[0]] + [along_y(terms[k], k) for k in range(1, 4)]
 
     grads = attention_backward(frames, heads, d_own, d_recv, p1, p2)
     grads = lax.all_to_all(grads, "seq", split_axis=0, concat_axis=0, tiled=True)
 
-    output = gated_output(frames, timesteps, seq, gate_table, latents, parts)
+    o_keep, o_send = project_home(seq, attn, attn_other, weights, c1, c3)
+    o_got = swap_z(o_send)
+    output = gated_output(frames, timesteps, seq, gate_table, latents, o_keep, o_got)
+
+    terms = ring_sum(dp, terms)
+    terms = [terms[0]] + [along_z(terms[k], k) for k in range(1, 4)]
+    total = terms[0].astype(F32) + terms[1].astype(F32)
+    total = total + terms[2].astype(F32) + terms[3].astype(F32)
     total = lax.ppermute(total, both, [(b, a) for a, b in moves])
-    grad_weight = total.astype(F32).T
+    grad_weight = total.T
     grad_qkv = unpack_heads(grads).transpose(1, 0, 2)
     return (output, grad_qkv, grad_weight)
 

time: 339 us -> 356 us (1.050)
  waiting for transfers between devices: 208 us -> 102 us
  Pallas kernels: 72 us -> 175 us
  starting transfers between devices: 34.3 us -> 63.7 us
  between operations: 14.1 us -> 0.86 us
  local copies, waits for them, and re-layouts: 6.09 us -> 11.6 us
    pallas_call x2 -> x8, Pallas kernels: 13.1 us -> 119 us  [the longest x1 96.5 us: assemble(): pl.pallas_call(assemble_kernel, out_shape=jax.ShapeDtypeStruct((8, 128, 1...]
    reduce_scatter x1 -> x0, waiting for transfers between devices: 87.3 us -> none  [body(): lax.psum_scatter(pair, 'dp', scatter_dimension=0, axis_index_groups=same_...]
    all_gather x1 -> x0, waiting for transfers between devices: 50.6 us -> none  [body(): lax.all_gather(piece, 'dp', axis=0, axis_index_groups=same_core, tiled=Fa...]
    ppermute x4 -> x31, starting transfers between devices: 0.16 us -> 45.6 us  [the longest x22 41.3 us: along(): return lax.ppermute(x, axis, moves)]
    ppermute x4 -> x31, waiting for transfers between devices: 69.3 us -> 92.3 us  [the longest x22 88.9 us: along(): return lax.ppermute(x, axis, moves)]
    all_to_all x2 -> x0, starting transfers between devices: 13.1 us -> none  [the longest x1 6.7 us: body(): lax.all_to_all(part.reshape(8, 128, 1536), 'seq', split_axis=0, concat_ax...]
    ppermute x1, waiting for transfers between devices: 0.01 us -> 9.37 us  [body(): total = lax.ppermute(total, both, [(b, a) for a, b in moves])]
    unnamed x12 -> x67, local copies, waits for them, and re-layouts: 6.09 us -> 11.6 us
  transfers between devices with their start and end apart: 12 -> 35, of which waited for: 4 -> 15; matrix products, arithmetic and copies ran while one was open for 1% -> 0% of each run, Pallas kernels for 20% -> 43%
where the time goes in v2:
time: 356 us; the launch traced here: 353 us
  Pallas kernels  175 us (49%)
  waiting for transfers between devices  102 us (29%)
  starting transfers between devices  63.7 us (18%)
  local copies, waits for them, and re-layouts  11.6 us (3%)
    pallas_call x1, Pallas kernels, assemble(): pl.pallas_call(assemble_kernel, out_shape=jax.ShapeDtypeStruct((8, 128, 1...  96.5 us
    ppermute x22, waiting for transfers between devices, along(): return lax.ppermute(x, axis, moves)  88.9 us
    ppermute x22, starting transfers between devices, along(): return lax.ppermute(x, axis, moves)  41.3 us
    unnamed x67, local copies, waits for them, and re-layouts  11.6 us
    pallas_call x1, Pallas kernels, attention_backward(): pl.pallas_call(bwd_kernel, out_shape=jax.ShapeDtypeStruct((8, 3, 128, 3 *...  11.1 us
    pallas_call x1, Pallas kernels, attention_forward(): pl.pallas_call(fwd_kernel, out_shape=(jax.ShapeDtypeStruct((1024, 3 * HD)...  9.82 us
    ppermute x1, waiting for transfers between devices, body(): total = lax.ppermute(total, both, [(b, a) for a, b in moves])  9.37 us
    pallas_call x2, Pallas kernels, dattn_part(): pl.pallas_call(dattn_kernel, out_shape=jax.ShapeDtypeStruct((1024, 384),...  9.08 us
  transfers between devices with their start and end apart: 35, of which 15 were waited for; matrix products, arithmetic and copies ran while one was open for 0% of the time, Pallas kernels for 43%

profile of v2, /device:TPU:32, one launch (start us, length us, event | category | flops | bytes accessed | tf_op | source)
XLA Modules:
  0.0 352.7 jit_solution(3371556151037749381)
XLA Ops:
  0.6 4.6 %collective-permute-start = (bf16[96,384]{1,0:T(8,128)(2,1)}, bf16[96,384]{1,0:T(8,128)(2,1)S(1)}, u32[]{:S(2)}, u32[]{:S(2)}) collective-permute-start(bf16[96,384]{1,0:T(8,128)(2,1)} %bitcast.23), channel_id=1, source_target_pairs={{0,0},{1,128},{2,2},{3,130},{4,4},{5,132},{6,6},{7,134},{8,8},{9,1... | collective-permute-start | bytes 221192 | tf_op jit(solution)/shard_map/ppermute | solution.py:567
  5.3 5.8 %pack_heads.1 = bf16[8,3,128,384]{3,2,1,0:T(8,128)(2,1)} custom-call(bf16[3,128,3072]{2,1,0:T(8,128)(2,1)} %bitcast.18), custom_call_target="tpu_custom_call" | custom-call | tf_op jit(solution)/shard_map/pack_heads/pallas_call | solution.py:211
  11.1 3.0 gated_cotangent.1
  14.1 5.9 %all-to-all-start = ((bf16[8,3,128,384]{3,2,1,0:T(8,128)(2,1)}), bf16[8,3,128,384]{3,2,1,0:T(8,128)(2,1)S(1)}, u32[]{:S(2)}, u32[]{:S(2)}) async-start(bf16[8,3,128,384]{3,2,1,0:T(8,128)(2,1)} %pack_heads.1), calls=%async_computation | async-start | bytes 4718592 | tf_op jit(solution)/shard_map/all_to_all | solution.py:571
  20.0 3.3 collective-permute-start.4
  23.3 5.4 %collective-permute-start.3 = (bf16[96,384]{1,0:T(8,128)(2,1)S(1)}, bf16[96,384]{1,0:T(8,128)(2,1)S(1)}, u32[]{:S(2)}, u32[]{:S(2)}) collective-permute-start(bf16[96,384]{1,0:T(8,128)(2,1)S(1)} %collective-permute-done.refs_0_), channel_id=1, source_target_pairs={{0,32},{8,40},{16,48},{24,56},{32,0},{40,8},{48,16},{56,24},{64,96... | collective-permute-start | bytes 221192 | tf_op jit(solution)/shard_map/ppermute | solution.py:538
  31.3 35.3 %collective-permute-done.3.refs_2_ = bf16[96,384]{1,0:T(8,128)(2,1)S(1)} collective-permute-done((bf16[96,384]{1,0:T(8,128)(2,1)S(1)}, bf16[96,384]{1,0:T(8,128)(2,1)S(1)}, u32[]{:S(2)}, u32[]{:S(2)}) %collective-permute-start.3) | collective-permute-done | bytes 73760 | tf_op jit(solution)/shard_map/ppermute | solution.py:538
  72.9 9.8 %collective-permute-done.7.refs_3_ = bf16[4,96,384]{2,1,0:T(8,128)(2,1)S(1)} collective-permute-done((bf16[4,96,384]{2,1,0:T(8,128)(2,1)}, bf16[4,96,384]{2,1,0:T(8,128)(2,1)S(1)}, u32[]{:S(2)}, u32[]{:S(2)}) %collective-permute-start.7) | collective-permute-done | bytes 294944 | tf_op jit(solution)/shard_map/ppermute | solution.py:538
  87.6 9.8 %attention_forward.1 = (bf16[1024,384]{1,0:T(8,128)(2,1)}, bf16[3,640,640]{2,1,0:T(8,128)(2,1)}, bf16[3,384,384]{2,1,0:T(8,128)(2,1)}) custom-call(s32[1,3]{1,0:T(1,128)} %frames_ref.7, bf16[8,3,128,384]{3,2,1,0:T(8,128)(2,1)} %copy-done), custom_call_target="tpu_custom_call" | custom-call | tf_op jit(solution)/shard_map/attention_forward/pallas_call | solution.py:112
  101.8 3.1 collective-permute-start.17
  105.0 6.8 %collective-permute-done.13.refs_2_ = bf16[128,1536]{1,0:T(8,128)(2,1)S(1)} collective-permute-done((bf16[128,1536]{1,0:T(8,128)(2,1)S(1)}, bf16[128,1536]{1,0:T(8,128)(2,1)S(1)}, u32[]{:S(2)}, u32[]{:S(2)}) %collective-permute-start.13) | collective-permute-done | bytes 393248 | tf_op jit(solution)/shard_map/ppermute | solution.py:538
  114.3 4.2 %collective-permute-done.16.refs_4_ = bf16[128,1536]{1,0:T(8,128)(2,1)S(1)} collective-permute-done((bf16[128,1536]{1,0:T(8,128)(2,1)S(1)}, bf16[128,1536]{1,0:T(8,128)(2,1)S(1)}, u32[]{:S(2)}, u32[]{:S(2)}) %collective-permute-start.16) | collective-permute-done | bytes 393248 | tf_op jit(solution)/shard_map/ppermute | solution.py:538
  120.1 96.5 %assemble.1 = bf16[8,128,1536]{2,1,0:T(8,128)(2,1)} custom-call(s32[1]{0:T(128)} %bitcast.seq_ref, bf16[128,1536]{1,0:T(8,128)(2,1)} %get-tuple-element.52.refs_0_, bf16[128,1536]{1,0:T(8,128)(2,1)} %copy-done.8, bf16[128,1536]{1,0:T(8,128)(2,1)} %copy-done.10, bf16[128,1536]{1,0:T(8,128)(2,1)} %collective-permute-done.14.refs_3_, ...), custom_call_target="tpu_custom_call" | custom-call | tf_op jit(solution)/shard_map/assemble/pallas_call | solution.py:275
  217.5 7.1 %dweight_part.1 = (bf16[2,8,96,384]{3,2,1,0:T(8,128)(2,1)}, bf16[2,8,96,384]{3,2,1,0:T(8,128)(2,1)}) custom-call(s32[1]{0:T(128)} %bitcast.3.dp_ref.core_ref, bf16[1024,1536]{1,0:T(8,128)(2,1)} %bitcast.15, bf16[1024,384]{1,0:T(8,128)(2,1)} %get-tuple-element.47.a_ref.a1_ref.a3_ref.a0_ref, bf16[1024,384]{1,0:T(8,128)(2,1)} %copy-done.1), custom_call_target="tpu_custom_call" | custom-call | tf_op jit(solution)/shard_map/dweight_part/pallas_call | solution.py:462
  230.1 3.3 weave.1
  233.4 4.5 %dattn_part.3 = bf16[1024,384]{1,0:T(8,128)(2,1)} custom-call(bf16[1024,1536]{1,0:T(8,128)(2,1)} %bitcast.16, bf16[2,1536,384]{2,1,0:T(8,128)(2,1)} %bitcast.10), custom_call_target="tpu_custom_call" | custom-call | tf_op jit(solution)/shard_map/dattn_part/pallas_call | solution.py:323
  238.2 4.1 %project_far.1 = (bf16[128,1536]{1,0:T(8,128)(2,1)}, bf16[128,1536]{1,0:T(8,128)(2,1)}) custom-call(s32[1]{0:T(128)} %bitcast.seq_ref, bf16[1024,384]{1,0:T(8,128)(2,1)} %get-tuple-element.47.a_ref.a1_ref.a3_ref.a0_ref, bf16[1024,384]{1,0:T(8,128)(2,1)} %copy-done.1, bf16[2,1536,384]{2,1,0:T(8,128)(2,1)} %bitcast.11), custom_call_target="tpu_custom_call" | custom-call | tf_op jit(solution)/shard_map/project_far/pallas_call | solution.py:420
  242.3 3.2 collective-permute-start.21
  245.5 4.6 %dattn_part.2.own_ref = f32[1024,384]{1,0:T(8,128)} custom-call(bf16[1024,1536]{1,0:T(8,128)(2,1)} %bitcast.17, bf16[2,1536,384]{2,1,0:T(8,128)(2,1)} %bitcast.12), custom_call_target="tpu_custom_call" | custom-call | tf_op jit(solution)/shard_map/dattn_part/pallas_call | solution.py:323
  250.1 4.5 %collective-permute-done.20.up_ref = bf16[128,1536]{1,0:T(8,128)(2,1)S(1)} collective-permute-done((bf16[128,1536]{1,0:T(8,128)(2,1)}, bf16[128,1536]{1,0:T(8,128)(2,1)S(1)}, u32[]{:S(2)}, u32[]{:S(2)}) %collective-permute-start.20) | collective-permute-done | bytes 393248 | tf_op jit(solution)/shard_map/ppermute | solution.py:538
  256.1 4.9 %project_near.1 = (bf16[256,1536]{1,0:T(8,128)(2,1)}, bf16[256,1536]{1,0:T(8,128)(2,1)}) custom-call(s32[1]{0:T(128)} %bitcast.seq_ref, bf16[1024,384]{1,0:T(8,128)(2,1)} %get-tuple-element.47.a_ref.a1_ref.a3_ref.a0_ref, bf16[1024,384]{1,0:T(8,128)(2,1)} %copy-done.1, bf16[1024,384]{1,0:T(8,128)(2,1)} %get-tuple-element.47.a_ref.a1_ref.a3_ref.a0_ref, ...), custom_call_target="tpu_custom_call" | custom-call | tf_op jit(solution)/shard_map/project_near/pallas_call | solution.py:430
  261.9 11.1 %attention_backward.1 = bf16[8,3,128,384]{3,2,1,0:T(8,128)(2,1)} custom-call(s32[1,3]{1,0:T(1,128)} %frames_ref.7, bf16[8,3,128,384]{3,2,1,0:T(8,128)(2,1)} %copy-done, f32[1024,384]{1,0:T(8,128)} %dattn_part.2.own_ref, bf16[1024,384]{1,0:T(8,128)(2,1)} %copy-done.6, bf16[3,640,640]{2,1,0:T(8,128)(2,1)} %get-tuple-element.65.p1_ref, ...), custom_call_target="tpu_custom_call" | custom-call | tf_op jit(solution)/shard_map/attention_backward/pallas_call | solution.py:180
  273.0 5.2 %all-to-all-start.1 = ((bf16[8,3,128,384]{3,2,1,0:T(8,128)(2,1)}), bf16[8,3,128,384]{3,2,1,0:T(8,128)(2,1)S(1)}, u32[]{:S(2)}, u32[]{:S(2)}) async-start(bf16[8,3,128,384]{3,2,1,0:T(8,128)(2,1)} %attention_backward.1), calls=%async_computation.1 | async-start | bytes 4718592 | tf_op jit(solution)/shard_map/all_to_all | solution.py:600
  284.9 4.2 %collective-permute-start.27 = (bf16[4,96,384]{2,1,0:T(8,128)(2,1)}, bf16[4,96,384]{2,1,0:T(8,128)(2,1)}, u32[]{:S(2)}, u32[]{:S(2)}) collective-permute-start(bf16[4,96,384]{2,1,0:T(8,128)(2,1)} %get-tuple-element.71), channel_id=1, source_target_pairs={{0,128},{8,136},{16,144},{24,152},{32,160},{40,168},{48,176},{56,1... | collective-permute-start | bytes 884744 | tf_op jit(solution)/shard_map/ppermute | solution.py:538
  289.2 5.8 %collective-permute-done.26.b_ref = bf16[4,96,384]{2,1,0:T(8,128)(2,1)S(1)} collective-permute-done((bf16[4,96,384]{2,1,0:T(8,128)(2,1)}, bf16[4,96,384]{2,1,0:T(8,128)(2,1)S(1)}, u32[]{:S(2)}, u32[]{:S(2)}) %collective-permute-start.26) | collective-permute-done | bytes 294944 | tf_op jit(solution)/shard_map/ppermute | solution.py:538
  294.9 5.9 %collective-permute-done.27.c_ref = bf16[4,96,384]{2,1,0:T(8,128)(2,1)} collective-permute-done((bf16[4,96,384]{2,1,0:T(8,128)(2,1)}, bf16[4,96,384]{2,1,0:T(8,128)(2,1)}, u32[]{:S(2)}, u32[]{:S(2)}) %collective-permute-start.27) | collective-permute-done | bytes 294944 | tf_op jit(solution)/shard_map/ppermute | solution.py:538
  306.3 3.1 collective-permute-start.31
  309.3 13.5 %collective-permute-done.23.c1_ref = bf16[256,1536]{1,0:T(8,128)(2,1)S(1)} collective-permute-done((bf16[256,1536]{1,0:T(8,128)(2,1)}, bf16[256,1536]{1,0:T(8,128)(2,1)S(1)}, u32[]{:S(2)}, u32[]{:S(2)}) %collective-permute-start.23) | collective-permute-done | bytes 786464 | tf_op jit(solution)/shard_map/ppermute | solution.py:538
  323.7 4.6 %project_home.1 = (f32[128,1536]{1,0:T(8,128)}, bf16[128,1536]{1,0:T(8,128)(2,1)}) custom-call(s32[1]{0:T(128)} %bitcast.seq_ref, bf16[1024,384]{1,0:T(8,128)(2,1)} %get-tuple-element.47.a_ref.a1_ref.a3_ref.a0_ref, bf16[1024,384]{1,0:T(8,128)(2,1)} %copy-done.1, bf16[2,1536,384]{2,1,0:T(8,128)(2,1)} %bitcast.14, bf16[256,1536]{1,0:T(8,128)(2,1)} %copy-done.5, ...), custom_call_target="tpu_custom_call" | custom-call | tf_op jit(solution)/shard_map/project_home/pallas_call | solution.py:440
  331.3 9.4 %collective-permute-done.32 = f32[96,384]{1,0:T(8,128)S(1)} collective-permute-done((f32[96,384]{1,0:T(8,128)S(1)}, f32[96,384]{1,0:T(8,128)S(1)}, u32[]{:S(2)}, u32[]{:S(2)}) %collective-permute-start.32) | collective-permute-done | bytes 147488 | tf_op jit(solution)/shard_map/ppermute | solution.py:610
  341.4 3.5 gated_output.1
  346.3 5.8 %unpack_heads.1 = bf16[3,128,3072]{2,1,0:T(8,128)(2,1)} custom-call(bf16[8,3,128,384]{3,2,1,0:T(8,128)(2,1)} %copy-done.2), custom_call_target="tpu_custom_call" | custom-call | tf_op jit(solution)/shard_map/unpack_heads/pallas_call | solution.py:226
  (123 shorter events, 50.5 us)
Async XLA Ops:
  0.6 13.4 %collective-permute-start = (bf16[96,384]{1,0:T(8,128)(2,1)}, bf16[96,384]{1,0:T(8,128)(2,1)S(1)}, u32[]{:S(2)}, u32[]{:S(2)}) collective-permute-start(bf16[96,384]{1,0:T(8,128)(2,1)} %bitcast.23), channel_id=1, source_target_pairs={{0,0},{1,128},{2,2},{3,130},{4,4},{5,132},{6,6},{7,134},{8,8},{9,1... | collective-permute-start | bytes 221192 | tf_op jit(solution)/shard_map/ppermute | solution.py:567
  14.1 70.2 %all-to-all-start = ((bf16[8,3,128,384]{3,2,1,0:T(8,128)(2,1)}), bf16[8,3,128,384]{3,2,1,0:T(8,128)(2,1)S(1)}, u32[]{:S(2)}, u32[]{:S(2)}) async-start(bf16[8,3,128,384]{3,2,1,0:T(8,128)(2,1)} %pack_heads.1), calls=%async_computation | async-start | bytes 4718592 | tf_op jit(solution)/shard_map/all_to_all | solution.py:571
  20.0 64.3 %collective-permute-start.1 = (bf16[128,1536]{1,0:T(8,128)(2,1)}, bf16[128,1536]{1,0:T(8,128)(2,1)S(1)}, u32[]{:S(2)}, u32[]{:S(2)}) collective-permute-start(bf16[128,1536]{1,0:T(8,128)(2,1)} %get-tuple-element.44), channel_id=1, source_target_pairs={{0,1},{1,0},{2,3},{3,2},{4,5},{5,4},{6,7},{7,6},{8,9},{9,8},{10,11... | collective-permute-start | bytes 1179656 | tf_op jit(solution)/shard_map/ppermute | solution.py:554
  20.0 11.3 %collective-permute-start.4 = (bf16[96,384]{1,0:T(8,128)(2,1)S(1)}, bf16[96,384]{1,0:T(8,128)(2,1)S(1)}, u32[]{:S(2)}, u32[]{:S(2)}) collective-permute-start(bf16[96,384]{1,0:T(8,128)(2,1)S(1)} %collective-permute-done.refs_0_), channel_id=1, source_target_pairs={{0,16},{8,24},{16,32},{24,40},{32,48},{40,56},{48,0},{56,8},{64,80... | collective-permute-start | bytes 221192 | tf_op jit(solution)/shard_map/ppermute | solution.py:538
  23.3 43.3 %collective-permute-start.3 = (bf16[96,384]{1,0:T(8,128)(2,1)S(1)}, bf16[96,384]{1,0:T(8,128)(2,1)S(1)}, u32[]{:S(2)}, u32[]{:S(2)}) collective-permute-start(bf16[96,384]{1,0:T(8,128)(2,1)S(1)} %collective-permute-done.refs_0_), channel_id=1, source_target_pairs={{0,32},{8,40},{16,48},{24,56},{32,0},{40,8},{48,16},{56,24},{64,96... | collective-permute-start | bytes 221192 | tf_op jit(solution)/shard_map/ppermute | solution.py:538
  28.6 37.9 %collective-permute-start.2 = (bf16[96,384]{1,0:T(8,128)(2,1)S(1)}, bf16[96,384]{1,0:T(8,128)(2,1)S(1)}, u32[]{:S(2)}, u32[]{:S(2)}) collective-permute-start(bf16[96,384]{1,0:T(8,128)(2,1)S(1)} %collective-permute-done.refs_0_), channel_id=1, source_target_pairs={{0,48},{8,56},{16,0},{24,8},{32,16},{40,24},{48,32},{56,40},{64,11... | collective-permute-start | bytes 221192 | tf_op jit(solution)/shard_map/ppermute | solution.py:538
  69.6 13.1 %collective-permute-start.7 = (bf16[4,96,384]{2,1,0:T(8,128)(2,1)}, bf16[4,96,384]{2,1,0:T(8,128)(2,1)S(1)}, u32[]{:S(2)}, u32[]{:S(2)}) collective-permute-start(bf16[4,96,384]{2,1,0:T(8,128)(2,1)} %stack_pieces.1.refs_0_), channel_id=1, source_target_pairs={{0,64},{8,72},{16,80},{24,88},{32,96},{40,104},{48,112},{56,120},{... | collective-permute-start | bytes 884744 | tf_op jit(solution)/shard_map/ppermute | solution.py:538
  70.3 12.5 %collective-permute-start.6 = (bf16[4,96,384]{2,1,0:T(8,128)(2,1)}, bf16[4,96,384]{2,1,0:T(8,128)(2,1)S(1)}, u32[]{:S(2)}, u32[]{:S(2)}) collective-permute-start(bf16[4,96,384]{2,1,0:T(8,128)(2,1)} %stack_pieces.1.refs_0_), channel_id=1, source_target_pairs={{0,128},{8,136},{16,144},{24,152},{32,160},{40,168},{48,176},{56,1... | collective-permute-start | bytes 884744 | tf_op jit(solution)/shard_map/ppermute | solution.py:538
  71.6 11.7 %collective-permute-start.5 = (bf16[4,96,384]{2,1,0:T(8,128)(2,1)}, bf16[4,96,384]{2,1,0:T(8,128)(2,1)S(1)}, u32[]{:S(2)}, u32[]{:S(2)}) collective-permute-start(bf16[4,96,384]{2,1,0:T(8,128)(2,1)} %stack_pieces.1.refs_0_), channel_id=1, source_target_pairs={{0,192},{8,200},{16,208},{24,216},{32,224},{40,232},{48,240},{56,2... | collective-permute-start | bytes 884744 | tf_op jit(solution)/shard_map/ppermute | solution.py:538
  84.3 17.4 %collective-permute-start.15 = (bf16[128,1536]{1,0:T(8,128)(2,1)S(1)}, bf16[128,1536]{1,0:T(8,128)(2,1)S(1)}, u32[]{:S(2)}, u32[]{:S(2)}) collective-permute-start(bf16[128,1536]{1,0:T(8,128)(2,1)S(1)} %copy-done.7), channel_id=1, source_target_pairs={{0,2},{1,3},{2,4},{3,5},{4,6},{5,7},{6,0},{7,1},{8,10},{9,11},{10,... | collective-permute-start | bytes 1179656 | tf_op jit(solution)/shard_map/ppermute | solution.py:538
  84.9 16.9 %collective-permute-start.14 = (bf16[128,1536]{1,0:T(8,128)(2,1)S(1)}, bf16[128,1536]{1,0:T(8,128)(2,1)}, u32[]{:S(2)}, u32[]{:S(2)}) collective-permute-start(bf16[128,1536]{1,0:T(8,128)(2,1)S(1)} %collective-permute-done.1.refs_1_), channel_id=1, source_target_pairs={{0,6},{1,7},{2,0},{3,1},{4,2},{5,3},{6,4},{7,5},{8,14},{9,15},{10,... | collective-permute-start | bytes 1179656 | tf_op jit(solution)/shard_map/ppermute | solution.py:538
  97.4 119.2 %collective-permute-start.8 = (bf16[1024,384]{1,0:T(8,128)(2,1)}, bf16[1024,384]{1,0:T(8,128)(2,1)S(1)}, u32[]{:S(2)}, u32[]{:S(2)}) collective-permute-start(bf16[1024,384]{1,0:T(8,128)(2,1)} %get-tuple-element.47.a_ref.a1_ref.a3_ref.a0_ref), channel_id=1, source_target_pairs={{0,1},{1,0},{2,3},{3,2},{4,5},{5,4},{6,7},{7,6},{8,9},{9,8},{10,11... | collective-permute-start | bytes 2359304 | tf_op jit(solution)/shard_map/ppermute | solution.py:554
  99.7 12.1 %collective-permute-start.13 = (bf16[128,1536]{1,0:T(8,128)(2,1)S(1)}, bf16[128,1536]{1,0:T(8,128)(2,1)S(1)}, u32[]{:S(2)}, u32[]{:S(2)}) collective-permute-start(bf16[128,1536]{1,0:T(8,128)(2,1)S(1)} %copy-done.7), channel_id=1, source_target_pairs={{0,6},{1,7},{2,0},{3,1},{4,2},{5,3},{6,4},{7,5},{8,14},{9,15},{10,... | collective-permute-start | bytes 1179656 | tf_op jit(solution)/shard_map/ppermute | solution.py:538
  101.1 13.3 %collective-permute-start.18 = (bf16[128,1536]{1,0:T(8,128)(2,1)S(1)}, bf16[128,1536]{1,0:T(8,128)(2,1)S(1)}, u32[]{:S(2)}, u32[]{:S(2)}) collective-permute-start(bf16[128,1536]{1,0:T(8,128)(2,1)S(1)} %collective-permute-done.1.refs_1_), channel_id=1, source_target_pairs={{0,2},{1,3},{2,4},{3,5},{4,6},{5,7},{6,0},{7,1},{8,10},{9,11},{10,... | collective-permute-start | bytes 1179656 | tf_op jit(solution)/shard_map/ppermute | solution.py:538
  101.7 16.8 %collective-permute-start.16 = (bf16[128,1536]{1,0:T(8,128)(2,1)S(1)}, bf16[128,1536]{1,0:T(8,128)(2,1)S(1)}, u32[]{:S(2)}, u32[]{:S(2)}) collective-permute-start(bf16[128,1536]{1,0:T(8,128)(2,1)S(1)} %collective-permute-done.15.refs_6_), channel_id=1, source_target_pairs={{0,2},{1,3},{2,4},{3,5},{4,6},{5,7},{6,0},{7,1},{8,10},{9,11},{10,... | collective-permute-start | bytes 1179656 | tf_op jit(solution)/shard_map/ppermute | solution.py:538
  101.8 16.7 %collective-permute-start.17 = (bf16[128,1536]{1,0:T(8,128)(2,1)}, bf16[128,1536]{1,0:T(8,128)(2,1)S(1)}, u32[]{:S(2)}, u32[]{:S(2)}) collective-permute-start(bf16[128,1536]{1,0:T(8,128)(2,1)} %collective-permute-done.14.refs_3_), channel_id=1, source_target_pairs={{0,6},{1,7},{2,0},{3,1},{4,2},{5,3},{6,4},{7,5},{8,14},{9,15},{10,... | collective-permute-start | bytes 1179656 | tf_op jit(solution)/shard_map/ppermute | solution.py:538
  224.6 36.5 %collective-permute-start.22 = (bf16[2,8,96,384]{3,2,1,0:T(8,128)(2,1)}, bf16[2,8,96,384]{3,2,1,0:T(8,128)(2,1)S(1)}, u32[]{:S(2)}, u32[]{:S(2)}) collective-permute-start(bf16[2,8,96,384]{3,2,1,0:T(8,128)(2,1)} %get-tuple-element.58), channel_id=1, source_target_pairs={{0,8},{8,0},{16,24},{24,16},{32,40},{40,32},{48,56},{56,48},{64,72... | collective-permute-start | bytes 3538952 | tf_op jit(solution)/shard_map/ppermute | solution.py:558
  225.6 3.5 collective-permute-start.12
  237.9 23.2 %collective-permute-start.19 = (bf16[1024,384]{1,0:T(8,128)(2,1)}, bf16[1024,384]{1,0:T(8,128)(2,1)S(1)}, u32[]{:S(2)}, u32[]{:S(2)}) collective-permute-start(bf16[1024,384]{1,0:T(8,128)(2,1)} %dattn_part.3), channel_id=1, source_target_pairs={{0,1},{1,0},{2,3},{3,2},{4,5},{5,4},{6,7},{7,6},{8,9},{9,8},{10,11... | collective-permute-start | bytes 2359304 | tf_op jit(solution)/shard_map/ppermute | solution.py:554
  242.3 12.3 %collective-permute-start.20 = (bf16[128,1536]{1,0:T(8,128)(2,1)}, bf16[128,1536]{1,0:T(8,128)(2,1)S(1)}, u32[]{:S(2)}, u32[]{:S(2)}) collective-permute-start(bf16[128,1536]{1,0:T(8,128)(2,1)} %get-tuple-element.54), channel_id=1, source_target_pairs={{0,2},{1,3},{2,4},{3,5},{4,6},{5,7},{6,0},{7,1},{8,10},{9,11},{10,... | collective-permute-start | bytes 1179656 | tf_op jit(solution)/shard_map/ppermute | solution.py:538
  242.3 12.3 %collective-permute-start.21 = (bf16[128,1536]{1,0:T(8,128)(2,1)}, bf16[128,1536]{1,0:T(8,128)(2,1)S(1)}, u32[]{:S(2)}, u32[]{:S(2)}) collective-permute-start(bf16[128,1536]{1,0:T(8,128)(2,1)} %get-tuple-element.55), channel_id=1, source_target_pairs={{0,6},{1,7},{2,0},{3,1},{4,2},{5,3},{6,4},{7,5},{8,14},{9,15},{10,... | collective-permute-start | bytes 1179656 | tf_op jit(solution)/shard_map/ppermute | solution.py:538
  273.0 71.9 %all-to-all-start.1 = ((bf16[8,3,128,384]{3,2,1,0:T(8,128)(2,1)}), bf16[8,3,128,384]{3,2,1,0:T(8,128)(2,1)S(1)}, u32[]{:S(2)}, u32[]{:S(2)}) async-start(bf16[8,3,128,384]{3,2,1,0:T(8,128)(2,1)} %attention_backward.1), calls=%async_computation.1 | async-start | bytes 4718592 | tf_op jit(solution)/shard_map/all_to_all | solution.py:600
  278.2 44.7 %collective-permute-start.23 = (bf16[256,1536]{1,0:T(8,128)(2,1)}, bf16[256,1536]{1,0:T(8,128)(2,1)S(1)}, u32[]{:S(2)}, u32[]{:S(2)}) collective-permute-start(bf16[256,1536]{1,0:T(8,128)(2,1)} %get-tuple-element.59), channel_id=1, source_target_pairs={{0,2},{1,3},{2,4},{3,5},{4,6},{5,7},{6,0},{7,1},{8,10},{9,11},{10,... | collective-permute-start | bytes 2359304 | tf_op jit(solution)/shard_map/ppermute | solution.py:538
  279.7 43.2 %collective-permute-start.24 = (bf16[256,1536]{1,0:T(8,128)(2,1)}, bf16[256,1536]{1,0:T(8,128)(2,1)}, u32[]{:S(2)}, u32[]{:S(2)}) collective-permute-start(bf16[256,1536]{1,0:T(8,128)(2,1)} %get-tuple-element.60), channel_id=1, source_target_pairs={{0,6},{1,7},{2,0},{3,1},{4,2},{5,3},{6,4},{7,5},{8,14},{9,15},{10,... | collective-permute-start | bytes 2359304 | tf_op jit(solution)/shard_map/ppermute | solution.py:538
  284.1 10.8 %collective-permute-start.26 = (bf16[4,96,384]{2,1,0:T(8,128)(2,1)}, bf16[4,96,384]{2,1,0:T(8,128)(2,1)S(1)}, u32[]{:S(2)}, u32[]{:S(2)}) collective-permute-start(bf16[4,96,384]{2,1,0:T(8,128)(2,1)} %get-tuple-element.70), channel_id=1, source_target_pairs={{0,64},{8,72},{16,80},{24,88},{32,96},{40,104},{48,112},{56,120},{... | collective-permute-start | bytes 884744 | tf_op jit(solution)/shard_map/ppermute | solution.py:538
  284.9 15.9 %collective-permute-start.27 = (bf16[4,96,384]{2,1,0:T(8,128)(2,1)}, bf16[4,96,384]{2,1,0:T(8,128)(2,1)}, u32[]{:S(2)}, u32[]{:S(2)}) collective-permute-start(bf16[4,96,384]{2,1,0:T(8,128)(2,1)} %get-tuple-element.71), channel_id=1, source_target_pairs={{0,128},{8,136},{16,144},{24,152},{32,160},{40,168},{48,176},{56,1... | collective-permute-start | bytes 884744 | tf_op jit(solution)/shard_map/ppermute | solution.py:538
  289.2 11.7 %collective-permute-start.28 = (bf16[4,96,384]{2,1,0:T(8,128)(2,1)}, bf16[4,96,384]{2,1,0:T(8,128)(2,1)}, u32[]{:S(2)}, u32[]{:S(2)}) collective-permute-start(bf16[4,96,384]{2,1,0:T(8,128)(2,1)} %get-tuple-element.72), channel_id=1, source_target_pairs={{0,192},{8,200},{16,208},{24,216},{32,224},{40,232},{48,240},{56,2... | collective-permute-start | bytes 884744 | tf_op jit(solution)/shard_map/ppermute | solution.py:538
  302.9 26.0 %collective-permute-start.29 = (bf16[96,384]{1,0:T(8,128)(2,1)}, bf16[96,384]{1,0:T(8,128)(2,1)S(1)}, u32[]{:S(2)}, u32[]{:S(2)}) collective-permute-start(bf16[96,384]{1,0:T(8,128)(2,1)} %get-tuple-element.74), channel_id=1, source_target_pairs={{0,16},{8,24},{16,32},{24,40},{32,48},{40,56},{48,0},{56,8},{64,80... | collective-permute-start | bytes 221192 | tf_op jit(solution)/shard_map/ppermute | solution.py:538
  304.1 24.7 %collective-permute-start.30 = (bf16[96,384]{1,0:T(8,128)(2,1)}, bf16[96,384]{1,0:T(8,128)(2,1)S(1)}, u32[]{:S(2)}, u32[]{:S(2)}) collective-permute-start(bf16[96,384]{1,0:T(8,128)(2,1)} %get-tuple-element.75), channel_id=1, source_target_pairs={{0,32},{8,40},{16,48},{24,56},{32,0},{40,8},{48,16},{56,24},{64,96... | collective-permute-start | bytes 221192 | tf_op jit(solution)/shard_map/ppermute | solution.py:538
  306.3 22.6 %collective-permute-start.31 = (bf16[96,384]{1,0:T(8,128)(2,1)}, bf16[96,384]{1,0:T(8,128)(2,1)S(1)}, u32[]{:S(2)}, u32[]{:S(2)}) collective-permute-start(bf16[96,384]{1,0:T(8,128)(2,1)} %get-tuple-element.76), channel_id=1, source_target_pairs={{0,48},{8,56},{16,0},{24,8},{32,16},{40,24},{48,32},{56,40},{64,11... | collective-permute-start | bytes 221192 | tf_op jit(solution)/shard_map/ppermute | solution.py:538
  328.3 12.4 %collective-permute-start.25 = (bf16[128,1536]{1,0:T(8,128)(2,1)}, bf16[128,1536]{1,0:T(8,128)(2,1)S(1)}, u32[]{:S(2)}, u32[]{:S(2)}) collective-permute-start(bf16[128,1536]{1,0:T(8,128)(2,1)} %get-tuple-element.62), channel_id=1, source_target_pairs={{0,1},{1,0},{2,3},{3,2},{4,5},{5,4},{6,7},{7,6},{8,9},{9,8},{10,11... | collective-permute-start | bytes 1179656 | tf_op jit(solution)/shard_map/ppermute | solution.py:554
  328.9 11.8 %collective-permute-start.32 = (f32[96,384]{1,0:T(8,128)S(1)}, f32[96,384]{1,0:T(8,128)S(1)}, u32[]{:S(2)}, u32[]{:S(2)}) collective-permute-start(f32[96,384]{1,0:T(8,128)S(1)} %convert_add_fusion), channel_id=1, source_target_pairs={{0,0},{128,1},{2,2},{130,3},{4,4},{132,5},{6,6},{134,7},{8,8},{136... | collective-permute-start | bytes 442376 | tf_op jit(solution)/shard_map/ppermute | solution.py:610
  (36 other events, 281.4 us)

commit v3 on v2

--- a/solution.py
+++ b/solution.py
@@ -259,29 +259,6 @@
     )(frames, steps, seq, table, table, cotangent, cotangent)
 
 
-def assemble_kernel(seq_ref, *refs):
-    blocks, out_ref, sems = refs[:8], refs[8], refs[9]
-    x, z = seq_ref[0] // 2, seq_ref[0] % 2
-    copies = []
-    for i, block in enumerate(blocks):
-        place = 2 * ((x + i // 2) % 4) + (z ^ (i % 2))
-        copies.append(pltpu.make_async_copy(block, out_ref.at[place], sems.at[i]))
-        copies[-1].start()
-    for copy in copies:
-        copy.wait()
-
-
-def assemble(seq, blocks):
-    return pl.pallas_call(
-        assemble_kernel,
-        out_shape=jax.ShapeDtypeStruct((8, 128, 1536), BF),
-        in_specs=[pl.BlockSpec(memory_space=pltpu.SMEM)] + [pl.BlockSpec(memory_space=pl.ANY)] * 8,
-        out_specs=pl.BlockSpec(memory_space=pl.ANY),
-        scratch_shapes=[pltpu.SemaphoreType.DMA((8,))],
-        name="assemble",
-    )(seq, *blocks)
-
-
 def output_kernel(
     frames_ref, steps_ref, seq_ref, t0_ref, t1_ref, l0_ref, l1_ref, own_ref, other_ref, out_ref
 ):
@@ -315,55 +292,37 @@
     )(frames, steps, seq, table, table, latents, latents, own, other)
 
 
-def dattn_kernel(d_ref, w_ref, out_ref):
-    out_ref[...] = dot_nn(d_ref[...], w_ref[0]).astype(out_ref.dtype)
-
-
-def dattn_part(dproj, weights, which, dtype):
+def dattn_kernel(seq_ref, *refs):
+    blocks, (w_ref, dproj_ref, other_ref, own_ref) = refs[:8], refs[8:]
+    x, z = seq_ref[0] // 2, seq_ref[0] % 2
+    for i, block in enumerate(blocks):
+        place = 2 * ((x + i // 2) % 4) + (z ^ (i % 2))
+        dproj_ref[pl.ds(pl.multiple_of(place * 128, 128), 128), :] = block[...]
+    for m in range(2):
+        rows = slice(m * 512, (m + 1) * 512)
+        d = dproj_ref[rows, :]
+        other_ref[rows, :] = dot_nn(d, w_ref[1]).astype(BF)
+        own_ref[rows, :] = dot_nn(d, w_ref[0])
+
+
+def dattn_parts(seq, blocks, weights):
+    vmem = pl.BlockSpec(memory_space=pltpu.VMEM)
     return pl.pallas_call(
         dattn_kernel,
-        out_shape=jax.ShapeDtypeStruct((1024, 384), dtype),
-        grid=(2,),
-        in_specs=[
-            pl.BlockSpec((512, 1536), lambda m: (m, 0)),
-            pl.BlockSpec((1, 1536, 384), lambda m: (which, 0, 0)),
-        ],
-        out_specs=pl.BlockSpec((512, 384), lambda m: (m, 0)),
+        out_shape=(
+            jax.ShapeDtypeStruct((1024, 1536), BF),
+            jax.ShapeDtypeStruct((1024, 384), BF),
+            jax.ShapeDtypeStruct((1024, 384), F32),
+        ),
+        in_specs=[pl.BlockSpec(memory_space=pltpu.SMEM)] + [vmem] * 9,
+        out_specs=(
+            pl.BlockSpec((1024, 1536), lambda: (0, 0)),
+            pl.BlockSpec((1024, 384), lambda: (0, 0)),
+            pl.BlockSpec((1024, 384), lambda: (0, 0)),
+        ),
         compiler_params=pltpu.CompilerParams(vmem_limit_bytes=VMEM_LIMIT),
-        name="dattn_part",
-    )(dproj, weights)
-
-
-def weave_kernel(dp_ref, *refs):
-    out_ref = refs[8]
-    y, zh, core = dp_ref[0] // 8, dp_ref[0] // 2 % 4, dp_ref[0] % 2
-    for flip in range(2):
-        for k in range(4):
-            for m in range(4):
-                place = 4 * ((y + k) % 4) + (zh + m) % 4
-                out_ref[place, core ^ flip] = refs[4 * flip + k][m]
-
-
-def weave(dp, mine, theirs):
-    return pl.pallas_call(
-        weave_kernel,
-        out_shape=jax.ShapeDtypeStruct((16, 2, 96, 384), BF),
-        in_specs=[pl.BlockSpec(memory_space=pltpu.SMEM)]
-        + [pl.BlockSpec((4, 96, 384), lambda: (0, 0, 0))] * 8,
-        out_specs=pl.BlockSpec((16, 2, 96, 384), lambda: (0, 0, 0, 0)),
-        name="weave",
-    )(dp, *mine, *theirs)
-
-
-def stack_kernel(*refs):
-    for i, ref in enumerate(refs[:-1]):
-        refs[-1][i] = ref[...]
-
-
-def stack_pieces(pieces):
-    return pl.pallas_call(
-        stack_kernel, out_shape=jax.ShapeDtypeStruct((4, 96, 384), BF), name="stack_pieces"
-    )(*pieces)
+        name="dattn_parts",
+    )(seq, *blocks, weights)
 
 
 def rows_spec(k):
@@ -565,29 +524,24 @@
     moves = piece_moves(lax.axis_size("dp"), lax.axis_size("seq"))
 
     piece = lax.ppermute(out_weight.T, both, moves)
+    packed = pack_heads(qkv_input.transpose(1, 0, 2))
+    packed, piece = lax.optimization_barrier((packed, piece))
+    weights = lax.all_gather(piece, "dp", axis=0, tiled=True).reshape(2, 1536, 384)
+    heads = lax.all_to_all(packed, "seq", split_axis=0, concat_axis=0, tiled=True)
+
     keep, send = gated_cotangent(frames, timesteps, seq, gate_table, cotangent)
-    packed = pack_heads(qkv_input.transpose(1, 0, 2))
-    packed, piece, keep, send = lax.optimization_barrier((packed, piece, keep, send))
-    heads = lax.all_to_all(packed, "seq", split_axis=0, concat_axis=0, tiled=True)
     got = swap_z(send)
-
-    pieces = stack_pieces([piece] + [along_z(piece, -k) for k in range(1, 4)])
-    mine = [pieces] + [along_y(pieces, -k) for k in range(1, 4)]
-    heads, keep, got, mine = lax.optimization_barrier((heads, keep, got, mine))
-
     b1 = [along_x(keep, -1), along_x(got, -1)]
     b3 = [along_x(keep, 1), along_x(got, 1)]
     b2 = [along_x(b3[0], 1), along_x(b1[1], -1)]
-    theirs = [swap_core(p) for p in mine]
+
+    heads, weights = lax.optimization_barrier((heads, weights))
     attn, p1, p2 = attention_forward(frames, heads)
     attn_other = swap_z(attn)
-    weights = weave(dp, mine, theirs).reshape(2, 1536, 384)
-    dproj = assemble(seq, [keep, got, *b1, *b2, *b3]).reshape(1024, 1536)
-
-    d_recv = swap_z(dattn_part(dproj, weights, 1, BF))
+    dproj, d_send, d_own = dattn_parts(seq, [keep, got, *b1, *b2, *b3], weights)
+    d_recv = swap_z(d_send)
     up, down = project_far(seq, attn, attn_other, weights)
     up, down = along_x(up, 1), along_x(down, -1)
-    d_own = dattn_part(dproj, weights, 0, F32)
     w_keep, w_send = dweight_part(dp, dproj, attn, attn_other)
     w_got = swap_core(w_send)
     t1, t3 = project_near(seq, attn, attn_other, weights, up, down)

time: 356 us -> 251 us (0.71)
  Pallas kernels: 175 us -> 71.8 us
  starting transfers between devices: 63.7 us -> 49.4 us
  between operations: 0.86 us -> 14.2 us
  waiting for transfers between devices: 102 us -> 106 us
    pallas_call x5 -> x1, Pallas kernels: 111 us -> 7.42 us  [dattn_parts(): pl.pallas_call(dattn_kernel, out_shape=(jax.ShapeDtypeStruct((1024, 1536)...]
    ppermute x4, waiting for transfers between devices: 0.01 us -> 37.9 us  [swap_z(): lax.ppermute(x, 'seq', [(i, i ^ 1) for i in range(lax.axis_size('seq'))])]
    ppermute x22 -> x16, waiting for transfers between devices: 88.9 us -> 52 us  [along(): return lax.ppermute(x, axis, moves)]
    ppermute x22 -> x16, starting transfers between devices: 41.3 us -> 27.5 us  [along(): return lax.ppermute(x, axis, moves)]
    all_gather x0 -> x1, waiting for transfers between devices: none -> 6.49 us  [body(): lax.all_gather(piece, 'dp', axis=0, tiled=True).reshape(2, 1536, 384)]
    unnamed x67 -> x41, local copies, waits for them, and re-layouts: 11.6 us -> 9.25 us
  transfers between devices with their start and end apart: 35 -> 26, of which waited for: 15 -> 9; matrix products, arithmetic and copies ran while one was open for 0% -> 0% of each run, Pallas kernels for 43% -> 19%
where the time goes in v3:
time: 251 us; the launch traced here: 250 us
  waiting for transfers between devices  106 us (42%)
  Pallas kernels  71.8 us (29%)
  starting transfers between devices  49.4 us (20%)
  between operations  14.2 us (6%)
  local copies, waits for them, and re-layouts  9.25 us (4%)
    ppermute x16, waiting for transfers between devices, along(): return lax.ppermute(x, axis, moves)  52 us
    ppermute x4, waiting for transfers between devices, swap_z(): lax.ppermute(x, 'seq', [(i, i ^ 1) for i in range(lax.axis_size('seq'))])  37.9 us
    ppermute x16, starting transfers between devices, along(): return lax.ppermute(x, axis, moves)  27.5 us
    pallas_call x1, Pallas kernels, attention_backward(): pl.pallas_call(bwd_kernel, out_shape=jax.ShapeDtypeStruct((8, 3, 128, 3 *...  11.2 us
    pallas_call x1, Pallas kernels, attention_forward(): pl.pallas_call(fwd_kernel, out_shape=(jax.ShapeDtypeStruct((1024, 3 * HD)...  9.82 us
    ppermute x1, waiting for transfers between devices, body(): total = lax.ppermute(total, both, [(b, a) for a, b in moves])  9.4 us
    unnamed x41, local copies, waits for them, and re-layouts  9.25 us
    pallas_call x1, Pallas kernels, dattn_parts(): pl.pallas_call(dattn_kernel, out_shape=(jax.ShapeDtypeStruct((1024, 1536)...  7.42 us
  transfers between devices with their start and end apart: 26, of which 9 were waited for; matrix products, arithmetic and copies ran while one was open for 0% of the time, Pallas kernels for 19%

profile of v3, /device:TPU:32, one launch (start us, length us, event | category | flops | bytes accessed | tf_op | source)
XLA Modules:
  0.0 250.4 jit_solution(10564224884510720028)
XLA Ops:
  7.2 4.6 %collective-permute-start = (bf16[96,384]{1,0:T(8,128)(2,1)}, bf16[96,384]{1,0:T(8,128)(2,1)S(1)}, u32[]{:S(2)}, u32[]{:S(2)}) collective-permute-start(bf16[96,384]{1,0:T(8,128)(2,1)} %bitcast.18), channel_id=1, source_target_pairs={{0,0},{1,128},{2,2},{3,130},{4,4},{5,132},{6,6},{7,134},{8,8},{9,1... | collective-permute-start | bytes 221192 | tf_op jit(solution)/shard_map/ppermute | solution.py:526
  11.9 5.8 %pack_heads.1 = bf16[8,3,128,384]{3,2,1,0:T(8,128)(2,1)} custom-call(bf16[3,128,3072]{2,1,0:T(8,128)(2,1)} %bitcast.13), custom_call_target="tpu_custom_call" | custom-call | tf_op jit(solution)/shard_map/pack_heads/pallas_call | solution.py:211
  18.3 5.8 %all-to-all-start = ((bf16[8,3,128,384]{3,2,1,0:T(8,128)(2,1)}), bf16[8,3,128,384]{3,2,1,0:T(8,128)(2,1)S(1)}, u32[]{:S(2)}, u32[]{:S(2)}) async-start(bf16[8,3,128,384]{3,2,1,0:T(8,128)(2,1)} %pack_heads.1), calls=%async_computation | async-start | bytes 4718592 | tf_op jit(solution)/shard_map/all_to_all | solution.py:530
  24.1 3.0 %gated_cotangent.1 = (bf16[128,1536]{1,0:T(8,128)(2,1)}, bf16[128,1536]{1,0:T(8,128)(2,1)}) custom-call(s32[1,3]{1,0:T(1,128)} %frames_ref.7, s32[1,3]{1,0:T(1,128)} %steps_ref.3, s32[1]{0:T(128)} %bitcast.seq_ref, f32[64,3072]{1,0:T(8,128)} %t1_ref.3, f32[64,3072]{1,0:T(8,128)} %t1_ref.3, bf16[128,3072]{1,0:T(8,128)(2,1)} %c1_ref.1, bf16[128,3072]{1,0:T(8,128)(2,1)} %c1_ref.1), custom_call_target="tpu_custom_call" | custom-call | tf_op jit(solution)/shard_map/gated_cotangent/pallas_call | solution.py:249
  27.1 2.0 collective-permute-start.5
  29.1 37.9 %collective-permute-done.2.refs_1_ = bf16[128,1536]{1,0:T(8,128)(2,1)S(1)} collective-permute-done((bf16[128,1536]{1,0:T(8,128)(2,1)}, bf16[128,1536]{1,0:T(8,128)(2,1)S(1)}, u32[]{:S(2)}, u32[]{:S(2)}) %collective-permute-start.2) | collective-permute-done | bytes 393248 | tf_op jit(solution)/shard_map/ppermute | solution.py:513
  67.0 2.1 collective-permute-start.4
  69.1 6.5 %all-gather.2.cloned.1.call-done = bf16[3072,384]{1,0:T(8,128)(2,1)} async-done(((bf16[96,384]{1,0:T(8,128)(2,1)}), bf16[3072,384]{1,0:T(8,128)(2,1)}) %all-gather.2.cloned.1.call-update) | async-done | bytes 2359312 | tf_op jit(solution)/shard_map/all_gather | solution.py:529
  75.6 9.8 %attention_forward.1 = (bf16[1024,384]{1,0:T(8,128)(2,1)}, bf16[3,640,640]{2,1,0:T(8,128)(2,1)}, bf16[3,384,384]{2,1,0:T(8,128)(2,1)}) custom-call(s32[1,3]{1,0:T(1,128)} %frames_ref.7, bf16[8,3,128,384]{3,2,1,0:T(8,128)(2,1)} %copy-done), custom_call_target="tpu_custom_call" | custom-call | tf_op jit(solution)/shard_map/attention_forward/pallas_call | solution.py:112
  86.9 2.7 %collective-permute-start.3 = (bf16[128,1536]{1,0:T(8,128)(2,1)S(1)}, bf16[128,1536]{1,0:T(8,128)(2,1)S(1)}, u32[]{:S(2)}, u32[]{:S(2)}) collective-permute-start(bf16[128,1536]{1,0:T(8,128)(2,1)S(1)} %copy-done.6), channel_id=1, source_target_pairs={{0,6},{1,7},{2,0},{3,1},{4,2},{5,3},{6,4},{7,5},{8,14},{9,15},{10,... | collective-permute-start | bytes 1179656 | tf_op jit(solution)/shard_map/ppermute | solution.py:497
  90.4 2.5 %collective-permute-start.7 = (bf16[128,1536]{1,0:T(8,128)(2,1)}, bf16[128,1536]{1,0:T(8,128)(2,1)S(1)}, u32[]{:S(2)}, u32[]{:S(2)}) collective-permute-start(bf16[128,1536]{1,0:T(8,128)(2,1)} %collective-permute-done.4.refs_3_), channel_id=1, source_target_pairs={{0,6},{1,7},{2,0},{3,1},{4,2},{5,3},{6,4},{7,5},{8,14},{9,15},{10,... | collective-permute-start | bytes 1179656 | tf_op jit(solution)/shard_map/ppermute | solution.py:497
  92.9 6.2 %collective-permute-done.3.refs_2_ = bf16[128,1536]{1,0:T(8,128)(2,1)S(1)} collective-permute-done((bf16[128,1536]{1,0:T(8,128)(2,1)S(1)}, bf16[128,1536]{1,0:T(8,128)(2,1)S(1)}, u32[]{:S(2)}, u32[]{:S(2)}) %collective-permute-start.3) | collective-permute-done | bytes 393248 | tf_op jit(solution)/shard_map/ppermute | solution.py:497
  99.1 10.9 %collective-permute-done.6.refs_4_ = bf16[128,1536]{1,0:T(8,128)(2,1)S(1)} collective-permute-done((bf16[128,1536]{1,0:T(8,128)(2,1)S(1)}, bf16[128,1536]{1,0:T(8,128)(2,1)S(1)}, u32[]{:S(2)}, u32[]{:S(2)}) %collective-permute-start.6) | collective-permute-done | bytes 393248 | tf_op jit(solution)/shard_map/ppermute | solution.py:497
  111.6 7.4 %dattn_parts.1 = (bf16[1024,1536]{1,0:T(8,128)(2,1)}, bf16[1024,384]{1,0:T(8,128)(2,1)}, f32[1024,384]{1,0:T(8,128)}) custom-call(s32[1]{0:T(128)} %bitcast.seq_ref, bf16[128,1536]{1,0:T(8,128)(2,1)} %get-tuple-element.41.refs_0_, bf16[128,1536]{1,0:T(8,128)(2,1)} %copy-done.7, bf16[128,1536]{1,0:T(8,128)(2,1)} %copy-done.9, ...), custom_call_target="tpu_custom_call" | custom-call | tf_op jit(solution)/shard_map/dattn_parts/pallas_call | solution.py:310
  119.9 7.0 %dweight_part.1 = (bf16[2,8,96,384]{3,2,1,0:T(8,128)(2,1)}, bf16[2,8,96,384]{3,2,1,0:T(8,128)(2,1)}) custom-call(s32[1]{0:T(128)} %bitcast.4.core_ref.dp_ref, bf16[1024,1536]{1,0:T(8,128)(2,1)} %get-tuple-element.49.d_ref, bf16[1024,384]{1,0:T(8,128)(2,1)} %get-tuple-element.39.a_ref.a1_ref.a3_ref.a0_ref, bf16[1024,384]{1,0:T(8,128)(2,1)} %copy-done.1), custom_call_target="tpu_custom_call" | custom-call | tf_op jit(solution)/shard_map/dweight_part/pallas_call | solution.py:421
  127.6 4.1 %project_far.1 = (bf16[128,1536]{1,0:T(8,128)(2,1)}, bf16[128,1536]{1,0:T(8,128)(2,1)}) custom-call(s32[1]{0:T(128)} %bitcast.seq_ref, bf16[1024,384]{1,0:T(8,128)(2,1)} %get-tuple-element.39.a_ref.a1_ref.a3_ref.a0_ref, bf16[1024,384]{1,0:T(8,128)(2,1)} %copy-done.1, bf16[2,1536,384]{2,1,0:T(8,128)(2,1)} %bitcast.10), custom_call_target="tpu_custom_call" | custom-call | tf_op jit(solution)/shard_map/project_far/pallas_call | solution.py:379
  131.6 3.2 %collective-permute-start.11 = (bf16[128,1536]{1,0:T(8,128)(2,1)}, bf16[128,1536]{1,0:T(8,128)(2,1)S(1)}, u32[]{:S(2)}, u32[]{:S(2)}) collective-permute-start(bf16[128,1536]{1,0:T(8,128)(2,1)} %get-tuple-element.46), channel_id=1, source_target_pairs={{0,6},{1,7},{2,0},{3,1},{4,2},{5,3},{6,4},{7,5},{8,14},{9,15},{10,... | collective-permute-start | bytes 1179656 | tf_op jit(solution)/shard_map/ppermute | solution.py:497
  134.8 9.2 %collective-permute-done.10.up_ref = bf16[128,1536]{1,0:T(8,128)(2,1)S(1)} collective-permute-done((bf16[128,1536]{1,0:T(8,128)(2,1)}, bf16[128,1536]{1,0:T(8,128)(2,1)S(1)}, u32[]{:S(2)}, u32[]{:S(2)}) %collective-permute-start.10) | collective-permute-done | bytes 393248 | tf_op jit(solution)/shard_map/ppermute | solution.py:497
  145.5 5.0 %project_near.1 = (bf16[256,1536]{1,0:T(8,128)(2,1)}, bf16[256,1536]{1,0:T(8,128)(2,1)}) custom-call(s32[1]{0:T(128)} %bitcast.seq_ref, bf16[1024,384]{1,0:T(8,128)(2,1)} %get-tuple-element.39.a_ref.a1_ref.a3_ref.a0_ref, bf16[1024,384]{1,0:T(8,128)(2,1)} %copy-done.1, bf16[1024,384]{1,0:T(8,128)(2,1)} %get-tuple-element.39.a_ref.a1_ref.a3_ref.a0_ref, ...), custom_call_target="tpu_custom_call" | custom-call | tf_op jit(solution)/shard_map/project_near/pallas_call | solution.py:389
  151.4 11.2 %attention_backward.1 = bf16[8,3,128,384]{3,2,1,0:T(8,128)(2,1)} custom-call(s32[1,3]{1,0:T(1,128)} %frames_ref.7, bf16[8,3,128,384]{3,2,1,0:T(8,128)(2,1)} %copy-done, f32[1024,384]{1,0:T(8,128)} %get-tuple-element.55.own_ref, bf16[1024,384]{1,0:T(8,128)(2,1)} %copy-done.5, bf16[3,640,640]{2,1,0:T(8,128)(2,1)} %get-tuple-element.57.p1_ref, ...), custom_call_target="tpu_custom_call" | custom-call | tf_op jit(solution)/shard_map/attention_backward/pallas_call | solution.py:180
  162.6 5.2 %all-to-all-start.1 = ((bf16[8,3,128,384]{3,2,1,0:T(8,128)(2,1)}), bf16[8,3,128,384]{3,2,1,0:T(8,128)(2,1)S(1)}, u32[]{:S(2)}, u32[]{:S(2)}) async-start(bf16[8,3,128,384]{3,2,1,0:T(8,128)(2,1)} %attention_backward.1), calls=%async_computation.1 | async-start | bytes 4718592 | tf_op jit(solution)/shard_map/all_to_all | solution.py:554
  171.0 2.7 %pair_sum.1 = (bf16[4,96,384]{2,1,0:T(8,128)(2,1)}, bf16[4,96,384]{2,1,0:T(8,128)(2,1)}, bf16[4,96,384]{2,1,0:T(8,128)(2,1)}, bf16[4,96,384]{2,1,0:T(8,128)(2,1)}) custom-call(s32[1]{0:T(128)} %bitcast.4.core_ref.dp_ref, bf16[4,4,96,384]{3,2,1,0:T(8,128)(2,1)} %bitcast.15, bf16[4,4,96,384]{3,2,1,0:T(8,128)(2,1)} %bitcast.16), custom_call_target="tpu_custom_call" | custom-call | tf_op jit(solution)/shard_map/pair_sum/pallas_call | solution.py:450
  178.0 10.7 %collective-permute-done.16.b_ref = bf16[4,96,384]{2,1,0:T(8,128)(2,1)S(1)} collective-permute-done((bf16[4,96,384]{2,1,0:T(8,128)(2,1)}, bf16[4,96,384]{2,1,0:T(8,128)(2,1)S(1)}, u32[]{:S(2)}, u32[]{:S(2)}) %collective-permute-start.16) | collective-permute-done | bytes 294944 | tf_op jit(solution)/shard_map/ppermute | solution.py:497
  189.4 2.0 ring_sum.1
  192.6 3.5 %collective-permute-start.20 = (bf16[96,384]{1,0:T(8,128)(2,1)}, bf16[96,384]{1,0:T(8,128)(2,1)S(1)}, u32[]{:S(2)}, u32[]{:S(2)}) collective-permute-start(bf16[96,384]{1,0:T(8,128)(2,1)} %get-tuple-element.67), channel_id=1, source_target_pairs={{0,32},{8,40},{16,48},{24,56},{32,0},{40,8},{48,16},{56,24},{64,96... | collective-permute-start | bytes 221192 | tf_op jit(solution)/shard_map/ppermute | solution.py:497
  196.0 2.1 collective-permute-start.21
  198.1 14.4 %collective-permute-done.13.c1_ref = bf16[256,1536]{1,0:T(8,128)(2,1)S(1)} collective-permute-done((bf16[256,1536]{1,0:T(8,128)(2,1)}, bf16[256,1536]{1,0:T(8,128)(2,1)S(1)}, u32[]{:S(2)}, u32[]{:S(2)}) %collective-permute-start.13) | collective-permute-done | bytes 786464 | tf_op jit(solution)/shard_map/ppermute | solution.py:497
  213.4 4.6 %project_home.1 = (f32[128,1536]{1,0:T(8,128)}, bf16[128,1536]{1,0:T(8,128)(2,1)}) custom-call(s32[1]{0:T(128)} %bitcast.seq_ref, bf16[1024,384]{1,0:T(8,128)(2,1)} %get-tuple-element.39.a_ref.a1_ref.a3_ref.a0_ref, bf16[1024,384]{1,0:T(8,128)(2,1)} %copy-done.1, bf16[2,1536,384]{2,1,0:T(8,128)(2,1)} %bitcast.12, bf16[256,1536]{1,0:T(8,128)(2,1)} %copy-done.4, ...), custom_call_target="tpu_custom_call" | custom-call | tf_op jit(solution)/shard_map/project_home/pallas_call | solution.py:399
  218.6 3.5 %collective-permute-start.22 = (f32[96,384]{1,0:T(8,128)S(1)}, f32[96,384]{1,0:T(8,128)S(1)}, u32[]{:S(2)}, u32[]{:S(2)}) collective-permute-start(f32[96,384]{1,0:T(8,128)S(1)} %convert_add_fusion), channel_id=1, source_target_pairs={{0,0},{128,1},{2,2},{130,3},{4,4},{132,5},{6,6},{134,7},{8,8},{136... | collective-permute-start | bytes 442376 | tf_op jit(solution)/shard_map/ppermute | solution.py:564
  222.1 9.4 %collective-permute-done.22 = f32[96,384]{1,0:T(8,128)S(1)} collective-permute-done((f32[96,384]{1,0:T(8,128)S(1)}, f32[96,384]{1,0:T(8,128)S(1)}, u32[]{:S(2)}, u32[]{:S(2)}) %collective-permute-start.22) | collective-permute-done | bytes 147488 | tf_op jit(solution)/shard_map/ppermute | solution.py:564
  232.2 3.5 %gated_output.1 = bf16[128,3072]{1,0:T(8,128)(2,1)} custom-call(s32[1,3]{1,0:T(1,128)} %frames_ref.7, s32[1,3]{1,0:T(1,128)} %steps_ref.3, s32[1]{0:T(128)} %bitcast.seq_ref, f32[64,3072]{1,0:T(8,128)} %t1_ref.3, f32[64,3072]{1,0:T(8,128)} %t1_ref.3, bf16[128,3072]{1,0:T(8,128)(2,1)} %l1_ref.1, bf16[128,3072]{1,0:T(8,128)(2,1)} %l1_ref.1, ...), custom_call_target="tpu_custom_call" | custom-call | tf_op jit(solution)/shard_map/gated_output/pallas_call | solution.py:282
  237.1 5.8 %unpack_heads.1 = bf16[3,128,3072]{2,1,0:T(8,128)(2,1)} custom-call(bf16[8,3,128,384]{3,2,1,0:T(8,128)(2,1)} %copy-done.2), custom_call_target="tpu_custom_call" | custom-call | tf_op jit(solution)/shard_map/unpack_heads/pallas_call | solution.py:226
  (76 shorter events, 22.2 us)
Async XLA Ops:
  7.2 68.5 %all-gather.2.cloned.1.call-start = ((), (), s32[]{:S(2)}) async-start(), calls=%async_computation.2 | async-start | bytes 2433024 | tf_op jit(solution)/shard_map/all_gather | solution.py:529
  7.2 10.4 %collective-permute-start = (bf16[96,384]{1,0:T(8,128)(2,1)}, bf16[96,384]{1,0:T(8,128)(2,1)S(1)}, u32[]{:S(2)}, u32[]{:S(2)}) collective-permute-start(bf16[96,384]{1,0:T(8,128)(2,1)} %bitcast.18), channel_id=1, source_target_pairs={{0,0},{1,128},{2,2},{3,130},{4,4},{5,132},{6,6},{7,134},{8,8},{9,1... | collective-permute-start | bytes 221192 | tf_op jit(solution)/shard_map/ppermute | solution.py:526
  18.3 50.8 %all-to-all-start = ((bf16[8,3,128,384]{3,2,1,0:T(8,128)(2,1)}), bf16[8,3,128,384]{3,2,1,0:T(8,128)(2,1)S(1)}, u32[]{:S(2)}, u32[]{:S(2)}) async-start(bf16[8,3,128,384]{3,2,1,0:T(8,128)(2,1)} %pack_heads.1), calls=%async_computation | async-start | bytes 4718592 | tf_op jit(solution)/shard_map/all_to_all | solution.py:530
  27.1 59.8 %copy-start.6 = (bf16[128,1536]{1,0:T(8,128)(2,1)S(1)}, bf16[128,1536]{1,0:T(8,128)(2,1)}, u32[]{:S(2)}) copy-start(bf16[128,1536]{1,0:T(8,128)(2,1)} %get-tuple-element.41.refs_0_) | copy-start | bytes 1179652
  27.1 40.0 %collective-permute-start.2 = (bf16[128,1536]{1,0:T(8,128)(2,1)}, bf16[128,1536]{1,0:T(8,128)(2,1)S(1)}, u32[]{:S(2)}, u32[]{:S(2)}) collective-permute-start(bf16[128,1536]{1,0:T(8,128)(2,1)} %get-tuple-element.42), channel_id=1, source_target_pairs={{0,1},{1,0},{2,3},{3,2},{4,5},{5,4},{6,7},{7,6},{8,9},{9,8},{10,11... | collective-permute-start | bytes 1179656 | tf_op jit(solution)/shard_map/ppermute | solution.py:513
  27.1 62.5 %collective-permute-start.5 = (bf16[128,1536]{1,0:T(8,128)(2,1)}, bf16[128,1536]{1,0:T(8,128)(2,1)S(1)}, u32[]{:S(2)}, u32[]{:S(2)}) collective-permute-start(bf16[128,1536]{1,0:T(8,128)(2,1)} %get-tuple-element.41.refs_0_), channel_id=1, source_target_pairs={{0,2},{1,3},{2,4},{3,5},{4,6},{5,7},{6,0},{7,1},{8,10},{9,11},{10,... | collective-permute-start | bytes 1179656 | tf_op jit(solution)/shard_map/ppermute | solution.py:497
  67.0 42.9 %copy-start.7 = (bf16[128,1536]{1,0:T(8,128)(2,1)}, bf16[128,1536]{1,0:T(8,128)(2,1)S(1)}, u32[]{:S(2)}) copy-start(bf16[128,1536]{1,0:T(8,128)(2,1)S(1)} %collective-permute-done.2.refs_1_) | copy-start | bytes 1179652
  67.0 23.3 %collective-permute-start.4 = (bf16[128,1536]{1,0:T(8,128)(2,1)S(1)}, bf16[128,1536]{1,0:T(8,128)(2,1)}, u32[]{:S(2)}, u32[]{:S(2)}) collective-permute-start(bf16[128,1536]{1,0:T(8,128)(2,1)S(1)} %collective-permute-done.2.refs_1_), channel_id=1, source_target_pairs={{0,6},{1,7},{2,0},{3,1},{4,2},{5,3},{6,4},{7,5},{8,14},{9,15},{10,... | collective-permute-start | bytes 1179656 | tf_op jit(solution)/shard_map/ppermute | solution.py:497
  85.4 33.6 %collective-permute-start.1 = (bf16[1024,384]{1,0:T(8,128)(2,1)}, bf16[1024,384]{1,0:T(8,128)(2,1)S(1)}, u32[]{:S(2)}, u32[]{:S(2)}) collective-permute-start(bf16[1024,384]{1,0:T(8,128)(2,1)} %get-tuple-element.39.a_ref.a1_ref.a3_ref.a0_ref), channel_id=1, source_target_pairs={{0,1},{1,0},{2,3},{3,2},{4,5},{5,4},{6,7},{7,6},{8,9},{9,8},{10,11... | collective-permute-start | bytes 2359304 | tf_op jit(solution)/shard_map/ppermute | solution.py:513
  86.9 12.2 %collective-permute-start.3 = (bf16[128,1536]{1,0:T(8,128)(2,1)S(1)}, bf16[128,1536]{1,0:T(8,128)(2,1)S(1)}, u32[]{:S(2)}, u32[]{:S(2)}) collective-permute-start(bf16[128,1536]{1,0:T(8,128)(2,1)S(1)} %copy-done.6), channel_id=1, source_target_pairs={{0,6},{1,7},{2,0},{3,1},{4,2},{5,3},{6,4},{7,5},{8,14},{9,15},{10,... | collective-permute-start | bytes 1179656 | tf_op jit(solution)/shard_map/ppermute | solution.py:497
  89.6 20.4 %collective-permute-start.8 = (bf16[128,1536]{1,0:T(8,128)(2,1)S(1)}, bf16[128,1536]{1,0:T(8,128)(2,1)S(1)}, u32[]{:S(2)}, u32[]{:S(2)}) collective-permute-start(bf16[128,1536]{1,0:T(8,128)(2,1)S(1)} %collective-permute-done.2.refs_1_), channel_id=1, source_target_pairs={{0,2},{1,3},{2,4},{3,5},{4,6},{5,7},{6,0},{7,1},{8,10},{9,11},{10,... | collective-permute-start | bytes 1179656 | tf_op jit(solution)/shard_map/ppermute | solution.py:497
  89.6 20.4 %copy-start.8 = (bf16[128,1536]{1,0:T(8,128)(2,1)}, bf16[128,1536]{1,0:T(8,128)(2,1)S(1)}, u32[]{:S(2)}) copy-start(bf16[128,1536]{1,0:T(8,128)(2,1)S(1)} %collective-permute-done.5.refs_6_) | copy-start | bytes 1179652
  89.6 20.4 %collective-permute-start.6 = (bf16[128,1536]{1,0:T(8,128)(2,1)S(1)}, bf16[128,1536]{1,0:T(8,128)(2,1)S(1)}, u32[]{:S(2)}, u32[]{:S(2)}) collective-permute-start(bf16[128,1536]{1,0:T(8,128)(2,1)S(1)} %collective-permute-done.5.refs_6_), channel_id=1, source_target_pairs={{0,2},{1,3},{2,4},{3,5},{4,6},{5,7},{6,0},{7,1},{8,10},{9,11},{10,... | collective-permute-start | bytes 1179656 | tf_op jit(solution)/shard_map/ppermute | solution.py:497
  90.4 19.6 %collective-permute-start.7 = (bf16[128,1536]{1,0:T(8,128)(2,1)}, bf16[128,1536]{1,0:T(8,128)(2,1)S(1)}, u32[]{:S(2)}, u32[]{:S(2)}) collective-permute-start(bf16[128,1536]{1,0:T(8,128)(2,1)} %collective-permute-done.4.refs_3_), channel_id=1, source_target_pairs={{0,6},{1,7},{2,0},{3,1},{4,2},{5,3},{6,4},{7,5},{8,14},{9,15},{10,... | collective-permute-start | bytes 1179656 | tf_op jit(solution)/shard_map/ppermute | solution.py:497
  99.1 10.9 %copy-start.9 = (bf16[128,1536]{1,0:T(8,128)(2,1)}, bf16[128,1536]{1,0:T(8,128)(2,1)S(1)}, u32[]{:S(2)}) copy-start(bf16[128,1536]{1,0:T(8,128)(2,1)S(1)} %collective-permute-done.3.refs_2_) | copy-start | bytes 1179652
  126.9 23.6 %collective-permute-start.12 = (bf16[2,8,96,384]{3,2,1,0:T(8,128)(2,1)}, bf16[2,8,96,384]{3,2,1,0:T(8,128)(2,1)S(1)}, u32[]{:S(2)}, u32[]{:S(2)}) collective-permute-start(bf16[2,8,96,384]{3,2,1,0:T(8,128)(2,1)} %get-tuple-element.50), channel_id=1, source_target_pairs={{0,8},{8,0},{16,24},{24,16},{32,40},{40,32},{48,56},{56,48},{64,72... | collective-permute-start | bytes 3538952 | tf_op jit(solution)/shard_map/ppermute | solution.py:517
  126.9 23.6 %collective-permute-start.9 = (bf16[1024,384]{1,0:T(8,128)(2,1)S(1)}, bf16[1024,384]{1,0:T(8,128)(2,1)S(1)}, u32[]{:S(2)}, u32[]{:S(2)}) collective-permute-start(bf16[1024,384]{1,0:T(8,128)(2,1)S(1)} %copy-done.19), channel_id=1, source_target_pairs={{0,1},{1,0},{2,3},{3,2},{4,5},{5,4},{6,7},{7,6},{8,9},{9,8},{10,11... | collective-permute-start | bytes 2359304 | tf_op jit(solution)/shard_map/ppermute | solution.py:513
  131.6 12.4 %collective-permute-start.10 = (bf16[128,1536]{1,0:T(8,128)(2,1)}, bf16[128,1536]{1,0:T(8,128)(2,1)S(1)}, u32[]{:S(2)}, u32[]{:S(2)}) collective-permute-start(bf16[128,1536]{1,0:T(8,128)(2,1)} %get-tuple-element.45), channel_id=1, source_target_pairs={{0,2},{1,3},{2,4},{3,5},{4,6},{5,7},{6,0},{7,1},{8,10},{9,11},{10,... | collective-permute-start | bytes 1179656 | tf_op jit(solution)/shard_map/ppermute | solution.py:497
  131.6 12.4 %collective-permute-start.11 = (bf16[128,1536]{1,0:T(8,128)(2,1)}, bf16[128,1536]{1,0:T(8,128)(2,1)S(1)}, u32[]{:S(2)}, u32[]{:S(2)}) collective-permute-start(bf16[128,1536]{1,0:T(8,128)(2,1)} %get-tuple-element.46), channel_id=1, source_target_pairs={{0,6},{1,7},{2,0},{3,1},{4,2},{5,3},{6,4},{7,5},{8,14},{9,15},{10,... | collective-permute-start | bytes 1179656 | tf_op jit(solution)/shard_map/ppermute | solution.py:497
  150.6 12.1 %copy-start.3 = (bf16[2,8,96,384]{3,2,1,0:T(8,128)(2,1)}, bf16[2,8,96,384]{3,2,1,0:T(8,128)(2,1)S(1)}, u32[]{:S(2)}) copy-start(bf16[2,8,96,384]{3,2,1,0:T(8,128)(2,1)S(1)} %collective-permute-done.12) | copy-start | bytes 3538948
  162.6 73.1 %all-to-all-start.1 = ((bf16[8,3,128,384]{3,2,1,0:T(8,128)(2,1)}), bf16[8,3,128,384]{3,2,1,0:T(8,128)(2,1)S(1)}, u32[]{:S(2)}, u32[]{:S(2)}) async-start(bf16[8,3,128,384]{3,2,1,0:T(8,128)(2,1)} %attention_backward.1), calls=%async_computation.1 | async-start | bytes 4718592 | tf_op jit(solution)/shard_map/all_to_all | solution.py:554
  167.8 44.7 %collective-permute-start.13 = (bf16[256,1536]{1,0:T(8,128)(2,1)}, bf16[256,1536]{1,0:T(8,128)(2,1)S(1)}, u32[]{:S(2)}, u32[]{:S(2)}) collective-permute-start(bf16[256,1536]{1,0:T(8,128)(2,1)} %get-tuple-element.51), channel_id=1, source_target_pairs={{0,2},{1,3},{2,4},{3,5},{4,6},{5,7},{6,0},{7,1},{8,10},{9,11},{10,... | collective-permute-start | bytes 2359304 | tf_op jit(solution)/shard_map/ppermute | solution.py:497
  169.3 43.2 %collective-permute-start.14 = (bf16[256,1536]{1,0:T(8,128)(2,1)}, bf16[256,1536]{1,0:T(8,128)(2,1)}, u32[]{:S(2)}, u32[]{:S(2)}) collective-permute-start(bf16[256,1536]{1,0:T(8,128)(2,1)} %get-tuple-element.52), channel_id=1, source_target_pairs={{0,6},{1,7},{2,0},{3,1},{4,2},{5,3},{6,4},{7,5},{8,14},{9,15},{10,... | collective-permute-start | bytes 2359304 | tf_op jit(solution)/shard_map/ppermute | solution.py:497
  173.7 14.9 %collective-permute-start.16 = (bf16[4,96,384]{2,1,0:T(8,128)(2,1)}, bf16[4,96,384]{2,1,0:T(8,128)(2,1)S(1)}, u32[]{:S(2)}, u32[]{:S(2)}) collective-permute-start(bf16[4,96,384]{2,1,0:T(8,128)(2,1)} %get-tuple-element.62), channel_id=1, source_target_pairs={{0,64},{8,72},{16,80},{24,88},{32,96},{40,104},{48,112},{56,120},{... | collective-permute-start | bytes 884744 | tf_op jit(solution)/shard_map/ppermute | solution.py:497
  175.1 13.5 %collective-permute-start.17 = (bf16[4,96,384]{2,1,0:T(8,128)(2,1)}, bf16[4,96,384]{2,1,0:T(8,128)(2,1)}, u32[]{:S(2)}, u32[]{:S(2)}) collective-permute-start(bf16[4,96,384]{2,1,0:T(8,128)(2,1)} %get-tuple-element.63), channel_id=1, source_target_pairs={{0,128},{8,136},{16,144},{24,152},{32,160},{40,168},{48,176},{56,1... | collective-permute-start | bytes 884744 | tf_op jit(solution)/shard_map/ppermute | solution.py:497
  176.7 12.6 %collective-permute-start.18 = (bf16[4,96,384]{2,1,0:T(8,128)(2,1)}, bf16[4,96,384]{2,1,0:T(8,128)(2,1)}, u32[]{:S(2)}, u32[]{:S(2)}) collective-permute-start(bf16[4,96,384]{2,1,0:T(8,128)(2,1)} %get-tuple-element.64), channel_id=1, source_target_pairs={{0,192},{8,200},{16,208},{24,216},{32,224},{40,232},{48,240},{56,2... | collective-permute-start | bytes 884744 | tf_op jit(solution)/shard_map/ppermute | solution.py:497
  191.4 27.2 %collective-permute-start.19 = (bf16[96,384]{1,0:T(8,128)(2,1)}, bf16[96,384]{1,0:T(8,128)(2,1)S(1)}, u32[]{:S(2)}, u32[]{:S(2)}) collective-permute-start(bf16[96,384]{1,0:T(8,128)(2,1)} %get-tuple-element.66), channel_id=1, source_target_pairs={{0,16},{8,24},{16,32},{24,40},{32,48},{40,56},{48,0},{56,8},{64,80... | collective-permute-start | bytes 221192 | tf_op jit(solution)/shard_map/ppermute | solution.py:497
  192.6 26.0 %collective-permute-start.20 = (bf16[96,384]{1,0:T(8,128)(2,1)}, bf16[96,384]{1,0:T(8,128)(2,1)S(1)}, u32[]{:S(2)}, u32[]{:S(2)}) collective-permute-start(bf16[96,384]{1,0:T(8,128)(2,1)} %get-tuple-element.67), channel_id=1, source_target_pairs={{0,32},{8,40},{16,48},{24,56},{32,0},{40,8},{48,16},{56,24},{64,96... | collective-permute-start | bytes 221192 | tf_op jit(solution)/shard_map/ppermute | solution.py:497
  196.0 22.5 %copy-start.17 = (bf16[96,384]{1,0:T(8,128)(2,1)S(1)}, bf16[96,384]{1,0:T(8,128)(2,1)}, u32[]{:S(2)}) copy-start(bf16[96,384]{1,0:T(8,128)(2,1)} %get-tuple-element.65) | copy-start | bytes 221188
  196.0 22.5 %collective-permute-start.21 = (bf16[96,384]{1,0:T(8,128)(2,1)}, bf16[96,384]{1,0:T(8,128)(2,1)S(1)}, u32[]{:S(2)}, u32[]{:S(2)}) collective-permute-start(bf16[96,384]{1,0:T(8,128)(2,1)} %get-tuple-element.68), channel_id=1, source_target_pairs={{0,48},{8,56},{16,0},{24,8},{32,16},{40,24},{48,32},{56,40},{64,11... | collective-permute-start | bytes 221192 | tf_op jit(solution)/shard_map/ppermute | solution.py:497
  218.0 13.5 %collective-permute-start.15 = (bf16[128,1536]{1,0:T(8,128)(2,1)}, bf16[128,1536]{1,0:T(8,128)(2,1)S(1)}, u32[]{:S(2)}, u32[]{:S(2)}) collective-permute-start(bf16[128,1536]{1,0:T(8,128)(2,1)} %get-tuple-element.54), channel_id=1, source_target_pairs={{0,1},{1,0},{2,3},{3,2},{4,5},{5,4},{6,7},{7,6},{8,9},{9,8},{10,11... | collective-permute-start | bytes 1179656 | tf_op jit(solution)/shard_map/ppermute | solution.py:513
  218.6 12.9 %collective-permute-start.22 = (f32[96,384]{1,0:T(8,128)S(1)}, f32[96,384]{1,0:T(8,128)S(1)}, u32[]{:S(2)}, u32[]{:S(2)}) collective-permute-start(f32[96,384]{1,0:T(8,128)S(1)} %convert_add_fusion), channel_id=1, source_target_pairs={{0,0},{128,1},{2,2},{130,3},{4,4},{132,5},{6,6},{134,7},{8,8},{136... | collective-permute-start | bytes 442376 | tf_op jit(solution)/shard_map/ppermute | solution.py:564
  (14 other events, 23.6 us)
Sparse Core Ops, SparseCore 0:
  18.4 57.1 all-gather.1

commit v4 on v3

--- a/solution.py
+++ b/solution.py
@@ -14,6 +14,10 @@
 
 BF = jnp.bfloat16
 F32 = jnp.float32
+
+
+def cost(us):
+    return pl.CostEstimate(flops=int(us * 1e9), transcendentals=0, bytes_accessed=int(us * 3e6))
 
 
 def dot_nt(a, b):
@@ -128,6 +132,7 @@
             scratch_shapes=[pltpu.VMEM((1024, HD), BF)] * 3,
         ),
         compiler_params=pltpu.CompilerParams(vmem_limit_bytes=VMEM_LIMIT),
+        cost_estimate=cost(10),
         name="attention_forward",
     )(frames, heads)
 
@@ -199,6 +204,7 @@
             ],
         ),
         compiler_params=pltpu.CompilerParams(vmem_limit_bytes=VMEM_LIMIT),
+        cost_estimate=cost(11),
         name="attention_backward",
     )(frames, heads, own, other, p1, p2)
 
@@ -214,6 +220,7 @@
         grid=(8,),
         in_specs=[pl.BlockSpec((3, 128, 384), lambda j: (0, 0, j))],
         out_specs=pl.BlockSpec((1, 3, 128, 384), lambda j: (j, 0, 0, 0)),
+        cost_estimate=cost(6),
         name="pack_heads",
     )(qkv)
 
@@ -229,6 +236,7 @@
         grid=(8,),
         in_specs=[pl.BlockSpec((1, 3, 128, 384), lambda j: (j, 0, 0, 0))],
         out_specs=pl.BlockSpec((3, 128, 384), lambda j: (0, 0, j)),
+        cost_estimate=cost(6),
         name="unpack_heads",
     )(grads)
 
@@ -255,6 +263,7 @@
             in_specs=[half(64, 0), half(64, 1), half(128, 0), half(128, 1)],
             out_specs=(out, out),
         ),
+        cost_estimate=cost(3),
         name="gated_cotangent",
     )(frames, steps, seq, table, table, cotangent, cotangent)
 
@@ -288,6 +297,7 @@
             in_specs=[half(64, 0), half(64, 1), half(128, 0), half(128, 1), whole, whole],
             out_specs=pl.BlockSpec((128, 3072), lambda n, *_: (0, 0)),
         ),
+        cost_estimate=cost(3),
         name="gated_output",
     )(frames, steps, seq, table, table, latents, latents, own, other)
 
@@ -321,6 +331,7 @@
             pl.BlockSpec((1024, 384), lambda: (0, 0)),
         ),
         compiler_params=pltpu.CompilerParams(vmem_limit_bytes=VMEM_LIMIT),
+        cost_estimate=cost(7),
         name="dattn_parts",
     )(seq, *blocks, weights)
 
@@ -371,6 +382,7 @@
             num_scalar_prefetch=1, grid=(3,), in_specs=in_specs, out_specs=out_specs
         ),
         compiler_params=pltpu.CompilerParams(vmem_limit_bytes=VMEM_LIMIT),
+        cost_estimate=cost(4),
         name=name,
     )
 
@@ -435,6 +447,7 @@
             ),
         ),
         compiler_params=pltpu.CompilerParams(vmem_limit_bytes=VMEM_LIMIT),
+        cost_estimate=cost(7),
         name="dweight_part",
     )(core, dproj, own, other)
 
@@ -453,6 +466,7 @@
         in_specs=[pl.BlockSpec(memory_space=pltpu.SMEM)]
         + [pl.BlockSpec((4, 4, 96, 384), lambda: (0, 0, 0, 0))] * 2,
         out_specs=(pl.BlockSpec((4, 96, 384), lambda: (0, 0, 0)),) * 4,
+        cost_estimate=cost(3),
         name="pair_sum",
     )(dp, keep.reshape(4, 4, 96, 384), got.reshape(4, 4, 96, 384))
 
@@ -472,6 +486,7 @@
         in_specs=[pl.BlockSpec(memory_space=pltpu.SMEM)]
         + [pl.BlockSpec((4, 96, 384), lambda: (0, 0, 0))] * 4,
         out_specs=(pl.BlockSpec((96, 384), lambda: (0, 0)),) * 4,
+        cost_estimate=cost(2),
         name="ring_sum",
     )(dp, *parts)
 
@@ -524,47 +539,51 @@
     moves = piece_moves(lax.axis_size("dp"), lax.axis_size("seq"))
 
     piece = lax.ppermute(out_weight.T, both, moves)
+    keep, send = gated_cotangent(frames, timesteps, seq, gate_table, cotangent)
+    got = swap_z(send)
+    b1_keep, b3_keep = along_x(keep, -1), along_x(keep, 1)
     packed = pack_heads(qkv_input.transpose(1, 0, 2))
-    packed, piece = lax.optimization_barrier((packed, piece))
+    packed, piece, got, b1_keep, b3_keep = lax.optimization_barrier(
+        (packed, piece, got, b1_keep, b3_keep)
+    )
     weights = lax.all_gather(piece, "dp", axis=0, tiled=True).reshape(2, 1536, 384)
     heads = lax.all_to_all(packed, "seq", split_axis=0, concat_axis=0, tiled=True)
 
-    keep, send = gated_cotangent(frames, timesteps, seq, gate_table, cotangent)
-    got = swap_z(send)
-    b1 = [along_x(keep, -1), along_x(got, -1)]
-    b3 = [along_x(keep, 1), along_x(got, 1)]
-    b2 = [along_x(b3[0], 1), along_x(b1[1], -1)]
-
-    heads, weights = lax.optimization_barrier((heads, weights))
+    b1 = [b1_keep, along_x(got, -1)]
+    b3 = [b3_keep, along_x(got, 1)]
+    late, weights = lax.optimization_barrier((b1[1], weights))
+    b2 = [along_x(b3[0], 1), along_x(late, -1)]
+
     attn, p1, p2 = attention_forward(frames, heads)
     attn_other = swap_z(attn)
     dproj, d_send, d_own = dattn_parts(seq, [keep, got, *b1, *b2, *b3], weights)
     d_recv = swap_z(d_send)
     up, down = project_far(seq, attn, attn_other, weights)
     up, down = along_x(up, 1), along_x(down, -1)
+    t1, t3 = project_near(seq, attn, attn_other, weights, up, down)
+    d_own, d_recv, t1, t3 = lax.optimization_barrier((d_own, d_recv, t1, t3))
+    c1, c3 = along_x(t1, 1), along_x(t3, -1)
+
+    grads = attention_backward(frames, heads, d_own, d_recv, p1, p2)
+    grads, c1, c3, dproj = lax.optimization_barrier((grads, c1, c3, dproj))
     w_keep, w_send = dweight_part(dp, dproj, attn, attn_other)
     w_got = swap_core(w_send)
-    t1, t3 = project_near(seq, attn, attn_other, weights, up, down)
-    d_own, d_recv, t1, t3, w_got = lax.optimization_barrier((d_own, d_recv, t1, t3, w_got))
-    c1, c3 = along_x(t1, 1), along_x(t3, -1)
+    grads = lax.all_to_all(grads, "seq", split_axis=0, concat_axis=0, tiled=True)
     terms = pair_sum(dp, w_keep, w_got)
     terms = [terms[0]] + [along_y(terms[k], k) for k in range(1, 4)]
 
-    grads = attention_backward(frames, heads, d_own, d_recv, p1, p2)
-    grads = lax.all_to_all(grads, "seq", split_axis=0, concat_axis=0, tiled=True)
-
     o_keep, o_send = project_home(seq, attn, attn_other, weights, c1, c3)
-    o_got = swap_z(o_send)
-    output = gated_output(frames, timesteps, seq, gate_table, latents, o_keep, o_got)
-
+    terms, o_send = lax.optimization_barrier((terms, o_send))
     terms = ring_sum(dp, terms)
     terms = [terms[0]] + [along_z(terms[k], k) for k in range(1, 4)]
     total = terms[0].astype(F32) + terms[1].astype(F32)
     total = total + terms[2].astype(F32) + terms[3].astype(F32)
     total = lax.ppermute(total, both, [(b, a) for a, b in moves])
-    grad_weight = total.T
-    grad_qkv = unpack_heads(grads).transpose(1, 0, 2)
-    return (output, grad_qkv, grad_weight)
+    o_got = swap_z(o_send)
+    grad_qkv = unpack_heads(grads)
+    grad_qkv, o_got = lax.optimization_barrier((grad_qkv, o_got))
+    output = gated_output(frames, timesteps, seq, gate_table, latents, o_keep, o_got)
+    return (output, grad_qkv.transpose(1, 0, 2), total.T)
 
 
 def solution(mesh):

time: 251 us -> 243 us (0.968)
  waiting for transfers between devices: 106 us -> 97.4 us
    ppermute x4, waiting for transfers between devices: 37.9 us -> 15.5 us  [swap_z(): lax.ppermute(x, 'seq', [(i, i ^ 1) for i in range(lax.axis_size('seq'))])]
    all_gather x1, waiting for transfers between devices: 6.49 us -> 14.5 us  [body(): lax.all_gather(piece, 'dp', axis=0, tiled=True).reshape(2, 1536, 384)]
    ppermute x16, waiting for transfers between devices: 52 us -> 57.6 us  [along(): return lax.ppermute(x, axis, moves)]
    ppermute x1, waiting for transfers between devices: 0.01 us -> 3.06 us  [swap_core(): lax.ppermute(x, 'dp', [(i, i ^ 1) for i in range(lax.axis_size('dp'))])]
    ppermute x1, waiting for transfers between devices: 9.4 us -> 6.67 us  [body(): total = lax.ppermute(total, both, [(b, a) for a, b in moves])]
    unnamed x41 -> x37, local copies, waits for them, and re-layouts: 9.25 us -> 9.26 us
  transfers between devices with their start and end apart: 26 -> 26, of which waited for: 9 -> 13; matrix products, arithmetic and copies ran while one was open for 0% -> 0% of each run, Pallas kernels for 19% -> 27%
where the time goes in v4:
time: 243 us; the launch traced here: 242 us
  waiting for transfers between devices  97.4 us (40%)
  Pallas kernels  71.8 us (30%)
  starting transfers between devices  48.5 us (20%)
  between operations  14.2 us (6%)
  local copies, waits for them, and re-layouts  9.26 us (4%)
    ppermute x16, waiting for transfers between devices, along(): return lax.ppermute(x, axis, moves)  57.6 us
    ppermute x16, starting transfers between devices, along(): return lax.ppermute(x, axis, moves)  26.3 us
    ppermute x4, waiting for transfers between devices, swap_z(): lax.ppermute(x, 'seq', [(i, i ^ 1) for i in range(lax.axis_size('seq'))])  15.5 us
    all_gather x1, waiting for transfers between devices, body(): lax.all_gather(piece, 'dp', axis=0, tiled=True).reshape(2, 1536, 384)  14.5 us
    pallas_call x1, Pallas kernels, attention_backward(): pl.pallas_call(bwd_kernel, out_shape=jax.ShapeDtypeStruct((8, 3, 128, 3 *...  11.1 us
    pallas_call x1, Pallas kernels, attention_forward(): pl.pallas_call(fwd_kernel, out_shape=(jax.ShapeDtypeStruct((1024, 3 * HD)...  9.81 us
    unnamed x37, local copies, waits for them, and re-layouts  9.26 us
    pallas_call x1, Pallas kernels, dattn_parts(): pl.pallas_call(dattn_kernel, out_shape=(jax.ShapeDtypeStruct((1024, 1536)...  7.41 us
  transfers between devices with their start and end apart: 26, of which 13 were waited for; matrix products, arithmetic and copies ran while one was open for 0% of the time, Pallas kernels for 27%

profile of v4, /device:TPU:32, one launch (start us, length us, event | category | flops | bytes accessed | tf_op | source)
XLA Modules:
  0.0 242.0 jit_solution(994115361319336515)
XLA Ops:
  7.2 3.1 %gated_cotangent.1 = (bf16[128,1536]{1,0:T(8,128)(2,1)}, bf16[128,1536]{1,0:T(8,128)(2,1)}) custom-call(s32[1,3]{1,0:T(1,128)} %frames_ref.7, s32[1,3]{1,0:T(1,128)} %steps_ref.3, s32[1]{0:T(128)} %bitcast.seq_ref, f32[64,3072]{1,0:T(8,128)} %t1_ref.3, f32[64,3072]{1,0:T(8,128)} %t1_ref.3, bf16[128,3072]{1,0:T(8,128)(2,1)} %c1_ref.1, bf16[128,3072]{1,0:T(8,128)(2,1)} %c1_ref.1), custom_call_target="tpu_custom_call" | custom-call | flops 3000000000 | bytes 9000000 | tf_op jit(solution)/shard_map/gated_cotangent/pallas_call | solution.py:257
  13.6 4.6 %collective-permute-start = (bf16[96,384]{1,0:T(8,128)(2,1)S(1)}, bf16[96,384]{1,0:T(8,128)(2,1)S(1)}, u32[]{:S(2)}, u32[]{:S(2)}) collective-permute-start(bf16[96,384]{1,0:T(8,128)(2,1)S(1)} %bitcast.16), channel_id=1, source_target_pairs={{0,0},{1,128},{2,2},{3,130},{4,4},{5,132},{6,6},{7,134},{8,8},{9,1... | collective-permute-start | bytes 221192 | tf_op jit(solution)/shard_map/ppermute | solution.py:541
  18.3 5.8 %pack_heads.1 = bf16[8,3,128,384]{3,2,1,0:T(8,128)(2,1)} custom-call(bf16[3,128,3072]{2,1,0:T(8,128)(2,1)} %bitcast.10), custom_call_target="tpu_custom_call" | custom-call | flops 6000000000 | bytes 18000000 | tf_op jit(solution)/shard_map/pack_heads/pallas_call | solution.py:217
  24.1 4.4 %collective-permute-done.1.refs_1_ = bf16[128,1536]{1,0:T(8,128)(2,1)S(1)} collective-permute-done((bf16[128,1536]{1,0:T(8,128)(2,1)}, bf16[128,1536]{1,0:T(8,128)(2,1)S(1)}, u32[]{:S(2)}, u32[]{:S(2)}) %collective-permute-start.1) | collective-permute-done | bytes 393248 | tf_op jit(solution)/shard_map/ppermute | solution.py:528
  29.3 5.1 %all-to-all-start = ((bf16[8,3,128,384]{3,2,1,0:T(8,128)(2,1)}), bf16[8,3,128,384]{3,2,1,0:T(8,128)(2,1)S(1)}, u32[]{:S(2)}, u32[]{:S(2)}) async-start(bf16[8,3,128,384]{3,2,1,0:T(8,128)(2,1)} %pack_heads.1), calls=%async_computation | async-start | bytes 4718592 | tf_op jit(solution)/shard_map/all_to_all | solution.py:550
  34.4 2.7 %collective-permute-start.5 = (bf16[128,1536]{1,0:T(8,128)(2,1)S(1)}, bf16[128,1536]{1,0:T(8,128)(2,1)S(1)}, u32[]{:S(2)}, u32[]{:S(2)}) collective-permute-start(bf16[128,1536]{1,0:T(8,128)(2,1)S(1)} %collective-permute-done.1.refs_1_), channel_id=1, source_target_pairs={{0,6},{1,7},{2,0},{3,1},{4,2},{5,3},{6,4},{7,5},{8,14},{9,15},{10,... | collective-permute-start | bytes 1179656 | tf_op jit(solution)/shard_map/ppermute | solution.py:512
  37.9 30.8 %collective-permute-done.5.refs_3_ = bf16[128,1536]{1,0:T(8,128)(2,1)S(1)} collective-permute-done((bf16[128,1536]{1,0:T(8,128)(2,1)S(1)}, bf16[128,1536]{1,0:T(8,128)(2,1)S(1)}, u32[]{:S(2)}, u32[]{:S(2)}) %collective-permute-start.5) | collective-permute-done | bytes 393248 | tf_op jit(solution)/shard_map/ppermute | solution.py:512
  68.7 14.5 %all-gather.2.cloned.1.call-done = bf16[3072,384]{1,0:T(8,128)(2,1)} async-done(((bf16[96,384]{1,0:T(8,128)(2,1)}), bf16[3072,384]{1,0:T(8,128)(2,1)}) %all-gather.2.cloned.1.call-update) | async-done | bytes 2359312 | tf_op jit(solution)/shard_map/all_gather | solution.py:549
  83.2 2.7 %collective-permute-start.7 = (bf16[128,1536]{1,0:T(8,128)(2,1)S(1)}, bf16[128,1536]{1,0:T(8,128)(2,1)}, u32[]{:S(2)}, u32[]{:S(2)}) collective-permute-start(bf16[128,1536]{1,0:T(8,128)(2,1)S(1)} %collective-permute-done.5.refs_3_), channel_id=1, source_target_pairs={{0,6},{1,7},{2,0},{3,1},{4,2},{5,3},{6,4},{7,5},{8,14},{9,15},{10,... | collective-permute-start | bytes 1179656 | tf_op jit(solution)/shard_map/ppermute | solution.py:512
  87.3 9.8 %attention_forward.1 = (bf16[1024,384]{1,0:T(8,128)(2,1)}, bf16[3,640,640]{2,1,0:T(8,128)(2,1)}, bf16[3,384,384]{2,1,0:T(8,128)(2,1)}) custom-call(s32[1,3]{1,0:T(1,128)} %frames_ref.7, bf16[8,3,128,384]{3,2,1,0:T(8,128)(2,1)} %copy-done.1), custom_call_target="tpu_custom_call" | custom-call | flops 10000000000 | bytes 30000000 | tf_op jit(solution)/shard_map/attention_forward/pallas_call | solution.py:116
  99.4 7.4 %dattn_parts.1 = (bf16[1024,1536]{1,0:T(8,128)(2,1)}, bf16[1024,384]{1,0:T(8,128)(2,1)}, f32[1024,384]{1,0:T(8,128)}) custom-call(s32[1]{0:T(128)} %bitcast.seq_ref, bf16[128,1536]{1,0:T(8,128)(2,1)} %get-tuple-element.50.refs_0_, bf16[128,1536]{1,0:T(8,128)(2,1)} %copy-done.8, bf16[128,1536]{1,0:T(8,128)(2,1)} %copy-done.7, bf16[128,1536]{1,0:T(8,128)(2,1)} %copy-done.10, ...), custom_call_target="tpu_custom_call" | custom-call | flops 7000000000 | bytes 21000000 | tf_op jit(solution)/shard_map/dattn_parts/pallas_call | solution.py:320
  106.8 11.1 %collective-permute-done.4.b_ref.b1_ref.b3_ref.a1_ref = bf16[1024,384]{1,0:T(8,128)(2,1)S(1)} collective-permute-done((bf16[1024,384]{1,0:T(8,128)(2,1)}, bf16[1024,384]{1,0:T(8,128)(2,1)S(1)}, u32[]{:S(2)}, u32[]{:S(2)}) %collective-permute-start.4) | collective-permute-done | bytes 786464 | tf_op jit(solution)/shard_map/ppermute | solution.py:528
  118.8 4.1 %project_far.1 = (bf16[128,1536]{1,0:T(8,128)(2,1)}, bf16[128,1536]{1,0:T(8,128)(2,1)}) custom-call(s32[1]{0:T(128)} %bitcast.seq_ref, bf16[1024,384]{1,0:T(8,128)(2,1)} %get-tuple-element.52.a_ref.a1_ref.a3_ref.a0_ref, bf16[1024,384]{1,0:T(8,128)(2,1)} %copy-done.4, bf16[2,1536,384]{2,1,0:T(8,128)(2,1)} %bitcast.12), custom_call_target="tpu_custom_call" | custom-call | flops 4000000000 | bytes 12000000 | tf_op jit(solution)/shard_map/project_far/pallas_call | solution.py:391
  122.9 3.2 %collective-permute-start.11 = (bf16[128,1536]{1,0:T(8,128)(2,1)}, bf16[128,1536]{1,0:T(8,128)(2,1)S(1)}, u32[]{:S(2)}, u32[]{:S(2)}) collective-permute-start(bf16[128,1536]{1,0:T(8,128)(2,1)} %get-tuple-element.62), channel_id=1, source_target_pairs={{0,6},{1,7},{2,0},{3,1},{4,2},{5,3},{6,4},{7,5},{8,14},{9,15},{10,... | collective-permute-start | bytes 1179656 | tf_op jit(solution)/shard_map/ppermute | solution.py:512
  126.1 8.0 %collective-permute-done.10.up_ref = bf16[128,1536]{1,0:T(8,128)(2,1)S(1)} collective-permute-done((bf16[128,1536]{1,0:T(8,128)(2,1)}, bf16[128,1536]{1,0:T(8,128)(2,1)S(1)}, u32[]{:S(2)}, u32[]{:S(2)}) %collective-permute-start.10) | collective-permute-done | bytes 393248 | tf_op jit(solution)/shard_map/ppermute | solution.py:512
  135.6 4.9 %project_near.1 = (bf16[256,1536]{1,0:T(8,128)(2,1)}, bf16[256,1536]{1,0:T(8,128)(2,1)}) custom-call(s32[1]{0:T(128)} %bitcast.seq_ref, bf16[1024,384]{1,0:T(8,128)(2,1)} %get-tuple-element.52.a_ref.a1_ref.a3_ref.a0_ref, bf16[1024,384]{1,0:T(8,128)(2,1)} %copy-done.4, bf16[1024,384]{1,0:T(8,128)(2,1)} %get-tuple-element.52.a_ref.a1_ref.a3_ref.a0_ref, ...), custom_call_target="tpu_custom_call" | custom-call | flops 4000000000 | bytes 12000000 | tf_op jit(solution)/shard_map/project_near/pallas_call | solution.py:401
  140.7 3.2 %collective-permute-start.13 = (bf16[256,1536]{1,0:T(8,128)(2,1)}, bf16[256,1536]{1,0:T(8,128)(2,1)}, u32[]{:S(2)}, u32[]{:S(2)}) collective-permute-start(bf16[256,1536]{1,0:T(8,128)(2,1)} %get-tuple-element.70), channel_id=1, source_target_pairs={{0,6},{1,7},{2,0},{3,1},{4,2},{5,3},{6,4},{7,5},{8,14},{9,15},{10,... | collective-permute-start | bytes 2359304 | tf_op jit(solution)/shard_map/ppermute | solution.py:512
  143.9 11.1 %attention_backward.1 = bf16[8,3,128,384]{3,2,1,0:T(8,128)(2,1)} custom-call(s32[1,3]{1,0:T(1,128)} %frames_ref.7, bf16[8,3,128,384]{3,2,1,0:T(8,128)(2,1)} %copy-done.1, f32[1024,384]{1,0:T(8,128)} %get-tuple-element.65.own_ref, bf16[1024,384]{1,0:T(8,128)(2,1)} %copy-done.5, bf16[3,640,640]{2,1,0:T(8,128)(2,1)} %get-tuple-element.67.p1_ref, ...), custom_call_target="tpu_custom_call" | custom-call | flops 11000000512 | bytes 33000000 | tf_op jit(solution)/shard_map/attention_backward/pallas_call | solution.py:185
  155.0 4.5 %collective-permute-done.12.c1_ref = bf16[256,1536]{1,0:T(8,128)(2,1)} collective-permute-done((bf16[256,1536]{1,0:T(8,128)(2,1)}, bf16[256,1536]{1,0:T(8,128)(2,1)}, u32[]{:S(2)}, u32[]{:S(2)}) %collective-permute-start.12) | collective-permute-done | bytes 786464 | tf_op jit(solution)/shard_map/ppermute | solution.py:512
  159.5 5.7 %all-to-all-start.1 = ((bf16[8,3,128,384]{3,2,1,0:T(8,128)(2,1)}), bf16[8,3,128,384]{3,2,1,0:T(8,128)(2,1)S(1)}, u32[]{:S(2)}, u32[]{:S(2)}) async-start(bf16[8,3,128,384]{3,2,1,0:T(8,128)(2,1)} %attention_backward.1), calls=%async_computation.1 | async-start | bytes 4718592 | tf_op jit(solution)/shard_map/all_to_all | solution.py:571
  165.2 6.9 %dweight_part.1 = (bf16[2,8,96,384]{3,2,1,0:T(8,128)(2,1)}, bf16[2,8,96,384]{3,2,1,0:T(8,128)(2,1)}) custom-call(s32[1]{0:T(128)} %bitcast.4.core_ref.dp_ref, bf16[1024,1536]{1,0:T(8,128)(2,1)} %get-tuple-element.76.d_ref, bf16[1024,384]{1,0:T(8,128)(2,1)} %get-tuple-element.52.a_ref.a1_ref.a3_ref.a0_ref, bf16[1024,384]{1,0:T(8,128)(2,1)} %copy-done.4), custom_call_target="tpu_custom_call" | custom-call | flops 7000000000 | bytes 21000000 | tf_op jit(solution)/shard_map/dweight_part/pallas_call | solution.py:433
  172.1 3.1 %collective-permute-done.14 = bf16[2,8,96,384]{3,2,1,0:T(8,128)(2,1)S(1)} collective-permute-done((bf16[2,8,96,384]{3,2,1,0:T(8,128)(2,1)}, bf16[2,8,96,384]{3,2,1,0:T(8,128)(2,1)S(1)}, u32[]{:S(2)}, u32[]{:S(2)}) %collective-permute-start.14) | collective-permute-done | bytes 1179680 | tf_op jit(solution)/shard_map/ppermute | solution.py:532
  176.2 2.8 %pair_sum.1 = (bf16[4,96,384]{2,1,0:T(8,128)(2,1)}, bf16[4,96,384]{2,1,0:T(8,128)(2,1)}, bf16[4,96,384]{2,1,0:T(8,128)(2,1)}, bf16[4,96,384]{2,1,0:T(8,128)(2,1)}) custom-call(s32[1]{0:T(128)} %bitcast.4.core_ref.dp_ref, bf16[4,4,96,384]{3,2,1,0:T(8,128)(2,1)} %bitcast.18, bf16[4,4,96,384]{3,2,1,0:T(8,128)(2,1)} %bitcast.15), custom_call_target="tpu_custom_call" | custom-call | flops 3000000000 | bytes 9000000 | tf_op jit(solution)/shard_map/pair_sum/pallas_call | solution.py:463
  182.6 4.6 %project_home.1 = (f32[128,1536]{1,0:T(8,128)}, bf16[128,1536]{1,0:T(8,128)(2,1)}) custom-call(s32[1]{0:T(128)} %bitcast.seq_ref, bf16[1024,384]{1,0:T(8,128)(2,1)} %get-tuple-element.52.a_ref.a1_ref.a3_ref.a0_ref, bf16[1024,384]{1,0:T(8,128)(2,1)} %copy-done.4, bf16[2,1536,384]{2,1,0:T(8,128)(2,1)} %bitcast.14, ...), custom_call_target="tpu_custom_call" | custom-call | flops 4000000000 | bytes 12000000 | tf_op jit(solution)/shard_map/project_home/pallas_call | solution.py:411
  187.2 8.6 %collective-permute-done.15.b_ref = bf16[4,96,384]{2,1,0:T(8,128)(2,1)S(1)} collective-permute-done((bf16[4,96,384]{2,1,0:T(8,128)(2,1)}, bf16[4,96,384]{2,1,0:T(8,128)(2,1)S(1)}, u32[]{:S(2)}, u32[]{:S(2)}) %collective-permute-start.15) | collective-permute-done | bytes 294944 | tf_op jit(solution)/shard_map/ppermute | solution.py:512
  200.2 3.5 %collective-permute-start.20 = (bf16[96,384]{1,0:T(8,128)(2,1)}, bf16[96,384]{1,0:T(8,128)(2,1)S(1)}, u32[]{:S(2)}, u32[]{:S(2)}) collective-permute-start(bf16[96,384]{1,0:T(8,128)(2,1)} %get-tuple-element.93), channel_id=1, source_target_pairs={{0,32},{8,40},{16,48},{24,56},{32,0},{40,8},{48,16},{56,24},{64,96... | collective-permute-start | bytes 221192 | tf_op jit(solution)/shard_map/ppermute | solution.py:512
  203.7 2.3 collective-permute-start.21
  206.4 3.3 %collective-permute-done.20 = bf16[96,384]{1,0:T(8,128)(2,1)S(1)} collective-permute-done((bf16[96,384]{1,0:T(8,128)(2,1)}, bf16[96,384]{1,0:T(8,128)(2,1)S(1)}, u32[]{:S(2)}, u32[]{:S(2)}) %collective-permute-start.20) | collective-permute-done | bytes 73760 | tf_op jit(solution)/shard_map/ppermute | solution.py:512
  212.0 4.3 %collective-permute-start.22 = (f32[96,384]{1,0:T(8,128)S(1)}, f32[96,384]{1,0:T(8,128)S(1)}, u32[]{:S(2)}, u32[]{:S(2)}) collective-permute-start(f32[96,384]{1,0:T(8,128)S(1)} %convert_add_fusion), channel_id=1, source_target_pairs={{0,0},{128,1},{2,2},{130,3},{4,4},{132,5},{6,6},{134,7},{8,8},{136... | collective-permute-start | bytes 442376 | tf_op jit(solution)/shard_map/ppermute | solution.py:581
  216.4 6.7 %collective-permute-done.22 = f32[96,384]{1,0:T(8,128)S(1)} collective-permute-done((f32[96,384]{1,0:T(8,128)S(1)}, f32[96,384]{1,0:T(8,128)S(1)}, u32[]{:S(2)}, u32[]{:S(2)}) %collective-permute-start.22) | collective-permute-done | bytes 147488 | tf_op jit(solution)/shard_map/ppermute | solution.py:581
  224.5 5.8 %unpack_heads.1 = bf16[3,128,3072]{2,1,0:T(8,128)(2,1)} custom-call(bf16[8,3,128,384]{3,2,1,0:T(8,128)(2,1)} %copy-done), custom_call_target="tpu_custom_call" | custom-call | flops 6000000000 | bytes 18000000 | tf_op jit(solution)/shard_map/unpack_heads/pallas_call | solution.py:233
  231.1 3.5 %gated_output.1 = bf16[128,3072]{1,0:T(8,128)(2,1)} custom-call(s32[1,3]{1,0:T(1,128)} %frames_ref.7, s32[1,3]{1,0:T(1,128)} %steps_ref.3, s32[1]{0:T(128)} %bitcast.seq_ref, f32[64,3072]{1,0:T(8,128)} %t1_ref.3, f32[64,3072]{1,0:T(8,128)} %t1_ref.3, bf16[128,3072]{1,0:T(8,128)(2,1)} %l1_ref.1, bf16[128,3072]{1,0:T(8,128)(2,1)} %l1_ref.1, ...), custom_call_target="tpu_custom_call" | custom-call | flops 3000000000 | bytes 9000000 | tf_op jit(solution)/shard_map/gated_output/pallas_call | solution.py:291
  (72 shorter events, 25.9 us)
Async XLA Ops:
  7.2 76.0 %all-gather.2.cloned.1.call-start = ((), (), s32[]{:S(2)}) async-start(), calls=%async_computation.2 | async-start | bytes 2433024 | tf_op jit(solution)/shard_map/all_gather | solution.py:549
  7.2 6.3 %copy-start.17 = (bf16[384,96]{0,1:T(8,128)(2,1)S(1)}, bf16[384,96]{0,1:T(8,128)(2,1)}, u32[]{:S(2)}) copy-start(bf16[384,96]{0,1:T(8,128)(2,1)} %param.10) | copy-start | bytes 221188
  10.3 18.2 %collective-permute-start.3 = (bf16[128,1536]{1,0:T(8,128)(2,1)}, bf16[128,1536]{1,0:T(8,128)(2,1)S(1)}, u32[]{:S(2)}, u32[]{:S(2)}) collective-permute-start(bf16[128,1536]{1,0:T(8,128)(2,1)} %get-tuple-element.50.refs_0_), channel_id=1, source_target_pairs={{0,2},{1,3},{2,4},{3,5},{4,6},{5,7},{6,0},{7,1},{8,10},{9,11},{10,... | collective-permute-start | bytes 1179656 | tf_op jit(solution)/shard_map/ppermute | solution.py:512
  11.8 16.7 %collective-permute-start.2 = (bf16[128,1536]{1,0:T(8,128)(2,1)}, bf16[128,1536]{1,0:T(8,128)(2,1)S(1)}, u32[]{:S(2)}, u32[]{:S(2)}) collective-permute-start(bf16[128,1536]{1,0:T(8,128)(2,1)} %get-tuple-element.50.refs_0_), channel_id=1, source_target_pairs={{0,6},{1,7},{2,0},{3,1},{4,2},{5,3},{6,4},{7,5},{8,14},{9,15},{10,... | collective-permute-start | bytes 1179656 | tf_op jit(solution)/shard_map/ppermute | solution.py:512
  13.6 10.5 %collective-permute-start = (bf16[96,384]{1,0:T(8,128)(2,1)S(1)}, bf16[96,384]{1,0:T(8,128)(2,1)S(1)}, u32[]{:S(2)}, u32[]{:S(2)}) collective-permute-start(bf16[96,384]{1,0:T(8,128)(2,1)S(1)} %bitcast.16), channel_id=1, source_target_pairs={{0,0},{1,128},{2,2},{3,130},{4,4},{5,132},{6,6},{7,134},{8,8},{9,1... | collective-permute-start | bytes 221192 | tf_op jit(solution)/shard_map/ppermute | solution.py:541
  18.2 10.3 %collective-permute-start.1 = (bf16[128,1536]{1,0:T(8,128)(2,1)}, bf16[128,1536]{1,0:T(8,128)(2,1)S(1)}, u32[]{:S(2)}, u32[]{:S(2)}) collective-permute-start(bf16[128,1536]{1,0:T(8,128)(2,1)} %get-tuple-element.49), channel_id=1, source_target_pairs={{0,1},{1,0},{2,3},{3,2},{4,5},{5,4},{6,7},{7,6},{8,9},{9,8},{10,11... | collective-permute-start | bytes 1179656 | tf_op jit(solution)/shard_map/ppermute | solution.py:528
  24.1 4.5 %copy-start.2 = (bf16[96,384]{1,0:T(8,128)(2,1)}, bf16[96,384]{1,0:T(8,128)(2,1)S(1)}, u32[]{:S(2)}) copy-start(bf16[96,384]{1,0:T(8,128)(2,1)S(1)} %collective-permute-done) | copy-start | bytes 221188
  28.5 68.6 %copy-start.8 = (bf16[128,1536]{1,0:T(8,128)(2,1)}, bf16[128,1536]{1,0:T(8,128)(2,1)S(1)}, u32[]{:S(2)}) copy-start(bf16[128,1536]{1,0:T(8,128)(2,1)S(1)} %collective-permute-done.1.refs_1_) | copy-start | bytes 1179652
  28.5 8.6 %copy-start.6 = (bf16[128,1536]{1,0:T(8,128)(2,1)}, bf16[128,1536]{1,0:T(8,128)(2,1)S(1)}, u32[]{:S(2)}) copy-start(bf16[128,1536]{1,0:T(8,128)(2,1)S(1)} %collective-permute-done.3.refs_6_) | copy-start | bytes 1179652
  29.3 56.6 %all-to-all-start = ((bf16[8,3,128,384]{3,2,1,0:T(8,128)(2,1)}), bf16[8,3,128,384]{3,2,1,0:T(8,128)(2,1)S(1)}, u32[]{:S(2)}, u32[]{:S(2)}) async-start(bf16[8,3,128,384]{3,2,1,0:T(8,128)(2,1)} %pack_heads.1), calls=%async_computation | async-start | bytes 4718592 | tf_op jit(solution)/shard_map/all_to_all | solution.py:550
  34.4 34.3 %collective-permute-start.5 = (bf16[128,1536]{1,0:T(8,128)(2,1)S(1)}, bf16[128,1536]{1,0:T(8,128)(2,1)S(1)}, u32[]{:S(2)}, u32[]{:S(2)}) collective-permute-start(bf16[128,1536]{1,0:T(8,128)(2,1)S(1)} %collective-permute-done.1.refs_1_), channel_id=1, source_target_pairs={{0,6},{1,7},{2,0},{3,1},{4,2},{5,3},{6,4},{7,5},{8,14},{9,15},{10,... | collective-permute-start | bytes 1179656 | tf_op jit(solution)/shard_map/ppermute | solution.py:512
  37.1 62.3 %collective-permute-start.8 = (bf16[128,1536]{1,0:T(8,128)(2,1)S(1)}, bf16[128,1536]{1,0:T(8,128)(2,1)}, u32[]{:S(2)}, u32[]{:S(2)}) collective-permute-start(bf16[128,1536]{1,0:T(8,128)(2,1)S(1)} %collective-permute-done.1.refs_1_), channel_id=1, source_target_pairs={{0,2},{1,3},{2,4},{3,5},{4,6},{5,7},{6,0},{7,1},{8,10},{9,11},{10,... | collective-permute-start | bytes 1179656 | tf_op jit(solution)/shard_map/ppermute | solution.py:512
  37.1 62.3 %collective-permute-start.6 = (bf16[128,1536]{1,0:T(8,128)(2,1)S(1)}, bf16[128,1536]{1,0:T(8,128)(2,1)}, u32[]{:S(2)}, u32[]{:S(2)}) collective-permute-start(bf16[128,1536]{1,0:T(8,128)(2,1)S(1)} %collective-permute-done.3.refs_6_), channel_id=1, source_target_pairs={{0,2},{1,3},{2,4},{3,5},{4,6},{5,7},{6,0},{7,1},{8,10},{9,11},{10,... | collective-permute-start | bytes 1179656 | tf_op jit(solution)/shard_map/ppermute | solution.py:512
  68.7 28.4 %copy-start.10 = (bf16[128,1536]{1,0:T(8,128)(2,1)}, bf16[128,1536]{1,0:T(8,128)(2,1)S(1)}, u32[]{:S(2)}) copy-start(bf16[128,1536]{1,0:T(8,128)(2,1)S(1)} %collective-permute-done.5.refs_3_) | copy-start | bytes 1179652
  83.2 16.2 %collective-permute-start.7 = (bf16[128,1536]{1,0:T(8,128)(2,1)S(1)}, bf16[128,1536]{1,0:T(8,128)(2,1)}, u32[]{:S(2)}, u32[]{:S(2)}) collective-permute-start(bf16[128,1536]{1,0:T(8,128)(2,1)S(1)} %collective-permute-done.5.refs_3_), channel_id=1, source_target_pairs={{0,6},{1,7},{2,0},{3,1},{4,2},{5,3},{6,4},{7,5},{8,14},{9,15},{10,... | collective-permute-start | bytes 1179656 | tf_op jit(solution)/shard_map/ppermute | solution.py:512
  97.1 20.8 %collective-permute-start.4 = (bf16[1024,384]{1,0:T(8,128)(2,1)}, bf16[1024,384]{1,0:T(8,128)(2,1)S(1)}, u32[]{:S(2)}, u32[]{:S(2)}) collective-permute-start(bf16[1024,384]{1,0:T(8,128)(2,1)} %get-tuple-element.52.a_ref.a1_ref.a3_ref.a0_ref), channel_id=1, source_target_pairs={{0,1},{1,0},{2,3},{3,2},{4,5},{5,4},{6,7},{7,6},{8,9},{9,8},{10,11... | collective-permute-start | bytes 2359304 | tf_op jit(solution)/shard_map/ppermute | solution.py:528
  106.8 33.8 %collective-permute-start.9 = (bf16[1024,384]{1,0:T(8,128)(2,1)}, bf16[1024,384]{1,0:T(8,128)(2,1)S(1)}, u32[]{:S(2)}, u32[]{:S(2)}) collective-permute-start(bf16[1024,384]{1,0:T(8,128)(2,1)} %get-tuple-element.60), channel_id=1, source_target_pairs={{0,1},{1,0},{2,3},{3,2},{4,5},{5,4},{6,7},{7,6},{8,9},{9,8},{10,11... | collective-permute-start | bytes 2359304 | tf_op jit(solution)/shard_map/ppermute | solution.py:528
  122.9 11.2 %collective-permute-start.10 = (bf16[128,1536]{1,0:T(8,128)(2,1)}, bf16[128,1536]{1,0:T(8,128)(2,1)S(1)}, u32[]{:S(2)}, u32[]{:S(2)}) collective-permute-start(bf16[128,1536]{1,0:T(8,128)(2,1)} %get-tuple-element.61), channel_id=1, source_target_pairs={{0,2},{1,3},{2,4},{3,5},{4,6},{5,7},{6,0},{7,1},{8,10},{9,11},{10,... | collective-permute-start | bytes 1179656 | tf_op jit(solution)/shard_map/ppermute | solution.py:512
  122.9 11.2 %collective-permute-start.11 = (bf16[128,1536]{1,0:T(8,128)(2,1)}, bf16[128,1536]{1,0:T(8,128)(2,1)S(1)}, u32[]{:S(2)}, u32[]{:S(2)}) collective-permute-start(bf16[128,1536]{1,0:T(8,128)(2,1)} %get-tuple-element.62), channel_id=1, source_target_pairs={{0,6},{1,7},{2,0},{3,1},{4,2},{5,3},{6,4},{7,5},{8,14},{9,15},{10,... | collective-permute-start | bytes 1179656 | tf_op jit(solution)/shard_map/ppermute | solution.py:512
  140.6 18.9 %collective-permute-start.12 = (bf16[256,1536]{1,0:T(8,128)(2,1)}, bf16[256,1536]{1,0:T(8,128)(2,1)}, u32[]{:S(2)}, u32[]{:S(2)}) collective-permute-start(bf16[256,1536]{1,0:T(8,128)(2,1)} %get-tuple-element.69), channel_id=1, source_target_pairs={{0,2},{1,3},{2,4},{3,5},{4,6},{5,7},{6,0},{7,1},{8,10},{9,11},{10,... | collective-permute-start | bytes 2359304 | tf_op jit(solution)/shard_map/ppermute | solution.py:512
  140.7 18.8 %collective-permute-start.13 = (bf16[256,1536]{1,0:T(8,128)(2,1)}, bf16[256,1536]{1,0:T(8,128)(2,1)}, u32[]{:S(2)}, u32[]{:S(2)}) collective-permute-start(bf16[256,1536]{1,0:T(8,128)(2,1)} %get-tuple-element.70), channel_id=1, source_target_pairs={{0,6},{1,7},{2,0},{3,1},{4,2},{5,3},{6,4},{7,5},{8,14},{9,15},{10,... | collective-permute-start | bytes 2359304 | tf_op jit(solution)/shard_map/ppermute | solution.py:512
  159.5 63.6 %all-to-all-start.1 = ((bf16[8,3,128,384]{3,2,1,0:T(8,128)(2,1)}), bf16[8,3,128,384]{3,2,1,0:T(8,128)(2,1)S(1)}, u32[]{:S(2)}, u32[]{:S(2)}) async-start(bf16[8,3,128,384]{3,2,1,0:T(8,128)(2,1)} %attention_backward.1), calls=%async_computation.1 | async-start | bytes 4718592 | tf_op jit(solution)/shard_map/all_to_all | solution.py:571
  172.1 3.1 %collective-permute-start.14 = (bf16[2,8,96,384]{3,2,1,0:T(8,128)(2,1)}, bf16[2,8,96,384]{3,2,1,0:T(8,128)(2,1)S(1)}, u32[]{:S(2)}, u32[]{:S(2)}) collective-permute-start(bf16[2,8,96,384]{3,2,1,0:T(8,128)(2,1)} %get-tuple-element.78), channel_id=1, source_target_pairs={{0,8},{8,0},{16,24},{24,16},{32,40},{40,32},{48,56},{56,48},{64,72... | collective-permute-start | bytes 3538952 | tf_op jit(solution)/shard_map/ppermute | solution.py:532
  179.0 16.8 %collective-permute-start.15 = (bf16[4,96,384]{2,1,0:T(8,128)(2,1)}, bf16[4,96,384]{2,1,0:T(8,128)(2,1)S(1)}, u32[]{:S(2)}, u32[]{:S(2)}) collective-permute-start(bf16[4,96,384]{2,1,0:T(8,128)(2,1)} %get-tuple-element.80), channel_id=1, source_target_pairs={{0,64},{8,72},{16,80},{24,88},{32,96},{40,104},{48,112},{56,120},{... | collective-permute-start | bytes 884744 | tf_op jit(solution)/shard_map/ppermute | solution.py:512
  179.0 16.8 %collective-permute-start.16 = (bf16[4,96,384]{2,1,0:T(8,128)(2,1)}, bf16[4,96,384]{2,1,0:T(8,128)(2,1)S(1)}, u32[]{:S(2)}, u32[]{:S(2)}) collective-permute-start(bf16[4,96,384]{2,1,0:T(8,128)(2,1)} %get-tuple-element.81), channel_id=1, source_target_pairs={{0,128},{8,136},{16,144},{24,152},{32,160},{40,168},{48,176},{56,1... | collective-permute-start | bytes 884744 | tf_op jit(solution)/shard_map/ppermute | solution.py:512
  181.2 15.3 %collective-permute-start.17 = (bf16[4,96,384]{2,1,0:T(8,128)(2,1)}, bf16[4,96,384]{2,1,0:T(8,128)(2,1)S(1)}, u32[]{:S(2)}, u32[]{:S(2)}) collective-permute-start(bf16[4,96,384]{2,1,0:T(8,128)(2,1)} %get-tuple-element.82), channel_id=1, source_target_pairs={{0,192},{8,200},{16,208},{24,216},{32,224},{40,232},{48,240},{56,2... | collective-permute-start | bytes 884744 | tf_op jit(solution)/shard_map/ppermute | solution.py:512
  197.2 19.2 %copy-start.9 = (bf16[128,1536]{1,0:T(8,128)(2,1)S(1)}, bf16[128,1536]{1,0:T(8,128)(2,1)}, u32[]{:S(2)}) copy-start(bf16[128,1536]{1,0:T(8,128)(2,1)} %get-tuple-element.84) | copy-start | bytes 1179652
  199.2 7.2 %collective-permute-start.19 = (bf16[96,384]{1,0:T(8,128)(2,1)}, bf16[96,384]{1,0:T(8,128)(2,1)S(1)}, u32[]{:S(2)}, u32[]{:S(2)}) collective-permute-start(bf16[96,384]{1,0:T(8,128)(2,1)} %get-tuple-element.92), channel_id=1, source_target_pairs={{0,16},{8,24},{16,32},{24,40},{32,48},{40,56},{48,0},{56,8},{64,80... | collective-permute-start | bytes 221192 | tf_op jit(solution)/shard_map/ppermute | solution.py:512
  200.2 9.5 %collective-permute-start.20 = (bf16[96,384]{1,0:T(8,128)(2,1)}, bf16[96,384]{1,0:T(8,128)(2,1)S(1)}, u32[]{:S(2)}, u32[]{:S(2)}) collective-permute-start(bf16[96,384]{1,0:T(8,128)(2,1)} %get-tuple-element.93), channel_id=1, source_target_pairs={{0,32},{8,40},{16,48},{24,56},{32,0},{40,8},{48,16},{56,24},{64,96... | collective-permute-start | bytes 221192 | tf_op jit(solution)/shard_map/ppermute | solution.py:512
  203.7 7.4 %collective-permute-start.21 = (bf16[96,384]{1,0:T(8,128)(2,1)}, bf16[96,384]{1,0:T(8,128)(2,1)S(1)}, u32[]{:S(2)}, u32[]{:S(2)}) collective-permute-start(bf16[96,384]{1,0:T(8,128)(2,1)} %get-tuple-element.94), channel_id=1, source_target_pairs={{0,48},{8,56},{16,0},{24,8},{32,16},{40,24},{48,32},{56,40},{64,11... | collective-permute-start | bytes 221192 | tf_op jit(solution)/shard_map/ppermute | solution.py:512
  212.0 11.1 %collective-permute-start.22 = (f32[96,384]{1,0:T(8,128)S(1)}, f32[96,384]{1,0:T(8,128)S(1)}, u32[]{:S(2)}, u32[]{:S(2)}) collective-permute-start(f32[96,384]{1,0:T(8,128)S(1)} %convert_add_fusion), channel_id=1, source_target_pairs={{0,0},{128,1},{2,2},{130,3},{4,4},{132,5},{6,6},{134,7},{8,8},{136... | collective-permute-start | bytes 442376 | tf_op jit(solution)/shard_map/ppermute | solution.py:581
  216.3 13.9 %collective-permute-start.18 = (bf16[128,1536]{1,0:T(8,128)(2,1)S(1)}, bf16[128,1536]{1,0:T(8,128)(2,1)S(1)}, u32[]{:S(2)}, u32[]{:S(2)}) collective-permute-start(bf16[128,1536]{1,0:T(8,128)(2,1)S(1)} %copy-done.9), channel_id=1, source_target_pairs={{0,1},{1,0},{2,3},{3,2},{4,5},{5,4},{6,7},{7,6},{8,9},{9,8},{10,11... | collective-permute-start | bytes 1179656 | tf_op jit(solution)/shard_map/ppermute | solution.py:528
  (12 other events, 14.7 us)
Sparse Core Ops, SparseCore 0:
  28.7 54.4 all-gather.1

commit v5 on v4

--- a/solution.py
+++ b/solution.py
@@ -210,33 +210,35 @@
 
 
 def pack_kernel(in_ref, out_ref):
-    out_ref[0] = in_ref[...]
+    for j in range(4):
+        out_ref[j] = in_ref[:, :, j * 384 : (j + 1) * 384]
 
 
 def pack_heads(qkv):
     return pl.pallas_call(
         pack_kernel,
         out_shape=jax.ShapeDtypeStruct((8, 3, 128, 384), BF),
-        grid=(8,),
-        in_specs=[pl.BlockSpec((3, 128, 384), lambda j: (0, 0, j))],
-        out_specs=pl.BlockSpec((1, 3, 128, 384), lambda j: (j, 0, 0, 0)),
-        cost_estimate=cost(6),
+        grid=(2,),
+        in_specs=[pl.BlockSpec((3, 128, 1536), lambda j: (0, 0, j))],
+        out_specs=pl.BlockSpec((4, 3, 128, 384), lambda j: (j, 0, 0, 0)),
+        cost_estimate=cost(3),
         name="pack_heads",
     )(qkv)
 
 
 def unpack_kernel(in_ref, out_ref):
-    out_ref[...] = in_ref[0]
+    for j in range(4):
+        out_ref[:, :, j * 384 : (j + 1) * 384] = in_ref[j]
 
 
 def unpack_heads(grads):
     return pl.pallas_call(
         unpack_kernel,
         out_shape=jax.ShapeDtypeStruct((3, 128, 3072), BF),
-        grid=(8,),
-        in_specs=[pl.BlockSpec((1, 3, 128, 384), lambda j: (j, 0, 0, 0))],
-        out_specs=pl.BlockSpec((3, 128, 384), lambda j: (0, 0, j)),
-        cost_estimate=cost(6),
+        grid=(2,),
+        in_specs=[pl.BlockSpec((4, 3, 128, 384), lambda j: (j, 0, 0, 0))],
+        out_specs=pl.BlockSpec((3, 128, 1536), lambda j: (0, 0, j)),
+        cost_estimate=cost(3),
         name="unpack_heads",
     )(grads)
 
@@ -417,58 +419,61 @@
     )(seq, own, other, weights, c1, c3)
 
 
-def dweight_kernel(core_ref, d_ref, a0_ref, a1_ref, keep_ref, send_ref):
-    d = d_ref[...]
-    even = core_ref[0] % 2 == 0
-    for z, a_ref in enumerate((a0_ref, a1_ref)):
-        g = dot_tn(d, a_ref[...]).astype(BF)
-        for i in range(2):
-            p0, p1 = g[i * 192 : i * 192 + 96], g[i * 192 + 96 : i * 192 + 192]
-            keep_ref[z, i] = jnp.where(even, p0, p1)
-            send_ref[z, i] = jnp.where(even, p1, p0)
-
-
-def dweight_part(core, dproj, own, other):
-    pieces = jax.ShapeDtypeStruct((2, 8, 96, 384), BF)
+def dweight_kernel(dp_ref, d_ref, a_ref, keep_ref, send_ref):
+    even = dp_ref[0] % 2 == 0
+    g = dot_tn(d_ref[...], a_ref[...]).astype(BF)
+    for i in range(4):
+        p0, p1 = g[i * 192 : i * 192 + 96], g[i * 192 + 96 : i * 192 + 192]
+        keep_ref[i] = jnp.where(even, p0, p1)
+        send_ref[i] = jnp.where(even, p1, p0)
+
+
+def dweight_part(dp, dproj, attn):
+    pieces = jax.ShapeDtypeStruct((8, 96, 384), BF)
     return pl.pallas_call(
         dweight_kernel,
         out_shape=(pieces, pieces),
         grid_spec=pltpu.PrefetchScalarGridSpec(
             num_scalar_prefetch=1,
-            grid=(4,),
+            grid=(2,),
             in_specs=[
-                pl.BlockSpec((1024, 384), lambda n, c: (0, n)),
-                pl.BlockSpec((1024, 384), lambda n, c: (0, 0)),
+                pl.BlockSpec((1024, 768), lambda n, c: (0, n)),
                 pl.BlockSpec((1024, 384), lambda n, c: (0, 0)),
             ],
             out_specs=(
-                pl.BlockSpec((2, 2, 96, 384), lambda n, c: (0, n, 0, 0)),
-                pl.BlockSpec((2, 2, 96, 384), lambda n, c: (0, n, 0, 0)),
+                pl.BlockSpec((4, 96, 384), lambda n, c: (n, 0, 0)),
+                pl.BlockSpec((4, 96, 384), lambda n, c: (n, 0, 0)),
             ),
         ),
         compiler_params=pltpu.CompilerParams(vmem_limit_bytes=VMEM_LIMIT),
-        cost_estimate=cost(7),
+        cost_estimate=cost(4),
         name="dweight_part",
-    )(core, dproj, own, other)
-
-
-def pair_kernel(dp_ref, keep_ref, got_ref, *out_refs):
+    )(dp, dproj, attn)
+
+
+def pair_kernel(dp_ref, k0_ref, g0_ref, k1_ref, g1_ref, *out_refs):
     y = dp_ref[0] // 8
     for k, out_ref in enumerate(out_refs):
         at = (y + k) % 4
-        out_ref[...] = (keep_ref[at].astype(F32) + got_ref[at].astype(F32)).astype(BF)
-
-
-def pair_sum(dp, keep, got):
+        for half, (keep_ref, got_ref) in enumerate(((k0_ref, g0_ref), (k1_ref, g1_ref))):
+
+            @pl.when(at // 2 == half)
+            def _(keep_ref=keep_ref, got_ref=got_ref, out_ref=out_ref, at=at):
+                total = keep_ref[at % 2].astype(F32) + got_ref[at % 2].astype(F32)
+                out_ref[...] = total.astype(BF)
+
+
+def pair_sum(dp, keep0, got0, keep1, got1):
+    terms = [t.reshape(2, 4, 96, 384) for t in (keep0, got0, keep1, got1)]
     return pl.pallas_call(
         pair_kernel,
         out_shape=(jax.ShapeDtypeStruct((4, 96, 384), BF),) * 4,
         in_specs=[pl.BlockSpec(memory_space=pltpu.SMEM)]
-        + [pl.BlockSpec((4, 4, 96, 384), lambda: (0, 0, 0, 0))] * 2,
+        + [pl.BlockSpec((2, 4, 96, 384), lambda: (0, 0, 0, 0))] * 4,
         out_specs=(pl.BlockSpec((4, 96, 384), lambda: (0, 0, 0)),) * 4,
         cost_estimate=cost(3),
         name="pair_sum",
-    )(dp, keep.reshape(4, 4, 96, 384), got.reshape(4, 4, 96, 384))
+    )(dp, *terms)
 
 
 def ring_kernel(dp_ref, a_ref, b_ref, c_ref, d_ref, *out_refs):
@@ -539,14 +544,13 @@
     moves = piece_moves(lax.axis_size("dp"), lax.axis_size("seq"))
 
     piece = lax.ppermute(out_weight.T, both, moves)
+    packed = pack_heads(qkv_input.transpose(1, 0, 2))
+    packed, piece, cotangent = lax.optimization_barrier((packed, piece, cotangent))
+    weights = lax.all_gather(piece, "dp", axis=0, tiled=True).reshape(2, 1536, 384)
     keep, send = gated_cotangent(frames, timesteps, seq, gate_table, cotangent)
     got = swap_z(send)
     b1_keep, b3_keep = along_x(keep, -1), along_x(keep, 1)
-    packed = pack_heads(qkv_input.transpose(1, 0, 2))
-    packed, piece, got, b1_keep, b3_keep = lax.optimization_barrier(
-        (packed, piece, got, b1_keep, b3_keep)
-    )
-    weights = lax.all_gather(piece, "dp", axis=0, tiled=True).reshape(2, 1536, 384)
+    packed, got, b1_keep, b3_keep = lax.optimization_barrier((packed, got, b1_keep, b3_keep))
     heads = lax.all_to_all(packed, "seq", split_axis=0, concat_axis=0, tiled=True)
 
     b1 = [b1_keep, along_x(got, -1)]
@@ -558,18 +562,23 @@
     attn_other = swap_z(attn)
     dproj, d_send, d_own = dattn_parts(seq, [keep, got, *b1, *b2, *b3], weights)
     d_recv = swap_z(d_send)
+    keep0, send0 = dweight_part(dp, dproj, attn)
+    attn_other, keep0 = lax.optimization_barrier((attn_other, keep0))
+    got0 = swap_core(send0)
     up, down = project_far(seq, attn, attn_other, weights)
+    behind, _ = lax.optimization_barrier((dproj, up))
+    keep1, send1 = dweight_part(dp, behind, attn_other)
+    got1 = swap_core(send1)
     up, down = along_x(up, 1), along_x(down, -1)
+    up, keep1 = lax.optimization_barrier((up, keep1))
     t1, t3 = project_near(seq, attn, attn_other, weights, up, down)
     d_own, d_recv, t1, t3 = lax.optimization_barrier((d_own, d_recv, t1, t3))
     c1, c3 = along_x(t1, 1), along_x(t3, -1)
+    terms = pair_sum(dp, keep0, got0, keep1, got1)
 
     grads = attention_backward(frames, heads, d_own, d_recv, p1, p2)
-    grads, c1, c3, dproj = lax.optimization_barrier((grads, c1, c3, dproj))
-    w_keep, w_send = dweight_part(dp, dproj, attn, attn_other)
-    w_got = swap_core(w_send)
+    grads, c1, c3, terms = lax.optimization_barrier((grads, c1, c3, terms))
     grads = lax.all_to_all(grads, "seq", split_axis=0, concat_axis=0, tiled=True)
-    terms = pair_sum(dp, w_keep, w_got)
     terms = [terms[0]] + [along_y(terms[k], k) for k in range(1, 4)]
 
     o_keep, o_send = project_home(seq, attn, attn_other, weights, c1, c3)

time: 243 us -> 215 us (0.88)
  waiting for transfers between devices: 97.4 us -> 70.1 us
  Pallas kernels: 71.8 us -> 68 us
    ppermute x16, waiting for transfers between devices: 57.6 us -> 44.6 us  [along(): return lax.ppermute(x, axis, moves)]
    all_gather x1, waiting for transfers between devices: 14.5 us -> 6.31 us  [body(): lax.all_gather(piece, 'dp', axis=0, tiled=True).reshape(2, 1536, 384)]
    ppermute x1 -> x2, waiting for transfers between devices: 3.06 us -> 0.01 us  [swap_core(): lax.ppermute(x, 'dp', [(i, i ^ 1) for i in range(lax.axis_size('dp'))])]
    pallas_call x1, Pallas kernels: 5.78 us -> 2.78 us  [pack_heads(): pl.pallas_call(pack_kernel, out_shape=jax.ShapeDtypeStruct((8, 3, 128, 38...]
    pallas_call x1, Pallas kernels: 5.77 us -> 2.77 us  [unpack_heads(): pl.pallas_call(unpack_kernel, out_shape=jax.ShapeDtypeStruct((3, 128, 307...]
    pallas_call x1 -> x2, Pallas kernels: 6.92 us -> 8.99 us  [dweight_part(): pl.pallas_call(dweight_kernel, out_shape=(pieces, pieces), grid_spec=pltp...]
  transfers between devices with their start and end apart: 26 -> 27, of which waited for: 13 -> 15; matrix products, arithmetic and copies ran while one was open for 0% -> 0% of each run, Pallas kernels for 27% -> 30%
where the time goes in v5:
time: 215 us; the launch traced here: 214 us
  waiting for transfers between devices  70.1 us (33%)
  Pallas kernels  68 us (32%)
  starting transfers between devices  50.8 us (24%)
  between operations  14.1 us (7%)
  local copies, waits for them, and re-layouts  10.5 us (5%)
    ppermute x16, waiting for transfers between devices, along(): return lax.ppermute(x, axis, moves)  44.6 us
    ppermute x16, starting transfers between devices, along(): return lax.ppermute(x, axis, moves)  27.7 us
    ppermute x4, waiting for transfers between devices, swap_z(): lax.ppermute(x, 'seq', [(i, i ^ 1) for i in range(lax.axis_size('seq'))])  13.6 us
    pallas_call x1, Pallas kernels, attention_backward(): pl.pallas_call(bwd_kernel, out_shape=jax.ShapeDtypeStruct((8, 3, 128, 3 *...  11.1 us
    unnamed x37, local copies, waits for them, and re-layouts  10.5 us
    pallas_call x1, Pallas kernels, attention_forward(): pl.pallas_call(fwd_kernel, out_shape=(jax.ShapeDtypeStruct((1024, 3 * HD)...  9.81 us
    pallas_call x2, Pallas kernels, dweight_part(): pl.pallas_call(dweight_kernel, out_shape=(pieces, pieces), grid_spec=pltp...  8.99 us
    pallas_call x1, Pallas kernels, dattn_parts(): pl.pallas_call(dattn_kernel, out_shape=(jax.ShapeDtypeStruct((1024, 1536)...  7.39 us
  transfers between devices with their start and end apart: 27, of which 15 were waited for; matrix products, arithmetic and copies ran while one was open for 0% of the time, Pallas kernels for 30%

profile of v5, /device:TPU:32, one launch (start us, length us, event | category | flops | bytes accessed | tf_op | source)
XLA Modules:
  0.0 214.5 jit_solution(3138699012024567797)
XLA Ops:
  7.2 4.6 %collective-permute-start = (bf16[96,384]{1,0:T(8,128)(2,1)}, bf16[96,384]{1,0:T(8,128)(2,1)S(1)}, u32[]{:S(2)}, u32[]{:S(2)}) collective-permute-start(bf16[96,384]{1,0:T(8,128)(2,1)} %bitcast.18), channel_id=1, source_target_pairs={{0,0},{1,128},{2,2},{3,130},{4,4},{5,132},{6,6},{7,134},{8,8},{9,1... | collective-permute-start | bytes 221192 | tf_op jit(solution)/shard_map/ppermute | solution.py:546
  11.9 2.8 %pack_heads.1 = bf16[8,3,128,384]{3,2,1,0:T(8,128)(2,1)} custom-call(bf16[3,128,3072]{2,1,0:T(8,128)(2,1)} %bitcast.12), custom_call_target="tpu_custom_call" | custom-call | flops 3000000000 | bytes 9000000 | tf_op jit(solution)/shard_map/pack_heads/pallas_call | solution.py:218
  15.8 3.0 %gated_cotangent.1 = (bf16[128,1536]{1,0:T(8,128)(2,1)}, bf16[128,1536]{1,0:T(8,128)(2,1)}) custom-call(s32[1,3]{1,0:T(1,128)} %frames_ref.7, s32[1,3]{1,0:T(1,128)} %steps_ref.3, s32[1]{0:T(128)} %bitcast.seq_ref, f32[64,3072]{1,0:T(8,128)} %t1_ref.3, f32[64,3072]{1,0:T(8,128)} %t1_ref.3, bf16[128,3072]{1,0:T(8,128)(2,1)} %c1_ref, bf16[128,3072]{1,0:T(8,128)(2,1)} %c1_ref), custom_call_target="tpu_custom_call" | custom-call | flops 3000000000 | bytes 9000000 | tf_op jit(solution)/shard_map/gated_cotangent/pallas_call | solution.py:259
  22.1 7.0 %collective-permute-done.1.refs_1_ = bf16[128,1536]{1,0:T(8,128)(2,1)S(1)} collective-permute-done((bf16[128,1536]{1,0:T(8,128)(2,1)}, bf16[128,1536]{1,0:T(8,128)(2,1)S(1)}, u32[]{:S(2)}, u32[]{:S(2)}) %collective-permute-start.1) | collective-permute-done | bytes 393248 | tf_op jit(solution)/shard_map/ppermute | solution.py:533
  30.5 5.9 %all-to-all-start = ((bf16[8,3,128,384]{3,2,1,0:T(8,128)(2,1)}), bf16[8,3,128,384]{3,2,1,0:T(8,128)(2,1)S(1)}, u32[]{:S(2)}, u32[]{:S(2)}) async-start(bf16[8,3,128,384]{3,2,1,0:T(8,128)(2,1)} %pack_heads.1), calls=%async_computation | async-start | bytes 4718592 | tf_op jit(solution)/shard_map/all_to_all | solution.py:554
  36.4 2.7 %collective-permute-start.5 = (bf16[128,1536]{1,0:T(8,128)(2,1)S(1)}, bf16[128,1536]{1,0:T(8,128)(2,1)}, u32[]{:S(2)}, u32[]{:S(2)}) collective-permute-start(bf16[128,1536]{1,0:T(8,128)(2,1)S(1)} %collective-permute-done.1.refs_1_), channel_id=1, source_target_pairs={{0,6},{1,7},{2,0},{3,1},{4,2},{5,3},{6,4},{7,5},{8,14},{9,15},{10,... | collective-permute-start | bytes 1179656 | tf_op jit(solution)/shard_map/ppermute | solution.py:517
  39.9 29.9 %collective-permute-done.5.refs_3_ = bf16[128,1536]{1,0:T(8,128)(2,1)} collective-permute-done((bf16[128,1536]{1,0:T(8,128)(2,1)S(1)}, bf16[128,1536]{1,0:T(8,128)(2,1)}, u32[]{:S(2)}, u32[]{:S(2)}) %collective-permute-start.5) | collective-permute-done | bytes 393248 | tf_op jit(solution)/shard_map/ppermute | solution.py:517
  69.8 6.3 %all-gather.2.cloned.1.call-done = bf16[3072,384]{1,0:T(8,128)(2,1)} async-done(((bf16[96,384]{1,0:T(8,128)(2,1)}), bf16[3072,384]{1,0:T(8,128)(2,1)}) %all-gather.2.cloned.1.call-update) | async-done | bytes 2359312 | tf_op jit(solution)/shard_map/all_gather | solution.py:549
  76.1 2.7 %collective-permute-start.7 = (bf16[128,1536]{1,0:T(8,128)(2,1)}, bf16[128,1536]{1,0:T(8,128)(2,1)}, u32[]{:S(2)}, u32[]{:S(2)}) collective-permute-start(bf16[128,1536]{1,0:T(8,128)(2,1)} %collective-permute-done.5.refs_3_), channel_id=1, source_target_pairs={{0,6},{1,7},{2,0},{3,1},{4,2},{5,3},{6,4},{7,5},{8,14},{9,15},{10,... | collective-permute-start | bytes 1179656 | tf_op jit(solution)/shard_map/ppermute | solution.py:517
  80.2 9.8 %attention_forward.1 = (bf16[1024,384]{1,0:T(8,128)(2,1)}, bf16[3,640,640]{2,1,0:T(8,128)(2,1)}, bf16[3,384,384]{2,1,0:T(8,128)(2,1)}) custom-call(s32[1,3]{1,0:T(1,128)} %frames_ref.7, bf16[8,3,128,384]{3,2,1,0:T(8,128)(2,1)} %copy-done), custom_call_target="tpu_custom_call" | custom-call | flops 10000000000 | bytes 30000000 | tf_op jit(solution)/shard_map/attention_forward/pallas_call | solution.py:116
  91.9 7.4 %dattn_parts.1 = (bf16[1024,1536]{1,0:T(8,128)(2,1)}, bf16[1024,384]{1,0:T(8,128)(2,1)}, f32[1024,384]{1,0:T(8,128)}) custom-call(s32[1]{0:T(128)} %bitcast.seq_ref, bf16[128,1536]{1,0:T(8,128)(2,1)} %get-tuple-element.64.refs_0_, bf16[128,1536]{1,0:T(8,128)(2,1)} %copy-done.9, bf16[128,1536]{1,0:T(8,128)(2,1)} %collective-permute-done.2.refs_2_, ...), custom_call_target="tpu_custom_call" | custom-call | flops 7000000000 | bytes 21000000 | tf_op jit(solution)/shard_map/dattn_parts/pallas_call | solution.py:322
  99.4 4.5 %dweight_part.2 = (bf16[8,96,384]{2,1,0:T(8,128)(2,1)}, bf16[8,96,384]{2,1,0:T(8,128)(2,1)}) custom-call(s32[1]{0:T(128)} %bitcast.3.dp_ref, bf16[1024,1536]{1,0:T(8,128)(2,1)} %get-tuple-element.79.d_ref, bf16[1024,384]{1,0:T(8,128)(2,1)} %get-tuple-element.66.a_ref.a1_ref.a3_ref), custom_call_target="tpu_custom_call" | custom-call | flops 4000000000 | bytes 12000000 | tf_op jit(solution)/shard_map/dweight_part/pallas_call | solution.py:433
  103.9 6.7 %collective-permute-done.4.b_ref.a_ref.b1_ref.b3_ref = bf16[1024,384]{1,0:T(8,128)(2,1)S(1)} collective-permute-done((bf16[1024,384]{1,0:T(8,128)(2,1)}, bf16[1024,384]{1,0:T(8,128)(2,1)S(1)}, u32[]{:S(2)}, u32[]{:S(2)}) %collective-permute-start.4) | collective-permute-done | bytes 786464 | tf_op jit(solution)/shard_map/ppermute | solution.py:533
  111.5 4.1 %project_far.1 = (bf16[128,1536]{1,0:T(8,128)(2,1)}, bf16[128,1536]{1,0:T(8,128)(2,1)}) custom-call(s32[1]{0:T(128)} %bitcast.seq_ref, bf16[1024,384]{1,0:T(8,128)(2,1)} %get-tuple-element.66.a_ref.a1_ref.a3_ref, bf16[1024,384]{1,0:T(8,128)(2,1)} %copy-done.3, bf16[2,1536,384]{2,1,0:T(8,128)(2,1)} %bitcast.14), custom_call_target="tpu_custom_call" | custom-call | flops 4000000000 | bytes 12000000 | tf_op jit(solution)/shard_map/project_far/pallas_call | solution.py:393
  115.6 3.2 %collective-permute-start.11 = (bf16[128,1536]{1,0:T(8,128)(2,1)}, bf16[128,1536]{1,0:T(8,128)(2,1)S(1)}, u32[]{:S(2)}, u32[]{:S(2)}) collective-permute-start(bf16[128,1536]{1,0:T(8,128)(2,1)} %get-tuple-element.82), channel_id=1, source_target_pairs={{0,6},{1,7},{2,0},{3,1},{4,2},{5,3},{6,4},{7,5},{8,14},{9,15},{10,... | collective-permute-start | bytes 1179656 | tf_op jit(solution)/shard_map/ppermute | solution.py:517
  118.8 4.5 %dweight_part.3 = (bf16[8,96,384]{2,1,0:T(8,128)(2,1)}, bf16[8,96,384]{2,1,0:T(8,128)(2,1)}) custom-call(s32[1]{0:T(128)} %bitcast.3.dp_ref, bf16[1024,1536]{1,0:T(8,128)(2,1)} %get-tuple-element.79.d_ref, bf16[1024,384]{1,0:T(8,128)(2,1)} %copy-done.3), custom_call_target="tpu_custom_call" | custom-call | flops 4000000000 | bytes 12000000 | tf_op jit(solution)/shard_map/dweight_part/pallas_call | solution.py:433
  123.8 2.7 %collective-permute-done.10.up_ref = bf16[128,1536]{1,0:T(8,128)(2,1)S(1)} collective-permute-done((bf16[128,1536]{1,0:T(8,128)(2,1)}, bf16[128,1536]{1,0:T(8,128)(2,1)S(1)}, u32[]{:S(2)}, u32[]{:S(2)}) %collective-permute-start.10) | collective-permute-done | bytes 393248 | tf_op jit(solution)/shard_map/ppermute | solution.py:517
  128.1 4.9 %project_near.1 = (bf16[256,1536]{1,0:T(8,128)(2,1)}, bf16[256,1536]{1,0:T(8,128)(2,1)}) custom-call(s32[1]{0:T(128)} %bitcast.seq_ref, bf16[1024,384]{1,0:T(8,128)(2,1)} %get-tuple-element.66.a_ref.a1_ref.a3_ref, bf16[1024,384]{1,0:T(8,128)(2,1)} %copy-done.3, bf16[1024,384]{1,0:T(8,128)(2,1)} %get-tuple-element.66.a_ref.a1_ref.a3_ref, ...), custom_call_target="tpu_custom_call" | custom-call | flops 4000000000 | bytes 12000000 | tf_op jit(solution)/shard_map/project_near/pallas_call | solution.py:403
  133.1 3.2 %collective-permute-start.13 = (bf16[256,1536]{1,0:T(8,128)(2,1)}, bf16[256,1536]{1,0:T(8,128)(2,1)S(1)}, u32[]{:S(2)}, u32[]{:S(2)}) collective-permute-start(bf16[256,1536]{1,0:T(8,128)(2,1)} %get-tuple-element.90), channel_id=1, source_target_pairs={{0,6},{1,7},{2,0},{3,1},{4,2},{5,3},{6,4},{7,5},{8,14},{9,15},{10,... | collective-permute-start | bytes 2359304 | tf_op jit(solution)/shard_map/ppermute | solution.py:517
  136.3 11.1 %attention_backward.1 = bf16[8,3,128,384]{3,2,1,0:T(8,128)(2,1)} custom-call(s32[1,3]{1,0:T(1,128)} %frames_ref.7, bf16[8,3,128,384]{3,2,1,0:T(8,128)(2,1)} %copy-done, f32[1024,384]{1,0:T(8,128)} %get-tuple-element.85.own_ref, bf16[1024,384]{1,0:T(8,128)(2,1)} %copy-done.4, bf16[3,640,640]{2,1,0:T(8,128)(2,1)} %get-tuple-element.87.p1_ref, ...), custom_call_target="tpu_custom_call" | custom-call | flops 11000000512 | bytes 33000000 | tf_op jit(solution)/shard_map/attention_backward/pallas_call | solution.py:185
  148.3 3.0 %pair_sum.1 = (bf16[4,96,384]{2,1,0:T(8,128)(2,1)}, bf16[4,96,384]{2,1,0:T(8,128)(2,1)}, bf16[4,96,384]{2,1,0:T(8,128)(2,1)}, bf16[4,96,384]{2,1,0:T(8,128)(2,1)}) custom-call(s32[1]{0:T(128)} %bitcast.3.dp_ref, bf16[2,4,96,384]{3,2,1,0:T(8,128)(2,1)} %bitcast.20, bf16[2,4,96,384]{3,2,1,0:T(8,128)(2,1)} %bitcast.17, bf16[2,4,96,384]{3,2,1,0:T(8,128)(2,1)} %bitcast.21, ...), custom_call_target="tpu_custom_call" | custom-call | flops 3000000000 | bytes 9000000 | tf_op jit(solution)/shard_map/pair_sum/pallas_call | solution.py:468
  152.7 5.6 %all-to-all-start.1 = ((bf16[8,3,128,384]{3,2,1,0:T(8,128)(2,1)}), bf16[8,3,128,384]{3,2,1,0:T(8,128)(2,1)S(1)}, u32[]{:S(2)}, u32[]{:S(2)}) async-start(bf16[8,3,128,384]{3,2,1,0:T(8,128)(2,1)} %attention_backward.1), calls=%async_computation.1 | async-start | bytes 4718592 | tf_op jit(solution)/shard_map/all_to_all | solution.py:581
  159.2 2.7 %collective-permute-start.17 = (bf16[4,96,384]{2,1,0:T(8,128)(2,1)}, bf16[4,96,384]{2,1,0:T(8,128)(2,1)S(1)}, u32[]{:S(2)}, u32[]{:S(2)}) collective-permute-start(bf16[4,96,384]{2,1,0:T(8,128)(2,1)} %get-tuple-element.105), channel_id=1, source_target_pairs={{0,128},{8,136},{16,144},{24,152},{32,160},{40,168},{48,176},{56,1... | collective-permute-start | bytes 884744 | tf_op jit(solution)/shard_map/ppermute | solution.py:517
  163.3 4.6 %project_home.1 = (f32[128,1536]{1,0:T(8,128)}, bf16[128,1536]{1,0:T(8,128)(2,1)}) custom-call(s32[1]{0:T(128)} %bitcast.seq_ref, bf16[1024,384]{1,0:T(8,128)(2,1)} %get-tuple-element.66.a_ref.a1_ref.a3_ref, bf16[1024,384]{1,0:T(8,128)(2,1)} %copy-done.3, bf16[2,1536,384]{2,1,0:T(8,128)(2,1)} %bitcast.16, bf16[256,1536]{1,0:T(8,128)(2,1)} %copy-done.5, ...), custom_call_target="tpu_custom_call" | custom-call | flops 4000000000 | bytes 12000000 | tf_op jit(solution)/shard_map/project_home/pallas_call | solution.py:413
  168.3 3.2 %collective-permute-done.17.c_ref = bf16[4,96,384]{2,1,0:T(8,128)(2,1)S(1)} collective-permute-done((bf16[4,96,384]{2,1,0:T(8,128)(2,1)}, bf16[4,96,384]{2,1,0:T(8,128)(2,1)S(1)}, u32[]{:S(2)}, u32[]{:S(2)}) %collective-permute-start.17) | collective-permute-done | bytes 294944 | tf_op jit(solution)/shard_map/ppermute | solution.py:517
  175.7 3.4 %collective-permute-start.21 = (bf16[96,384]{1,0:T(8,128)(2,1)}, bf16[96,384]{1,0:T(8,128)(2,1)S(1)}, u32[]{:S(2)}, u32[]{:S(2)}) collective-permute-start(bf16[96,384]{1,0:T(8,128)(2,1)} %get-tuple-element.117), channel_id=1, source_target_pairs={{0,32},{8,40},{16,48},{24,56},{32,0},{40,8},{48,16},{56,24},{64,96... | collective-permute-start | bytes 221192 | tf_op jit(solution)/shard_map/ppermute | solution.py:517
  179.1 2.5 %collective-permute-start.22 = (bf16[96,384]{1,0:T(8,128)(2,1)}, bf16[96,384]{1,0:T(8,128)(2,1)S(1)}, u32[]{:S(2)}, u32[]{:S(2)}) collective-permute-start(bf16[96,384]{1,0:T(8,128)(2,1)} %get-tuple-element.118), channel_id=1, source_target_pairs={{0,48},{8,56},{16,0},{24,8},{32,16},{40,24},{48,32},{56,40},{64,11... | collective-permute-start | bytes 221192 | tf_op jit(solution)/shard_map/ppermute | solution.py:517
  182.5 5.2 %collective-permute-done.21 = bf16[96,384]{1,0:T(8,128)(2,1)S(1)} collective-permute-done((bf16[96,384]{1,0:T(8,128)(2,1)}, bf16[96,384]{1,0:T(8,128)(2,1)S(1)}, u32[]{:S(2)}, u32[]{:S(2)}) %collective-permute-start.21) | collective-permute-done | bytes 73760 | tf_op jit(solution)/shard_map/ppermute | solution.py:517
  189.1 4.3 %collective-permute-start.23 = (f32[96,384]{1,0:T(8,128)S(1)}, f32[96,384]{1,0:T(8,128)S(1)}, u32[]{:S(2)}, u32[]{:S(2)}) collective-permute-start(f32[96,384]{1,0:T(8,128)S(1)} %convert_add_fusion), channel_id=1, source_target_pairs={{0,0},{128,1},{2,2},{130,3},{4,4},{132,5},{6,6},{134,7},{8,8},{136... | collective-permute-start | bytes 442376 | tf_op jit(solution)/shard_map/ppermute | solution.py:590
  193.5 5.0 %collective-permute-done.23 = f32[96,384]{1,0:T(8,128)S(1)} collective-permute-done((f32[96,384]{1,0:T(8,128)S(1)}, f32[96,384]{1,0:T(8,128)S(1)}, u32[]{:S(2)}, u32[]{:S(2)}) %collective-permute-start.23) | collective-permute-done | bytes 147488 | tf_op jit(solution)/shard_map/ppermute | solution.py:590
  200.0 2.8 %unpack_heads.1 = bf16[3,128,3072]{2,1,0:T(8,128)(2,1)} custom-call(bf16[8,3,128,384]{3,2,1,0:T(8,128)(2,1)} %copy-done.1), custom_call_target="tpu_custom_call" | custom-call | flops 3000000000 | bytes 9000000 | tf_op jit(solution)/shard_map/unpack_heads/pallas_call | solution.py:235
  203.5 3.5 %gated_output.1 = bf16[128,3072]{1,0:T(8,128)(2,1)} custom-call(s32[1,3]{1,0:T(1,128)} %frames_ref.7, s32[1,3]{1,0:T(1,128)} %steps_ref.3, s32[1]{0:T(128)} %bitcast.seq_ref, f32[64,3072]{1,0:T(8,128)} %t1_ref.3, f32[64,3072]{1,0:T(8,128)} %t1_ref.3, bf16[128,3072]{1,0:T(8,128)(2,1)} %l1_ref.1, bf16[128,3072]{1,0:T(8,128)(2,1)} %l1_ref.1, ...), custom_call_target="tpu_custom_call" | custom-call | flops 3000000000 | bytes 9000000 | tf_op jit(solution)/shard_map/gated_output/pallas_call | solution.py:293
  (75 shorter events, 27.6 us)
Async XLA Ops:
  7.2 68.9 %all-gather.2.cloned.1.call-start = ((), (), s32[]{:S(2)}) async-start(), calls=%async_computation.2 | async-start | bytes 2433024 | tf_op jit(solution)/shard_map/all_gather | solution.py:549
  7.2 8.0 %collective-permute-start = (bf16[96,384]{1,0:T(8,128)(2,1)}, bf16[96,384]{1,0:T(8,128)(2,1)S(1)}, u32[]{:S(2)}, u32[]{:S(2)}) collective-permute-start(bf16[96,384]{1,0:T(8,128)(2,1)} %bitcast.18), channel_id=1, source_target_pairs={{0,0},{1,128},{2,2},{3,130},{4,4},{5,132},{6,6},{7,134},{8,8},{9,1... | collective-permute-start | bytes 221192 | tf_op jit(solution)/shard_map/ppermute | solution.py:546
  18.8 10.3 %collective-permute-start.1 = (bf16[128,1536]{1,0:T(8,128)(2,1)}, bf16[128,1536]{1,0:T(8,128)(2,1)S(1)}, u32[]{:S(2)}, u32[]{:S(2)}) collective-permute-start(bf16[128,1536]{1,0:T(8,128)(2,1)} %get-tuple-element.63), channel_id=1, source_target_pairs={{0,1},{1,0},{2,3},{3,2},{4,5},{5,4},{6,7},{7,6},{8,9},{9,8},{10,11... | collective-permute-start | bytes 1179656 | tf_op jit(solution)/shard_map/ppermute | solution.py:533
  18.8 11.7 %collective-permute-start.3 = (bf16[128,1536]{1,0:T(8,128)(2,1)}, bf16[128,1536]{1,0:T(8,128)(2,1)}, u32[]{:S(2)}, u32[]{:S(2)}) collective-permute-start(bf16[128,1536]{1,0:T(8,128)(2,1)} %get-tuple-element.64.refs_0_), channel_id=1, source_target_pairs={{0,2},{1,3},{2,4},{3,5},{4,6},{5,7},{6,0},{7,1},{8,10},{9,11},{10,... | collective-permute-start | bytes 1179656 | tf_op jit(solution)/shard_map/ppermute | solution.py:517
  20.4 10.1 %collective-permute-start.2 = (bf16[128,1536]{1,0:T(8,128)(2,1)}, bf16[128,1536]{1,0:T(8,128)(2,1)}, u32[]{:S(2)}, u32[]{:S(2)}) collective-permute-start(bf16[128,1536]{1,0:T(8,128)(2,1)} %get-tuple-element.64.refs_0_), channel_id=1, source_target_pairs={{0,6},{1,7},{2,0},{3,1},{4,2},{5,3},{6,4},{7,5},{8,14},{9,15},{10,... | collective-permute-start | bytes 1179656 | tf_op jit(solution)/shard_map/ppermute | solution.py:517
  29.1 10.0 %copy-start.9 = (bf16[128,1536]{1,0:T(8,128)(2,1)}, bf16[128,1536]{1,0:T(8,128)(2,1)S(1)}, u32[]{:S(2)}) copy-start(bf16[128,1536]{1,0:T(8,128)(2,1)S(1)} %collective-permute-done.1.refs_1_) | copy-start | bytes 1179652
  30.5 48.3 %all-to-all-start = ((bf16[8,3,128,384]{3,2,1,0:T(8,128)(2,1)}), bf16[8,3,128,384]{3,2,1,0:T(8,128)(2,1)S(1)}, u32[]{:S(2)}, u32[]{:S(2)}) async-start(bf16[8,3,128,384]{3,2,1,0:T(8,128)(2,1)} %pack_heads.1), calls=%async_computation | async-start | bytes 4718592 | tf_op jit(solution)/shard_map/all_to_all | solution.py:554
  36.4 33.4 %collective-permute-start.5 = (bf16[128,1536]{1,0:T(8,128)(2,1)S(1)}, bf16[128,1536]{1,0:T(8,128)(2,1)}, u32[]{:S(2)}, u32[]{:S(2)}) collective-permute-start(bf16[128,1536]{1,0:T(8,128)(2,1)S(1)} %collective-permute-done.1.refs_1_), channel_id=1, source_target_pairs={{0,6},{1,7},{2,0},{3,1},{4,2},{5,3},{6,4},{7,5},{8,14},{9,15},{10,... | collective-permute-start | bytes 1179656 | tf_op jit(solution)/shard_map/ppermute | solution.py:517
  39.0 52.8 %collective-permute-start.8 = (bf16[128,1536]{1,0:T(8,128)(2,1)S(1)}, bf16[128,1536]{1,0:T(8,128)(2,1)}, u32[]{:S(2)}, u32[]{:S(2)}) collective-permute-start(bf16[128,1536]{1,0:T(8,128)(2,1)S(1)} %collective-permute-done.1.refs_1_), channel_id=1, source_target_pairs={{0,2},{1,3},{2,4},{3,5},{4,6},{5,7},{6,0},{7,1},{8,10},{9,11},{10,... | collective-permute-start | bytes 1179656 | tf_op jit(solution)/shard_map/ppermute | solution.py:517
  39.0 52.8 %collective-permute-start.6 = (bf16[128,1536]{1,0:T(8,128)(2,1)}, bf16[128,1536]{1,0:T(8,128)(2,1)}, u32[]{:S(2)}, u32[]{:S(2)}) collective-permute-start(bf16[128,1536]{1,0:T(8,128)(2,1)} %collective-permute-done.3.refs_6_), channel_id=1, source_target_pairs={{0,2},{1,3},{2,4},{3,5},{4,6},{5,7},{6,0},{7,1},{8,10},{9,11},{10,... | collective-permute-start | bytes 1179656 | tf_op jit(solution)/shard_map/ppermute | solution.py:517
  76.1 15.8 %collective-permute-start.7 = (bf16[128,1536]{1,0:T(8,128)(2,1)}, bf16[128,1536]{1,0:T(8,128)(2,1)}, u32[]{:S(2)}, u32[]{:S(2)}) collective-permute-start(bf16[128,1536]{1,0:T(8,128)(2,1)} %collective-permute-done.5.refs_3_), channel_id=1, source_target_pairs={{0,6},{1,7},{2,0},{3,1},{4,2},{5,3},{6,4},{7,5},{8,14},{9,15},{10,... | collective-permute-start | bytes 1179656 | tf_op jit(solution)/shard_map/ppermute | solution.py:517
  90.0 20.6 %collective-permute-start.4 = (bf16[1024,384]{1,0:T(8,128)(2,1)}, bf16[1024,384]{1,0:T(8,128)(2,1)S(1)}, u32[]{:S(2)}, u32[]{:S(2)}) collective-permute-start(bf16[1024,384]{1,0:T(8,128)(2,1)} %get-tuple-element.66.a_ref.a1_ref.a3_ref), channel_id=1, source_target_pairs={{0,1},{1,0},{2,3},{3,2},{4,5},{5,4},{6,7},{7,6},{8,9},{9,8},{10,11... | collective-permute-start | bytes 2359304 | tf_op jit(solution)/shard_map/ppermute | solution.py:533
  99.3 33.7 %collective-permute-start.9 = (bf16[1024,384]{1,0:T(8,128)(2,1)}, bf16[1024,384]{1,0:T(8,128)(2,1)S(1)}, u32[]{:S(2)}, u32[]{:S(2)}) collective-permute-start(bf16[1024,384]{1,0:T(8,128)(2,1)} %get-tuple-element.77), channel_id=1, source_target_pairs={{0,1},{1,0},{2,3},{3,2},{4,5},{5,4},{6,7},{7,6},{8,9},{9,8},{10,11... | collective-permute-start | bytes 2359304 | tf_op jit(solution)/shard_map/ppermute | solution.py:533
  111.5 7.4 %copy-start.7 = (bf16[8,96,384]{2,1,0:T(8,128)(2,1)S(1)}, bf16[8,96,384]{2,1,0:T(8,128)(2,1)}, u32[]{:S(2)}) copy-start(bf16[8,96,384]{2,1,0:T(8,128)(2,1)} %get-tuple-element.92) | copy-start | bytes 1769476
  115.6 11.0 %collective-permute-start.10 = (bf16[128,1536]{1,0:T(8,128)(2,1)}, bf16[128,1536]{1,0:T(8,128)(2,1)S(1)}, u32[]{:S(2)}, u32[]{:S(2)}) collective-permute-start(bf16[128,1536]{1,0:T(8,128)(2,1)} %get-tuple-element.78), channel_id=1, source_target_pairs={{0,2},{1,3},{2,4},{3,5},{4,6},{5,7},{6,0},{7,1},{8,10},{9,11},{10,... | collective-permute-start | bytes 1179656 | tf_op jit(solution)/shard_map/ppermute | solution.py:517
  115.6 11.0 %collective-permute-start.11 = (bf16[128,1536]{1,0:T(8,128)(2,1)}, bf16[128,1536]{1,0:T(8,128)(2,1)S(1)}, u32[]{:S(2)}, u32[]{:S(2)}) collective-permute-start(bf16[128,1536]{1,0:T(8,128)(2,1)} %get-tuple-element.82), channel_id=1, source_target_pairs={{0,6},{1,7},{2,0},{3,1},{4,2},{5,3},{6,4},{7,5},{8,14},{9,15},{10,... | collective-permute-start | bytes 1179656 | tf_op jit(solution)/shard_map/ppermute | solution.py:517
  118.8 28.6 %collective-permute-start.14 = (bf16[8,96,384]{2,1,0:T(8,128)(2,1)S(1)}, bf16[8,96,384]{2,1,0:T(8,128)(2,1)S(1)}, u32[]{:S(2)}, u32[]{:S(2)}) collective-permute-start(bf16[8,96,384]{2,1,0:T(8,128)(2,1)S(1)} %copy-done.7), channel_id=1, source_target_pairs={{0,8},{8,0},{16,24},{24,16},{32,40},{40,32},{48,56},{56,48},{64,72... | collective-permute-start | bytes 1769480 | tf_op jit(solution)/shard_map/ppermute | solution.py:537
  123.3 24.1 %collective-permute-start.15 = (bf16[8,96,384]{2,1,0:T(8,128)(2,1)}, bf16[8,96,384]{2,1,0:T(8,128)(2,1)}, u32[]{:S(2)}, u32[]{:S(2)}) collective-permute-start(bf16[8,96,384]{2,1,0:T(8,128)(2,1)} %get-tuple-element.94), channel_id=1, source_target_pairs={{0,8},{8,0},{16,24},{24,16},{32,40},{40,32},{48,56},{56,48},{64,72... | collective-permute-start | bytes 1769480 | tf_op jit(solution)/shard_map/ppermute | solution.py:537
  133.0 18.6 %collective-permute-start.12 = (bf16[256,1536]{1,0:T(8,128)(2,1)}, bf16[256,1536]{1,0:T(8,128)(2,1)S(1)}, u32[]{:S(2)}, u32[]{:S(2)}) collective-permute-start(bf16[256,1536]{1,0:T(8,128)(2,1)} %get-tuple-element.89), channel_id=1, source_target_pairs={{0,2},{1,3},{2,4},{3,5},{4,6},{5,7},{6,0},{7,1},{8,10},{9,11},{10,... | collective-permute-start | bytes 2359304 | tf_op jit(solution)/shard_map/ppermute | solution.py:517
  133.1 18.5 %collective-permute-start.13 = (bf16[256,1536]{1,0:T(8,128)(2,1)}, bf16[256,1536]{1,0:T(8,128)(2,1)S(1)}, u32[]{:S(2)}, u32[]{:S(2)}) collective-permute-start(bf16[256,1536]{1,0:T(8,128)(2,1)} %get-tuple-element.90), channel_id=1, source_target_pairs={{0,6},{1,7},{2,0},{3,1},{4,2},{5,3},{6,4},{7,5},{8,14},{9,15},{10,... | collective-permute-start | bytes 2359304 | tf_op jit(solution)/shard_map/ppermute | solution.py:517
  151.6 10.3 %copy-start.14 = (bf16[4,96,384]{2,1,0:T(8,128)(2,1)S(1)}, bf16[4,96,384]{2,1,0:T(8,128)(2,1)}, u32[]{:S(2)}) copy-start(bf16[4,96,384]{2,1,0:T(8,128)(2,1)} %get-tuple-element.106) | copy-start | bytes 884740
  152.7 45.9 %all-to-all-start.1 = ((bf16[8,3,128,384]{3,2,1,0:T(8,128)(2,1)}), bf16[8,3,128,384]{3,2,1,0:T(8,128)(2,1)S(1)}, u32[]{:S(2)}, u32[]{:S(2)}) async-start(bf16[8,3,128,384]{3,2,1,0:T(8,128)(2,1)} %attention_backward.1), calls=%async_computation.1 | async-start | bytes 4718592 | tf_op jit(solution)/shard_map/all_to_all | solution.py:581
  158.3 9.9 %collective-permute-start.16 = (bf16[4,96,384]{2,1,0:T(8,128)(2,1)}, bf16[4,96,384]{2,1,0:T(8,128)(2,1)S(1)}, u32[]{:S(2)}, u32[]{:S(2)}) collective-permute-start(bf16[4,96,384]{2,1,0:T(8,128)(2,1)} %get-tuple-element.104), channel_id=1, source_target_pairs={{0,64},{8,72},{16,80},{24,88},{32,96},{40,104},{48,112},{56,120},{... | collective-permute-start | bytes 884744 | tf_op jit(solution)/shard_map/ppermute | solution.py:517
  159.2 12.2 %collective-permute-start.17 = (bf16[4,96,384]{2,1,0:T(8,128)(2,1)}, bf16[4,96,384]{2,1,0:T(8,128)(2,1)S(1)}, u32[]{:S(2)}, u32[]{:S(2)}) collective-permute-start(bf16[4,96,384]{2,1,0:T(8,128)(2,1)} %get-tuple-element.105), channel_id=1, source_target_pairs={{0,128},{8,136},{16,144},{24,152},{32,160},{40,168},{48,176},{56,1... | collective-permute-start | bytes 884744 | tf_op jit(solution)/shard_map/ppermute | solution.py:517
  161.9 9.7 %collective-permute-start.18 = (bf16[4,96,384]{2,1,0:T(8,128)(2,1)S(1)}, bf16[4,96,384]{2,1,0:T(8,128)(2,1)S(1)}, u32[]{:S(2)}, u32[]{:S(2)}) collective-permute-start(bf16[4,96,384]{2,1,0:T(8,128)(2,1)S(1)} %copy-done.14), channel_id=1, source_target_pairs={{0,192},{8,200},{16,208},{24,216},{32,224},{40,232},{48,240},{56,2... | collective-permute-start | bytes 884744 | tf_op jit(solution)/shard_map/ppermute | solution.py:517
  168.3 4.6 %copy-start.15 = (bf16[4,96,384]{2,1,0:T(8,128)(2,1)}, bf16[4,96,384]{2,1,0:T(8,128)(2,1)S(1)}, u32[]{:S(2)}) copy-start(bf16[4,96,384]{2,1,0:T(8,128)(2,1)S(1)} %collective-permute-done.16.b_ref) | copy-start | bytes 884740
  172.9 20.5 %copy-start.10 = (bf16[128,1536]{1,0:T(8,128)(2,1)S(1)}, bf16[128,1536]{1,0:T(8,128)(2,1)}, u32[]{:S(2)}) copy-start(bf16[128,1536]{1,0:T(8,128)(2,1)} %get-tuple-element.108) | copy-start | bytes 1179652
  175.0 7.5 %collective-permute-start.20 = (bf16[96,384]{1,0:T(8,128)(2,1)}, bf16[96,384]{1,0:T(8,128)(2,1)S(1)}, u32[]{:S(2)}, u32[]{:S(2)}) collective-permute-start(bf16[96,384]{1,0:T(8,128)(2,1)} %get-tuple-element.116), channel_id=1, source_target_pairs={{0,16},{8,24},{16,32},{24,40},{32,48},{40,56},{48,0},{56,8},{64,80... | collective-permute-start | bytes 221192 | tf_op jit(solution)/shard_map/ppermute | solution.py:517
  175.7 12.0 %collective-permute-start.21 = (bf16[96,384]{1,0:T(8,128)(2,1)}, bf16[96,384]{1,0:T(8,128)(2,1)S(1)}, u32[]{:S(2)}, u32[]{:S(2)}) collective-permute-start(bf16[96,384]{1,0:T(8,128)(2,1)} %get-tuple-element.117), channel_id=1, source_target_pairs={{0,32},{8,40},{16,48},{24,56},{32,0},{40,8},{48,16},{56,24},{64,96... | collective-permute-start | bytes 221192 | tf_op jit(solution)/shard_map/ppermute | solution.py:517
  179.1 9.1 %collective-permute-start.22 = (bf16[96,384]{1,0:T(8,128)(2,1)}, bf16[96,384]{1,0:T(8,128)(2,1)S(1)}, u32[]{:S(2)}, u32[]{:S(2)}) collective-permute-start(bf16[96,384]{1,0:T(8,128)(2,1)} %get-tuple-element.118), channel_id=1, source_target_pairs={{0,48},{8,56},{16,0},{24,8},{32,16},{40,24},{48,32},{56,40},{64,11... | collective-permute-start | bytes 221192 | tf_op jit(solution)/shard_map/ppermute | solution.py:517
  189.1 9.4 %collective-permute-start.23 = (f32[96,384]{1,0:T(8,128)S(1)}, f32[96,384]{1,0:T(8,128)S(1)}, u32[]{:S(2)}, u32[]{:S(2)}) collective-permute-start(f32[96,384]{1,0:T(8,128)S(1)} %convert_add_fusion), channel_id=1, source_target_pairs={{0,0},{128,1},{2,2},{130,3},{4,4},{132,5},{6,6},{134,7},{8,8},{136... | collective-permute-start | bytes 442376 | tf_op jit(solution)/shard_map/ppermute | solution.py:590
  193.4 9.3 %collective-permute-start.19 = (bf16[128,1536]{1,0:T(8,128)(2,1)S(1)}, bf16[128,1536]{1,0:T(8,128)(2,1)S(1)}, u32[]{:S(2)}, u32[]{:S(2)}) collective-permute-start(bf16[128,1536]{1,0:T(8,128)(2,1)S(1)} %copy-done.10), channel_id=1, source_target_pairs={{0,1},{1,0},{2,3},{3,2},{4,5},{5,4},{6,7},{7,6},{8,9},{9,8},{10,11... | collective-permute-start | bytes 1179656 | tf_op jit(solution)/shard_map/ppermute | solution.py:533
  (13 other events, 14.3 us)
Sparse Core Ops, SparseCore 0:
  15.9 60.0 all-gather.1

commit v6 on v5

--- a/solution.py
+++ b/solution.py
@@ -10,10 +10,21 @@
 LONG = 640
 REST = 384
 LOG2E = 1.4426950408889634
-VMEM_LIMIT = 56 * 1024 * 1024
+VMEM_LIMIT = 32 * 1024 * 1024
 
 BF = jnp.bfloat16
 F32 = jnp.float32
+VMEM = pl.BlockSpec(memory_space=pltpu.VMEM)
+SMEM = pl.BlockSpec(memory_space=pltpu.SMEM)
+PARAMS = pltpu.CompilerParams(vmem_limit_bytes=VMEM_LIMIT)
+
+
+def shape(dims, dtype=BF):
+    return jax.ShapeDtypeStruct(dims, dtype)
+
+
+def whole(dims):
+    return pl.BlockSpec(dims, lambda: (0,) * len(dims))
 
 
 def cost(us):
@@ -83,56 +94,50 @@
 def fwd_kernel(frames_ref, qkv_ref, attn_ref, p1_ref, p2_ref, q_s, k_s, v_s):
     start, lead = clip_places(frames_ref)
     start = pl.multiple_of(start, FRAME)
-    q_s[...] = qkv_ref[:, 0].reshape(1024, HD)
-    k_s[...] = qkv_ref[:, 1].reshape(1024, HD)
-    v_s[...] = qkv_ref[:, 2].reshape(1024, HD)
+    places = rest_places(start)
     factor = LOG2E / (HD**0.5)
-    q1, q2 = load_split(q_s, start)
-    k1, k2 = load_split(k_s, start)
-    v1, v2 = load_split(v_s, start)
-    places = rest_places(start)
-    for long, (q, k, v, p_ref) in ((True, (q1, k1, v1, p1_ref)), (False, (q2, k2, v2, p2_ref))):
-        vt = v.astype(F32).T.astype(BF)
-        for at, size in spans(LONG if long else REST):
-            s = dot_nt(k, q[at : at + size])
-            if not long:
-                s = jnp.where(rest_mask(lead, at, size), s, F32(-1e30))
-            top = jnp.max(s, axis=0, keepdims=True)
-            e = jnp.exp2((s - top) * F32(factor))
-            total = jnp.sum(e, axis=0, keepdims=True)
-            p = (e * (1.0 / total)).astype(BF)
-            p_ref[0, :, at : at + size] = p
-            o = dot_nn(vt, p).T.astype(BF)
-            if long:
-                attn_ref[pl.ds(start + at, size), :] = o
-            else:
-                for t in range(size // FRAME):
-                    attn_ref[pl.ds(places[at // FRAME + t], FRAME), :] = o[
-                        t * FRAME : (t + 1) * FRAME
-                    ]
+
+    def head(h, carry):
+        lanes = pl.ds(pl.multiple_of(h * HD, HD), HD)
+        q_s[...] = qkv_ref[:, 0, :, lanes].reshape(1024, HD)
+        k_s[...] = qkv_ref[:, 1, :, lanes].reshape(1024, HD)
+        v_s[...] = qkv_ref[:, 2, :, lanes].reshape(1024, HD)
+        q1, q2 = load_split(q_s, start)
+        k1, k2 = load_split(k_s, start)
+        v1, v2 = load_split(v_s, start)
+        for long, (q, k, v, p_ref) in ((True, (q1, k1, v1, p1_ref)), (False, (q2, k2, v2, p2_ref))):
+            vt = v.astype(F32).T.astype(BF)
+            for at, size in spans(LONG if long else REST):
+                s = dot_nt(k, q[at : at + size])
+                if not long:
+                    s = jnp.where(rest_mask(lead, at, size), s, F32(-1e30))
+                top = jnp.max(s, axis=0, keepdims=True)
+                e = jnp.exp2((s - top) * F32(factor))
+                total = jnp.sum(e, axis=0, keepdims=True)
+                p = (e * (1.0 / total)).astype(BF)
+                p_ref[h, :, at : at + size] = p
+                o = dot_nn(vt, p).T.astype(BF)
+                if long:
+                    attn_ref[pl.ds(start + at, size), lanes] = o
+                else:
+                    for t in range(size // FRAME):
+                        attn_ref[pl.ds(places[at // FRAME + t], FRAME), lanes] = o[
+                            t * FRAME : (t + 1) * FRAME
+                        ]
+        return carry
+
+    lax.fori_loop(0, 3, head, 0)
 
 
 def attention_forward(frames, heads):
     return pl.pallas_call(
         fwd_kernel,
-        out_shape=(
-            jax.ShapeDtypeStruct((1024, 3 * HD), BF),
-            jax.ShapeDtypeStruct((3, LONG, LONG), BF),
-            jax.ShapeDtypeStruct((3, REST, REST), BF),
-        ),
-        grid_spec=pltpu.PrefetchScalarGridSpec(
-            num_scalar_prefetch=1,
-            grid=(3,),
-            in_specs=[pl.BlockSpec((8, 3, 128, HD), lambda h, f: (0, 0, 0, h))],
-            out_specs=(
-                pl.BlockSpec((1024, HD), lambda h, f: (0, h)),
-                pl.BlockSpec((1, LONG, LONG), lambda h, f: (h, 0, 0)),
-                pl.BlockSpec((1, REST, REST), lambda h, f: (h, 0, 0)),
-            ),
-            scratch_shapes=[pltpu.VMEM((1024, HD), BF)] * 3,
-        ),
-        compiler_params=pltpu.CompilerParams(vmem_limit_bytes=VMEM_LIMIT),
-        cost_estimate=cost(10),
+        out_shape=(shape((1024, 3 * HD)), shape((3, LONG, LONG)), shape((3, REST, REST))),
+        in_specs=[SMEM, VMEM],
+        out_specs=(whole((1024, 3 * HD)), VMEM, VMEM),
+        scratch_shapes=[pltpu.VMEM((1024, HD), BF)] * 3,
+        compiler_params=PARAMS,
+        cost_estimate=cost(0.1),
         name="attention_forward",
     )(frames, heads)
 
@@ -142,16 +147,8 @@
 ):
     start, lead = clip_places(frames_ref)
     start = pl.multiple_of(start, FRAME)
-    q_s[...] = qkv_ref[:, 0].reshape(1024, HD)
-    k_s[...] = qkv_ref[:, 1].reshape(1024, HD)
-    v_s[...] = qkv_ref[:, 2].reshape(1024, HD)
-    d_s[...] = (own_ref[...] + other_ref[...].astype(F32)).astype(BF)
+    places = rest_places(start)
     scale = 1.0 / (HD**0.5)
-    q1, q2 = load_split(q_s, start)
-    k1, k2 = load_split(k_s, start)
-    v1, v2 = load_split(v_s, start)
-    d1, d2 = load_split(d_s, start)
-    places = rest_places(start)
 
     def put(which, long, value):
         if long:
@@ -160,51 +157,54 @@
             for t in range(REST // FRAME):
                 g_s[which, pl.ds(places[t], FRAME), :] = value[t * FRAME : (t + 1) * FRAME]
 
-    for long, (q, k, v, d, p_ref, ds_ref) in (
-        (True, (q1, k1, v1, d1, p1_ref, ds1)),
-        (False, (q2, k2, v2, d2, p2_ref, ds2)),
-    ):
-        kt = k.astype(F32).T.astype(BF)
-        parts = []
-        for at, size in spans(LONG if long else REST):
-            dp = dot_nt(v, d[at : at + size]).astype(BF).astype(F32)
-            p = p_ref[0, :, at : at + size].astype(F32)
-            pd = p * dp
-            delta = jnp.sum(pd, axis=0, keepdims=True)
-            ds = ((pd - p * delta) * F32(scale)).astype(BF)
-            ds_ref[:, at : at + size] = ds
-            parts.append(dot_nn(kt, ds).T.astype(BF))
-        put(0, long, jnp.concatenate(parts, axis=0))
-        put(1, long, dot_nn(ds_ref[...], q).astype(BF))
-        put(2, long, dot_nn(p_ref[0], d).astype(BF))
-    for which in range(3):
-        out_ref[:, which] = g_s[which].reshape(8, 128, HD)
+    def head(h, carry):
+        lanes = pl.ds(pl.multiple_of(h * HD, HD), HD)
+        q_s[...] = qkv_ref[:, 0, :, lanes].reshape(1024, HD)
+        k_s[...] = qkv_ref[:, 1, :, lanes].reshape(1024, HD)
+        v_s[...] = qkv_ref[:, 2, :, lanes].reshape(1024, HD)
+        d_s[...] = (own_ref[:, lanes] + other_ref[:, lanes].astype(F32)).astype(BF)
+        q1, q2 = load_split(q_s, start)
+        k1, k2 = load_split(k_s, start)
+        v1, v2 = load_split(v_s, start)
+        d1, d2 = load_split(d_s, start)
+        for long, (q, k, v, d, p_ref, ds_ref) in (
+            (True, (q1, k1, v1, d1, p1_ref, ds1)),
+            (False, (q2, k2, v2, d2, p2_ref, ds2)),
+        ):
+            kt = k.astype(F32).T.astype(BF)
+            parts = []
+            for at, size in spans(LONG if long else REST):
+                dp = dot_nt(v, d[at : at + size]).astype(BF).astype(F32)
+                p = p_ref[h, :, at : at + size].astype(F32)
+                pd = p * dp
+                delta = jnp.sum(pd, axis=0, keepdims=True)
+                ds = ((pd - p * delta) * F32(scale)).astype(BF)
+                ds_ref[:, at : at + size] = ds
+                parts.append(dot_nn(kt, ds).T.astype(BF))
+            put(0, long, jnp.concatenate(parts, axis=0))
+            put(1, long, dot_nn(ds_ref[...], q).astype(BF))
+            put(2, long, dot_nn(p_ref[h], d).astype(BF))
+        for which in range(3):
+            out_ref[:, which, :, lanes] = g_s[which].reshape(8, 128, HD)
+        return carry
+
+    lax.fori_loop(0, 3, head, 0)
 
 
 def attention_backward(frames, heads, own, other, p1, p2):
     return pl.pallas_call(
         bwd_kernel,
-        out_shape=jax.ShapeDtypeStruct((8, 3, 128, 3 * HD), BF),
-        grid_spec=pltpu.PrefetchScalarGridSpec(
-            num_scalar_prefetch=1,
-            grid=(3,),
-            in_specs=[
-                pl.BlockSpec((8, 3, 128, HD), lambda h, f: (0, 0, 0, h)),
-                pl.BlockSpec((1024, HD), lambda h, f: (0, h)),
-                pl.BlockSpec((1024, HD), lambda h, f: (0, h)),
-                pl.BlockSpec((1, LONG, LONG), lambda h, f: (h, 0, 0)),
-                pl.BlockSpec((1, REST, REST), lambda h, f: (h, 0, 0)),
-            ],
-            out_specs=pl.BlockSpec((8, 3, 128, HD), lambda h, f: (0, 0, 0, h)),
-            scratch_shapes=[pltpu.VMEM((1024, HD), BF)] * 4
-            + [
-                pltpu.VMEM((LONG, LONG), BF),
-                pltpu.VMEM((REST, REST), BF),
-                pltpu.VMEM((3, 1024, HD), BF),
-            ],
-        ),
-        compiler_params=pltpu.CompilerParams(vmem_limit_bytes=VMEM_LIMIT),
-        cost_estimate=cost(11),
+        out_shape=shape((8, 3, 128, 3 * HD)),
+        in_specs=[SMEM, VMEM, VMEM, VMEM, VMEM, VMEM],
+        out_specs=whole((8, 3, 128, 3 * HD)),
+        scratch_shapes=[pltpu.VMEM((1024, HD), BF)] * 4
+        + [
+            pltpu.VMEM((LONG, LONG), BF),
+            pltpu.VMEM((REST, REST), BF),
+            pltpu.VMEM((3, 1024, HD), BF),
+        ],
+        compiler_params=PARAMS,
+        cost_estimate=cost(10),
         name="attention_backward",
     )(frames, heads, own, other, p1, p2)
 
@@ -227,17 +227,17 @@
 
 
 def unpack_kernel(in_ref, out_ref):
-    for j in range(4):
+    for j in range(8):
         out_ref[:, :, j * 384 : (j + 1) * 384] = in_ref[j]
 
 
 def unpack_heads(grads):
     return pl.pallas_call(
         unpack_kernel,
-        out_shape=jax.ShapeDtypeStruct((3, 128, 3072), BF),
-        grid=(2,),
-        in_specs=[pl.BlockSpec((4, 3, 128, 384), lambda j: (j, 0, 0, 0))],
-        out_specs=pl.BlockSpec((3, 128, 1536), lambda j: (0, 0, j)),
+        out_shape=shape((3, 128, 3072)),
+        in_specs=[VMEM],
+        out_specs=whole((3, 128, 3072)),
+        compiler_params=PARAMS,
         cost_estimate=cost(3),
         name="unpack_heads",
     )(grads)
@@ -289,14 +289,13 @@
     def half(rows, flip):
         return pl.BlockSpec((rows, 1536), lambda n, f, t, s: (0, s[0] % 2 ^ flip))
 
-    whole = pl.BlockSpec((128, 1536), lambda n, *_: (0, 0))
     return pl.pallas_call(
         output_kernel,
         out_shape=jax.ShapeDtypeStruct((128, 3072), BF),
         grid_spec=pltpu.PrefetchScalarGridSpec(
             num_scalar_prefetch=3,
             grid=(1,),
-            in_specs=[half(64, 0), half(64, 1), half(128, 0), half(128, 1), whole, whole],
+            in_specs=[half(64, 0), half(64, 1), half(128, 0), half(128, 1), VMEM, VMEM],
             out_specs=pl.BlockSpec((128, 3072), lambda n, *_: (0, 0)),
         ),
         cost_estimate=cost(3),
@@ -318,7 +317,6 @@
 
 
 def dattn_parts(seq, blocks, weights):
-    vmem = pl.BlockSpec(memory_space=pltpu.VMEM)
     return pl.pallas_call(
         dattn_kernel,
         out_shape=(
@@ -326,126 +324,94 @@
             jax.ShapeDtypeStruct((1024, 384), BF),
             jax.ShapeDtypeStruct((1024, 384), F32),
         ),
-        in_specs=[pl.BlockSpec(memory_space=pltpu.SMEM)] + [vmem] * 9,
-        out_specs=(
-            pl.BlockSpec((1024, 1536), lambda: (0, 0)),
-            pl.BlockSpec((1024, 384), lambda: (0, 0)),
-            pl.BlockSpec((1024, 384), lambda: (0, 0)),
-        ),
+        in_specs=[SMEM] + [VMEM] * 9,
+        out_specs=(VMEM, whole((1024, 384)), VMEM),
         compiler_params=pltpu.CompilerParams(vmem_limit_bytes=VMEM_LIMIT),
         cost_estimate=cost(7),
         name="dattn_parts",
     )(seq, *blocks, weights)
 
 
-def rows_spec(k):
-    return pl.BlockSpec((256, 384), lambda n, s: ((s[0] // 2 + k) % 4, 0))
-
-
-W_SPEC = pl.BlockSpec((2, 512, 384), lambda n, s: (0, n, 0))
-TWO_SPEC = pl.BlockSpec((256, 512), lambda n, s: (0, n))
-ONE_SPEC = pl.BlockSpec((128, 512), lambda n, s: (0, n))
-ONE_BF = jax.ShapeDtypeStruct((128, 1536), BF)
-TWO_BF = jax.ShapeDtypeStruct((256, 1536), BF)
-
-
-def project(own_ref, other_ref, w_ref):
-    return dot_nt(own_ref[...], w_ref[0]) + dot_nt(other_ref[...], w_ref[1])
+def project(seq_ref, k, own_ref, other_ref, w_ref):
+    rows = pl.ds(pl.multiple_of((seq_ref[0] // 2 + k) % 4 * 256, 256), 256)
+    return dot_nt(own_ref[rows, :], w_ref[0]) + dot_nt(other_ref[rows, :], w_ref[1])
 
 
 def far_kernel(seq_ref, a_ref, b_ref, w_ref, up_ref, down_ref):
-    part = project(a_ref, b_ref, w_ref).astype(BF)
+    part = project(seq_ref, 2, a_ref, b_ref, w_ref).astype(BF)
     up_ref[...] = part[:128]
     down_ref[...] = part[128:]
 
 
-def near_kernel(seq_ref, a1_ref, b1_ref, a3_ref, b3_ref, w_ref, up_ref, down_ref, t1_ref, t3_ref):
-    p1 = project(a1_ref, b1_ref, w_ref)
+def near_kernel(seq_ref, a_ref, b_ref, w_ref, up_ref, down_ref, t1_ref, t3_ref):
+    p1 = project(seq_ref, 1, a_ref, b_ref, w_ref)
     t1_ref[:128] = (p1[:128] + up_ref[...].astype(F32)).astype(BF)
     t1_ref[128:] = p1[128:].astype(BF)
-    p3 = project(a3_ref, b3_ref, w_ref)
+    p3 = project(seq_ref, 3, a_ref, b_ref, w_ref)
     t3_ref[:128] = p3[:128].astype(BF)
     t3_ref[128:] = (p3[128:] + down_ref[...].astype(F32)).astype(BF)
 
 
 def home_kernel(seq_ref, a_ref, b_ref, w_ref, c1_ref, c3_ref, keep_ref, send_ref):
-    part = project(a_ref, b_ref, w_ref)
+    part = project(seq_ref, 0, a_ref, b_ref, w_ref)
     part = part + c1_ref[...].astype(F32) + c3_ref[...].astype(F32)
     first = seq_ref[0] % 2 == 0
     keep_ref[...] = jnp.where(first, part[:128], part[128:])
     send_ref[...] = jnp.where(first, part[128:], part[:128]).astype(BF)
 
 
-def project_call(kernel, name, in_specs, out_shape, out_specs):
+def project_call(kernel, name, inputs, out_shape, out_specs):
     return pl.pallas_call(
         kernel,
         out_shape=out_shape,
-        grid_spec=pltpu.PrefetchScalarGridSpec(
-            num_scalar_prefetch=1, grid=(3,), in_specs=in_specs, out_specs=out_specs
-        ),
-        compiler_params=pltpu.CompilerParams(vmem_limit_bytes=VMEM_LIMIT),
-        cost_estimate=cost(4),
+        in_specs=[SMEM] + [VMEM] * inputs,
+        out_specs=out_specs,
+        compiler_params=PARAMS,
+        cost_estimate=cost(3),
         name=name,
     )
 
 
 def project_far(seq, own, other, weights):
-    return project_call(
-        far_kernel,
-        "project_far",
-        [rows_spec(2), rows_spec(2), W_SPEC],
-        (ONE_BF, ONE_BF),
-        (ONE_SPEC, ONE_SPEC),
-    )(seq, own, other, weights)
+    one = whole((128, 1536))
+    call = project_call(far_kernel, "project_far", 3, (shape((128, 1536)),) * 2, (one, one))
+    return call(seq, own, other, weights)
 
 
 def project_near(seq, own, other, weights, up, down):
-    return project_call(
-        near_kernel,
-        "project_near",
-        [rows_spec(1), rows_spec(1), rows_spec(3), rows_spec(3), W_SPEC, ONE_SPEC, ONE_SPEC],
-        (TWO_BF, TWO_BF),
-        (TWO_SPEC, TWO_SPEC),
-    )(seq, own, other, own, other, weights, up, down)
+    two = whole((256, 1536))
+    call = project_call(near_kernel, "project_near", 5, (shape((256, 1536)),) * 2, (two, two))
+    return call(seq, own, other, weights, up, down)
 
 
 def project_home(seq, own, other, weights, c1, c3):
-    return project_call(
+    call = project_call(
         home_kernel,
         "project_home",
-        [rows_spec(0), rows_spec(0), W_SPEC, TWO_SPEC, TWO_SPEC],
-        (jax.ShapeDtypeStruct((128, 1536), F32), ONE_BF),
-        (ONE_SPEC, ONE_SPEC),
-    )(seq, own, other, weights, c1, c3)
+        5,
+        (shape((128, 1536), F32), shape((128, 1536))),
+        (VMEM, whole((128, 1536))),
+    )
+    return call(seq, own, other, weights, c1, c3)
 
 
 def dweight_kernel(dp_ref, d_ref, a_ref, keep_ref, send_ref):
     even = dp_ref[0] % 2 == 0
-    g = dot_tn(d_ref[...], a_ref[...]).astype(BF)
-    for i in range(4):
-        p0, p1 = g[i * 192 : i * 192 + 96], g[i * 192 + 96 : i * 192 + 192]
-        keep_ref[i] = jnp.where(even, p0, p1)
-        send_ref[i] = jnp.where(even, p1, p0)
+    for n in range(2):
+        g = dot_tn(d_ref[:, n * 768 : (n + 1) * 768], a_ref[...]).astype(BF)
+        for i in range(4):
+            p0, p1 = g[i * 192 : i * 192 + 96], g[i * 192 + 96 : i * 192 + 192]
+            keep_ref[n * 4 + i] = jnp.where(even, p0, p1)
+            send_ref[n * 4 + i] = jnp.where(even, p1, p0)
 
 
 def dweight_part(dp, dproj, attn):
-    pieces = jax.ShapeDtypeStruct((8, 96, 384), BF)
     return pl.pallas_call(
         dweight_kernel,
-        out_shape=(pieces, pieces),
-        grid_spec=pltpu.PrefetchScalarGridSpec(
-            num_scalar_prefetch=1,
-            grid=(2,),
-            in_specs=[
-                pl.BlockSpec((1024, 768), lambda n, c: (0, n)),
-                pl.BlockSpec((1024, 384), lambda n, c: (0, 0)),
-            ],
-            out_specs=(
-                pl.BlockSpec((4, 96, 384), lambda n, c: (n, 0, 0)),
-                pl.BlockSpec((4, 96, 384), lambda n, c: (n, 0, 0)),
-            ),
-        ),
-        compiler_params=pltpu.CompilerParams(vmem_limit_bytes=VMEM_LIMIT),
+        out_shape=(shape((8, 96, 384)), shape((8, 96, 384))),
+        in_specs=[SMEM, VMEM, VMEM],
+        out_specs=(VMEM, whole((8, 96, 384))),
+        compiler_params=PARAMS,
         cost_estimate=cost(4),
         name="dweight_part",
     )(dp, dproj, attn)
@@ -468,8 +434,7 @@
     return pl.pallas_call(
         pair_kernel,
         out_shape=(jax.ShapeDtypeStruct((4, 96, 384), BF),) * 4,
-        in_specs=[pl.BlockSpec(memory_space=pltpu.SMEM)]
-        + [pl.BlockSpec((2, 4, 96, 384), lambda: (0, 0, 0, 0))] * 4,
+        in_specs=[SMEM] + [VMEM] * 4,
         out_specs=(pl.BlockSpec((4, 96, 384), lambda: (0, 0, 0)),) * 4,
         cost_estimate=cost(3),
         name="pair_sum",
@@ -488,8 +453,7 @@
     return pl.pallas_call(
         ring_kernel,
         out_shape=(jax.ShapeDtypeStruct((96, 384), BF),) * 4,
-        in_specs=[pl.BlockSpec(memory_space=pltpu.SMEM)]
-        + [pl.BlockSpec((4, 96, 384), lambda: (0, 0, 0))] * 4,
+        in_specs=[SMEM] + [VMEM] * 4,
         out_specs=(pl.BlockSpec((96, 384), lambda: (0, 0)),) * 4,
         cost_estimate=cost(2),
         name="ring_sum",
@@ -555,8 +519,7 @@
 
     b1 = [b1_keep, along_x(got, -1)]
     b3 = [b3_keep, along_x(got, 1)]
-    late, weights = lax.optimization_barrier((b1[1], weights))
-    b2 = [along_x(b3[0], 1), along_x(late, -1)]
+    b2 = [along_x(b3[0], 1), along_x(b1[1], -1)]
 
     attn, p1, p2 = attention_forward(frames, heads)
     attn_other = swap_z(attn)

time: 215 us -> 205 us (0.953)
  Pallas kernels: 68 us -> 55.4 us
  waiting for transfers between devices: 70.1 us -> 64 us
  starting transfers between devices: 50.8 us -> 56.6 us
  local copies, waits for them, and re-layouts: 10.5 us -> 13.5 us
    pallas_call x8, Pallas kernels: 46.3 us -> 36 us  [the longest x1 10.1 us: attention_backward(): pl.pallas_call(bwd_kernel, out_shape=shape((8, 3, 128, 3 * HD)), in_specs...]
    all_gather x1, waiting for transfers between devices: 6.31 us -> 0.02 us  [body(): lax.all_gather(piece, 'dp', axis=0, tiled=True).reshape(2, 1536, 384)]
    ppermute x16, starting transfers between devices: 27.7 us -> 33.4 us  [along(): return lax.ppermute(x, axis, moves)]
    unnamed x37 -> x43, local copies, waits for them, and re-layouts: 10.5 us -> 13.5 us
    pallas_call x1, Pallas kernels: 7.39 us -> 5.18 us  [dattn_parts(): pl.pallas_call(dattn_kernel, out_shape=(jax.ShapeDtypeStruct((1024, 1536)...]
  transfers between devices with their start and end apart: 27 -> 27, of which waited for: 15 -> 11; matrix products, arithmetic and copies ran while one was open for 0% -> 0% of each run, Pallas kernels for 30% -> 25%
where the time goes in v6:
time: 205 us
  waiting for transfers between devices  64 us (31%)
  starting transfers between devices  56.6 us (28%)
  Pallas kernels  55.4 us (27%)
  between operations  14.2 us (7%)
  local copies, waits for them, and re-layouts  13.5 us (7%)
    ppermute x16, waiting for transfers between devices, along(): return lax.ppermute(x, axis, moves)  43.7 us
    ppermute x16, starting transfers between devices, along(): return lax.ppermute(x, axis, moves)  33.4 us
    ppermute x4, waiting for transfers between devices, swap_z(): lax.ppermute(x, 'seq', [(i, i ^ 1) for i in range(lax.axis_size('seq'))])  14.3 us
    unnamed x43, local copies, waits for them, and re-layouts  13.5 us
    pallas_call x1, Pallas kernels, attention_backward(): pl.pallas_call(bwd_kernel, out_shape=shape((8, 3, 128, 3 * HD)), in_specs...  10.1 us
    pallas_call x1, Pallas kernels, attention_forward(): pl.pallas_call(fwd_kernel, out_shape=(shape((1024, 3 * HD)), shape((3, LO...  8.65 us
    pallas_call x2, Pallas kernels, dweight_part(): pl.pallas_call(dweight_kernel, out_shape=(shape((8, 96, 384)), shape((8,...  6.05 us
    all_to_all x1, starting transfers between devices, body(): lax.all_to_all(grads, 'seq', split_axis=0, concat_axis=0, tiled=True)  5.82 us
  transfers between devices with their start and end apart: 27, of which 11 were waited for; matrix products, arithmetic and copies ran while one was open for 0% of the time, Pallas kernels for 25%

profile of v6, /device:TPU:32, one launch (start us, length us, event | category | flops | bytes accessed | tf_op | source)
XLA Modules:
  0.0 204.7 jit_solution(14213402612440255330)
XLA Ops:
  7.2 4.6 %collective-permute-start = (bf16[96,384]{1,0:T(8,128)(2,1)}, bf16[96,384]{1,0:T(8,128)(2,1)S(1)}, u32[]{:S(2)}, u32[]{:S(2)}) collective-permute-start(bf16[96,384]{1,0:T(8,128)(2,1)} %bitcast.21), channel_id=1, source_target_pairs={{0,0},{1,128},{2,2},{3,130},{4,4},{5,132},{6,6},{7,134},{8,8},{9,1... | collective-permute-start | bytes 221192 | tf_op jit(solution)/shard_map/ppermute | solution.py:510
  11.9 2.8 %pack_heads.1 = bf16[8,3,128,384]{3,2,1,0:T(8,128)(2,1)} custom-call(bf16[3,128,3072]{2,1,0:T(8,128)(2,1)} %bitcast.18), custom_call_target="tpu_custom_call" | custom-call | flops 3000000000 | bytes 9000000 | tf_op jit(solution)/shard_map/pack_heads/pallas_call | solution.py:218
  15.8 3.0 %gated_cotangent.1 = (bf16[128,1536]{1,0:T(8,128)(2,1)}, bf16[128,1536]{1,0:T(8,128)(2,1)}) custom-call(s32[1,3]{1,0:T(1,128)} %frames_ref.7, s32[1,3]{1,0:T(1,128)} %steps_ref.3, s32[1]{0:T(128)} %bitcast.seq_ref, f32[64,3072]{1,0:T(8,128)} %t1_ref.3, f32[64,3072]{1,0:T(8,128)} %t1_ref.3, bf16[128,3072]{1,0:T(8,128)(2,1)} %c1_ref, bf16[128,3072]{1,0:T(8,128)(2,1)} %c1_ref), custom_call_target="tpu_custom_call" | custom-call | flops 3000000000 | bytes 9000000 | tf_op jit(solution)/shard_map/gated_cotangent/pallas_call | solution.py:259
  20.4 1.7 collective-permute-start.2
  22.1 7.0 %collective-permute-done.1.refs_1_ = bf16[128,1536]{1,0:T(8,128)(2,1)} collective-permute-done((bf16[128,1536]{1,0:T(8,128)(2,1)}, bf16[128,1536]{1,0:T(8,128)(2,1)}, u32[]{:S(2)}, u32[]{:S(2)}) %collective-permute-start.1) | collective-permute-done | bytes 393248 | tf_op jit(solution)/shard_map/ppermute | solution.py:497
  31.2 5.8 %all-to-all-start = ((bf16[8,3,128,384]{3,2,1,0:T(8,128)(2,1)}), bf16[8,3,128,384]{3,2,1,0:T(8,128)(2,1)S(1)}, u32[]{:S(2)}, u32[]{:S(2)}) async-start(bf16[8,3,128,384]{3,2,1,0:T(8,128)(2,1)} %pack_heads.1), calls=%async_computation | async-start | bytes 4718592 | tf_op jit(solution)/shard_map/all_to_all | solution.py:518
  37.0 2.7 %collective-permute-start.5 = (bf16[128,1536]{1,0:T(8,128)(2,1)}, bf16[128,1536]{1,0:T(8,128)(2,1)}, u32[]{:S(2)}, u32[]{:S(2)}) collective-permute-start(bf16[128,1536]{1,0:T(8,128)(2,1)} %collective-permute-done.1.refs_1_), channel_id=1, source_target_pairs={{0,6},{1,7},{2,0},{3,1},{4,2},{5,3},{6,4},{7,5},{8,14},{9,15},{10,... | collective-permute-start | bytes 1179656 | tf_op jit(solution)/shard_map/ppermute | solution.py:481
  40.5 29.9 %collective-permute-done.5.refs_3_ = bf16[128,1536]{1,0:T(8,128)(2,1)} collective-permute-done((bf16[128,1536]{1,0:T(8,128)(2,1)}, bf16[128,1536]{1,0:T(8,128)(2,1)}, u32[]{:S(2)}, u32[]{:S(2)}) %collective-permute-start.5) | collective-permute-done | bytes 393248 | tf_op jit(solution)/shard_map/ppermute | solution.py:481
  71.9 8.7 %attention_forward.1 = (bf16[1024,384]{1,0:T(8,128)(2,1)}, bf16[3,640,640]{2,1,0:T(8,128)(2,1)S(1)}, bf16[3,384,384]{2,1,0:T(8,128)(2,1)S(1)}) custom-call(s32[1,3]{1,0:T(1,128)S(1)} %copy-done, bf16[8,3,128,384]{3,2,1,0:T(8,128)(2,1)S(1)} %all-to-all-done.qkv_ref), custom_call_target="tpu_custom_call" | custom-call | flops 100000000 | bytes 300000 | tf_op jit(solution)/shard_map/attention_forward/pallas_call | solution.py:133
  86.9 5.2 %dattn_parts.1 = (bf16[1024,1536]{1,0:T(8,128)(2,1)S(1)}, bf16[1024,384]{1,0:T(8,128)(2,1)S(1)}, f32[1024,384]{1,0:T(8,128)S(1)}) custom-call(s32[1]{0:T(128)} %bitcast.seq_ref, bf16[128,1536]{1,0:T(8,128)(2,1)S(1)} %copy-done.6, bf16[128,1536]{1,0:T(8,128)(2,1)} %collective-permute-done.1.refs_1_, bf16[128,1536]{1,0:T(8,128)(2,1)S(1)} %copy-done.8, ...), custom_call_target="tpu_custom_call" | custom-call | flops 7000000000 | bytes 21000000 | tf_op jit(solution)/shard_map/dattn_parts/pallas_call | solution.py:320
  93.2 3.1 %dweight_part.2 = (bf16[8,96,384]{2,1,0:T(8,128)(2,1)S(1)}, bf16[8,96,384]{2,1,0:T(8,128)(2,1)S(1)}) custom-call(s32[1]{0:T(128)} %bitcast.3.dp_ref, bf16[1024,1536]{1,0:T(8,128)(2,1)S(1)} %get-tuple-element.75.d_ref, bf16[1024,384]{1,0:T(8,128)(2,1)} %get-tuple-element.64.a_ref), custom_call_target="tpu_custom_call" | custom-call | flops 4000000000 | bytes 12000000 | tf_op jit(solution)/shard_map/dweight_part/pallas_call | solution.py:409
  96.3 6.5 %collective-permute-done.4.b_ref.a_ref = bf16[1024,384]{1,0:T(8,128)(2,1)} collective-permute-done((bf16[1024,384]{1,0:T(8,128)(2,1)}, bf16[1024,384]{1,0:T(8,128)(2,1)}, u32[]{:S(2)}, u32[]{:S(2)}) %collective-permute-start.4) | collective-permute-done | bytes 786464 | tf_op jit(solution)/shard_map/ppermute | solution.py:497
  102.8 2.4 %project_far.1 = (bf16[128,1536]{1,0:T(8,128)(2,1)S(1)}, bf16[128,1536]{1,0:T(8,128)(2,1)S(1)}) custom-call(s32[1]{0:T(128)} %bitcast.seq_ref, bf16[1024,384]{1,0:T(8,128)(2,1)} %get-tuple-element.64.a_ref, bf16[1024,384]{1,0:T(8,128)(2,1)} %collective-permute-done.4.b_ref.a_ref, bf16[2,1536,384]{2,1,0:T(8,128)(2,1)S(1)} %bitcast.12), custom_call_target="tpu_custom_call" | custom-call | flops 3000000000 | bytes 9000000 | tf_op jit(solution)/shard_map/project_far/pallas_call | solution.py:378
  105.8 2.7 %collective-permute-start.11 = (bf16[128,1536]{1,0:T(8,128)(2,1)S(1)}, bf16[128,1536]{1,0:T(8,128)(2,1)S(1)}, u32[]{:S(2)}, u32[]{:S(2)}) collective-permute-start(bf16[128,1536]{1,0:T(8,128)(2,1)S(1)} %get-tuple-element.78), channel_id=1, source_target_pairs={{0,6},{1,7},{2,0},{3,1},{4,2},{5,3},{6,4},{7,5},{8,14},{9,15},{10,... | collective-permute-start | bytes 1179656 | tf_op jit(solution)/shard_map/ppermute | solution.py:481
  108.5 3.0 %dweight_part.3 = (bf16[8,96,384]{2,1,0:T(8,128)(2,1)S(1)}, bf16[8,96,384]{2,1,0:T(8,128)(2,1)S(1)}) custom-call(s32[1]{0:T(128)} %bitcast.3.dp_ref, bf16[1024,1536]{1,0:T(8,128)(2,1)S(1)} %get-tuple-element.75.d_ref, bf16[1024,384]{1,0:T(8,128)(2,1)} %collective-permute-done.4.b_ref.a_ref), custom_call_target="tpu_custom_call" | custom-call | flops 4000000000 | bytes 12000000 | tf_op jit(solution)/shard_map/dweight_part/pallas_call | solution.py:409
  112.1 2.2 %collective-permute-done.10.up_ref = bf16[128,1536]{1,0:T(8,128)(2,1)S(1)} collective-permute-done((bf16[128,1536]{1,0:T(8,128)(2,1)S(1)}, bf16[128,1536]{1,0:T(8,128)(2,1)S(1)}, u32[]{:S(2)}, u32[]{:S(2)}) %collective-permute-start.10) | collective-permute-done | bytes 393248 | tf_op jit(solution)/shard_map/ppermute | solution.py:481
  114.3 4.3 %project_near.1 = (bf16[256,1536]{1,0:T(8,128)(2,1)}, bf16[256,1536]{1,0:T(8,128)(2,1)}) custom-call(s32[1]{0:T(128)} %bitcast.seq_ref, bf16[1024,384]{1,0:T(8,128)(2,1)} %get-tuple-element.64.a_ref, bf16[1024,384]{1,0:T(8,128)(2,1)} %collective-permute-done.4.b_ref.a_ref, bf16[2,1536,384]{2,1,0:T(8,128)(2,1)S(1)} %bitcast.13, ...), custom_call_target="tpu_custom_call" | custom-call | flops 3000000000 | bytes 9000000 | tf_op jit(solution)/shard_map/project_near/pallas_call | solution.py:384
  119.2 2.6 %collective-permute-start.13 = (bf16[256,1536]{1,0:T(8,128)(2,1)}, bf16[256,1536]{1,0:T(8,128)(2,1)}, u32[]{:S(2)}, u32[]{:S(2)}) collective-permute-start(bf16[256,1536]{1,0:T(8,128)(2,1)} %get-tuple-element.86), channel_id=1, source_target_pairs={{0,6},{1,7},{2,0},{3,1},{4,2},{5,3},{6,4},{7,5},{8,14},{9,15},{10,... | collective-permute-start | bytes 2359304 | tf_op jit(solution)/shard_map/ppermute | solution.py:481
  121.8 10.1 %attention_backward.1 = bf16[8,3,128,384]{3,2,1,0:T(8,128)(2,1)} custom-call(s32[1,3]{1,0:T(1,128)S(1)} %copy-done, bf16[8,3,128,384]{3,2,1,0:T(8,128)(2,1)S(1)} %all-to-all-done.qkv_ref, f32[1024,384]{1,0:T(8,128)S(1)} %get-tuple-element.81.own_ref, bf16[1024,384]{1,0:T(8,128)(2,1)S(1)} %collective-permute-done.9.other_ref, ...), custom_call_target="tpu_custom_call" | custom-call | flops 10000000000 | bytes 30000000 | tf_op jit(solution)/shard_map/attention_backward/pallas_call | solution.py:195
  133.5 3.0 %pair_sum.1 = (bf16[4,96,384]{2,1,0:T(8,128)(2,1)}, bf16[4,96,384]{2,1,0:T(8,128)(2,1)}, bf16[4,96,384]{2,1,0:T(8,128)(2,1)}, bf16[4,96,384]{2,1,0:T(8,128)(2,1)}) custom-call(s32[1]{0:T(128)} %bitcast.3.dp_ref, bf16[2,4,96,384]{3,2,1,0:T(8,128)(2,1)} %bitcast.15, bf16[2,4,96,384]{3,2,1,0:T(8,128)(2,1)} %bitcast.19, bf16[2,4,96,384]{3,2,1,0:T(8,128)(2,1)} %bitcast.16, ...), custom_call_target="tpu_custom_call" | custom-call | flops 3000000000 | bytes 9000000 | tf_op jit(solution)/shard_map/pair_sum/pallas_call | solution.py:434
  137.4 5.8 %all-to-all-start.1 = ((bf16[8,3,128,384]{3,2,1,0:T(8,128)(2,1)}), bf16[8,3,128,384]{3,2,1,0:T(8,128)(2,1)S(1)}, u32[]{:S(2)}, u32[]{:S(2)}) async-start(bf16[8,3,128,384]{3,2,1,0:T(8,128)(2,1)} %attention_backward.1), calls=%async_computation.1 | async-start | bytes 4718592 | tf_op jit(solution)/shard_map/all_to_all | solution.py:544
  144.1 3.3 %collective-permute-start.17 = (bf16[4,96,384]{2,1,0:T(8,128)(2,1)S(1)}, bf16[4,96,384]{2,1,0:T(8,128)(2,1)S(1)}, u32[]{:S(2)}, u32[]{:S(2)}) collective-permute-start(bf16[4,96,384]{2,1,0:T(8,128)(2,1)S(1)} %copy-done.17), channel_id=1, source_target_pairs={{0,128},{8,136},{16,144},{24,152},{32,160},{40,168},{48,176},{56,1... | collective-permute-start | bytes 884744 | tf_op jit(solution)/shard_map/ppermute | solution.py:481
  150.4 2.9 %project_home.1 = (f32[128,1536]{1,0:T(8,128)S(1)}, bf16[128,1536]{1,0:T(8,128)(2,1)S(1)}) custom-call(s32[1]{0:T(128)} %bitcast.seq_ref, bf16[1024,384]{1,0:T(8,128)(2,1)} %get-tuple-element.64.a_ref, bf16[1024,384]{1,0:T(8,128)(2,1)} %collective-permute-done.4.b_ref.a_ref, bf16[2,1536,384]{2,1,0:T(8,128)(2,1)S(1)} %bitcast.14, ...), custom_call_target="tpu_custom_call" | custom-call | flops 3000000000 | bytes 9000000 | tf_op jit(solution)/shard_map/project_home/pallas_call | solution.py:395
  154.2 2.6 %collective-permute-done.17.c_ref = bf16[4,96,384]{2,1,0:T(8,128)(2,1)S(1)} collective-permute-done((bf16[4,96,384]{2,1,0:T(8,128)(2,1)S(1)}, bf16[4,96,384]{2,1,0:T(8,128)(2,1)S(1)}, u32[]{:S(2)}, u32[]{:S(2)}) %collective-permute-start.17) | collective-permute-done | bytes 294944 | tf_op jit(solution)/shard_map/ppermute | solution.py:481
  158.3 2.0 ring_sum.1
  160.3 5.8 %collective-permute-start.20 = (bf16[96,384]{1,0:T(8,128)(2,1)}, bf16[96,384]{1,0:T(8,128)(2,1)S(1)}, u32[]{:S(2)}, u32[]{:S(2)}) collective-permute-start(bf16[96,384]{1,0:T(8,128)(2,1)} %get-tuple-element.112), channel_id=1, source_target_pairs={{0,16},{8,24},{16,32},{24,40},{32,48},{40,56},{48,0},{56,8},{64,80... | collective-permute-start | bytes 221192 | tf_op jit(solution)/shard_map/ppermute | solution.py:481
  166.1 4.6 %collective-permute-start.21 = (bf16[96,384]{1,0:T(8,128)(2,1)}, bf16[96,384]{1,0:T(8,128)(2,1)S(1)}, u32[]{:S(2)}, u32[]{:S(2)}) collective-permute-start(bf16[96,384]{1,0:T(8,128)(2,1)} %get-tuple-element.113), channel_id=1, source_target_pairs={{0,32},{8,40},{16,48},{24,56},{32,0},{40,8},{48,16},{56,24},{64,96... | collective-permute-start | bytes 221192 | tf_op jit(solution)/shard_map/ppermute | solution.py:481
  170.7 2.7 %collective-permute-start.22 = (bf16[96,384]{1,0:T(8,128)(2,1)}, bf16[96,384]{1,0:T(8,128)(2,1)S(1)}, u32[]{:S(2)}, u32[]{:S(2)}) collective-permute-start(bf16[96,384]{1,0:T(8,128)(2,1)} %get-tuple-element.114), channel_id=1, source_target_pairs={{0,48},{8,56},{16,0},{24,8},{32,16},{40,24},{48,32},{56,40},{64,11... | collective-permute-start | bytes 221192 | tf_op jit(solution)/shard_map/ppermute | solution.py:481
  173.3 6.8 %collective-permute-done.21 = bf16[96,384]{1,0:T(8,128)(2,1)S(1)} collective-permute-done((bf16[96,384]{1,0:T(8,128)(2,1)}, bf16[96,384]{1,0:T(8,128)(2,1)S(1)}, u32[]{:S(2)}, u32[]{:S(2)}) %collective-permute-start.21) | collective-permute-done | bytes 73760 | tf_op jit(solution)/shard_map/ppermute | solution.py:481
  181.0 4.0 %collective-permute-start.23 = (f32[96,384]{1,0:T(8,128)S(1)}, f32[96,384]{1,0:T(8,128)S(1)}, u32[]{:S(2)}, u32[]{:S(2)}) collective-permute-start(f32[96,384]{1,0:T(8,128)S(1)} %convert_add_fusion), channel_id=1, source_target_pairs={{0,0},{128,1},{2,2},{130,3},{4,4},{132,5},{6,6},{134,7},{8,8},{136... | collective-permute-start | bytes 442376 | tf_op jit(solution)/shard_map/ppermute | solution.py:553
  185.1 5.3 %collective-permute-done.23 = f32[96,384]{1,0:T(8,128)S(1)} collective-permute-done((f32[96,384]{1,0:T(8,128)S(1)}, f32[96,384]{1,0:T(8,128)S(1)}, u32[]{:S(2)}, u32[]{:S(2)}) %collective-permute-start.23) | collective-permute-done | bytes 147488 | tf_op jit(solution)/shard_map/ppermute | solution.py:553
  193.6 3.5 %gated_output.1 = bf16[128,3072]{1,0:T(8,128)(2,1)} custom-call(s32[1,3]{1,0:T(1,128)} %frames_ref.7, s32[1,3]{1,0:T(1,128)} %steps_ref.3, s32[1]{0:T(128)} %bitcast.seq_ref, f32[64,3072]{1,0:T(8,128)} %t1_ref.3, f32[64,3072]{1,0:T(8,128)} %t1_ref.3, bf16[128,3072]{1,0:T(8,128)(2,1)} %l1_ref.1, bf16[128,3072]{1,0:T(8,128)(2,1)} %l1_ref.1, ...), custom_call_target="tpu_custom_call" | custom-call | flops 3000000000 | bytes 9000000 | tf_op jit(solution)/shard_map/gated_output/pallas_call | solution.py:292
  (81 shorter events, 30.0 us)
Async XLA Ops:
  7.2 76.1 %all-gather.2.cloned.1.call-start = ((), (), s32[]{:S(2)}) async-start(), calls=%async_computation.2 | async-start | bytes 2433024 | tf_op jit(solution)/shard_map/all_gather | solution.py:513
  7.2 8.0 %collective-permute-start = (bf16[96,384]{1,0:T(8,128)(2,1)}, bf16[96,384]{1,0:T(8,128)(2,1)S(1)}, u32[]{:S(2)}, u32[]{:S(2)}) collective-permute-start(bf16[96,384]{1,0:T(8,128)(2,1)} %bitcast.21), channel_id=1, source_target_pairs={{0,0},{1,128},{2,2},{3,130},{4,4},{5,132},{6,6},{7,134},{8,8},{9,1... | collective-permute-start | bytes 221192 | tf_op jit(solution)/shard_map/ppermute | solution.py:510
  18.8 10.4 %collective-permute-start.1 = (bf16[128,1536]{1,0:T(8,128)(2,1)}, bf16[128,1536]{1,0:T(8,128)(2,1)}, u32[]{:S(2)}, u32[]{:S(2)}) collective-permute-start(bf16[128,1536]{1,0:T(8,128)(2,1)} %get-tuple-element.61), channel_id=1, source_target_pairs={{0,1},{1,0},{2,3},{3,2},{4,5},{5,4},{6,7},{7,6},{8,9},{9,8},{10,11... | collective-permute-start | bytes 1179656 | tf_op jit(solution)/shard_map/ppermute | solution.py:497
  18.8 53.1 %copy-start = (s32[1,3]{1,0:T(1,128)S(1)}, s32[1,3]{1,0:T(1,128)}, u32[]{:S(2)}) copy-start(s32[1,3]{1,0:T(1,128)} %frames_ref.7) | copy-start | bytes 40
  18.8 11.7 %collective-permute-start.3 = (bf16[128,1536]{1,0:T(8,128)(2,1)}, bf16[128,1536]{1,0:T(8,128)(2,1)}, u32[]{:S(2)}, u32[]{:S(2)}) collective-permute-start(bf16[128,1536]{1,0:T(8,128)(2,1)} %get-tuple-element.62.refs_0_), channel_id=1, source_target_pairs={{0,2},{1,3},{2,4},{3,5},{4,6},{5,7},{6,0},{7,1},{8,10},{9,11},{10,... | collective-permute-start | bytes 1179656 | tf_op jit(solution)/shard_map/ppermute | solution.py:481
  20.4 10.1 %collective-permute-start.2 = (bf16[128,1536]{1,0:T(8,128)(2,1)}, bf16[128,1536]{1,0:T(8,128)(2,1)S(1)}, u32[]{:S(2)}, u32[]{:S(2)}) collective-permute-start(bf16[128,1536]{1,0:T(8,128)(2,1)} %get-tuple-element.62.refs_0_), channel_id=1, source_target_pairs={{0,6},{1,7},{2,0},{3,1},{4,2},{5,3},{6,4},{7,5},{8,14},{9,15},{10,... | collective-permute-start | bytes 1179656 | tf_op jit(solution)/shard_map/ppermute | solution.py:481
  31.2 40.7 %all-to-all-start = ((bf16[8,3,128,384]{3,2,1,0:T(8,128)(2,1)}), bf16[8,3,128,384]{3,2,1,0:T(8,128)(2,1)S(1)}, u32[]{:S(2)}, u32[]{:S(2)}) async-start(bf16[8,3,128,384]{3,2,1,0:T(8,128)(2,1)} %pack_heads.1), calls=%async_computation | async-start | bytes 4718592 | tf_op jit(solution)/shard_map/all_to_all | solution.py:518
  37.0 33.4 %collective-permute-start.5 = (bf16[128,1536]{1,0:T(8,128)(2,1)}, bf16[128,1536]{1,0:T(8,128)(2,1)}, u32[]{:S(2)}, u32[]{:S(2)}) collective-permute-start(bf16[128,1536]{1,0:T(8,128)(2,1)} %collective-permute-done.1.refs_1_), channel_id=1, source_target_pairs={{0,6},{1,7},{2,0},{3,1},{4,2},{5,3},{6,4},{7,5},{8,14},{9,15},{10,... | collective-permute-start | bytes 1179656 | tf_op jit(solution)/shard_map/ppermute | solution.py:481
  39.7 43.5 %collective-permute-start.8 = (bf16[128,1536]{1,0:T(8,128)(2,1)}, bf16[128,1536]{1,0:T(8,128)(2,1)}, u32[]{:S(2)}, u32[]{:S(2)}) collective-permute-start(bf16[128,1536]{1,0:T(8,128)(2,1)} %collective-permute-done.1.refs_1_), channel_id=1, source_target_pairs={{0,2},{1,3},{2,4},{3,5},{4,6},{5,7},{6,0},{7,1},{8,10},{9,11},{10,... | collective-permute-start | bytes 1179656 | tf_op jit(solution)/shard_map/ppermute | solution.py:481
  39.7 43.5 %collective-permute-start.6 = (bf16[128,1536]{1,0:T(8,128)(2,1)}, bf16[128,1536]{1,0:T(8,128)(2,1)}, u32[]{:S(2)}, u32[]{:S(2)}) collective-permute-start(bf16[128,1536]{1,0:T(8,128)(2,1)} %collective-permute-done.3.refs_6_), channel_id=1, source_target_pairs={{0,2},{1,3},{2,4},{3,5},{4,6},{5,7},{6,0},{7,1},{8,10},{9,11},{10,... | collective-permute-start | bytes 1179656 | tf_op jit(solution)/shard_map/ppermute | solution.py:481
  70.4 12.8 %collective-permute-start.7 = (bf16[128,1536]{1,0:T(8,128)(2,1)}, bf16[128,1536]{1,0:T(8,128)(2,1)}, u32[]{:S(2)}, u32[]{:S(2)}) collective-permute-start(bf16[128,1536]{1,0:T(8,128)(2,1)} %collective-permute-done.5.refs_3_), channel_id=1, source_target_pairs={{0,6},{1,7},{2,0},{3,1},{4,2},{5,3},{6,4},{7,5},{8,14},{9,15},{10,... | collective-permute-start | bytes 1179656 | tf_op jit(solution)/shard_map/ppermute | solution.py:481
  82.0 20.8 %collective-permute-start.4 = (bf16[1024,384]{1,0:T(8,128)(2,1)}, bf16[1024,384]{1,0:T(8,128)(2,1)}, u32[]{:S(2)}, u32[]{:S(2)}) collective-permute-start(bf16[1024,384]{1,0:T(8,128)(2,1)} %get-tuple-element.64.a_ref), channel_id=1, source_target_pairs={{0,1},{1,0},{2,3},{3,2},{4,5},{5,4},{6,7},{7,6},{8,9},{9,8},{10,11... | collective-permute-start | bytes 2359304 | tf_op jit(solution)/shard_map/ppermute | solution.py:497
  92.1 26.5 %collective-permute-start.9 = (bf16[1024,384]{1,0:T(8,128)(2,1)S(1)}, bf16[1024,384]{1,0:T(8,128)(2,1)S(1)}, u32[]{:S(2)}, u32[]{:S(2)}) collective-permute-start(bf16[1024,384]{1,0:T(8,128)(2,1)S(1)} %get-tuple-element.73), channel_id=1, source_target_pairs={{0,1},{1,0},{2,3},{3,2},{4,5},{5,4},{6,7},{7,6},{8,9},{9,8},{10,11... | collective-permute-start | bytes 2359304 | tf_op jit(solution)/shard_map/ppermute | solution.py:497
  93.2 9.6 %copy-start.4 = (bf16[3072,384]{1,0:T(8,128)(2,1)S(1)}, bf16[3072,384]{1,0:T(8,128)(2,1)}, u32[]{:S(2)}) copy-start(bf16[3072,384]{1,0:T(8,128)(2,1)} %all-gather.2.cloned.1.call-done) | copy-start | bytes 7077892
  96.3 8.9 %copy-start.9 = (bf16[8,96,384]{2,1,0:T(8,128)(2,1)}, bf16[8,96,384]{2,1,0:T(8,128)(2,1)S(1)}, u32[]{:S(2)}) copy-start(bf16[8,96,384]{2,1,0:T(8,128)(2,1)S(1)} %get-tuple-element.87) | copy-start | bytes 1769476
  105.2 9.1 %collective-permute-start.10 = (bf16[128,1536]{1,0:T(8,128)(2,1)S(1)}, bf16[128,1536]{1,0:T(8,128)(2,1)S(1)}, u32[]{:S(2)}, u32[]{:S(2)}) collective-permute-start(bf16[128,1536]{1,0:T(8,128)(2,1)S(1)} %get-tuple-element.74), channel_id=1, source_target_pairs={{0,2},{1,3},{2,4},{3,5},{4,6},{5,7},{6,0},{7,1},{8,10},{9,11},{10,... | collective-permute-start | bytes 1179656 | tf_op jit(solution)/shard_map/ppermute | solution.py:481
  105.8 8.5 %collective-permute-start.11 = (bf16[128,1536]{1,0:T(8,128)(2,1)S(1)}, bf16[128,1536]{1,0:T(8,128)(2,1)S(1)}, u32[]{:S(2)}, u32[]{:S(2)}) collective-permute-start(bf16[128,1536]{1,0:T(8,128)(2,1)S(1)} %get-tuple-element.78), channel_id=1, source_target_pairs={{0,6},{1,7},{2,0},{3,1},{4,2},{5,3},{6,4},{7,5},{8,14},{9,15},{10,... | collective-permute-start | bytes 1179656 | tf_op jit(solution)/shard_map/ppermute | solution.py:481
  108.5 23.4 %collective-permute-start.14 = (bf16[8,96,384]{2,1,0:T(8,128)(2,1)S(1)}, bf16[8,96,384]{2,1,0:T(8,128)(2,1)S(1)}, u32[]{:S(2)}, u32[]{:S(2)}) collective-permute-start(bf16[8,96,384]{2,1,0:T(8,128)(2,1)S(1)} %get-tuple-element.88), channel_id=1, source_target_pairs={{0,8},{8,0},{16,24},{24,16},{32,40},{40,32},{48,56},{56,48},{64,72... | collective-permute-start | bytes 1769480 | tf_op jit(solution)/shard_map/ppermute | solution.py:501
  111.5 20.4 %collective-permute-start.15 = (bf16[8,96,384]{2,1,0:T(8,128)(2,1)S(1)}, bf16[8,96,384]{2,1,0:T(8,128)(2,1)S(1)}, u32[]{:S(2)}, u32[]{:S(2)}) collective-permute-start(bf16[8,96,384]{2,1,0:T(8,128)(2,1)S(1)} %get-tuple-element.90), channel_id=1, source_target_pairs={{0,8},{8,0},{16,24},{24,16},{32,40},{40,32},{48,56},{56,48},{64,72... | collective-permute-start | bytes 1769480 | tf_op jit(solution)/shard_map/ppermute | solution.py:501
  114.3 7.5 %copy-start.2 = (bf16[3,640,640]{2,1,0:T(8,128)(2,1)S(1)}, bf16[3,640,640]{2,1,0:T(8,128)(2,1)}, u32[]{:S(2)}) copy-start(bf16[3,640,640]{2,1,0:T(8,128)(2,1)} %copy-done.1) | copy-start | bytes 7372804
  118.5 18.8 %collective-permute-start.12 = (bf16[256,1536]{1,0:T(8,128)(2,1)}, bf16[256,1536]{1,0:T(8,128)(2,1)}, u32[]{:S(2)}, u32[]{:S(2)}) collective-permute-start(bf16[256,1536]{1,0:T(8,128)(2,1)} %get-tuple-element.85), channel_id=1, source_target_pairs={{0,2},{1,3},{2,4},{3,5},{4,6},{5,7},{6,0},{7,1},{8,10},{9,11},{10,... | collective-permute-start | bytes 2359304 | tf_op jit(solution)/shard_map/ppermute | solution.py:481
  119.2 18.2 %collective-permute-start.13 = (bf16[256,1536]{1,0:T(8,128)(2,1)}, bf16[256,1536]{1,0:T(8,128)(2,1)}, u32[]{:S(2)}, u32[]{:S(2)}) collective-permute-start(bf16[256,1536]{1,0:T(8,128)(2,1)} %get-tuple-element.86), channel_id=1, source_target_pairs={{0,6},{1,7},{2,0},{3,1},{4,2},{5,3},{6,4},{7,5},{8,14},{9,15},{10,... | collective-permute-start | bytes 2359304 | tf_op jit(solution)/shard_map/ppermute | solution.py:481
  137.4 10.0 %copy-start.16 = (bf16[4,96,384]{2,1,0:T(8,128)(2,1)S(1)}, bf16[4,96,384]{2,1,0:T(8,128)(2,1)}, u32[]{:S(2)}) copy-start(bf16[4,96,384]{2,1,0:T(8,128)(2,1)} %get-tuple-element.102) | copy-start | bytes 884740
  137.4 53.1 %all-to-all-start.1 = ((bf16[8,3,128,384]{3,2,1,0:T(8,128)(2,1)}), bf16[8,3,128,384]{3,2,1,0:T(8,128)(2,1)S(1)}, u32[]{:S(2)}, u32[]{:S(2)}) async-start(bf16[8,3,128,384]{3,2,1,0:T(8,128)(2,1)} %attention_backward.1), calls=%async_computation.1 | async-start | bytes 4718592 | tf_op jit(solution)/shard_map/all_to_all | solution.py:544
  143.2 11.0 %collective-permute-start.16 = (bf16[4,96,384]{2,1,0:T(8,128)(2,1)}, bf16[4,96,384]{2,1,0:T(8,128)(2,1)S(1)}, u32[]{:S(2)}, u32[]{:S(2)}) collective-permute-start(bf16[4,96,384]{2,1,0:T(8,128)(2,1)} %get-tuple-element.100), channel_id=1, source_target_pairs={{0,64},{8,72},{16,80},{24,88},{32,96},{40,104},{48,112},{56,120},{... | collective-permute-start | bytes 884744 | tf_op jit(solution)/shard_map/ppermute | solution.py:481
  144.1 12.8 %collective-permute-start.17 = (bf16[4,96,384]{2,1,0:T(8,128)(2,1)S(1)}, bf16[4,96,384]{2,1,0:T(8,128)(2,1)S(1)}, u32[]{:S(2)}, u32[]{:S(2)}) collective-permute-start(bf16[4,96,384]{2,1,0:T(8,128)(2,1)S(1)} %copy-done.17), channel_id=1, source_target_pairs={{0,128},{8,136},{16,144},{24,152},{32,160},{40,168},{48,176},{56,1... | collective-permute-start | bytes 884744 | tf_op jit(solution)/shard_map/ppermute | solution.py:481
  147.4 9.5 %collective-permute-start.18 = (bf16[4,96,384]{2,1,0:T(8,128)(2,1)S(1)}, bf16[4,96,384]{2,1,0:T(8,128)(2,1)S(1)}, u32[]{:S(2)}, u32[]{:S(2)}) collective-permute-start(bf16[4,96,384]{2,1,0:T(8,128)(2,1)S(1)} %copy-done.16), channel_id=1, source_target_pairs={{0,192},{8,200},{16,208},{24,216},{32,224},{40,232},{48,240},{56,2... | collective-permute-start | bytes 884744 | tf_op jit(solution)/shard_map/ppermute | solution.py:481
  160.3 13.0 %collective-permute-start.20 = (bf16[96,384]{1,0:T(8,128)(2,1)}, bf16[96,384]{1,0:T(8,128)(2,1)S(1)}, u32[]{:S(2)}, u32[]{:S(2)}) collective-permute-start(bf16[96,384]{1,0:T(8,128)(2,1)} %get-tuple-element.112), channel_id=1, source_target_pairs={{0,16},{8,24},{16,32},{24,40},{32,48},{40,56},{48,0},{56,8},{64,80... | collective-permute-start | bytes 221192 | tf_op jit(solution)/shard_map/ppermute | solution.py:481
  166.1 14.0 %collective-permute-start.21 = (bf16[96,384]{1,0:T(8,128)(2,1)}, bf16[96,384]{1,0:T(8,128)(2,1)S(1)}, u32[]{:S(2)}, u32[]{:S(2)}) collective-permute-start(bf16[96,384]{1,0:T(8,128)(2,1)} %get-tuple-element.113), channel_id=1, source_target_pairs={{0,32},{8,40},{16,48},{24,56},{32,0},{40,8},{48,16},{56,24},{64,96... | collective-permute-start | bytes 221192 | tf_op jit(solution)/shard_map/ppermute | solution.py:481
  170.7 9.4 %collective-permute-start.22 = (bf16[96,384]{1,0:T(8,128)(2,1)}, bf16[96,384]{1,0:T(8,128)(2,1)S(1)}, u32[]{:S(2)}, u32[]{:S(2)}) collective-permute-start(bf16[96,384]{1,0:T(8,128)(2,1)} %get-tuple-element.114), channel_id=1, source_target_pairs={{0,48},{8,56},{16,0},{24,8},{32,16},{40,24},{48,32},{56,40},{64,11... | collective-permute-start | bytes 221192 | tf_op jit(solution)/shard_map/ppermute | solution.py:481
  181.0 9.4 %collective-permute-start.23 = (f32[96,384]{1,0:T(8,128)S(1)}, f32[96,384]{1,0:T(8,128)S(1)}, u32[]{:S(2)}, u32[]{:S(2)}) collective-permute-start(f32[96,384]{1,0:T(8,128)S(1)} %convert_add_fusion), channel_id=1, source_target_pairs={{0,0},{128,1},{2,2},{130,3},{4,4},{132,5},{6,6},{134,7},{8,8},{136... | collective-permute-start | bytes 442376 | tf_op jit(solution)/shard_map/ppermute | solution.py:553
  185.0 7.9 %collective-permute-start.19 = (bf16[128,1536]{1,0:T(8,128)(2,1)S(1)}, bf16[128,1536]{1,0:T(8,128)(2,1)S(1)}, u32[]{:S(2)}, u32[]{:S(2)}) collective-permute-start(bf16[128,1536]{1,0:T(8,128)(2,1)S(1)} %get-tuple-element.104), channel_id=1, source_target_pairs={{0,1},{1,0},{2,3},{3,2},{4,5},{5,4},{6,7},{7,6},{8,9},{9,8},{10,11... | collective-permute-start | bytes 1179656 | tf_op jit(solution)/shard_map/ppermute | solution.py:497
  (16 other events, 29.3 us)
Sparse Core Ops, SparseCore 0:
  15.9 59.7 all-gather.1

commit v7 on v6

--- a/solution.py
+++ b/solution.py
@@ -65,7 +65,7 @@
 def spans(total):
     out, at = [], 0
     while at < total:
-        size = min(256, total - at)
+        size = min(128, total - at)
         out.append((at, size))
         at += size
     return out
@@ -326,7 +326,7 @@
         ),
         in_specs=[SMEM] + [VMEM] * 9,
         out_specs=(VMEM, whole((1024, 384)), VMEM),
-        compiler_params=pltpu.CompilerParams(vmem_limit_bytes=VMEM_LIMIT),
+        compiler_params=PARAMS,
         cost_estimate=cost(7),
         name="dattn_parts",
     )(seq, *blocks, weights)
@@ -436,6 +436,7 @@
         out_shape=(jax.ShapeDtypeStruct((4, 96, 384), BF),) * 4,
         in_specs=[SMEM] + [VMEM] * 4,
         out_specs=(pl.BlockSpec((4, 96, 384), lambda: (0, 0, 0)),) * 4,
+        compiler_params=PARAMS,
         cost_estimate=cost(3),
         name="pair_sum",
     )(dp, *terms)
@@ -455,6 +456,7 @@
         out_shape=(jax.ShapeDtypeStruct((96, 384), BF),) * 4,
         in_specs=[SMEM] + [VMEM] * 4,
         out_specs=(pl.BlockSpec((96, 384), lambda: (0, 0)),) * 4,
+        compiler_params=PARAMS,
         cost_estimate=cost(2),
         name="ring_sum",
     )(dp, *parts)
@@ -508,12 +510,12 @@
     moves = piece_moves(lax.axis_size("dp"), lax.axis_size("seq"))
 
     piece = lax.ppermute(out_weight.T, both, moves)
-    packed = pack_heads(qkv_input.transpose(1, 0, 2))
-    packed, piece, cotangent = lax.optimization_barrier((packed, piece, cotangent))
+    keep, send = gated_cotangent(frames, timesteps, seq, gate_table, cotangent)
+    qkv_input, piece, keep, send = lax.optimization_barrier((qkv_input, piece, keep, send))
     weights = lax.all_gather(piece, "dp", axis=0, tiled=True).reshape(2, 1536, 384)
-    keep, send = gated_cotangent(frames, timesteps, seq, gate_table, cotangent)
     got = swap_z(send)
     b1_keep, b3_keep = along_x(keep, -1), along_x(keep, 1)
+    packed = pack_heads(qkv_input.transpose(1, 0, 2))
     packed, got, b1_keep, b3_keep = lax.optimization_barrier((packed, got, b1_keep, b3_keep))
     heads = lax.all_to_all(packed, "seq", split_axis=0, concat_axis=0, tiled=True)
 
@@ -538,23 +540,24 @@
     d_own, d_recv, t1, t3 = lax.optimization_barrier((d_own, d_recv, t1, t3))
     c1, c3 = along_x(t1, 1), along_x(t3, -1)
     terms = pair_sum(dp, keep0, got0, keep1, got1)
+    d_own, terms = lax.optimization_barrier((d_own, terms))
+    terms = [terms[0]] + [along_y(terms[k], k) for k in range(1, 4)]
 
     grads = attention_backward(frames, heads, d_own, d_recv, p1, p2)
-    grads, c1, c3, terms = lax.optimization_barrier((grads, c1, c3, terms))
+    grads, c1, c3 = lax.optimization_barrier((grads, c1, c3))
     grads = lax.all_to_all(grads, "seq", split_axis=0, concat_axis=0, tiled=True)
-    terms = [terms[0]] + [along_y(terms[k], k) for k in range(1, 4)]
 
     o_keep, o_send = project_home(seq, attn, attn_other, weights, c1, c3)
-    terms, o_send = lax.optimization_barrier((terms, o_send))
+    o_got = swap_z(o_send)
+    terms, o_keep = lax.optimization_barrier((terms, o_keep))
     terms = ring_sum(dp, terms)
     terms = [terms[0]] + [along_z(terms[k], k) for k in range(1, 4)]
+    output = gated_output(frames, timesteps, seq, gate_table, latents, o_keep, o_got)
+    terms, output = lax.optimization_barrier((terms, output))
     total = terms[0].astype(F32) + terms[1].astype(F32)
     total = total + terms[2].astype(F32) + terms[3].astype(F32)
     total = lax.ppermute(total, both, [(b, a) for a, b in moves])
-    o_got = swap_z(o_send)
     grad_qkv = unpack_heads(grads)
-    grad_qkv, o_got = lax.optimization_barrier((grad_qkv, o_got))
-    output = gated_output(frames, timesteps, seq, gate_table, latents, o_keep, o_got)
     return (output, grad_qkv.transpose(1, 0, 2), total.T)
 
 

time: 205 us -> 203 us (level)
  Pallas kernels: 55.4 us -> 44.2 us
  waiting for transfers between devices: 64 us -> 72.8 us
  local copies, waits for them, and re-layouts: 13.5 us -> 16.1 us
    ppermute x16, waiting for transfers between devices: 43.7 us -> 48.8 us  [along(): return lax.ppermute(x, axis, moves)]
    ppermute x4, waiting for transfers between devices: 14.3 us -> 18.2 us  [swap_z(): lax.ppermute(x, 'seq', [(i, i ^ 1) for i in range(lax.axis_size('seq'))])]
    pallas_call x1, Pallas kernels: 8.65 us -> 6.02 us  [attention_forward(): pl.pallas_call(fwd_kernel, out_shape=(shape((1024, 3 * HD)), shape((3, LO...]
    pallas_call x1, Pallas kernels: 10.1 us -> 7.44 us  [attention_backward(): pl.pallas_call(bwd_kernel, out_shape=shape((8, 3, 128, 3 * HD)), in_specs...]
    pallas_call x1, Pallas kernels: 2.97 us -> 0.38 us  [pair_sum(): pl.pallas_call(pair_kernel, out_shape=(jax.ShapeDtypeStruct((4, 96, 384),...]
    unnamed x43 -> x47, local copies, waits for them, and re-layouts: 13.5 us -> 16.1 us
  transfers between devices with their start and end apart: 27 -> 27, of which waited for: 11 -> 14; matrix products, arithmetic and copies ran while one was open for 0% -> 0% of each run, Pallas kernels for 25% -> 21%
where the time goes in v7:
time: 203 us; the launch traced here: 202 us
  waiting for transfers between devices  72.8 us (36%)
  starting transfers between devices  55.2 us (27%)
  Pallas kernels  44.2 us (22%)
  local copies, waits for them, and re-layouts  16.1 us (8%)
  between operations  14.2 us (7%)
    ppermute x16, waiting for transfers between devices, along(): return lax.ppermute(x, axis, moves)  48.8 us
    ppermute x16, starting transfers between devices, along(): return lax.ppermute(x, axis, moves)  33.2 us
    ppermute x4, waiting for transfers between devices, swap_z(): lax.ppermute(x, 'seq', [(i, i ^ 1) for i in range(lax.axis_size('seq'))])  18.2 us
    unnamed x47, local copies, waits for them, and re-layouts  16.1 us
    pallas_call x1, Pallas kernels, attention_backward(): pl.pallas_call(bwd_kernel, out_shape=shape((8, 3, 128, 3 * HD)), in_specs...  7.44 us
    pallas_call x2, Pallas kernels, dweight_part(): pl.pallas_call(dweight_kernel, out_shape=(shape((8, 96, 384)), shape((8,...  6.05 us
    pallas_call x1, Pallas kernels, attention_forward(): pl.pallas_call(fwd_kernel, out_shape=(shape((1024, 3 * HD)), shape((3, LO...  6.02 us
    all_to_all x1, starting transfers between devices, body(): lax.all_to_all(packed, 'seq', split_axis=0, concat_axis=0, tiled=True)  5.77 us
  transfers between devices with their start and end apart: 27, of which 14 were waited for; matrix products, arithmetic and copies ran while one was open for 0% of the time, Pallas kernels for 21%

profile of v7, /device:TPU:32, one launch (start us, length us, event | category | flops | bytes accessed | tf_op | source)
XLA Modules:
  0.0 202.5 jit_solution(9765273535943693386)
XLA Ops:
  7.2 4.6 %collective-permute-start = (bf16[96,384]{1,0:T(8,128)(2,1)}, bf16[96,384]{1,0:T(8,128)(2,1)S(1)}, u32[]{:S(2)}, u32[]{:S(2)}) collective-permute-start(bf16[96,384]{1,0:T(8,128)(2,1)} %bitcast.21), channel_id=1, source_target_pairs={{0,0},{1,128},{2,2},{3,130},{4,4},{5,132},{6,6},{7,134},{8,8},{9,1... | collective-permute-start | bytes 221192 | tf_op jit(solution)/shard_map/ppermute | solution.py:512
  11.9 3.0 %gated_cotangent.1 = (bf16[128,1536]{1,0:T(8,128)(2,1)}, bf16[128,1536]{1,0:T(8,128)(2,1)}) custom-call(s32[1,3]{1,0:T(1,128)} %frames_ref.7, s32[1,3]{1,0:T(1,128)} %steps_ref.3, s32[1]{0:T(128)} %bitcast.1.seq_ref, f32[64,3072]{1,0:T(8,128)} %t1_ref.3, f32[64,3072]{1,0:T(8,128)} %t1_ref.3, bf16[128,3072]{1,0:T(8,128)(2,1)} %c1_ref.1, bf16[128,3072]{1,0:T(8,128)(2,1)} %c1_ref.1), custom_call_target="tpu_custom_call" | custom-call | flops 3000000000 | bytes 9000000 | tf_op jit(solution)/shard_map/gated_cotangent/pallas_call | solution.py:259
  17.5 1.7 collective-permute-start.2
  19.2 2.8 %pack_heads.1 = bf16[8,3,128,384]{3,2,1,0:T(8,128)(2,1)} custom-call(bf16[3,128,3072]{2,1,0:T(8,128)(2,1)} %bitcast.20), custom_call_target="tpu_custom_call" | custom-call | flops 3000000000 | bytes 9000000 | tf_op jit(solution)/shard_map/pack_heads/pallas_call | solution.py:218
  22.0 4.5 %collective-permute-done.1.refs_1_ = bf16[128,1536]{1,0:T(8,128)(2,1)} collective-permute-done((bf16[128,1536]{1,0:T(8,128)(2,1)}, bf16[128,1536]{1,0:T(8,128)(2,1)}, u32[]{:S(2)}, u32[]{:S(2)}) %collective-permute-start.1) | collective-permute-done | bytes 393248 | tf_op jit(solution)/shard_map/ppermute | solution.py:499
  28.5 5.8 %all-to-all-start = ((bf16[8,3,128,384]{3,2,1,0:T(8,128)(2,1)}), bf16[8,3,128,384]{3,2,1,0:T(8,128)(2,1)S(1)}, u32[]{:S(2)}, u32[]{:S(2)}) async-start(bf16[8,3,128,384]{3,2,1,0:T(8,128)(2,1)} %pack_heads.1), calls=%async_computation | async-start | bytes 4718592 | tf_op jit(solution)/shard_map/all_to_all | solution.py:520
  34.3 2.7 %collective-permute-start.4 = (bf16[128,1536]{1,0:T(8,128)(2,1)}, bf16[128,1536]{1,0:T(8,128)(2,1)}, u32[]{:S(2)}, u32[]{:S(2)}) collective-permute-start(bf16[128,1536]{1,0:T(8,128)(2,1)} %collective-permute-done.1.refs_1_), channel_id=1, source_target_pairs={{0,6},{1,7},{2,0},{3,1},{4,2},{5,3},{6,4},{7,5},{8,14},{9,15},{10,... | collective-permute-start | bytes 1179656 | tf_op jit(solution)/shard_map/ppermute | solution.py:483
  37.8 30.1 %collective-permute-done.4.refs_3_ = bf16[128,1536]{1,0:T(8,128)(2,1)} collective-permute-done((bf16[128,1536]{1,0:T(8,128)(2,1)}, bf16[128,1536]{1,0:T(8,128)(2,1)}, u32[]{:S(2)}, u32[]{:S(2)}) %collective-permute-start.4) | collective-permute-done | bytes 393248 | tf_op jit(solution)/shard_map/ppermute | solution.py:483
  69.4 6.0 %attention_forward.1 = (bf16[1024,384]{1,0:T(8,128)(2,1)}, bf16[3,640,640]{2,1,0:T(8,128)(2,1)S(1)}, bf16[3,384,384]{2,1,0:T(8,128)(2,1)S(1)}) custom-call(s32[1,3]{1,0:T(1,128)S(1)} %copy-done.1, bf16[8,3,128,384]{3,2,1,0:T(8,128)(2,1)S(1)} %all-to-all-done.qkv_ref), custom_call_target="tpu_custom_call" | custom-call | flops 100000000 | bytes 300000 | tf_op jit(solution)/shard_map/attention_forward/pallas_call | solution.py:133
  82.4 5.2 %dattn_parts.1 = (bf16[1024,1536]{1,0:T(8,128)(2,1)S(1)}, bf16[1024,384]{1,0:T(8,128)(2,1)S(1)}, f32[1024,384]{1,0:T(8,128)S(1)}) custom-call(s32[1]{0:T(128)} %bitcast.1.seq_ref, bf16[128,1536]{1,0:T(8,128)(2,1)S(1)} %copy-done.11, bf16[128,1536]{1,0:T(8,128)(2,1)} %collective-permute-done.1.refs_1_, bf16[128,1536]{1,0:T(8,128)(2,1)S(1)} %copy-done.13, ...), custom_call_target="tpu_custom_call" | custom-call | flops 7000000000 | bytes 21000000 | tf_op jit(solution)/shard_map/dattn_parts/pallas_call | solution.py:320
  87.9 3.1 %dweight_part.2 = (bf16[8,96,384]{2,1,0:T(8,128)(2,1)S(1)}, bf16[8,96,384]{2,1,0:T(8,128)(2,1)S(1)}) custom-call(s32[1]{0:T(128)} %bitcast.dp_ref, bf16[1024,1536]{1,0:T(8,128)(2,1)S(1)} %get-tuple-element.81.d_ref, bf16[1024,384]{1,0:T(8,128)(2,1)} %get-tuple-element.76.a_ref), custom_call_target="tpu_custom_call" | custom-call | flops 4000000000 | bytes 12000000 | tf_op jit(solution)/shard_map/dweight_part/pallas_call | solution.py:409
  91.3 6.4 %collective-permute-done.9.b_ref.a_ref = bf16[1024,384]{1,0:T(8,128)(2,1)} collective-permute-done((bf16[1024,384]{1,0:T(8,128)(2,1)}, bf16[1024,384]{1,0:T(8,128)(2,1)}, u32[]{:S(2)}, u32[]{:S(2)}) %collective-permute-start.9) | collective-permute-done | bytes 786464 | tf_op jit(solution)/shard_map/ppermute | solution.py:499
  97.7 2.4 %project_far.1 = (bf16[128,1536]{1,0:T(8,128)(2,1)S(1)}, bf16[128,1536]{1,0:T(8,128)(2,1)S(1)}) custom-call(s32[1]{0:T(128)} %bitcast.1.seq_ref, bf16[1024,384]{1,0:T(8,128)(2,1)} %get-tuple-element.76.a_ref, bf16[1024,384]{1,0:T(8,128)(2,1)} %collective-permute-done.9.b_ref.a_ref, bf16[2,1536,384]{2,1,0:T(8,128)(2,1)S(1)} %bitcast.12), custom_call_target="tpu_custom_call" | custom-call | flops 3000000000 | bytes 9000000 | tf_op jit(solution)/shard_map/project_far/pallas_call | solution.py:378
  100.7 2.7 %collective-permute-start.11 = (bf16[128,1536]{1,0:T(8,128)(2,1)S(1)}, bf16[128,1536]{1,0:T(8,128)(2,1)S(1)}, u32[]{:S(2)}, u32[]{:S(2)}) collective-permute-start(bf16[128,1536]{1,0:T(8,128)(2,1)S(1)} %get-tuple-element.84), channel_id=1, source_target_pairs={{0,6},{1,7},{2,0},{3,1},{4,2},{5,3},{6,4},{7,5},{8,14},{9,15},{10,... | collective-permute-start | bytes 1179656 | tf_op jit(solution)/shard_map/ppermute | solution.py:483
  103.4 3.0 %dweight_part.3 = (bf16[8,96,384]{2,1,0:T(8,128)(2,1)S(1)}, bf16[8,96,384]{2,1,0:T(8,128)(2,1)S(1)}) custom-call(s32[1]{0:T(128)} %bitcast.dp_ref, bf16[1024,1536]{1,0:T(8,128)(2,1)S(1)} %get-tuple-element.81.d_ref, bf16[1024,384]{1,0:T(8,128)(2,1)} %collective-permute-done.9.b_ref.a_ref), custom_call_target="tpu_custom_call" | custom-call | flops 4000000000 | bytes 12000000 | tf_op jit(solution)/shard_map/dweight_part/pallas_call | solution.py:409
  106.4 2.7 %collective-permute-done.10.up_ref = bf16[128,1536]{1,0:T(8,128)(2,1)S(1)} collective-permute-done((bf16[128,1536]{1,0:T(8,128)(2,1)S(1)}, bf16[128,1536]{1,0:T(8,128)(2,1)S(1)}, u32[]{:S(2)}, u32[]{:S(2)}) %collective-permute-start.10) | collective-permute-done | bytes 393248 | tf_op jit(solution)/shard_map/ppermute | solution.py:483
  109.1 3.2 %project_near.1 = (bf16[256,1536]{1,0:T(8,128)(2,1)S(1)}, bf16[256,1536]{1,0:T(8,128)(2,1)S(1)}) custom-call(s32[1]{0:T(128)} %bitcast.1.seq_ref, bf16[1024,384]{1,0:T(8,128)(2,1)} %get-tuple-element.76.a_ref, bf16[1024,384]{1,0:T(8,128)(2,1)} %collective-permute-done.9.b_ref.a_ref, bf16[2,1536,384]{2,1,0:T(8,128)(2,1)S(1)} %bitcast.13, ...), custom_call_target="tpu_custom_call" | custom-call | flops 3000000000 | bytes 9000000 | tf_op jit(solution)/shard_map/project_near/pallas_call | solution.py:384
  113.2 2.6 %collective-permute-start.18 = (bf16[256,1536]{1,0:T(8,128)(2,1)S(1)}, bf16[256,1536]{1,0:T(8,128)(2,1)S(1)}, u32[]{:S(2)}, u32[]{:S(2)}) collective-permute-start(bf16[256,1536]{1,0:T(8,128)(2,1)S(1)} %get-tuple-element.105), channel_id=1, source_target_pairs={{0,6},{1,7},{2,0},{3,1},{4,2},{5,3},{6,4},{7,5},{8,14},{9,15},{10,... | collective-permute-start | bytes 2359304 | tf_op jit(solution)/shard_map/ppermute | solution.py:483
  118.4 7.4 %attention_backward.1 = bf16[8,3,128,384]{3,2,1,0:T(8,128)(2,1)S(1)} custom-call(s32[1,3]{1,0:T(1,128)S(1)} %copy-done.1, bf16[8,3,128,384]{3,2,1,0:T(8,128)(2,1)S(1)} %all-to-all-done.qkv_ref, f32[1024,384]{1,0:T(8,128)S(1)} %get-tuple-element.100.own_ref, bf16[1024,384]{1,0:T(8,128)(2,1)S(1)} %collective-permute-done.8.other_ref, ...), custom_call_target="tpu_custom_call" | custom-call | flops 10000000000 | bytes 30000000 | tf_op jit(solution)/shard_map/attention_backward/pallas_call | solution.py:195
  127.2 4.3 %collective-permute-done.17.c1_ref = bf16[256,1536]{1,0:T(8,128)(2,1)S(1)} collective-permute-done((bf16[256,1536]{1,0:T(8,128)(2,1)S(1)}, bf16[256,1536]{1,0:T(8,128)(2,1)S(1)}, u32[]{:S(2)}, u32[]{:S(2)}) %collective-permute-start.17) | collective-permute-done | bytes 786464 | tf_op jit(solution)/shard_map/ppermute | solution.py:483
  133.3 4.9 %all-to-all-start.1 = ((bf16[8,3,128,384]{3,2,1,0:T(8,128)(2,1)}), bf16[8,3,128,384]{3,2,1,0:T(8,128)(2,1)S(1)}, u32[]{:S(2)}, u32[]{:S(2)}) async-start(bf16[8,3,128,384]{3,2,1,0:T(8,128)(2,1)} %copy-done), calls=%async_computation.1 | async-start | bytes 4718592 | tf_op jit(solution)/shard_map/all_to_all | solution.py:548
  138.3 3.2 %collective-permute-start.15 = (bf16[4,96,384]{2,1,0:T(8,128)(2,1)}, bf16[4,96,384]{2,1,0:T(8,128)(2,1)S(1)}, u32[]{:S(2)}, u32[]{:S(2)}) collective-permute-start(bf16[4,96,384]{2,1,0:T(8,128)(2,1)} %copy-done.16), channel_id=1, source_target_pairs={{0,128},{8,136},{16,144},{24,152},{32,160},{40,168},{48,176},{56,1... | collective-permute-start | bytes 884744 | tf_op jit(solution)/shard_map/ppermute | solution.py:483
  145.6 2.5 %project_home.1 = (f32[128,1536]{1,0:T(8,128)S(1)}, bf16[128,1536]{1,0:T(8,128)(2,1)S(1)}) custom-call(s32[1]{0:T(128)} %bitcast.1.seq_ref, bf16[1024,384]{1,0:T(8,128)(2,1)} %get-tuple-element.76.a_ref, bf16[1024,384]{1,0:T(8,128)(2,1)} %collective-permute-done.9.b_ref.a_ref, bf16[2,1536,384]{2,1,0:T(8,128)(2,1)S(1)} %bitcast.14, ...), custom_call_target="tpu_custom_call" | custom-call | flops 3000000000 | bytes 9000000 | tf_op jit(solution)/shard_map/project_home/pallas_call | solution.py:395
  148.4 3.1 %collective-permute-done.15.c_ref = bf16[4,96,384]{2,1,0:T(8,128)(2,1)S(1)} collective-permute-done((bf16[4,96,384]{2,1,0:T(8,128)(2,1)}, bf16[4,96,384]{2,1,0:T(8,128)(2,1)S(1)}, u32[]{:S(2)}, u32[]{:S(2)}) %collective-permute-start.15) | collective-permute-done | bytes 294944 | tf_op jit(solution)/shard_map/ppermute | solution.py:483
  152.2 3.6 %collective-permute-start.19 = (bf16[96,384]{1,0:T(8,128)(2,1)S(1)}, bf16[96,384]{1,0:T(8,128)(2,1)S(1)}, u32[]{:S(2)}, u32[]{:S(2)}) collective-permute-start(bf16[96,384]{1,0:T(8,128)(2,1)S(1)} %get-tuple-element.114), channel_id=1, source_target_pairs={{0,16},{8,24},{16,32},{24,40},{32,48},{40,56},{48,0},{56,8},{64,80... | collective-permute-start | bytes 221192 | tf_op jit(solution)/shard_map/ppermute | solution.py:483
  155.9 7.4 %collective-permute-start.20 = (bf16[96,384]{1,0:T(8,128)(2,1)S(1)}, bf16[96,384]{1,0:T(8,128)(2,1)S(1)}, u32[]{:S(2)}, u32[]{:S(2)}) collective-permute-start(bf16[96,384]{1,0:T(8,128)(2,1)S(1)} %get-tuple-element.115), channel_id=1, source_target_pairs={{0,32},{8,40},{16,48},{24,56},{32,0},{40,8},{48,16},{56,24},{64,96... | collective-permute-start | bytes 221192 | tf_op jit(solution)/shard_map/ppermute | solution.py:483
  163.2 2.7 %collective-permute-start.21 = (bf16[96,384]{1,0:T(8,128)(2,1)S(1)}, bf16[96,384]{1,0:T(8,128)(2,1)S(1)}, u32[]{:S(2)}, u32[]{:S(2)}) collective-permute-start(bf16[96,384]{1,0:T(8,128)(2,1)S(1)} %get-tuple-element.116), channel_id=1, source_target_pairs={{0,48},{8,56},{16,0},{24,8},{32,16},{40,24},{48,32},{56,40},{64,11... | collective-permute-start | bytes 221192 | tf_op jit(solution)/shard_map/ppermute | solution.py:483
  166.0 7.1 %collective-permute-done.22.other_ref = bf16[128,1536]{1,0:T(8,128)(2,1)S(1)} collective-permute-done((bf16[128,1536]{1,0:T(8,128)(2,1)S(1)}, bf16[128,1536]{1,0:T(8,128)(2,1)S(1)}, u32[]{:S(2)}, u32[]{:S(2)}) %collective-permute-start.22) | collective-permute-done | bytes 393248 | tf_op jit(solution)/shard_map/ppermute | solution.py:499
  173.8 3.5 %gated_output.1 = bf16[128,3072]{1,0:T(8,128)(2,1)} custom-call(s32[1,3]{1,0:T(1,128)} %frames_ref.7, s32[1,3]{1,0:T(1,128)} %steps_ref.3, s32[1]{0:T(128)} %bitcast.1.seq_ref, f32[64,3072]{1,0:T(8,128)} %t1_ref.3, f32[64,3072]{1,0:T(8,128)} %t1_ref.3, bf16[128,3072]{1,0:T(8,128)(2,1)} %l1_ref.1, bf16[128,3072]{1,0:T(8,128)(2,1)} %l1_ref.1, ...), custom_call_target="tpu_custom_call" | custom-call | flops 3000000000 | bytes 9000000 | tf_op jit(solution)/shard_map/gated_output/pallas_call | solution.py:292
  177.3 6.5 %collective-permute-done.20 = bf16[96,384]{1,0:T(8,128)(2,1)S(1)} collective-permute-done((bf16[96,384]{1,0:T(8,128)(2,1)S(1)}, bf16[96,384]{1,0:T(8,128)(2,1)S(1)}, u32[]{:S(2)}, u32[]{:S(2)}) %collective-permute-start.20) | collective-permute-done | bytes 73760 | tf_op jit(solution)/shard_map/ppermute | solution.py:483
  183.9 4.0 %collective-permute-start.23 = (f32[96,384]{1,0:T(8,128)S(1)}, f32[96,384]{1,0:T(8,128)S(1)}, u32[]{:S(2)}, u32[]{:S(2)}) collective-permute-start(f32[96,384]{1,0:T(8,128)S(1)} %convert_add_fusion), channel_id=1, source_target_pairs={{0,0},{128,1},{2,2},{130,3},{4,4},{132,5},{6,6},{134,7},{8,8},{136... | collective-permute-start | bytes 442376 | tf_op jit(solution)/shard_map/ppermute | solution.py:559
  187.9 5.4 %collective-permute-done.23 = f32[96,384]{1,0:T(8,128)S(1)} collective-permute-done((f32[96,384]{1,0:T(8,128)S(1)}, f32[96,384]{1,0:T(8,128)S(1)}, u32[]{:S(2)}, u32[]{:S(2)}) %collective-permute-start.23) | collective-permute-done | bytes 147488 | tf_op jit(solution)/shard_map/ppermute | solution.py:559
  (85 shorter events, 30.2 us)
Async XLA Ops:
  7.2 71.6 %all-gather.2.cloned.1.call-start = ((), (), s32[]{:S(2)}) async-start(), calls=%async_computation.2 | async-start | bytes 2433024 | tf_op jit(solution)/shard_map/all_gather | solution.py:515
  7.2 8.0 %collective-permute-start = (bf16[96,384]{1,0:T(8,128)(2,1)}, bf16[96,384]{1,0:T(8,128)(2,1)S(1)}, u32[]{:S(2)}, u32[]{:S(2)}) collective-permute-start(bf16[96,384]{1,0:T(8,128)(2,1)} %bitcast.21), channel_id=1, source_target_pairs={{0,0},{1,128},{2,2},{3,130},{4,4},{5,132},{6,6},{7,134},{8,8},{9,1... | collective-permute-start | bytes 221192 | tf_op jit(solution)/shard_map/ppermute | solution.py:512
  15.8 10.6 %collective-permute-start.1 = (bf16[128,1536]{1,0:T(8,128)(2,1)}, bf16[128,1536]{1,0:T(8,128)(2,1)}, u32[]{:S(2)}, u32[]{:S(2)}) collective-permute-start(bf16[128,1536]{1,0:T(8,128)(2,1)} %get-tuple-element.68), channel_id=1, source_target_pairs={{0,1},{1,0},{2,3},{3,2},{4,5},{5,4},{6,7},{7,6},{8,9},{9,8},{10,11... | collective-permute-start | bytes 1179656 | tf_op jit(solution)/shard_map/ppermute | solution.py:499
  15.9 11.8 %collective-permute-start.3 = (bf16[128,1536]{1,0:T(8,128)(2,1)}, bf16[128,1536]{1,0:T(8,128)(2,1)}, u32[]{:S(2)}, u32[]{:S(2)}) collective-permute-start(bf16[128,1536]{1,0:T(8,128)(2,1)} %get-tuple-element.66.refs_0_), channel_id=1, source_target_pairs={{0,2},{1,3},{2,4},{3,5},{4,6},{5,7},{6,0},{7,1},{8,10},{9,11},{10,... | collective-permute-start | bytes 1179656 | tf_op jit(solution)/shard_map/ppermute | solution.py:483
  17.5 10.3 %collective-permute-start.2 = (bf16[128,1536]{1,0:T(8,128)(2,1)}, bf16[128,1536]{1,0:T(8,128)(2,1)S(1)}, u32[]{:S(2)}, u32[]{:S(2)}) collective-permute-start(bf16[128,1536]{1,0:T(8,128)(2,1)} %get-tuple-element.66.refs_0_), channel_id=1, source_target_pairs={{0,6},{1,7},{2,0},{3,1},{4,2},{5,3},{6,4},{7,5},{8,14},{9,15},{10,... | collective-permute-start | bytes 1179656 | tf_op jit(solution)/shard_map/ppermute | solution.py:483
  22.0 47.4 %copy-start.1 = (s32[1,3]{1,0:T(1,128)S(1)}, s32[1,3]{1,0:T(1,128)}, u32[]{:S(2)}) copy-start(s32[1,3]{1,0:T(1,128)} %frames_ref.7) | copy-start | bytes 40
  28.5 40.9 %all-to-all-start = ((bf16[8,3,128,384]{3,2,1,0:T(8,128)(2,1)}), bf16[8,3,128,384]{3,2,1,0:T(8,128)(2,1)S(1)}, u32[]{:S(2)}, u32[]{:S(2)}) async-start(bf16[8,3,128,384]{3,2,1,0:T(8,128)(2,1)} %pack_heads.1), calls=%async_computation | async-start | bytes 4718592 | tf_op jit(solution)/shard_map/all_to_all | solution.py:520
  34.3 33.6 %collective-permute-start.4 = (bf16[128,1536]{1,0:T(8,128)(2,1)}, bf16[128,1536]{1,0:T(8,128)(2,1)}, u32[]{:S(2)}, u32[]{:S(2)}) collective-permute-start(bf16[128,1536]{1,0:T(8,128)(2,1)} %collective-permute-done.1.refs_1_), channel_id=1, source_target_pairs={{0,6},{1,7},{2,0},{3,1},{4,2},{5,3},{6,4},{7,5},{8,14},{9,15},{10,... | collective-permute-start | bytes 1179656 | tf_op jit(solution)/shard_map/ppermute | solution.py:483
  37.0 41.5 %collective-permute-start.7 = (bf16[128,1536]{1,0:T(8,128)(2,1)}, bf16[128,1536]{1,0:T(8,128)(2,1)}, u32[]{:S(2)}, u32[]{:S(2)}) collective-permute-start(bf16[128,1536]{1,0:T(8,128)(2,1)} %collective-permute-done.1.refs_1_), channel_id=1, source_target_pairs={{0,2},{1,3},{2,4},{3,5},{4,6},{5,7},{6,0},{7,1},{8,10},{9,11},{10,... | collective-permute-start | bytes 1179656 | tf_op jit(solution)/shard_map/ppermute | solution.py:483
  37.0 41.5 %collective-permute-start.5 = (bf16[128,1536]{1,0:T(8,128)(2,1)}, bf16[128,1536]{1,0:T(8,128)(2,1)}, u32[]{:S(2)}, u32[]{:S(2)}) collective-permute-start(bf16[128,1536]{1,0:T(8,128)(2,1)} %collective-permute-done.3.refs_6_), channel_id=1, source_target_pairs={{0,2},{1,3},{2,4},{3,5},{4,6},{5,7},{6,0},{7,1},{8,10},{9,11},{10,... | collective-permute-start | bytes 1179656 | tf_op jit(solution)/shard_map/ppermute | solution.py:483
  67.9 10.8 %collective-permute-start.6 = (bf16[128,1536]{1,0:T(8,128)(2,1)}, bf16[128,1536]{1,0:T(8,128)(2,1)}, u32[]{:S(2)}, u32[]{:S(2)}) collective-permute-start(bf16[128,1536]{1,0:T(8,128)(2,1)} %collective-permute-done.4.refs_3_), channel_id=1, source_target_pairs={{0,6},{1,7},{2,0},{3,1},{4,2},{5,3},{6,4},{7,5},{8,14},{9,15},{10,... | collective-permute-start | bytes 1179656 | tf_op jit(solution)/shard_map/ppermute | solution.py:483
  76.9 20.8 %collective-permute-start.9 = (bf16[1024,384]{1,0:T(8,128)(2,1)}, bf16[1024,384]{1,0:T(8,128)(2,1)}, u32[]{:S(2)}, u32[]{:S(2)}) collective-permute-start(bf16[1024,384]{1,0:T(8,128)(2,1)} %get-tuple-element.76.a_ref), channel_id=1, source_target_pairs={{0,1},{1,0},{2,3},{3,2},{4,5},{5,4},{6,7},{7,6},{8,9},{9,8},{10,11... | collective-permute-start | bytes 2359304 | tf_op jit(solution)/shard_map/ppermute | solution.py:499
  87.6 25.0 %collective-permute-start.8 = (bf16[1024,384]{1,0:T(8,128)(2,1)S(1)}, bf16[1024,384]{1,0:T(8,128)(2,1)S(1)}, u32[]{:S(2)}, u32[]{:S(2)}) collective-permute-start(bf16[1024,384]{1,0:T(8,128)(2,1)S(1)} %get-tuple-element.74), channel_id=1, source_target_pairs={{0,1},{1,0},{2,3},{3,2},{4,5},{5,4},{6,7},{7,6},{8,9},{9,8},{10,11... | collective-permute-start | bytes 2359304 | tf_op jit(solution)/shard_map/ppermute | solution.py:499
  87.9 9.8 %copy-start.5 = (bf16[3072,384]{1,0:T(8,128)(2,1)S(1)}, bf16[3072,384]{1,0:T(8,128)(2,1)}, u32[]{:S(2)}) copy-start(bf16[3072,384]{1,0:T(8,128)(2,1)} %all-gather.2.cloned.1.call-done) | copy-start | bytes 7077892
  91.0 24.8 %collective-permute-start.12 = (bf16[8,96,384]{2,1,0:T(8,128)(2,1)S(1)}, bf16[8,96,384]{2,1,0:T(8,128)(2,1)S(1)}, u32[]{:S(2)}, u32[]{:S(2)}) collective-permute-start(bf16[8,96,384]{2,1,0:T(8,128)(2,1)S(1)} %get-tuple-element.89), channel_id=1, source_target_pairs={{0,8},{8,0},{16,24},{24,16},{32,40},{40,32},{48,56},{56,48},{64,72... | collective-permute-start | bytes 1769480 | tf_op jit(solution)/shard_map/ppermute | solution.py:503
  100.1 9.1 %collective-permute-start.10 = (bf16[128,1536]{1,0:T(8,128)(2,1)S(1)}, bf16[128,1536]{1,0:T(8,128)(2,1)S(1)}, u32[]{:S(2)}, u32[]{:S(2)}) collective-permute-start(bf16[128,1536]{1,0:T(8,128)(2,1)S(1)} %get-tuple-element.80), channel_id=1, source_target_pairs={{0,2},{1,3},{2,4},{3,5},{4,6},{5,7},{6,0},{7,1},{8,10},{9,11},{10,... | collective-permute-start | bytes 1179656 | tf_op jit(solution)/shard_map/ppermute | solution.py:483
  100.7 8.5 %collective-permute-start.11 = (bf16[128,1536]{1,0:T(8,128)(2,1)S(1)}, bf16[128,1536]{1,0:T(8,128)(2,1)S(1)}, u32[]{:S(2)}, u32[]{:S(2)}) collective-permute-start(bf16[128,1536]{1,0:T(8,128)(2,1)S(1)} %get-tuple-element.84), channel_id=1, source_target_pairs={{0,6},{1,7},{2,0},{3,1},{4,2},{5,3},{6,4},{7,5},{8,14},{9,15},{10,... | collective-permute-start | bytes 1179656 | tf_op jit(solution)/shard_map/ppermute | solution.py:483
  106.3 9.5 %collective-permute-start.13 = (bf16[8,96,384]{2,1,0:T(8,128)(2,1)S(1)}, bf16[8,96,384]{2,1,0:T(8,128)(2,1)S(1)}, u32[]{:S(2)}, u32[]{:S(2)}) collective-permute-start(bf16[8,96,384]{2,1,0:T(8,128)(2,1)S(1)} %get-tuple-element.91), channel_id=1, source_target_pairs={{0,8},{8,0},{16,24},{24,16},{32,40},{40,32},{48,56},{56,48},{64,72... | collective-permute-start | bytes 1769480 | tf_op jit(solution)/shard_map/ppermute | solution.py:503
  112.6 18.9 %collective-permute-start.17 = (bf16[256,1536]{1,0:T(8,128)(2,1)S(1)}, bf16[256,1536]{1,0:T(8,128)(2,1)S(1)}, u32[]{:S(2)}, u32[]{:S(2)}) collective-permute-start(bf16[256,1536]{1,0:T(8,128)(2,1)S(1)} %get-tuple-element.104), channel_id=1, source_target_pairs={{0,2},{1,3},{2,4},{3,5},{4,6},{5,7},{6,0},{7,1},{8,10},{9,11},{10,... | collective-permute-start | bytes 2359304 | tf_op jit(solution)/shard_map/ppermute | solution.py:483
  113.2 19.2 %collective-permute-start.18 = (bf16[256,1536]{1,0:T(8,128)(2,1)S(1)}, bf16[256,1536]{1,0:T(8,128)(2,1)S(1)}, u32[]{:S(2)}, u32[]{:S(2)}) collective-permute-start(bf16[256,1536]{1,0:T(8,128)(2,1)S(1)} %get-tuple-element.105), channel_id=1, source_target_pairs={{0,6},{1,7},{2,0},{3,1},{4,2},{5,3},{6,4},{7,5},{8,14},{9,15},{10,... | collective-permute-start | bytes 2359304 | tf_op jit(solution)/shard_map/ppermute | solution.py:483
  118.4 7.5 %copy-start.19 = (bf16[4,96,384]{2,1,0:T(8,128)(2,1)}, bf16[4,96,384]{2,1,0:T(8,128)(2,1)S(1)}, u32[]{:S(2)}) copy-start(bf16[4,96,384]{2,1,0:T(8,128)(2,1)S(1)} %get-tuple-element.109.a_ref) | copy-start | bytes 884740
  127.2 14.2 %copy-start.15 = (bf16[4,96,384]{2,1,0:T(8,128)(2,1)S(1)}, bf16[4,96,384]{2,1,0:T(8,128)(2,1)}, u32[]{:S(2)}) copy-start(bf16[4,96,384]{2,1,0:T(8,128)(2,1)} %copy-done.14) | copy-start | bytes 884740
  133.3 9.5 %copy-start.8 = (bf16[256,1536]{1,0:T(8,128)(2,1)S(1)}, bf16[256,1536]{1,0:T(8,128)(2,1)}, u32[]{:S(2)}) copy-start(bf16[256,1536]{1,0:T(8,128)(2,1)} %copy-done.7) | copy-start | bytes 2359300
  133.3 60.0 %all-to-all-start.1 = ((bf16[8,3,128,384]{3,2,1,0:T(8,128)(2,1)}), bf16[8,3,128,384]{3,2,1,0:T(8,128)(2,1)S(1)}, u32[]{:S(2)}, u32[]{:S(2)}) async-start(bf16[8,3,128,384]{3,2,1,0:T(8,128)(2,1)} %copy-done), calls=%async_computation.1 | async-start | bytes 4718592 | tf_op jit(solution)/shard_map/all_to_all | solution.py:548
  138.2 10.2 %collective-permute-start.14 = (bf16[4,96,384]{2,1,0:T(8,128)(2,1)}, bf16[4,96,384]{2,1,0:T(8,128)(2,1)S(1)}, u32[]{:S(2)}, u32[]{:S(2)}) collective-permute-start(bf16[4,96,384]{2,1,0:T(8,128)(2,1)} %copy-done.17), channel_id=1, source_target_pairs={{0,64},{8,72},{16,80},{24,88},{32,96},{40,104},{48,112},{56,120},{... | collective-permute-start | bytes 884744 | tf_op jit(solution)/shard_map/ppermute | solution.py:483
  138.3 13.2 %collective-permute-start.15 = (bf16[4,96,384]{2,1,0:T(8,128)(2,1)}, bf16[4,96,384]{2,1,0:T(8,128)(2,1)S(1)}, u32[]{:S(2)}, u32[]{:S(2)}) collective-permute-start(bf16[4,96,384]{2,1,0:T(8,128)(2,1)} %copy-done.16), channel_id=1, source_target_pairs={{0,128},{8,136},{16,144},{24,152},{32,160},{40,168},{48,176},{56,1... | collective-permute-start | bytes 884744 | tf_op jit(solution)/shard_map/ppermute | solution.py:483
  141.5 10.6 %collective-permute-start.16 = (bf16[4,96,384]{2,1,0:T(8,128)(2,1)S(1)}, bf16[4,96,384]{2,1,0:T(8,128)(2,1)S(1)}, u32[]{:S(2)}, u32[]{:S(2)}) collective-permute-start(bf16[4,96,384]{2,1,0:T(8,128)(2,1)S(1)} %copy-done.15), channel_id=1, source_target_pairs={{0,192},{8,200},{16,208},{24,216},{32,224},{40,232},{48,240},{56,2... | collective-permute-start | bytes 884744 | tf_op jit(solution)/shard_map/ppermute | solution.py:483
  148.2 24.9 %collective-permute-start.22 = (bf16[128,1536]{1,0:T(8,128)(2,1)S(1)}, bf16[128,1536]{1,0:T(8,128)(2,1)S(1)}, u32[]{:S(2)}, u32[]{:S(2)}) collective-permute-start(bf16[128,1536]{1,0:T(8,128)(2,1)S(1)} %get-tuple-element.118), channel_id=1, source_target_pairs={{0,1},{1,0},{2,3},{3,2},{4,5},{5,4},{6,7},{7,6},{8,9},{9,8},{10,11... | collective-permute-start | bytes 1179656 | tf_op jit(solution)/shard_map/ppermute | solution.py:499
  152.2 25.1 %collective-permute-start.19 = (bf16[96,384]{1,0:T(8,128)(2,1)S(1)}, bf16[96,384]{1,0:T(8,128)(2,1)S(1)}, u32[]{:S(2)}, u32[]{:S(2)}) collective-permute-start(bf16[96,384]{1,0:T(8,128)(2,1)S(1)} %get-tuple-element.114), channel_id=1, source_target_pairs={{0,16},{8,24},{16,32},{24,40},{32,48},{40,56},{48,0},{56,8},{64,80... | collective-permute-start | bytes 221192 | tf_op jit(solution)/shard_map/ppermute | solution.py:483
  155.9 28.0 %collective-permute-start.20 = (bf16[96,384]{1,0:T(8,128)(2,1)S(1)}, bf16[96,384]{1,0:T(8,128)(2,1)S(1)}, u32[]{:S(2)}, u32[]{:S(2)}) collective-permute-start(bf16[96,384]{1,0:T(8,128)(2,1)S(1)} %get-tuple-element.115), channel_id=1, source_target_pairs={{0,32},{8,40},{16,48},{24,56},{32,0},{40,8},{48,16},{56,24},{64,96... | collective-permute-start | bytes 221192 | tf_op jit(solution)/shard_map/ppermute | solution.py:483
  163.2 20.6 %collective-permute-start.21 = (bf16[96,384]{1,0:T(8,128)(2,1)S(1)}, bf16[96,384]{1,0:T(8,128)(2,1)S(1)}, u32[]{:S(2)}, u32[]{:S(2)}) collective-permute-start(bf16[96,384]{1,0:T(8,128)(2,1)S(1)} %get-tuple-element.116), channel_id=1, source_target_pairs={{0,48},{8,56},{16,0},{24,8},{32,16},{40,24},{48,32},{56,40},{64,11... | collective-permute-start | bytes 221192 | tf_op jit(solution)/shard_map/ppermute | solution.py:483
  183.9 9.4 %collective-permute-start.23 = (f32[96,384]{1,0:T(8,128)S(1)}, f32[96,384]{1,0:T(8,128)S(1)}, u32[]{:S(2)}, u32[]{:S(2)}) collective-permute-start(f32[96,384]{1,0:T(8,128)S(1)} %convert_add_fusion), channel_id=1, source_target_pairs={{0,0},{128,1},{2,2},{130,3},{4,4},{132,5},{6,6},{134,7},{8,8},{136... | collective-permute-start | bytes 442376 | tf_op jit(solution)/shard_map/ppermute | solution.py:559
  (18 other events, 28.5 us)
Sparse Core Ops, SparseCore 0:
  15.9 60.1 all-gather.1

commit v8 on v7

--- a/solution.py
+++ b/solution.py
@@ -544,19 +544,19 @@
     terms = [terms[0]] + [along_y(terms[k], k) for k in range(1, 4)]
 
     grads = attention_backward(frames, heads, d_own, d_recv, p1, p2)
-    grads, c1, c3 = lax.optimization_barrier((grads, c1, c3))
-    grads = lax.all_to_all(grads, "seq", split_axis=0, concat_axis=0, tiled=True)
-
-    o_keep, o_send = project_home(seq, attn, attn_other, weights, c1, c3)
-    o_got = swap_z(o_send)
-    terms, o_keep = lax.optimization_barrier((terms, o_keep))
+    terms, grads = lax.optimization_barrier((terms, grads))
     terms = ring_sum(dp, terms)
     terms = [terms[0]] + [along_z(terms[k], k) for k in range(1, 4)]
-    output = gated_output(frames, timesteps, seq, gate_table, latents, o_keep, o_got)
-    terms, output = lax.optimization_barrier((terms, output))
+    o_keep, o_send = project_home(seq, attn, attn_other, weights, c1, c3)
+    grads, o_send, terms = lax.optimization_barrier((grads, o_send, terms))
+    o_got = swap_z(o_send)
+    grads = lax.all_to_all(grads, "seq", split_axis=0, concat_axis=0, tiled=True)
+
     total = terms[0].astype(F32) + terms[1].astype(F32)
     total = total + terms[2].astype(F32) + terms[3].astype(F32)
     total = lax.ppermute(total, both, [(b, a) for a, b in moves])
+    total, o_got = lax.optimization_barrier((total, o_got))
+    output = gated_output(frames, timesteps, seq, gate_table, latents, o_keep, o_got)
     grad_qkv = unpack_heads(grads)
     return (output, grad_qkv.transpose(1, 0, 2), total.T)
 

time: 203 us -> 205 us (level)
  local copies, waits for them, and re-layouts: 16.1 us -> 8.79 us
  waiting for transfers between devices: 72.8 us -> 78.9 us
    ppermute x1, waiting for transfers between devices: 5.41 us -> 32.3 us  [body(): total = lax.ppermute(total, both, [(b, a) for a, b in moves])]
    ppermute x16, waiting for transfers between devices: 48.8 us -> 35.1 us  [along(): return lax.ppermute(x, axis, moves)]
    unnamed x47 -> x23, local copies, waits for them, and re-layouts: 16.1 us -> 8.79 us
    ppermute x4, waiting for transfers between devices: 18.2 us -> 11.1 us  [swap_z(): lax.ppermute(x, 'seq', [(i, i ^ 1) for i in range(lax.axis_size('seq'))])]
  transfers between devices with their start and end apart: 27 -> 27, of which waited for: 14 -> 11; matrix products, arithmetic and copies ran while one was open for 0% -> 0% of each run, Pallas kernels for 21% -> 22%
where the time goes in v8:
time: 205 us; the launch traced here: 203 us
  waiting for transfers between devices  78.9 us (38%)
  starting transfers between devices  55.7 us (27%)
  Pallas kernels  45.6 us (22%)
  between operations  14.2 us (7%)
  local copies, waits for them, and re-layouts  8.79 us (4%)
    ppermute x16, waiting for transfers between devices, along(): return lax.ppermute(x, axis, moves)  35.1 us
    ppermute x16, starting transfers between devices, along(): return lax.ppermute(x, axis, moves)  33.1 us
    ppermute x1, waiting for transfers between devices, body(): total = lax.ppermute(total, both, [(b, a) for a, b in moves])  32.3 us
    ppermute x4, waiting for transfers between devices, swap_z(): lax.ppermute(x, 'seq', [(i, i ^ 1) for i in range(lax.axis_size('seq'))])  11.1 us
    pallas_call x1, Pallas kernels, attention_backward(): pl.pallas_call(bwd_kernel, out_shape=shape((8, 3, 128, 3 * HD)), in_specs...  8.96 us
    unnamed x23, local copies, waits for them, and re-layouts  8.79 us
    pallas_call x2, Pallas kernels, dweight_part(): pl.pallas_call(dweight_kernel, out_shape=(shape((8, 96, 384)), shape((8,...  6.05 us
    pallas_call x1, Pallas kernels, attention_forward(): pl.pallas_call(fwd_kernel, out_shape=(shape((1024, 3 * HD)), shape((3, LO...  6.02 us
  transfers between devices with their start and end apart: 27, of which 11 were waited for; matrix products, arithmetic and copies ran while one was open for 0% of the time, Pallas kernels for 22%

profile of v8, /device:TPU:32, one launch (start us, length us, event | category | flops | bytes accessed | tf_op | source)
XLA Modules:
  0.0 203.2 jit_solution(14185202733742331265)
XLA Ops:
  7.2 4.6 %collective-permute-start = (bf16[96,384]{1,0:T(8,128)(2,1)}, bf16[96,384]{1,0:T(8,128)(2,1)S(1)}, u32[]{:S(2)}, u32[]{:S(2)}) collective-permute-start(bf16[96,384]{1,0:T(8,128)(2,1)} %bitcast.21), channel_id=1, source_target_pairs={{0,0},{1,128},{2,2},{3,130},{4,4},{5,132},{6,6},{7,134},{8,8},{9,1... | collective-permute-start | bytes 221192 | tf_op jit(solution)/shard_map/ppermute | solution.py:512
  11.9 3.0 %gated_cotangent.1 = (bf16[128,1536]{1,0:T(8,128)(2,1)}, bf16[128,1536]{1,0:T(8,128)(2,1)}) custom-call(s32[1,3]{1,0:T(1,128)} %frames_ref.7, s32[1,3]{1,0:T(1,128)} %steps_ref.3, s32[1]{0:T(128)} %bitcast.seq_ref, f32[64,3072]{1,0:T(8,128)} %t1_ref.3, f32[64,3072]{1,0:T(8,128)} %t1_ref.3, bf16[128,3072]{1,0:T(8,128)(2,1)} %c1_ref.1, bf16[128,3072]{1,0:T(8,128)(2,1)} %c1_ref.1), custom_call_target="tpu_custom_call" | custom-call | flops 3000000000 | bytes 9000000 | tf_op jit(solution)/shard_map/gated_cotangent/pallas_call | solution.py:259
  15.9 1.6 collective-permute-start.3
  17.5 1.7 collective-permute-start.2
  19.2 2.8 %pack_heads.1 = bf16[8,3,128,384]{3,2,1,0:T(8,128)(2,1)} custom-call(bf16[3,128,3072]{2,1,0:T(8,128)(2,1)} %bitcast.20), custom_call_target="tpu_custom_call" | custom-call | flops 3000000000 | bytes 9000000 | tf_op jit(solution)/shard_map/pack_heads/pallas_call | solution.py:218
  22.0 4.5 %collective-permute-done.1.refs_1_ = bf16[128,1536]{1,0:T(8,128)(2,1)} collective-permute-done((bf16[128,1536]{1,0:T(8,128)(2,1)}, bf16[128,1536]{1,0:T(8,128)(2,1)}, u32[]{:S(2)}, u32[]{:S(2)}) %collective-permute-start.1) | collective-permute-done | bytes 393248 | tf_op jit(solution)/shard_map/ppermute | solution.py:499
  28.6 5.8 %all-to-all-start = ((bf16[8,3,128,384]{3,2,1,0:T(8,128)(2,1)}), bf16[8,3,128,384]{3,2,1,0:T(8,128)(2,1)S(1)}, u32[]{:S(2)}, u32[]{:S(2)}) async-start(bf16[8,3,128,384]{3,2,1,0:T(8,128)(2,1)} %pack_heads.1), calls=%async_computation | async-start | bytes 4718592 | tf_op jit(solution)/shard_map/all_to_all | solution.py:520
  34.3 2.7 %collective-permute-start.5 = (bf16[128,1536]{1,0:T(8,128)(2,1)}, bf16[128,1536]{1,0:T(8,128)(2,1)}, u32[]{:S(2)}, u32[]{:S(2)}) collective-permute-start(bf16[128,1536]{1,0:T(8,128)(2,1)} %collective-permute-done.1.refs_1_), channel_id=1, source_target_pairs={{0,6},{1,7},{2,0},{3,1},{4,2},{5,3},{6,4},{7,5},{8,14},{9,15},{10,... | collective-permute-start | bytes 1179656 | tf_op jit(solution)/shard_map/ppermute | solution.py:483
  37.8 30.1 %collective-permute-done.5.refs_3_ = bf16[128,1536]{1,0:T(8,128)(2,1)} collective-permute-done((bf16[128,1536]{1,0:T(8,128)(2,1)}, bf16[128,1536]{1,0:T(8,128)(2,1)}, u32[]{:S(2)}, u32[]{:S(2)}) %collective-permute-start.5) | collective-permute-done | bytes 393248 | tf_op jit(solution)/shard_map/ppermute | solution.py:483
  69.4 6.0 %attention_forward.1 = (bf16[1024,384]{1,0:T(8,128)(2,1)}, bf16[3,640,640]{2,1,0:T(8,128)(2,1)S(1)}, bf16[3,384,384]{2,1,0:T(8,128)(2,1)S(1)}) custom-call(s32[1,3]{1,0:T(1,128)S(1)} %copy-done, bf16[8,3,128,384]{3,2,1,0:T(8,128)(2,1)S(1)} %all-to-all-done.qkv_ref), custom_call_target="tpu_custom_call" | custom-call | flops 100000000 | bytes 300000 | tf_op jit(solution)/shard_map/attention_forward/pallas_call | solution.py:133
  76.9 1.6 collective-permute-start.4
  78.7 1.7 copy-done.3
  82.4 5.2 %dattn_parts.1 = (bf16[1024,1536]{1,0:T(8,128)(2,1)S(1)}, bf16[1024,384]{1,0:T(8,128)(2,1)S(1)}, f32[1024,384]{1,0:T(8,128)S(1)}) custom-call(s32[1]{0:T(128)} %bitcast.seq_ref, bf16[128,1536]{1,0:T(8,128)(2,1)S(1)} %copy-done.5, bf16[128,1536]{1,0:T(8,128)(2,1)} %collective-permute-done.1.refs_1_, bf16[128,1536]{1,0:T(8,128)(2,1)S(1)} %copy-done.7, ...), custom_call_target="tpu_custom_call" | custom-call | flops 7000000000 | bytes 21000000 | tf_op jit(solution)/shard_map/dattn_parts/pallas_call | solution.py:320
  87.9 3.1 %dweight_part.2 = (bf16[8,96,384]{2,1,0:T(8,128)(2,1)S(1)}, bf16[8,96,384]{2,1,0:T(8,128)(2,1)S(1)}) custom-call(s32[1]{0:T(128)} %bitcast.3.dp_ref, bf16[1024,1536]{1,0:T(8,128)(2,1)S(1)} %get-tuple-element.81.d_ref, bf16[1024,384]{1,0:T(8,128)(2,1)} %get-tuple-element.70.a_ref), custom_call_target="tpu_custom_call" | custom-call | flops 4000000000 | bytes 12000000 | tf_op jit(solution)/shard_map/dweight_part/pallas_call | solution.py:409
  91.3 6.4 %collective-permute-done.4.b_ref.a_ref = bf16[1024,384]{1,0:T(8,128)(2,1)} collective-permute-done((bf16[1024,384]{1,0:T(8,128)(2,1)}, bf16[1024,384]{1,0:T(8,128)(2,1)}, u32[]{:S(2)}, u32[]{:S(2)}) %collective-permute-start.4) | collective-permute-done | bytes 786464 | tf_op jit(solution)/shard_map/ppermute | solution.py:499
  97.7 2.4 %project_far.1 = (bf16[128,1536]{1,0:T(8,128)(2,1)S(1)}, bf16[128,1536]{1,0:T(8,128)(2,1)S(1)}) custom-call(s32[1]{0:T(128)} %bitcast.seq_ref, bf16[1024,384]{1,0:T(8,128)(2,1)} %get-tuple-element.70.a_ref, bf16[1024,384]{1,0:T(8,128)(2,1)} %collective-permute-done.4.b_ref.a_ref, bf16[2,1536,384]{2,1,0:T(8,128)(2,1)S(1)} %bitcast.12), custom_call_target="tpu_custom_call" | custom-call | flops 3000000000 | bytes 9000000 | tf_op jit(solution)/shard_map/project_far/pallas_call | solution.py:378
  100.7 2.7 %collective-permute-start.11 = (bf16[128,1536]{1,0:T(8,128)(2,1)S(1)}, bf16[128,1536]{1,0:T(8,128)(2,1)S(1)}, u32[]{:S(2)}, u32[]{:S(2)}) collective-permute-start(bf16[128,1536]{1,0:T(8,128)(2,1)S(1)} %get-tuple-element.84), channel_id=1, source_target_pairs={{0,6},{1,7},{2,0},{3,1},{4,2},{5,3},{6,4},{7,5},{8,14},{9,15},{10,... | collective-permute-start | bytes 1179656 | tf_op jit(solution)/shard_map/ppermute | solution.py:483
  103.4 3.0 %dweight_part.3 = (bf16[8,96,384]{2,1,0:T(8,128)(2,1)S(1)}, bf16[8,96,384]{2,1,0:T(8,128)(2,1)S(1)}) custom-call(s32[1]{0:T(128)} %bitcast.3.dp_ref, bf16[1024,1536]{1,0:T(8,128)(2,1)S(1)} %get-tuple-element.81.d_ref, bf16[1024,384]{1,0:T(8,128)(2,1)} %collective-permute-done.4.b_ref.a_ref), custom_call_target="tpu_custom_call" | custom-call | flops 4000000000 | bytes 12000000 | tf_op jit(solution)/shard_map/dweight_part/pallas_call | solution.py:409
  106.4 2.7 %collective-permute-done.10.up_ref = bf16[128,1536]{1,0:T(8,128)(2,1)S(1)} collective-permute-done((bf16[128,1536]{1,0:T(8,128)(2,1)S(1)}, bf16[128,1536]{1,0:T(8,128)(2,1)S(1)}, u32[]{:S(2)}, u32[]{:S(2)}) %collective-permute-start.10) | collective-permute-done | bytes 393248 | tf_op jit(solution)/shard_map/ppermute | solution.py:483
  109.1 3.2 %project_near.1 = (bf16[256,1536]{1,0:T(8,128)(2,1)S(1)}, bf16[256,1536]{1,0:T(8,128)(2,1)S(1)}) custom-call(s32[1]{0:T(128)} %bitcast.seq_ref, bf16[1024,384]{1,0:T(8,128)(2,1)} %get-tuple-element.70.a_ref, bf16[1024,384]{1,0:T(8,128)(2,1)} %collective-permute-done.4.b_ref.a_ref, bf16[2,1536,384]{2,1,0:T(8,128)(2,1)S(1)} %bitcast.13, ...), custom_call_target="tpu_custom_call" | custom-call | flops 3000000000 | bytes 9000000 | tf_op jit(solution)/shard_map/project_near/pallas_call | solution.py:384
  113.2 2.6 %collective-permute-start.13 = (bf16[256,1536]{1,0:T(8,128)(2,1)S(1)}, bf16[256,1536]{1,0:T(8,128)(2,1)S(1)}, u32[]{:S(2)}, u32[]{:S(2)}) collective-permute-start(bf16[256,1536]{1,0:T(8,128)(2,1)S(1)} %get-tuple-element.88), channel_id=1, source_target_pairs={{0,6},{1,7},{2,0},{3,1},{4,2},{5,3},{6,4},{7,5},{8,14},{9,15},{10,... | collective-permute-start | bytes 2359304 | tf_op jit(solution)/shard_map/ppermute | solution.py:483
  116.7 3.3 %collective-permute-start.17 = (bf16[4,96,384]{2,1,0:T(8,128)(2,1)S(1)}, bf16[4,96,384]{2,1,0:T(8,128)(2,1)S(1)}, u32[]{:S(2)}, u32[]{:S(2)}) collective-permute-start(bf16[4,96,384]{2,1,0:T(8,128)(2,1)S(1)} %get-tuple-element.101), channel_id=1, source_target_pairs={{0,128},{8,136},{16,144},{24,152},{32,160},{40,168},{48,176},{56,1... | collective-permute-start | bytes 884744 | tf_op jit(solution)/shard_map/ppermute | solution.py:483
  121.3 9.0 %attention_backward.1 = bf16[8,3,128,384]{3,2,1,0:T(8,128)(2,1)} custom-call(s32[1,3]{1,0:T(1,128)S(1)} %copy-done, bf16[8,3,128,384]{3,2,1,0:T(8,128)(2,1)S(1)} %all-to-all-done.qkv_ref, f32[1024,384]{1,0:T(8,128)S(1)} %get-tuple-element.103.own_ref, bf16[1024,384]{1,0:T(8,128)(2,1)S(1)} %collective-permute-done.9.other_ref, ...), custom_call_target="tpu_custom_call" | custom-call | flops 10000000000 | bytes 30000000 | tf_op jit(solution)/shard_map/attention_backward/pallas_call | solution.py:195
  131.2 3.9 %collective-permute-start.19 = (bf16[96,384]{1,0:T(8,128)(2,1)S(1)}, bf16[96,384]{1,0:T(8,128)(2,1)S(1)}, u32[]{:S(2)}, u32[]{:S(2)}) collective-permute-start(bf16[96,384]{1,0:T(8,128)(2,1)S(1)} %get-tuple-element.114), channel_id=1, source_target_pairs={{0,16},{8,24},{16,32},{24,40},{32,48},{40,56},{48,0},{56,8},{64,80... | collective-permute-start | bytes 221192 | tf_op jit(solution)/shard_map/ppermute | solution.py:483
  135.1 6.5 %collective-permute-start.20 = (bf16[96,384]{1,0:T(8,128)(2,1)S(1)}, bf16[96,384]{1,0:T(8,128)(2,1)S(1)}, u32[]{:S(2)}, u32[]{:S(2)}) collective-permute-start(bf16[96,384]{1,0:T(8,128)(2,1)S(1)} %get-tuple-element.115), channel_id=1, source_target_pairs={{0,32},{8,40},{16,48},{24,56},{32,0},{40,8},{48,16},{56,24},{64,96... | collective-permute-start | bytes 221192 | tf_op jit(solution)/shard_map/ppermute | solution.py:483
  141.6 2.7 %collective-permute-start.21 = (bf16[96,384]{1,0:T(8,128)(2,1)S(1)}, bf16[96,384]{1,0:T(8,128)(2,1)S(1)}, u32[]{:S(2)}, u32[]{:S(2)}) collective-permute-start(bf16[96,384]{1,0:T(8,128)(2,1)S(1)} %get-tuple-element.116), channel_id=1, source_target_pairs={{0,48},{8,56},{16,0},{24,8},{32,16},{40,24},{48,32},{56,40},{64,11... | collective-permute-start | bytes 221192 | tf_op jit(solution)/shard_map/ppermute | solution.py:483
  144.3 2.5 %project_home.1 = (f32[128,1536]{1,0:T(8,128)S(1)}, bf16[128,1536]{1,0:T(8,128)(2,1)S(1)}) custom-call(s32[1]{0:T(128)} %bitcast.seq_ref, bf16[1024,384]{1,0:T(8,128)(2,1)} %get-tuple-element.70.a_ref, bf16[1024,384]{1,0:T(8,128)(2,1)} %collective-permute-done.4.b_ref.a_ref, bf16[2,1536,384]{2,1,0:T(8,128)(2,1)S(1)} %bitcast.14, ...), custom_call_target="tpu_custom_call" | custom-call | flops 3000000000 | bytes 9000000 | tf_op jit(solution)/shard_map/project_home/pallas_call | solution.py:395
  147.7 5.6 %all-to-all-start.1 = ((bf16[8,3,128,384]{3,2,1,0:T(8,128)(2,1)}), bf16[8,3,128,384]{3,2,1,0:T(8,128)(2,1)S(1)}, u32[]{:S(2)}, u32[]{:S(2)}) async-start(bf16[8,3,128,384]{3,2,1,0:T(8,128)(2,1)} %attention_backward.1), calls=%async_computation.1 | async-start | bytes 4718592 | tf_op jit(solution)/shard_map/all_to_all | solution.py:553
  153.5 4.0 %collective-permute-start.22 = (f32[96,384]{1,0:T(8,128)S(1)}, f32[96,384]{1,0:T(8,128)S(1)}, u32[]{:S(2)}, u32[]{:S(2)}) collective-permute-start(f32[96,384]{1,0:T(8,128)S(1)} %convert_add_fusion), channel_id=1, source_target_pairs={{0,0},{128,1},{2,2},{130,3},{4,4},{132,5},{6,6},{134,7},{8,8},{136... | collective-permute-start | bytes 442376 | tf_op jit(solution)/shard_map/ppermute | solution.py:557
  157.5 32.3 %collective-permute-done.22 = f32[96,384]{1,0:T(8,128)S(1)} collective-permute-done((f32[96,384]{1,0:T(8,128)S(1)}, f32[96,384]{1,0:T(8,128)S(1)}, u32[]{:S(2)}, u32[]{:S(2)}) %collective-permute-start.22) | collective-permute-done | bytes 147488 | tf_op jit(solution)/shard_map/ppermute | solution.py:557
  190.5 3.5 %gated_output.1 = bf16[128,3072]{1,0:T(8,128)(2,1)} custom-call(s32[1,3]{1,0:T(1,128)} %frames_ref.7, s32[1,3]{1,0:T(1,128)} %steps_ref.3, s32[1]{0:T(128)} %bitcast.seq_ref, f32[64,3072]{1,0:T(8,128)} %t1_ref.3, f32[64,3072]{1,0:T(8,128)} %t1_ref.3, bf16[128,3072]{1,0:T(8,128)(2,1)} %l1_ref.1, bf16[128,3072]{1,0:T(8,128)(2,1)} %l1_ref.1, ...), custom_call_target="tpu_custom_call" | custom-call | flops 3000000000 | bytes 9000000 | tf_op jit(solution)/shard_map/gated_output/pallas_call | solution.py:292
  194.0 1.6 unpack_heads.1
  (61 shorter events, 17.0 us)
Async XLA Ops:
  7.2 71.6 %all-gather.2.cloned.1.call-start = ((), (), s32[]{:S(2)}) async-start(), calls=%async_computation.2 | async-start | bytes 2433024 | tf_op jit(solution)/shard_map/all_gather | solution.py:515
  7.2 8.0 %collective-permute-start = (bf16[96,384]{1,0:T(8,128)(2,1)}, bf16[96,384]{1,0:T(8,128)(2,1)S(1)}, u32[]{:S(2)}, u32[]{:S(2)}) collective-permute-start(bf16[96,384]{1,0:T(8,128)(2,1)} %bitcast.21), channel_id=1, source_target_pairs={{0,0},{1,128},{2,2},{3,130},{4,4},{5,132},{6,6},{7,134},{8,8},{9,1... | collective-permute-start | bytes 221192 | tf_op jit(solution)/shard_map/ppermute | solution.py:512
  15.8 10.6 %collective-permute-start.1 = (bf16[128,1536]{1,0:T(8,128)(2,1)}, bf16[128,1536]{1,0:T(8,128)(2,1)}, u32[]{:S(2)}, u32[]{:S(2)}) collective-permute-start(bf16[128,1536]{1,0:T(8,128)(2,1)} %get-tuple-element.67), channel_id=1, source_target_pairs={{0,1},{1,0},{2,3},{3,2},{4,5},{5,4},{6,7},{7,6},{8,9},{9,8},{10,11... | collective-permute-start | bytes 1179656 | tf_op jit(solution)/shard_map/ppermute | solution.py:499
  15.9 11.8 %collective-permute-start.3 = (bf16[128,1536]{1,0:T(8,128)(2,1)}, bf16[128,1536]{1,0:T(8,128)(2,1)}, u32[]{:S(2)}, u32[]{:S(2)}) collective-permute-start(bf16[128,1536]{1,0:T(8,128)(2,1)} %get-tuple-element.68.refs_0_), channel_id=1, source_target_pairs={{0,2},{1,3},{2,4},{3,5},{4,6},{5,7},{6,0},{7,1},{8,10},{9,11},{10,... | collective-permute-start | bytes 1179656 | tf_op jit(solution)/shard_map/ppermute | solution.py:483
  17.5 10.3 %collective-permute-start.2 = (bf16[128,1536]{1,0:T(8,128)(2,1)}, bf16[128,1536]{1,0:T(8,128)(2,1)S(1)}, u32[]{:S(2)}, u32[]{:S(2)}) collective-permute-start(bf16[128,1536]{1,0:T(8,128)(2,1)} %get-tuple-element.68.refs_0_), channel_id=1, source_target_pairs={{0,6},{1,7},{2,0},{3,1},{4,2},{5,3},{6,4},{7,5},{8,14},{9,15},{10,... | collective-permute-start | bytes 1179656 | tf_op jit(solution)/shard_map/ppermute | solution.py:483
  22.0 47.4 %copy-start = (s32[1,3]{1,0:T(1,128)S(1)}, s32[1,3]{1,0:T(1,128)}, u32[]{:S(2)}) copy-start(s32[1,3]{1,0:T(1,128)} %frames_ref.7) | copy-start | bytes 40
  28.6 40.9 %all-to-all-start = ((bf16[8,3,128,384]{3,2,1,0:T(8,128)(2,1)}), bf16[8,3,128,384]{3,2,1,0:T(8,128)(2,1)S(1)}, u32[]{:S(2)}, u32[]{:S(2)}) async-start(bf16[8,3,128,384]{3,2,1,0:T(8,128)(2,1)} %pack_heads.1), calls=%async_computation | async-start | bytes 4718592 | tf_op jit(solution)/shard_map/all_to_all | solution.py:520
  34.3 33.6 %collective-permute-start.5 = (bf16[128,1536]{1,0:T(8,128)(2,1)}, bf16[128,1536]{1,0:T(8,128)(2,1)}, u32[]{:S(2)}, u32[]{:S(2)}) collective-permute-start(bf16[128,1536]{1,0:T(8,128)(2,1)} %collective-permute-done.1.refs_1_), channel_id=1, source_target_pairs={{0,6},{1,7},{2,0},{3,1},{4,2},{5,3},{6,4},{7,5},{8,14},{9,15},{10,... | collective-permute-start | bytes 1179656 | tf_op jit(solution)/shard_map/ppermute | solution.py:483
  37.0 41.5 %collective-permute-start.8 = (bf16[128,1536]{1,0:T(8,128)(2,1)}, bf16[128,1536]{1,0:T(8,128)(2,1)}, u32[]{:S(2)}, u32[]{:S(2)}) collective-permute-start(bf16[128,1536]{1,0:T(8,128)(2,1)} %collective-permute-done.1.refs_1_), channel_id=1, source_target_pairs={{0,2},{1,3},{2,4},{3,5},{4,6},{5,7},{6,0},{7,1},{8,10},{9,11},{10,... | collective-permute-start | bytes 1179656 | tf_op jit(solution)/shard_map/ppermute | solution.py:483
  37.0 41.5 %collective-permute-start.6 = (bf16[128,1536]{1,0:T(8,128)(2,1)}, bf16[128,1536]{1,0:T(8,128)(2,1)}, u32[]{:S(2)}, u32[]{:S(2)}) collective-permute-start(bf16[128,1536]{1,0:T(8,128)(2,1)} %collective-permute-done.3.refs_6_), channel_id=1, source_target_pairs={{0,2},{1,3},{2,4},{3,5},{4,6},{5,7},{6,0},{7,1},{8,10},{9,11},{10,... | collective-permute-start | bytes 1179656 | tf_op jit(solution)/shard_map/ppermute | solution.py:483
  67.9 10.8 %collective-permute-start.7 = (bf16[128,1536]{1,0:T(8,128)(2,1)}, bf16[128,1536]{1,0:T(8,128)(2,1)}, u32[]{:S(2)}, u32[]{:S(2)}) collective-permute-start(bf16[128,1536]{1,0:T(8,128)(2,1)} %collective-permute-done.5.refs_3_), channel_id=1, source_target_pairs={{0,6},{1,7},{2,0},{3,1},{4,2},{5,3},{6,4},{7,5},{8,14},{9,15},{10,... | collective-permute-start | bytes 1179656 | tf_op jit(solution)/shard_map/ppermute | solution.py:483
  75.4 1.4 copy-start.1
  76.9 20.8 %collective-permute-start.4 = (bf16[1024,384]{1,0:T(8,128)(2,1)}, bf16[1024,384]{1,0:T(8,128)(2,1)}, u32[]{:S(2)}, u32[]{:S(2)}) collective-permute-start(bf16[1024,384]{1,0:T(8,128)(2,1)} %get-tuple-element.70.a_ref), channel_id=1, source_target_pairs={{0,1},{1,0},{2,3},{3,2},{4,5},{5,4},{6,7},{7,6},{8,9},{9,8},{10,11... | collective-permute-start | bytes 2359304 | tf_op jit(solution)/shard_map/ppermute | solution.py:499
  78.7 1.7 copy-start.3
  87.6 25.0 %collective-permute-start.9 = (bf16[1024,384]{1,0:T(8,128)(2,1)S(1)}, bf16[1024,384]{1,0:T(8,128)(2,1)S(1)}, u32[]{:S(2)}, u32[]{:S(2)}) collective-permute-start(bf16[1024,384]{1,0:T(8,128)(2,1)S(1)} %get-tuple-element.79), channel_id=1, source_target_pairs={{0,1},{1,0},{2,3},{3,2},{4,5},{5,4},{6,7},{7,6},{8,9},{9,8},{10,11... | collective-permute-start | bytes 2359304 | tf_op jit(solution)/shard_map/ppermute | solution.py:499
  87.9 9.8 %copy-start.4 = (bf16[3072,384]{1,0:T(8,128)(2,1)S(1)}, bf16[3072,384]{1,0:T(8,128)(2,1)}, u32[]{:S(2)}) copy-start(bf16[3072,384]{1,0:T(8,128)(2,1)} %all-gather.2.cloned.1.call-done) | copy-start | bytes 7077892
  91.0 24.8 %collective-permute-start.14 = (bf16[8,96,384]{2,1,0:T(8,128)(2,1)S(1)}, bf16[8,96,384]{2,1,0:T(8,128)(2,1)S(1)}, u32[]{:S(2)}, u32[]{:S(2)}) collective-permute-start(bf16[8,96,384]{2,1,0:T(8,128)(2,1)S(1)} %get-tuple-element.92), channel_id=1, source_target_pairs={{0,8},{8,0},{16,24},{24,16},{32,40},{40,32},{48,56},{56,48},{64,72... | collective-permute-start | bytes 1769480 | tf_op jit(solution)/shard_map/ppermute | solution.py:503
  100.1 9.1 %collective-permute-start.10 = (bf16[128,1536]{1,0:T(8,128)(2,1)S(1)}, bf16[128,1536]{1,0:T(8,128)(2,1)S(1)}, u32[]{:S(2)}, u32[]{:S(2)}) collective-permute-start(bf16[128,1536]{1,0:T(8,128)(2,1)S(1)} %get-tuple-element.80), channel_id=1, source_target_pairs={{0,2},{1,3},{2,4},{3,5},{4,6},{5,7},{6,0},{7,1},{8,10},{9,11},{10,... | collective-permute-start | bytes 1179656 | tf_op jit(solution)/shard_map/ppermute | solution.py:483
  100.7 8.5 %collective-permute-start.11 = (bf16[128,1536]{1,0:T(8,128)(2,1)S(1)}, bf16[128,1536]{1,0:T(8,128)(2,1)S(1)}, u32[]{:S(2)}, u32[]{:S(2)}) collective-permute-start(bf16[128,1536]{1,0:T(8,128)(2,1)S(1)} %get-tuple-element.84), channel_id=1, source_target_pairs={{0,6},{1,7},{2,0},{3,1},{4,2},{5,3},{6,4},{7,5},{8,14},{9,15},{10,... | collective-permute-start | bytes 1179656 | tf_op jit(solution)/shard_map/ppermute | solution.py:483
  106.3 9.5 %collective-permute-start.15 = (bf16[8,96,384]{2,1,0:T(8,128)(2,1)S(1)}, bf16[8,96,384]{2,1,0:T(8,128)(2,1)S(1)}, u32[]{:S(2)}, u32[]{:S(2)}) collective-permute-start(bf16[8,96,384]{2,1,0:T(8,128)(2,1)S(1)} %get-tuple-element.94), channel_id=1, source_target_pairs={{0,8},{8,0},{16,24},{24,16},{32,40},{40,32},{48,56},{56,48},{64,72... | collective-permute-start | bytes 1769480 | tf_op jit(solution)/shard_map/ppermute | solution.py:503
  112.6 31.8 %collective-permute-start.12 = (bf16[256,1536]{1,0:T(8,128)(2,1)S(1)}, bf16[256,1536]{1,0:T(8,128)(2,1)S(1)}, u32[]{:S(2)}, u32[]{:S(2)}) collective-permute-start(bf16[256,1536]{1,0:T(8,128)(2,1)S(1)} %get-tuple-element.87), channel_id=1, source_target_pairs={{0,2},{1,3},{2,4},{3,5},{4,6},{5,7},{6,0},{7,1},{8,10},{9,11},{10,... | collective-permute-start | bytes 2359304 | tf_op jit(solution)/shard_map/ppermute | solution.py:483
  113.2 31.1 %collective-permute-start.13 = (bf16[256,1536]{1,0:T(8,128)(2,1)S(1)}, bf16[256,1536]{1,0:T(8,128)(2,1)S(1)}, u32[]{:S(2)}, u32[]{:S(2)}) collective-permute-start(bf16[256,1536]{1,0:T(8,128)(2,1)S(1)} %get-tuple-element.88), channel_id=1, source_target_pairs={{0,6},{1,7},{2,0},{3,1},{4,2},{5,3},{6,4},{7,5},{8,14},{9,15},{10,... | collective-permute-start | bytes 2359304 | tf_op jit(solution)/shard_map/ppermute | solution.py:483
  115.8 5.5 %copy-start.2 = (bf16[3,640,640]{2,1,0:T(8,128)(2,1)S(1)}, bf16[3,640,640]{2,1,0:T(8,128)(2,1)}, u32[]{:S(2)}) copy-start(bf16[3,640,640]{2,1,0:T(8,128)(2,1)} %copy-done.1) | copy-start | bytes 7372804
  116.2 14.2 %collective-permute-start.16 = (bf16[4,96,384]{2,1,0:T(8,128)(2,1)S(1)}, bf16[4,96,384]{2,1,0:T(8,128)(2,1)S(1)}, u32[]{:S(2)}, u32[]{:S(2)}) collective-permute-start(bf16[4,96,384]{2,1,0:T(8,128)(2,1)S(1)} %get-tuple-element.100), channel_id=1, source_target_pairs={{0,64},{8,72},{16,80},{24,88},{32,96},{40,104},{48,112},{56,120},{... | collective-permute-start | bytes 884744 | tf_op jit(solution)/shard_map/ppermute | solution.py:483
  116.7 13.7 %collective-permute-start.17 = (bf16[4,96,384]{2,1,0:T(8,128)(2,1)S(1)}, bf16[4,96,384]{2,1,0:T(8,128)(2,1)S(1)}, u32[]{:S(2)}, u32[]{:S(2)}) collective-permute-start(bf16[4,96,384]{2,1,0:T(8,128)(2,1)S(1)} %get-tuple-element.101), channel_id=1, source_target_pairs={{0,128},{8,136},{16,144},{24,152},{32,160},{40,168},{48,176},{56,1... | collective-permute-start | bytes 884744 | tf_op jit(solution)/shard_map/ppermute | solution.py:483
  120.0 11.1 %collective-permute-start.18 = (bf16[4,96,384]{2,1,0:T(8,128)(2,1)S(1)}, bf16[4,96,384]{2,1,0:T(8,128)(2,1)S(1)}, u32[]{:S(2)}, u32[]{:S(2)}) collective-permute-start(bf16[4,96,384]{2,1,0:T(8,128)(2,1)S(1)} %get-tuple-element.102), channel_id=1, source_target_pairs={{0,192},{8,200},{16,208},{24,216},{32,224},{40,232},{48,240},{56,2... | collective-permute-start | bytes 884744 | tf_op jit(solution)/shard_map/ppermute | solution.py:483
  131.2 16.5 %collective-permute-start.19 = (bf16[96,384]{1,0:T(8,128)(2,1)S(1)}, bf16[96,384]{1,0:T(8,128)(2,1)S(1)}, u32[]{:S(2)}, u32[]{:S(2)}) collective-permute-start(bf16[96,384]{1,0:T(8,128)(2,1)S(1)} %get-tuple-element.114), channel_id=1, source_target_pairs={{0,16},{8,24},{16,32},{24,40},{32,48},{40,56},{48,0},{56,8},{64,80... | collective-permute-start | bytes 221192 | tf_op jit(solution)/shard_map/ppermute | solution.py:483
  135.1 12.6 %collective-permute-start.20 = (bf16[96,384]{1,0:T(8,128)(2,1)S(1)}, bf16[96,384]{1,0:T(8,128)(2,1)S(1)}, u32[]{:S(2)}, u32[]{:S(2)}) collective-permute-start(bf16[96,384]{1,0:T(8,128)(2,1)S(1)} %get-tuple-element.115), channel_id=1, source_target_pairs={{0,32},{8,40},{16,48},{24,56},{32,0},{40,8},{48,16},{56,24},{64,96... | collective-permute-start | bytes 221192 | tf_op jit(solution)/shard_map/ppermute | solution.py:483
  141.6 6.1 %collective-permute-start.21 = (bf16[96,384]{1,0:T(8,128)(2,1)S(1)}, bf16[96,384]{1,0:T(8,128)(2,1)S(1)}, u32[]{:S(2)}, u32[]{:S(2)}) collective-permute-start(bf16[96,384]{1,0:T(8,128)(2,1)S(1)} %get-tuple-element.116), channel_id=1, source_target_pairs={{0,48},{8,56},{16,0},{24,8},{32,16},{40,24},{48,32},{56,40},{64,11... | collective-permute-start | bytes 221192 | tf_op jit(solution)/shard_map/ppermute | solution.py:483
  147.7 46.3 %all-to-all-start.1 = ((bf16[8,3,128,384]{3,2,1,0:T(8,128)(2,1)}), bf16[8,3,128,384]{3,2,1,0:T(8,128)(2,1)S(1)}, u32[]{:S(2)}, u32[]{:S(2)}) async-start(bf16[8,3,128,384]{3,2,1,0:T(8,128)(2,1)} %attention_backward.1), calls=%async_computation.1 | async-start | bytes 4718592 | tf_op jit(solution)/shard_map/all_to_all | solution.py:553
  153.3 36.5 %collective-permute-start.23 = (bf16[128,1536]{1,0:T(8,128)(2,1)S(1)}, bf16[128,1536]{1,0:T(8,128)(2,1)S(1)}, u32[]{:S(2)}, u32[]{:S(2)}) collective-permute-start(bf16[128,1536]{1,0:T(8,128)(2,1)S(1)} %get-tuple-element.121), channel_id=1, source_target_pairs={{0,1},{1,0},{2,3},{3,2},{4,5},{5,4},{6,7},{7,6},{8,9},{9,8},{10,11... | collective-permute-start | bytes 1179656 | tf_op jit(solution)/shard_map/ppermute | solution.py:499
  153.5 36.3 %collective-permute-start.22 = (f32[96,384]{1,0:T(8,128)S(1)}, f32[96,384]{1,0:T(8,128)S(1)}, u32[]{:S(2)}, u32[]{:S(2)}) collective-permute-start(f32[96,384]{1,0:T(8,128)S(1)} %convert_add_fusion), channel_id=1, source_target_pairs={{0,0},{128,1},{2,2},{130,3},{4,4},{132,5},{6,6},{134,7},{8,8},{136... | collective-permute-start | bytes 442376 | tf_op jit(solution)/shard_map/ppermute | solution.py:557
  (6 other events, 5.0 us)
Sparse Core Ops, SparseCore 0:
  15.9 60.1 all-gather.1

commit v9 on v8

--- a/solution.py
+++ b/solution.py
@@ -546,17 +546,17 @@
     grads = attention_backward(frames, heads, d_own, d_recv, p1, p2)
     terms, grads = lax.optimization_barrier((terms, grads))
     terms = ring_sum(dp, terms)
-    terms = [terms[0]] + [along_z(terms[k], k) for k in range(1, 4)]
     o_keep, o_send = project_home(seq, attn, attn_other, weights, c1, c3)
     grads, o_send, terms = lax.optimization_barrier((grads, o_send, terms))
     o_got = swap_z(o_send)
     grads = lax.all_to_all(grads, "seq", split_axis=0, concat_axis=0, tiled=True)
 
+    terms = [terms[0]] + [along_z(terms[k], k) for k in range(1, 4)]
+    output = gated_output(frames, timesteps, seq, gate_table, latents, o_keep, o_got)
+    terms, output = lax.optimization_barrier((terms, output))
     total = terms[0].astype(F32) + terms[1].astype(F32)
     total = total + terms[2].astype(F32) + terms[3].astype(F32)
     total = lax.ppermute(total, both, [(b, a) for a, b in moves])
-    total, o_got = lax.optimization_barrier((total, o_got))
-    output = gated_output(frames, timesteps, seq, gate_table, latents, o_keep, o_got)
     grad_qkv = unpack_heads(grads)
     return (output, grad_qkv.transpose(1, 0, 2), total.T)
 

time: 205 us -> 207 us (level)
    ppermute x1, waiting for transfers between devices: 32.3 us -> 5.09 us  [body(): total = lax.ppermute(total, both, [(b, a) for a, b in moves])]
    ppermute x4, waiting for transfers between devices: 11.1 us -> 32.5 us  [swap_z(): lax.ppermute(x, 'seq', [(i, i ^ 1) for i in range(lax.axis_size('seq'))])]
    ppermute x16, waiting for transfers between devices: 35.1 us -> 41.3 us  [along(): return lax.ppermute(x, axis, moves)]
  transfers between devices with their start and end apart: 27 -> 27, of which waited for: 11 -> 14; matrix products, arithmetic and copies ran while one was open for 0% -> 0% of each run, Pallas kernels for 22% -> 20%
where the time goes in v9:
time: 207 us; the launch traced here: 204 us
  waiting for transfers between devices  79.3 us (38%)
  starting transfers between devices  56.2 us (27%)
  Pallas kernels  45.6 us (22%)
  between operations  14.2 us (7%)
  local copies, waits for them, and re-layouts  8.79 us (4%)
    ppermute x16, waiting for transfers between devices, along(): return lax.ppermute(x, axis, moves)  41.3 us
    ppermute x16, starting transfers between devices, along(): return lax.ppermute(x, axis, moves)  33.4 us
    ppermute x4, waiting for transfers between devices, swap_z(): lax.ppermute(x, 'seq', [(i, i ^ 1) for i in range(lax.axis_size('seq'))])  32.5 us
    pallas_call x1, Pallas kernels, attention_backward(): pl.pallas_call(bwd_kernel, out_shape=shape((8, 3, 128, 3 * HD)), in_specs...  8.96 us
    unnamed x23, local copies, waits for them, and re-layouts  8.79 us
    pallas_call x2, Pallas kernels, dweight_part(): pl.pallas_call(dweight_kernel, out_shape=(shape((8, 96, 384)), shape((8,...  6.05 us
    pallas_call x1, Pallas kernels, attention_forward(): pl.pallas_call(fwd_kernel, out_shape=(shape((1024, 3 * HD)), shape((3, LO...  6.02 us
    all_to_all x1, starting transfers between devices, body(): lax.all_to_all(packed, 'seq', split_axis=0, concat_axis=0, tiled=True)  5.77 us
  transfers between devices with their start and end apart: 27, of which 14 were waited for; matrix products, arithmetic and copies ran while one was open for 0% of the time, Pallas kernels for 20%

profile of v9, /device:TPU:32, one launch (start us, length us, event | category | flops | bytes accessed | tf_op | source)
XLA Modules:
  0.0 204.1 jit_solution(7787069030332871879)
XLA Ops:
  7.2 4.6 %collective-permute-start = (bf16[96,384]{1,0:T(8,128)(2,1)}, bf16[96,384]{1,0:T(8,128)(2,1)S(1)}, u32[]{:S(2)}, u32[]{:S(2)}) collective-permute-start(bf16[96,384]{1,0:T(8,128)(2,1)} %bitcast.21), channel_id=1, source_target_pairs={{0,0},{1,128},{2,2},{3,130},{4,4},{5,132},{6,6},{7,134},{8,8},{9,1... | collective-permute-start | bytes 221192 | tf_op jit(solution)/shard_map/ppermute | solution.py:512
  11.9 3.0 %gated_cotangent.1 = (bf16[128,1536]{1,0:T(8,128)(2,1)}, bf16[128,1536]{1,0:T(8,128)(2,1)}) custom-call(s32[1,3]{1,0:T(1,128)} %frames_ref.7, s32[1,3]{1,0:T(1,128)} %steps_ref.3, s32[1]{0:T(128)} %bitcast.seq_ref, f32[64,3072]{1,0:T(8,128)} %t1_ref.3, f32[64,3072]{1,0:T(8,128)} %t1_ref.3, bf16[128,3072]{1,0:T(8,128)(2,1)} %c1_ref.1, bf16[128,3072]{1,0:T(8,128)(2,1)} %c1_ref.1), custom_call_target="tpu_custom_call" | custom-call | flops 3000000000 | bytes 9000000 | tf_op jit(solution)/shard_map/gated_cotangent/pallas_call | solution.py:259
  17.5 1.7 collective-permute-start.2
  19.2 2.8 %pack_heads.1 = bf16[8,3,128,384]{3,2,1,0:T(8,128)(2,1)} custom-call(bf16[3,128,3072]{2,1,0:T(8,128)(2,1)} %bitcast.20), custom_call_target="tpu_custom_call" | custom-call | flops 3000000000 | bytes 9000000 | tf_op jit(solution)/shard_map/pack_heads/pallas_call | solution.py:218
  22.0 4.5 %collective-permute-done.1.refs_1_ = bf16[128,1536]{1,0:T(8,128)(2,1)} collective-permute-done((bf16[128,1536]{1,0:T(8,128)(2,1)}, bf16[128,1536]{1,0:T(8,128)(2,1)}, u32[]{:S(2)}, u32[]{:S(2)}) %collective-permute-start.1) | collective-permute-done | bytes 393248 | tf_op jit(solution)/shard_map/ppermute | solution.py:499
  28.6 5.8 %all-to-all-start = ((bf16[8,3,128,384]{3,2,1,0:T(8,128)(2,1)}), bf16[8,3,128,384]{3,2,1,0:T(8,128)(2,1)S(1)}, u32[]{:S(2)}, u32[]{:S(2)}) async-start(bf16[8,3,128,384]{3,2,1,0:T(8,128)(2,1)} %pack_heads.1), calls=%async_computation | async-start | bytes 4718592 | tf_op jit(solution)/shard_map/all_to_all | solution.py:520
  34.3 2.7 %collective-permute-start.4 = (bf16[128,1536]{1,0:T(8,128)(2,1)}, bf16[128,1536]{1,0:T(8,128)(2,1)}, u32[]{:S(2)}, u32[]{:S(2)}) collective-permute-start(bf16[128,1536]{1,0:T(8,128)(2,1)} %collective-permute-done.1.refs_1_), channel_id=1, source_target_pairs={{0,6},{1,7},{2,0},{3,1},{4,2},{5,3},{6,4},{7,5},{8,14},{9,15},{10,... | collective-permute-start | bytes 1179656 | tf_op jit(solution)/shard_map/ppermute | solution.py:483
  37.8 30.1 %collective-permute-done.4.refs_3_ = bf16[128,1536]{1,0:T(8,128)(2,1)} collective-permute-done((bf16[128,1536]{1,0:T(8,128)(2,1)}, bf16[128,1536]{1,0:T(8,128)(2,1)}, u32[]{:S(2)}, u32[]{:S(2)}) %collective-permute-start.4) | collective-permute-done | bytes 393248 | tf_op jit(solution)/shard_map/ppermute | solution.py:483
  69.4 6.0 %attention_forward.1 = (bf16[1024,384]{1,0:T(8,128)(2,1)}, bf16[3,640,640]{2,1,0:T(8,128)(2,1)S(1)}, bf16[3,384,384]{2,1,0:T(8,128)(2,1)S(1)}) custom-call(s32[1,3]{1,0:T(1,128)S(1)} %copy-done, bf16[8,3,128,384]{3,2,1,0:T(8,128)(2,1)S(1)} %all-to-all-done.qkv_ref), custom_call_target="tpu_custom_call" | custom-call | flops 100000000 | bytes 300000 | tf_op jit(solution)/shard_map/attention_forward/pallas_call | solution.py:133
  78.7 1.7 copy-done.3
  82.4 5.2 %dattn_parts.1 = (bf16[1024,1536]{1,0:T(8,128)(2,1)S(1)}, bf16[1024,384]{1,0:T(8,128)(2,1)S(1)}, f32[1024,384]{1,0:T(8,128)S(1)}) custom-call(s32[1]{0:T(128)} %bitcast.seq_ref, bf16[128,1536]{1,0:T(8,128)(2,1)S(1)} %copy-done.5, bf16[128,1536]{1,0:T(8,128)(2,1)} %collective-permute-done.1.refs_1_, bf16[128,1536]{1,0:T(8,128)(2,1)S(1)} %copy-done.7, ...), custom_call_target="tpu_custom_call" | custom-call | flops 7000000000 | bytes 21000000 | tf_op jit(solution)/shard_map/dattn_parts/pallas_call | solution.py:320
  87.9 3.1 %dweight_part.2 = (bf16[8,96,384]{2,1,0:T(8,128)(2,1)S(1)}, bf16[8,96,384]{2,1,0:T(8,128)(2,1)S(1)}) custom-call(s32[1]{0:T(128)} %bitcast.4.dp_ref, bf16[1024,1536]{1,0:T(8,128)(2,1)S(1)} %get-tuple-element.84.d_ref, bf16[1024,384]{1,0:T(8,128)(2,1)} %get-tuple-element.79.a_ref), custom_call_target="tpu_custom_call" | custom-call | flops 4000000000 | bytes 12000000 | tf_op jit(solution)/shard_map/dweight_part/pallas_call | solution.py:409
  91.3 6.4 %collective-permute-done.9.b_ref.a_ref = bf16[1024,384]{1,0:T(8,128)(2,1)} collective-permute-done((bf16[1024,384]{1,0:T(8,128)(2,1)}, bf16[1024,384]{1,0:T(8,128)(2,1)}, u32[]{:S(2)}, u32[]{:S(2)}) %collective-permute-start.9) | collective-permute-done | bytes 786464 | tf_op jit(solution)/shard_map/ppermute | solution.py:499
  97.7 2.4 %project_far.1 = (bf16[128,1536]{1,0:T(8,128)(2,1)S(1)}, bf16[128,1536]{1,0:T(8,128)(2,1)S(1)}) custom-call(s32[1]{0:T(128)} %bitcast.seq_ref, bf16[1024,384]{1,0:T(8,128)(2,1)} %get-tuple-element.79.a_ref, bf16[1024,384]{1,0:T(8,128)(2,1)} %collective-permute-done.9.b_ref.a_ref, bf16[2,1536,384]{2,1,0:T(8,128)(2,1)S(1)} %bitcast.12), custom_call_target="tpu_custom_call" | custom-call | flops 3000000000 | bytes 9000000 | tf_op jit(solution)/shard_map/project_far/pallas_call | solution.py:378
  100.7 2.7 %collective-permute-start.11 = (bf16[128,1536]{1,0:T(8,128)(2,1)S(1)}, bf16[128,1536]{1,0:T(8,128)(2,1)S(1)}, u32[]{:S(2)}, u32[]{:S(2)}) collective-permute-start(bf16[128,1536]{1,0:T(8,128)(2,1)S(1)} %get-tuple-element.87), channel_id=1, source_target_pairs={{0,6},{1,7},{2,0},{3,1},{4,2},{5,3},{6,4},{7,5},{8,14},{9,15},{10,... | collective-permute-start | bytes 1179656 | tf_op jit(solution)/shard_map/ppermute | solution.py:483
  103.4 3.0 %dweight_part.3 = (bf16[8,96,384]{2,1,0:T(8,128)(2,1)S(1)}, bf16[8,96,384]{2,1,0:T(8,128)(2,1)S(1)}) custom-call(s32[1]{0:T(128)} %bitcast.4.dp_ref, bf16[1024,1536]{1,0:T(8,128)(2,1)S(1)} %get-tuple-element.84.d_ref, bf16[1024,384]{1,0:T(8,128)(2,1)} %collective-permute-done.9.b_ref.a_ref), custom_call_target="tpu_custom_call" | custom-call | flops 4000000000 | bytes 12000000 | tf_op jit(solution)/shard_map/dweight_part/pallas_call | solution.py:409
  106.4 2.7 %collective-permute-done.10.up_ref = bf16[128,1536]{1,0:T(8,128)(2,1)S(1)} collective-permute-done((bf16[128,1536]{1,0:T(8,128)(2,1)S(1)}, bf16[128,1536]{1,0:T(8,128)(2,1)S(1)}, u32[]{:S(2)}, u32[]{:S(2)}) %collective-permute-start.10) | collective-permute-done | bytes 393248 | tf_op jit(solution)/shard_map/ppermute | solution.py:483
  109.1 3.2 %project_near.1 = (bf16[256,1536]{1,0:T(8,128)(2,1)S(1)}, bf16[256,1536]{1,0:T(8,128)(2,1)S(1)}) custom-call(s32[1]{0:T(128)} %bitcast.seq_ref, bf16[1024,384]{1,0:T(8,128)(2,1)} %get-tuple-element.79.a_ref, bf16[1024,384]{1,0:T(8,128)(2,1)} %collective-permute-done.9.b_ref.a_ref, bf16[2,1536,384]{2,1,0:T(8,128)(2,1)S(1)} %bitcast.13, ...), custom_call_target="tpu_custom_call" | custom-call | flops 3000000000 | bytes 9000000 | tf_op jit(solution)/shard_map/project_near/pallas_call | solution.py:384
  113.2 2.6 %collective-permute-start.18 = (bf16[256,1536]{1,0:T(8,128)(2,1)S(1)}, bf16[256,1536]{1,0:T(8,128)(2,1)S(1)}, u32[]{:S(2)}, u32[]{:S(2)}) collective-permute-start(bf16[256,1536]{1,0:T(8,128)(2,1)S(1)} %get-tuple-element.109), channel_id=1, source_target_pairs={{0,6},{1,7},{2,0},{3,1},{4,2},{5,3},{6,4},{7,5},{8,14},{9,15},{10,... | collective-permute-start | bytes 2359304 | tf_op jit(solution)/shard_map/ppermute | solution.py:483
  116.7 3.3 %collective-permute-start.15 = (bf16[4,96,384]{2,1,0:T(8,128)(2,1)S(1)}, bf16[4,96,384]{2,1,0:T(8,128)(2,1)S(1)}, u32[]{:S(2)}, u32[]{:S(2)}) collective-permute-start(bf16[4,96,384]{2,1,0:T(8,128)(2,1)S(1)} %get-tuple-element.101), channel_id=1, source_target_pairs={{0,128},{8,136},{16,144},{24,152},{32,160},{40,168},{48,176},{56,1... | collective-permute-start | bytes 884744 | tf_op jit(solution)/shard_map/ppermute | solution.py:483
  121.3 9.0 %attention_backward.1 = bf16[8,3,128,384]{3,2,1,0:T(8,128)(2,1)} custom-call(s32[1,3]{1,0:T(1,128)S(1)} %copy-done, bf16[8,3,128,384]{3,2,1,0:T(8,128)(2,1)S(1)} %all-to-all-done.qkv_ref, f32[1024,384]{1,0:T(8,128)S(1)} %get-tuple-element.103.own_ref, bf16[1024,384]{1,0:T(8,128)(2,1)S(1)} %collective-permute-done.8.other_ref, ...), custom_call_target="tpu_custom_call" | custom-call | flops 10000000000 | bytes 30000000 | tf_op jit(solution)/shard_map/attention_backward/pallas_call | solution.py:195
  131.5 2.5 %project_home.1 = (f32[128,1536]{1,0:T(8,128)S(1)}, bf16[128,1536]{1,0:T(8,128)(2,1)S(1)}) custom-call(s32[1]{0:T(128)} %bitcast.seq_ref, bf16[1024,384]{1,0:T(8,128)(2,1)} %get-tuple-element.79.a_ref, bf16[1024,384]{1,0:T(8,128)(2,1)} %collective-permute-done.9.b_ref.a_ref, bf16[2,1536,384]{2,1,0:T(8,128)(2,1)S(1)} %bitcast.14, ...), custom_call_target="tpu_custom_call" | custom-call | flops 3000000000 | bytes 9000000 | tf_op jit(solution)/shard_map/project_home/pallas_call | solution.py:395
  134.8 5.7 %all-to-all-start.1 = ((bf16[8,3,128,384]{3,2,1,0:T(8,128)(2,1)}), bf16[8,3,128,384]{3,2,1,0:T(8,128)(2,1)S(1)}, u32[]{:S(2)}, u32[]{:S(2)}) async-start(bf16[8,3,128,384]{3,2,1,0:T(8,128)(2,1)} %attention_backward.1), calls=%async_computation.1 | async-start | bytes 4718592 | tf_op jit(solution)/shard_map/all_to_all | solution.py:552
  140.5 3.6 %collective-permute-start.19 = (bf16[96,384]{1,0:T(8,128)(2,1)S(1)}, bf16[96,384]{1,0:T(8,128)(2,1)S(1)}, u32[]{:S(2)}, u32[]{:S(2)}) collective-permute-start(bf16[96,384]{1,0:T(8,128)(2,1)S(1)} %get-tuple-element.120), channel_id=1, source_target_pairs={{0,16},{8,24},{16,32},{24,40},{32,48},{40,56},{48,0},{56,8},{64,80... | collective-permute-start | bytes 221192 | tf_op jit(solution)/shard_map/ppermute | solution.py:483
  144.1 7.1 %collective-permute-start.20 = (bf16[96,384]{1,0:T(8,128)(2,1)S(1)}, bf16[96,384]{1,0:T(8,128)(2,1)S(1)}, u32[]{:S(2)}, u32[]{:S(2)}) collective-permute-start(bf16[96,384]{1,0:T(8,128)(2,1)S(1)} %get-tuple-element.121), channel_id=1, source_target_pairs={{0,32},{8,40},{16,48},{24,56},{32,0},{40,8},{48,16},{56,24},{64,96... | collective-permute-start | bytes 221192 | tf_op jit(solution)/shard_map/ppermute | solution.py:483
  151.2 2.7 %collective-permute-start.21 = (bf16[96,384]{1,0:T(8,128)(2,1)S(1)}, bf16[96,384]{1,0:T(8,128)(2,1)S(1)}, u32[]{:S(2)}, u32[]{:S(2)}) collective-permute-start(bf16[96,384]{1,0:T(8,128)(2,1)S(1)} %get-tuple-element.122), channel_id=1, source_target_pairs={{0,48},{8,56},{16,0},{24,8},{32,16},{40,24},{48,32},{56,40},{64,11... | collective-permute-start | bytes 221192 | tf_op jit(solution)/shard_map/ppermute | solution.py:483
  154.0 21.4 %collective-permute-done.22.other_ref = bf16[128,1536]{1,0:T(8,128)(2,1)S(1)} collective-permute-done((bf16[128,1536]{1,0:T(8,128)(2,1)S(1)}, bf16[128,1536]{1,0:T(8,128)(2,1)S(1)}, u32[]{:S(2)}, u32[]{:S(2)}) %collective-permute-start.22) | collective-permute-done | bytes 393248 | tf_op jit(solution)/shard_map/ppermute | solution.py:499
  176.1 3.5 %gated_output.1 = bf16[128,3072]{1,0:T(8,128)(2,1)} custom-call(s32[1,3]{1,0:T(1,128)} %frames_ref.7, s32[1,3]{1,0:T(1,128)} %steps_ref.3, s32[1]{0:T(128)} %bitcast.seq_ref, f32[64,3072]{1,0:T(8,128)} %t1_ref.3, f32[64,3072]{1,0:T(8,128)} %t1_ref.3, bf16[128,3072]{1,0:T(8,128)(2,1)} %l1_ref.1, bf16[128,3072]{1,0:T(8,128)(2,1)} %l1_ref.1, ...), custom_call_target="tpu_custom_call" | custom-call | flops 3000000000 | bytes 9000000 | tf_op jit(solution)/shard_map/gated_output/pallas_call | solution.py:292
  179.6 5.9 %collective-permute-done.20 = bf16[96,384]{1,0:T(8,128)(2,1)S(1)} collective-permute-done((bf16[96,384]{1,0:T(8,128)(2,1)S(1)}, bf16[96,384]{1,0:T(8,128)(2,1)S(1)}, u32[]{:S(2)}, u32[]{:S(2)}) %collective-permute-start.20) | collective-permute-done | bytes 73760 | tf_op jit(solution)/shard_map/ppermute | solution.py:483
  185.6 4.3 %collective-permute-start.23 = (f32[96,384]{1,0:T(8,128)S(1)}, f32[96,384]{1,0:T(8,128)S(1)}, u32[]{:S(2)}, u32[]{:S(2)}) collective-permute-start(f32[96,384]{1,0:T(8,128)S(1)} %convert_add_fusion), channel_id=1, source_target_pairs={{0,0},{128,1},{2,2},{130,3},{4,4},{132,5},{6,6},{134,7},{8,8},{136... | collective-permute-start | bytes 442376 | tf_op jit(solution)/shard_map/ppermute | solution.py:559
  189.9 5.1 %collective-permute-done.23 = f32[96,384]{1,0:T(8,128)S(1)} collective-permute-done((f32[96,384]{1,0:T(8,128)S(1)}, f32[96,384]{1,0:T(8,128)S(1)}, u32[]{:S(2)}, u32[]{:S(2)}) %collective-permute-start.23) | collective-permute-done | bytes 147488 | tf_op jit(solution)/shard_map/ppermute | solution.py:559
  195.0 1.6 unpack_heads.1
  (61 shorter events, 20.3 us)
Async XLA Ops:
  7.2 71.6 %all-gather.2.cloned.1.call-start = ((), (), s32[]{:S(2)}) async-start(), calls=%async_computation.2 | async-start | bytes 2433024 | tf_op jit(solution)/shard_map/all_gather | solution.py:515
  7.2 8.0 %collective-permute-start = (bf16[96,384]{1,0:T(8,128)(2,1)}, bf16[96,384]{1,0:T(8,128)(2,1)S(1)}, u32[]{:S(2)}, u32[]{:S(2)}) collective-permute-start(bf16[96,384]{1,0:T(8,128)(2,1)} %bitcast.21), channel_id=1, source_target_pairs={{0,0},{1,128},{2,2},{3,130},{4,4},{5,132},{6,6},{7,134},{8,8},{9,1... | collective-permute-start | bytes 221192 | tf_op jit(solution)/shard_map/ppermute | solution.py:512
  15.8 10.6 %collective-permute-start.1 = (bf16[128,1536]{1,0:T(8,128)(2,1)}, bf16[128,1536]{1,0:T(8,128)(2,1)}, u32[]{:S(2)}, u32[]{:S(2)}) collective-permute-start(bf16[128,1536]{1,0:T(8,128)(2,1)} %get-tuple-element.71), channel_id=1, source_target_pairs={{0,1},{1,0},{2,3},{3,2},{4,5},{5,4},{6,7},{7,6},{8,9},{9,8},{10,11... | collective-permute-start | bytes 1179656 | tf_op jit(solution)/shard_map/ppermute | solution.py:499
  15.9 11.8 %collective-permute-start.3 = (bf16[128,1536]{1,0:T(8,128)(2,1)}, bf16[128,1536]{1,0:T(8,128)(2,1)}, u32[]{:S(2)}, u32[]{:S(2)}) collective-permute-start(bf16[128,1536]{1,0:T(8,128)(2,1)} %get-tuple-element.69.refs_0_), channel_id=1, source_target_pairs={{0,2},{1,3},{2,4},{3,5},{4,6},{5,7},{6,0},{7,1},{8,10},{9,11},{10,... | collective-permute-start | bytes 1179656 | tf_op jit(solution)/shard_map/ppermute | solution.py:483
  17.5 10.3 %collective-permute-start.2 = (bf16[128,1536]{1,0:T(8,128)(2,1)}, bf16[128,1536]{1,0:T(8,128)(2,1)S(1)}, u32[]{:S(2)}, u32[]{:S(2)}) collective-permute-start(bf16[128,1536]{1,0:T(8,128)(2,1)} %get-tuple-element.69.refs_0_), channel_id=1, source_target_pairs={{0,6},{1,7},{2,0},{3,1},{4,2},{5,3},{6,4},{7,5},{8,14},{9,15},{10,... | collective-permute-start | bytes 1179656 | tf_op jit(solution)/shard_map/ppermute | solution.py:483
  22.0 47.4 %copy-start = (s32[1,3]{1,0:T(1,128)S(1)}, s32[1,3]{1,0:T(1,128)}, u32[]{:S(2)}) copy-start(s32[1,3]{1,0:T(1,128)} %frames_ref.7) | copy-start | bytes 40
  28.6 40.9 %all-to-all-start = ((bf16[8,3,128,384]{3,2,1,0:T(8,128)(2,1)}), bf16[8,3,128,384]{3,2,1,0:T(8,128)(2,1)S(1)}, u32[]{:S(2)}, u32[]{:S(2)}) async-start(bf16[8,3,128,384]{3,2,1,0:T(8,128)(2,1)} %pack_heads.1), calls=%async_computation | async-start | bytes 4718592 | tf_op jit(solution)/shard_map/all_to_all | solution.py:520
  34.3 33.6 %collective-permute-start.4 = (bf16[128,1536]{1,0:T(8,128)(2,1)}, bf16[128,1536]{1,0:T(8,128)(2,1)}, u32[]{:S(2)}, u32[]{:S(2)}) collective-permute-start(bf16[128,1536]{1,0:T(8,128)(2,1)} %collective-permute-done.1.refs_1_), channel_id=1, source_target_pairs={{0,6},{1,7},{2,0},{3,1},{4,2},{5,3},{6,4},{7,5},{8,14},{9,15},{10,... | collective-permute-start | bytes 1179656 | tf_op jit(solution)/shard_map/ppermute | solution.py:483
  37.0 41.5 %collective-permute-start.7 = (bf16[128,1536]{1,0:T(8,128)(2,1)}, bf16[128,1536]{1,0:T(8,128)(2,1)}, u32[]{:S(2)}, u32[]{:S(2)}) collective-permute-start(bf16[128,1536]{1,0:T(8,128)(2,1)} %collective-permute-done.1.refs_1_), channel_id=1, source_target_pairs={{0,2},{1,3},{2,4},{3,5},{4,6},{5,7},{6,0},{7,1},{8,10},{9,11},{10,... | collective-permute-start | bytes 1179656 | tf_op jit(solution)/shard_map/ppermute | solution.py:483
  37.0 41.5 %collective-permute-start.5 = (bf16[128,1536]{1,0:T(8,128)(2,1)}, bf16[128,1536]{1,0:T(8,128)(2,1)}, u32[]{:S(2)}, u32[]{:S(2)}) collective-permute-start(bf16[128,1536]{1,0:T(8,128)(2,1)} %collective-permute-done.3.refs_6_), channel_id=1, source_target_pairs={{0,2},{1,3},{2,4},{3,5},{4,6},{5,7},{6,0},{7,1},{8,10},{9,11},{10,... | collective-permute-start | bytes 1179656 | tf_op jit(solution)/shard_map/ppermute | solution.py:483
  67.9 10.8 %collective-permute-start.6 = (bf16[128,1536]{1,0:T(8,128)(2,1)}, bf16[128,1536]{1,0:T(8,128)(2,1)}, u32[]{:S(2)}, u32[]{:S(2)}) collective-permute-start(bf16[128,1536]{1,0:T(8,128)(2,1)} %collective-permute-done.4.refs_3_), channel_id=1, source_target_pairs={{0,6},{1,7},{2,0},{3,1},{4,2},{5,3},{6,4},{7,5},{8,14},{9,15},{10,... | collective-permute-start | bytes 1179656 | tf_op jit(solution)/shard_map/ppermute | solution.py:483
  75.4 1.4 copy-start.1
  76.9 20.8 %collective-permute-start.9 = (bf16[1024,384]{1,0:T(8,128)(2,1)}, bf16[1024,384]{1,0:T(8,128)(2,1)}, u32[]{:S(2)}, u32[]{:S(2)}) collective-permute-start(bf16[1024,384]{1,0:T(8,128)(2,1)} %get-tuple-element.79.a_ref), channel_id=1, source_target_pairs={{0,1},{1,0},{2,3},{3,2},{4,5},{5,4},{6,7},{7,6},{8,9},{9,8},{10,11... | collective-permute-start | bytes 2359304 | tf_op jit(solution)/shard_map/ppermute | solution.py:499
  78.7 1.7 copy-start.3
  87.6 25.0 %collective-permute-start.8 = (bf16[1024,384]{1,0:T(8,128)(2,1)S(1)}, bf16[1024,384]{1,0:T(8,128)(2,1)S(1)}, u32[]{:S(2)}, u32[]{:S(2)}) collective-permute-start(bf16[1024,384]{1,0:T(8,128)(2,1)S(1)} %get-tuple-element.77), channel_id=1, source_target_pairs={{0,1},{1,0},{2,3},{3,2},{4,5},{5,4},{6,7},{7,6},{8,9},{9,8},{10,11... | collective-permute-start | bytes 2359304 | tf_op jit(solution)/shard_map/ppermute | solution.py:499
  87.9 9.8 %copy-start.4 = (bf16[3072,384]{1,0:T(8,128)(2,1)S(1)}, bf16[3072,384]{1,0:T(8,128)(2,1)}, u32[]{:S(2)}) copy-start(bf16[3072,384]{1,0:T(8,128)(2,1)} %all-gather.2.cloned.1.call-done) | copy-start | bytes 7077892
  91.0 24.8 %collective-permute-start.12 = (bf16[8,96,384]{2,1,0:T(8,128)(2,1)S(1)}, bf16[8,96,384]{2,1,0:T(8,128)(2,1)S(1)}, u32[]{:S(2)}, u32[]{:S(2)}) collective-permute-start(bf16[8,96,384]{2,1,0:T(8,128)(2,1)S(1)} %get-tuple-element.92), channel_id=1, source_target_pairs={{0,8},{8,0},{16,24},{24,16},{32,40},{40,32},{48,56},{56,48},{64,72... | collective-permute-start | bytes 1769480 | tf_op jit(solution)/shard_map/ppermute | solution.py:503
  100.1 9.1 %collective-permute-start.10 = (bf16[128,1536]{1,0:T(8,128)(2,1)S(1)}, bf16[128,1536]{1,0:T(8,128)(2,1)S(1)}, u32[]{:S(2)}, u32[]{:S(2)}) collective-permute-start(bf16[128,1536]{1,0:T(8,128)(2,1)S(1)} %get-tuple-element.83), channel_id=1, source_target_pairs={{0,2},{1,3},{2,4},{3,5},{4,6},{5,7},{6,0},{7,1},{8,10},{9,11},{10,... | collective-permute-start | bytes 1179656 | tf_op jit(solution)/shard_map/ppermute | solution.py:483
  100.7 8.5 %collective-permute-start.11 = (bf16[128,1536]{1,0:T(8,128)(2,1)S(1)}, bf16[128,1536]{1,0:T(8,128)(2,1)S(1)}, u32[]{:S(2)}, u32[]{:S(2)}) collective-permute-start(bf16[128,1536]{1,0:T(8,128)(2,1)S(1)} %get-tuple-element.87), channel_id=1, source_target_pairs={{0,6},{1,7},{2,0},{3,1},{4,2},{5,3},{6,4},{7,5},{8,14},{9,15},{10,... | collective-permute-start | bytes 1179656 | tf_op jit(solution)/shard_map/ppermute | solution.py:483
  106.3 9.5 %collective-permute-start.13 = (bf16[8,96,384]{2,1,0:T(8,128)(2,1)S(1)}, bf16[8,96,384]{2,1,0:T(8,128)(2,1)S(1)}, u32[]{:S(2)}, u32[]{:S(2)}) collective-permute-start(bf16[8,96,384]{2,1,0:T(8,128)(2,1)S(1)} %get-tuple-element.94), channel_id=1, source_target_pairs={{0,8},{8,0},{16,24},{24,16},{32,40},{40,32},{48,56},{56,48},{64,72... | collective-permute-start | bytes 1769480 | tf_op jit(solution)/shard_map/ppermute | solution.py:503
  112.6 18.9 %collective-permute-start.17 = (bf16[256,1536]{1,0:T(8,128)(2,1)S(1)}, bf16[256,1536]{1,0:T(8,128)(2,1)S(1)}, u32[]{:S(2)}, u32[]{:S(2)}) collective-permute-start(bf16[256,1536]{1,0:T(8,128)(2,1)S(1)} %get-tuple-element.108), channel_id=1, source_target_pairs={{0,2},{1,3},{2,4},{3,5},{4,6},{5,7},{6,0},{7,1},{8,10},{9,11},{10,... | collective-permute-start | bytes 2359304 | tf_op jit(solution)/shard_map/ppermute | solution.py:483
  113.2 18.3 %collective-permute-start.18 = (bf16[256,1536]{1,0:T(8,128)(2,1)S(1)}, bf16[256,1536]{1,0:T(8,128)(2,1)S(1)}, u32[]{:S(2)}, u32[]{:S(2)}) collective-permute-start(bf16[256,1536]{1,0:T(8,128)(2,1)S(1)} %get-tuple-element.109), channel_id=1, source_target_pairs={{0,6},{1,7},{2,0},{3,1},{4,2},{5,3},{6,4},{7,5},{8,14},{9,15},{10,... | collective-permute-start | bytes 2359304 | tf_op jit(solution)/shard_map/ppermute | solution.py:483
  115.8 5.5 %copy-start.2 = (bf16[3,640,640]{2,1,0:T(8,128)(2,1)S(1)}, bf16[3,640,640]{2,1,0:T(8,128)(2,1)}, u32[]{:S(2)}) copy-start(bf16[3,640,640]{2,1,0:T(8,128)(2,1)} %copy-done.1) | copy-start | bytes 7372804
  116.2 14.2 %collective-permute-start.14 = (bf16[4,96,384]{2,1,0:T(8,128)(2,1)S(1)}, bf16[4,96,384]{2,1,0:T(8,128)(2,1)S(1)}, u32[]{:S(2)}, u32[]{:S(2)}) collective-permute-start(bf16[4,96,384]{2,1,0:T(8,128)(2,1)S(1)} %get-tuple-element.100), channel_id=1, source_target_pairs={{0,64},{8,72},{16,80},{24,88},{32,96},{40,104},{48,112},{56,120},{... | collective-permute-start | bytes 884744 | tf_op jit(solution)/shard_map/ppermute | solution.py:483
  116.7 13.7 %collective-permute-start.15 = (bf16[4,96,384]{2,1,0:T(8,128)(2,1)S(1)}, bf16[4,96,384]{2,1,0:T(8,128)(2,1)S(1)}, u32[]{:S(2)}, u32[]{:S(2)}) collective-permute-start(bf16[4,96,384]{2,1,0:T(8,128)(2,1)S(1)} %get-tuple-element.101), channel_id=1, source_target_pairs={{0,128},{8,136},{16,144},{24,152},{32,160},{40,168},{48,176},{56,1... | collective-permute-start | bytes 884744 | tf_op jit(solution)/shard_map/ppermute | solution.py:483
  120.0 11.1 %collective-permute-start.16 = (bf16[4,96,384]{2,1,0:T(8,128)(2,1)S(1)}, bf16[4,96,384]{2,1,0:T(8,128)(2,1)S(1)}, u32[]{:S(2)}, u32[]{:S(2)}) collective-permute-start(bf16[4,96,384]{2,1,0:T(8,128)(2,1)S(1)} %get-tuple-element.102), channel_id=1, source_target_pairs={{0,192},{8,200},{16,208},{24,216},{32,224},{40,232},{48,240},{56,2... | collective-permute-start | bytes 884744 | tf_op jit(solution)/shard_map/ppermute | solution.py:483
  134.8 60.2 %all-to-all-start.1 = ((bf16[8,3,128,384]{3,2,1,0:T(8,128)(2,1)}), bf16[8,3,128,384]{3,2,1,0:T(8,128)(2,1)S(1)}, u32[]{:S(2)}, u32[]{:S(2)}) async-start(bf16[8,3,128,384]{3,2,1,0:T(8,128)(2,1)} %attention_backward.1), calls=%async_computation.1 | async-start | bytes 4718592 | tf_op jit(solution)/shard_map/all_to_all | solution.py:552
  140.5 34.8 %collective-permute-start.22 = (bf16[128,1536]{1,0:T(8,128)(2,1)S(1)}, bf16[128,1536]{1,0:T(8,128)(2,1)S(1)}, u32[]{:S(2)}, u32[]{:S(2)}) collective-permute-start(bf16[128,1536]{1,0:T(8,128)(2,1)S(1)} %get-tuple-element.124), channel_id=1, source_target_pairs={{0,1},{1,0},{2,3},{3,2},{4,5},{5,4},{6,7},{7,6},{8,9},{9,8},{10,11... | collective-permute-start | bytes 1179656 | tf_op jit(solution)/shard_map/ppermute | solution.py:499
  140.5 39.1 %collective-permute-start.19 = (bf16[96,384]{1,0:T(8,128)(2,1)S(1)}, bf16[96,384]{1,0:T(8,128)(2,1)S(1)}, u32[]{:S(2)}, u32[]{:S(2)}) collective-permute-start(bf16[96,384]{1,0:T(8,128)(2,1)S(1)} %get-tuple-element.120), channel_id=1, source_target_pairs={{0,16},{8,24},{16,32},{24,40},{32,48},{40,56},{48,0},{56,8},{64,80... | collective-permute-start | bytes 221192 | tf_op jit(solution)/shard_map/ppermute | solution.py:483
  144.1 41.4 %collective-permute-start.20 = (bf16[96,384]{1,0:T(8,128)(2,1)S(1)}, bf16[96,384]{1,0:T(8,128)(2,1)S(1)}, u32[]{:S(2)}, u32[]{:S(2)}) collective-permute-start(bf16[96,384]{1,0:T(8,128)(2,1)S(1)} %get-tuple-element.121), channel_id=1, source_target_pairs={{0,32},{8,40},{16,48},{24,56},{32,0},{40,8},{48,16},{56,24},{64,96... | collective-permute-start | bytes 221192 | tf_op jit(solution)/shard_map/ppermute | solution.py:483
  151.2 34.3 %collective-permute-start.21 = (bf16[96,384]{1,0:T(8,128)(2,1)S(1)}, bf16[96,384]{1,0:T(8,128)(2,1)S(1)}, u32[]{:S(2)}, u32[]{:S(2)}) collective-permute-start(bf16[96,384]{1,0:T(8,128)(2,1)S(1)} %get-tuple-element.122), channel_id=1, source_target_pairs={{0,48},{8,56},{16,0},{24,8},{32,16},{40,24},{48,32},{56,40},{64,11... | collective-permute-start | bytes 221192 | tf_op jit(solution)/shard_map/ppermute | solution.py:483
  185.6 9.4 %collective-permute-start.23 = (f32[96,384]{1,0:T(8,128)S(1)}, f32[96,384]{1,0:T(8,128)S(1)}, u32[]{:S(2)}, u32[]{:S(2)}) collective-permute-start(f32[96,384]{1,0:T(8,128)S(1)} %convert_add_fusion), channel_id=1, source_target_pairs={{0,0},{128,1},{2,2},{130,3},{4,4},{132,5},{6,6},{134,7},{8,8},{136... | collective-permute-start | bytes 442376 | tf_op jit(solution)/shard_map/ppermute | solution.py:559
  (6 other events, 5.0 us)
Sparse Core Ops, SparseCore 0:
  15.9 60.1 all-gather.1
